TPU v7x, 256 devices: a whole 4x4x8 slice. The times are simulated.
256 devices in a mesh: rep: 32 (over y, z), shard: 8 (over x, core).
Axes of the slice: x: 4, y: 4, z: 8, core: 2. Of those that a mesh axis runs over, the one named last changes fastest.
Arguments:
- gradient: bfloat16 [32, 1024, 4096], P('rep', None, 'shard'), may hold values from -16 to 16
- feedback: bfloat16 [32, 1024, 4096], P('rep', None, 'shard'), may hold values from -4 to 4
- warm_start: float32 [1024, 64], replicated, may hold values from -6 to 6
- master: float32 [1024, 4096], P('rep', 'shard'), may hold values from -4 to 4
- moment: float32 [1024, 4096], P('rep', 'shard'), may hold values from -1.5 to 1.5
- second: float32 [1024, 4096], P('rep', 'shard'), may hold values from 0.005 to 0.5
Outputs:
- new_feedback: bfloat16 [32, 1024, 4096], P('rep', None, 'shard')
- weights: bfloat16 [1024, 4096], P(None, 'shard')
- master_out: float32 [1024, 4096], P('rep', 'shard')
- moment_out: float32 [1024, 4096], P('rep', 'shard')
- second_out: float32 [1024, 4096], P('rep', 'shard')
- right_factor: float32 [1024, 64], replicated
All inputs are finite; a program needn't handle non-finite values.
Results may differ from a plain program's by a relative error of at most 0.001.
Values may be sent and summed in bfloat16 or wider, within the bound.
No kernel may reach another device: no remote copies, remote signals or barrier semaphores. Data moves between devices by JAX's collectives and lax.ppermute only.
A program may use at most 64 MiB of HBM per device.

v0:
```python
import jax
import jax.numpy as jnp
from jax import lax
from jax.sharding import PartitionSpec as P

HIGHEST = lax.Precision.HIGHEST
beta_one = 0.9
beta_two = 0.95
learn_rate = 0.02
decay_rate = 0.1
adam_eps = 1e-08
ridge_rate = 1e-06


def lower_inverse(gram):
    matrix_order = gram.shape[0]
    identity = jnp.eye(matrix_order, dtype=jnp.float32)
    ridge_term = ridge_rate * jnp.trace(gram) / matrix_order
    cholesky_lower = jnp.linalg.cholesky(gram + ridge_term * identity)
    return jax.scipy.linalg.solve_triangular(cholesky_lower, identity, lower=True)


def contract_first(left, right):
    return lax.dot_general(
        left, right, (((0,), (0,)), ((), ())), precision=HIGHEST, preferred_element_type=jnp.float32
    )


def times_inverse(left, inverse):
    return jnp.dot(left, inverse.T, precision=HIGHEST, preferred_element_type=jnp.float32)


def on_device(gradient, feedback, warm_start, master, moment, second):
    replicas = lax.axis_size("rep")
    merged = gradient[0].astype(jnp.float32) + feedback[0].astype(jnp.float32)
    local_factor = contract_first(merged, warm_start)
    factor = lax.psum(local_factor, "rep") / replicas
    gram_part = contract_first(factor, factor)
    gram = lax.psum(gram_part, "shard")
    inverse = lower_inverse(gram)
    unit_basis = times_inverse(factor, inverse)
    projected = jnp.dot(merged, unit_basis, precision=HIGHEST, preferred_element_type=jnp.float32)
    right_factor = lax.psum(projected, ("rep", "shard")) / replicas
    approx = lax.dot_general(
        right_factor,
        unit_basis,
        (((1,), (1,)), ((), ())),
        precision=HIGHEST,
        preferred_element_type=jnp.float32,
    )
    new_feedback = (merged - approx).astype(jnp.bfloat16)[None]
    own_rows = master.shape[0]
    row_start = lax.axis_index("rep") * own_rows
    grad_rows = lax.dynamic_slice_in_dim(approx, row_start, own_rows, 0)
    moment_out = beta_one * moment + (1.0 - beta_one) * grad_rows
    second_out = beta_two * second + (1.0 - beta_two) * grad_rows * grad_rows
    master_out = master - learn_rate * (
        moment_out / (jnp.sqrt(second_out) + adam_eps) + decay_rate * master
    )
    weights = lax.all_gather(master_out.astype(jnp.bfloat16), "rep", axis=0, tiled=True)
    return (new_feedback, weights, master_out, moment_out, second_out, right_factor)


def solution(mesh):
    return jax.shard_map(
        on_device,
        mesh=mesh,
        in_specs=(
            P("rep", None, "shard"),
            P("rep", None, "shard"),
            P(),
            P("rep", "shard"),
            P("rep", "shard"),
            P("rep", "shard"),
        ),
        out_specs=(
            P("rep", None, "shard"),
            P(None, "shard"),
            P("rep", "shard"),
            P("rep", "shard"),
            P("rep", "shard"),
            P(),
        ),
        check_vma=False,
    )
```

profile of v0, /device:TPU:32, one launch (start us, length us, event | category | flops | bytes accessed | tf_op | source)
XLA Modules:
  0.0 532.4 jit_solution(15276774667782180067)
XLA Ops:
  7.2 0.9 copy-done
  8.1 3.8 fusion.2
  12.0 0.0 all-reduce.5.cloned.1.call-start
  12.0 143.1 %all-reduce.3.cloned.1.call-done = f32[512,64]{0,1:T(8,128)} async-done(((f32[512,64]{0,1:T(8,128)}), f32[512,64]{0,1:T(8,128)}) %all-reduce.3.cloned.1.call-update) | async-done | bytes 131088 | tf_op jit(solution)/shard_map/psum | solution.py:37
  155.2 1.2 fusion.8
  156.4 23.6 %psum.22 = f32[64,64]{1,0:T(8,128)S(1)} all-reduce(f32[64,64]{1,0:T(8,128)S(1)} %fusion.8), channel_id=1, replica_groups=mesh['rep'=32,'shard'=8] {'shard'}, use_global_device_ids=true, to_apply=%region_1.0 | all-reduce | flops 4096 | bytes 32768 | tf_op jit(solution)/shard_map/psum | solution.py:39
  180.0 0.6 select_reduce_fusion.1
  181.3 0.1 copy.12
  181.4 5.8 %cholesky.18 = f32[64,64]{1,0:T(8,128)S(1)} custom-call(f32[64,64]{1,0:T(8,128)S(1)} %fusion.16), custom_call_target="Cholesky" | custom-call | tf_op jit(solution)/shard_map/jit(cholesky)/cholesky | solution.py:19
  187.3 0.6 compare_reduce_fusion
  187.9 0.7 fusion.13
  188.6 4.9 custom-call.7
  193.5 0.2 fusion.14
  193.7 1.2 fusion.6
  194.9 3.0 fusion
  198.0 0.0 all-gather.2.cloned.1.call-start
  198.0 244.4 %all-reduce.5.cloned.1.call-done = f32[1024,64]{0,1:T(8,128)} async-done(((f32[1024,64]{0,1:T(8,128)}), f32[1024,64]{0,1:T(8,128)}) %all-reduce.5.cloned.1.call-update) | async-done | bytes 262160 | tf_op jit(solution)/shard_map/psum | solution.py:43
  442.4 1.0 broadcast_multiply_fusion
  443.4 1.8 fusion.21
  445.2 1.3 copy-done.3
  446.6 0.7 fusion.19
  447.3 3.0 fusion.5
  450.3 73.2 %all-gather.2.cloned.1.call-done = bf16[1024,512]{1,0:T(8,128)(2,1)} async-done(((bf16[32,512]{1,0:T(8,128)(2,1)}), bf16[1024,512]{1,0:T(8,128)(2,1)}) %all-gather.2.cloned.1.call-update) | async-done | bytes 1048592 | tf_op jit(solution)/shard_map/all_gather | solution.py:60
  523.6 2.3 copy.16
  (21 shorter events, 0.2 us)
Async XLA Ops:
  7.2 1.0 copy-start
  7.2 187.7 %copy-start.1 = (bf16[1,1024,512]{2,1,0:T(8,128)(2,1)S(1)}, bf16[1,1024,512]{2,1,0:T(8,128)(2,1)}, u32[]{:S(2)}) copy-start(bf16[1,1024,512]{2,1,0:T(8,128)(2,1)} %param.7) | copy-start | bytes 3145732
  7.2 187.7 %copy-start.2 = (bf16[1,1024,512]{2,1,0:T(8,128)(2,1)S(1)}, bf16[1,1024,512]{2,1,0:T(8,128)(2,1)}, u32[]{:S(2)}) copy-start(bf16[1,1024,512]{2,1,0:T(8,128)(2,1)} %param.6) | copy-start | bytes 3145732
  7.2 148.0 %all-reduce.3.cloned.1.call-start = ((), (), s32[]{:S(2)}) async-start(), calls=%async_computation | async-start | bytes 262144 | tf_op jit(solution)/shard_map/psum | solution.py:37
  12.0 430.4 %all-reduce.5.cloned.1.call-start = ((), (), s32[]{:S(2)}) async-start(), calls=%async_computation.1 | async-start | bytes 524288 | tf_op jit(solution)/shard_map/psum | solution.py:43
  197.9 248.6 %copy-start.5 = (f32[32,512]{1,0:T(8,128)S(1)}, f32[32,512]{1,0:T(8,128)}, u32[]{:S(2)}) copy-start(f32[32,512]{1,0:T(8,128)} %param.9) | copy-start | bytes 196612
  198.0 248.6 %copy-start.6 = (f32[32,512]{1,0:T(8,128)S(1)}, f32[32,512]{1,0:T(8,128)}, u32[]{:S(2)}) copy-start(f32[32,512]{1,0:T(8,128)} %param.11) | copy-start | bytes 196612
  198.0 248.6 %copy-start.7 = (f32[32,512]{1,0:T(8,128)S(1)}, f32[32,512]{1,0:T(8,128)}, u32[]{:S(2)}) copy-start(f32[32,512]{1,0:T(8,128)} %param.10) | copy-start | bytes 196612
  198.0 325.6 %all-gather.2.cloned.1.call-start = ((), (), s32[]{:S(2)}) async-start(), calls=%async_computation.2 | async-start | bytes 1081344 | tf_op jit(solution)/shard_map/all_gather | solution.py:60
  443.4 7.0 %copy-start.4 = (f32[1024,64]{0,1:T(8,128)}, f32[1024,64]{0,1:T(8,128)S(1)}, u32[]{:S(2)}) copy-start(f32[1024,64]{0,1:T(8,128)S(1)} %broadcast_multiply_fusion) | copy-start | bytes 786436
  445.2 1.3 copy-start.3
Sparse Core Ops, SparseCore 0:
  12.1 143.0 all-reduce.2
  198.1 244.2 all-reduce.4
  447.4 76.0 all-gather.1
where the time goes:
time: 534 us; the launch traced here: 532 us
  waiting for transfers between devices  461 us (86%)
  blocking collectives  23.6 us (4%)
  other arithmetic  17.4 us (3%)
  between operations  14.5 us (3%)
  matrix products  11.3 us (2%)
    psum x1, waiting for transfers between devices, on_device(): right_factor = lax.psum(projected, ('rep', 'shard')) / replicas  244 us
    psum x1, waiting for transfers between devices, on_device(): factor = lax.psum(local_factor, 'rep') / replicas  143 us
    all_gather x1, waiting for transfers between devices, on_device(): lax.all_gather(master_out.astype(jnp.bfloat16), 'rep', axis=0, tiled=True)  73.2 us
    psum x1, blocking collectives, on_device(): gram = lax.psum(gram_part, 'shard')  23.6 us
  transfers between devices with their start and end apart: 3, of which 3 were waited for; matrix products, arithmetic and copies ran while one was open for 1% of the time, Pallas kernels for 0%

commit v1 on v0

v1 whole, which is shorter than its diff:
```python
import jax
import jax.numpy as jnp
from jax import lax
from jax.sharding import PartitionSpec as P

HIGHEST = lax.Precision.HIGHEST
beta_one = 0.9
beta_two = 0.95
learn_rate = 0.02
decay_rate = 0.1
adam_eps = 1e-08
ridge_rate = 1e-06


def lower_inverse(gram):
    matrix_order = gram.shape[0]
    identity = jnp.eye(matrix_order, dtype=jnp.float32)
    ridge_term = ridge_rate * jnp.trace(gram) / matrix_order
    cholesky_lower = jnp.linalg.cholesky(gram + ridge_term * identity)
    return jax.scipy.linalg.solve_triangular(cholesky_lower, identity, lower=True)


def contract(left, right, left_dim, right_dim):
    return lax.dot_general(
        left,
        right,
        (((left_dim,), (right_dim,)), ((), ())),
        precision=HIGHEST,
        preferred_element_type=jnp.float32,
    )


def exchange(value, axis, distance):
    return lax.ppermute(value, axis, [(i, i ^ distance) for i in range(lax.axis_size(axis))])


def sum_by_doubling(value, axis):
    distance = 1
    while distance < lax.axis_size(axis):
        value = value + exchange(value, axis, distance)
        distance *= 2
    return value


def start_sum(value, axis):
    return [value] + [exchange(value, axis, d) for d in range(1, lax.axis_size(axis))]


def finish_sum(terms):
    while len(terms) > 1:
        terms = [a + b for a, b in zip(terms[::2], terms[1::2])]
    return terms[0]


def on_device(gradient, feedback, warm_start, master, moment, second):
    replicas = lax.axis_size("rep")
    merged = gradient[0].astype(jnp.float32) + feedback[0].astype(jnp.float32)
    rows, columns = merged.shape
    rank = warm_start.shape[1]
    own_rows = master.shape[0]
    half = own_rows // 2

    factor_t = sum_by_doubling(contract(warm_start, merged, 0, 0), "rep") / replicas
    gram_terms = start_sum(contract(factor_t, factor_t, 1, 1), "shard")

    projected = contract(merged, factor_t, 1, 1)
    packed = projected.reshape(replicas, 2, half, rank).transpose(0, 2, 1, 3)
    packed = packed.reshape(replicas, half, 2 * rank)
    received = lax.all_to_all(packed, "rep", 0, 0, tiled=True)
    own_terms = start_sum(received.sum(0), "shard")

    inverse = lower_inverse(finish_sum(gram_terms))
    unit_t = contract(inverse, factor_t, 1, 0)

    own_packed = finish_sum(own_terms)
    own_projected = jnp.concatenate([own_packed[:, :rank], own_packed[:, rank:]], 0)
    own_right = contract(own_projected, inverse, 1, 1) / replicas
    grad_rows = contract(own_right, unit_t, 1, 0)

    moment_out = beta_one * moment + (1.0 - beta_one) * grad_rows
    second_out = beta_two * second + (1.0 - beta_two) * grad_rows * grad_rows
    master_out = master - learn_rate * (
        moment_out / (jnp.sqrt(second_out) + adam_eps) + decay_rate * master
    )

    high = lax.reduce_precision(own_right, 8, 7)
    low = (own_right - high).astype(jnp.bfloat16)
    extra = own_rows * rank // columns
    block = jnp.concatenate(
        [
            master_out.astype(jnp.bfloat16),
            high.astype(jnp.bfloat16).reshape(extra, columns),
            low.reshape(extra, columns),
        ],
        0,
    )
    blocks = lax.all_to_all(
        jnp.broadcast_to(block[None], (replicas,) + block.shape), "rep", 0, 0, tiled=True
    )
    weights = blocks[:, :own_rows].reshape(rows, columns)
    high_all = blocks[:, own_rows : own_rows + extra].reshape(rows, rank).astype(jnp.float32)
    low_all = blocks[:, own_rows + extra :].reshape(rows, rank).astype(jnp.float32)
    right_factor = high_all + low_all
    approx = contract(right_factor, unit_t, 1, 0)
    new_feedback = (merged - approx).astype(jnp.bfloat16)[None]
    return (new_feedback, weights, master_out, moment_out, second_out, right_factor)


def solution(mesh):
    return jax.shard_map(
        on_device,
        mesh=mesh,
        in_specs=(
            P("rep", None, "shard"),
            P("rep", None, "shard"),
            P(),
            P("rep", "shard"),
            P("rep", "shard"),
            P("rep", "shard"),
        ),
        out_specs=(
            P("rep", None, "shard"),
            P(None, "shard"),
            P("rep", "shard"),
            P("rep", "shard"),
            P("rep", "shard"),
            P(),
        ),
        check_vma=False,
    )
```

time: 534 us -> 141 us (0.26)
  waiting for transfers between devices: 461 us -> 20.8 us
  starting transfers between devices: 0.12 us -> 44.3 us
  blocking collectives: 23.6 us -> 44 us
  between operations: 14.5 us -> 1.56 us
    psum x2 -> x0, waiting for transfers between devices: 387 us -> none  [the longest x1 244 us: on_device(): right_factor = lax.psum(projected, ('rep', 'shard')) / replicas]
    all_gather x1 -> x0, waiting for transfers between devices: 73.2 us -> none  [on_device(): lax.all_gather(master_out.astype(jnp.bfloat16), 'rep', axis=0, tiled=True)]
    all_to_all x0 -> x1, blocking collectives: none -> 44 us  [on_device(): lax.all_to_all(jnp.broadcast_to(block[None], (replicas,) + block.shape),...]
    ppermute x0 -> x19, starting transfers between devices: none -> 31.4 us  [exchange(): lax.ppermute(value, axis, [(i, i ^ distance) for i in range(lax.axis_size...]
    psum x1 -> x0, blocking collectives: 23.6 us -> none  [on_device(): gram = lax.psum(gram_part, 'shard')]
    ppermute x0 -> x19, waiting for transfers between devices: none -> 20.7 us  [exchange(): lax.ppermute(value, axis, [(i, i ^ distance) for i in range(lax.axis_size...]
    all_to_all x0 -> x1, starting transfers between devices: none -> 12.9 us  [on_device(): received = lax.all_to_all(packed, 'rep', 0, 0, tiled=True)]
    dot_general x5 -> x7, matrix products: 11.1 us -> 9.4 us  [contract(): lax.dot_general(left, right, (((left_dim,), (right_dim,)), ((), ())), pre...]
  transfers between devices with their start and end apart: 3 -> 20, of which waited for: 3 -> 8; matrix products, arithmetic and copies ran while one was open for 1% -> 12% of each run, Pallas kernels for 0% -> 0%
where the time goes in v1:
time: 141 us; the launch traced here: 140 us
  starting transfers between devices  44.3 us (31%)
  blocking collectives  44 us (31%)
  waiting for transfers between devices  20.8 us (15%)
  other arithmetic  14 us (10%)
  matrix products  9.61 us (7%)
  local copies, waits for them, and re-layouts  5.93 us (4%)
  between operations  1.56 us (1%)
    all_to_all x1, blocking collectives, on_device(): lax.all_to_all(jnp.broadcast_to(block[None], (replicas,) + block.shape),...  44 us
    ppermute x19, starting transfers between devices, exchange(): lax.ppermute(value, axis, [(i, i ^ distance) for i in range(lax.axis_size...  31.4 us
    ppermute x19, waiting for transfers between devices, exchange(): lax.ppermute(value, axis, [(i, i ^ distance) for i in range(lax.axis_size...  20.7 us
    all_to_all x1, starting transfers between devices, on_device(): received = lax.all_to_all(packed, 'rep', 0, 0, tiled=True)  12.9 us
    dot_general x7, matrix products, contract(): lax.dot_general(left, right, (((left_dim,), (right_dim,)), ((), ())), pre...  9.4 us
    another operation x3, other arithmetic, lower_inverse(): cholesky_lower = jnp.linalg.cholesky(gram + ridge_term * identity)  6.52 us
    another operation x2, other arithmetic, lower_inverse(): jax.scipy.linalg.solve_triangular(cholesky_lower, identity, lower=True)  5.55 us
    unnamed x17, local copies, waits for them, and re-layouts  2.93 us
  transfers between devices with their start and end apart: 20, of which 8 were waited for; matrix products, arithmetic and copies ran while one was open for 12% of the time, Pallas kernels for 0%

profile of v1, /device:TPU:32, one launch (start us, length us, event | category | flops | bytes accessed | tf_op | source)
XLA Modules:
  0.0 140.2 jit_solution(12727946524859878259)
XLA Ops:
  1.6 3.2 %fusion.4 = f32[64,512]{1,0:T(8,128)S(1)} fusion(f32[1024,64]{0,1:T(8,128)S(1)} %copy-done, bf16[1,1024,512]{2,1,0:T(8,128)(2,1)} %param.7, bf16[1,1024,512]{2,1,0:T(8,128)(2,1)} %param.6), kind=kOutput, calls=%fused_computation.7 | convolution fusion | flops 404226048 | bytes 2490368 | tf_op jit(solution)/shard_map/dot_general | solution.py:24
  4.8 1.9 %collective-permute-start = (f32[64,512]{1,0:T(8,128)S(1)}, f32[64,512]{1,0:T(8,128)S(1)}, u32[]{:S(2)}, u32[]{:S(2)}) collective-permute-start(f32[64,512]{1,0:T(8,128)S(1)} %fusion.4), channel_id=1, source_target_pairs={{0,8},{8,0},{16,24},{24,16},{32,40},{40,32},{48,56},{56,48},{64,72... | collective-permute-start | bytes 393224 | tf_op jit(solution)/shard_map/ppermute | solution.py:34
  6.7 3.4 %collective-permute-done = f32[64,512]{1,0:T(8,128)S(1)} collective-permute-done((f32[64,512]{1,0:T(8,128)S(1)}, f32[64,512]{1,0:T(8,128)S(1)}, u32[]{:S(2)}, u32[]{:S(2)}) %collective-permute-start) | collective-permute-done | bytes 131104 | tf_op jit(solution)/shard_map/ppermute | solution.py:34
  10.1 3.4 %collective-permute-start.1 = (f32[64,512]{1,0:T(8,128)S(1)}, f32[64,512]{1,0:T(8,128)S(1)}, u32[]{:S(2)}, u32[]{:S(2)}) collective-permute-start(f32[64,512]{1,0:T(8,128)S(1)} %add.106), channel_id=1, source_target_pairs={{0,16},{8,24},{16,0},{24,8},{32,48},{40,56},{48,32},{56,40},{64,80... | collective-permute-start | bytes 393224 | tf_op jit(solution)/shard_map/ppermute | solution.py:34
  13.5 4.6 %collective-permute-done.1 = f32[64,512]{1,0:T(8,128)S(1)} collective-permute-done((f32[64,512]{1,0:T(8,128)S(1)}, f32[64,512]{1,0:T(8,128)S(1)}, u32[]{:S(2)}, u32[]{:S(2)}) %collective-permute-start.1) | collective-permute-done | bytes 131104 | tf_op jit(solution)/shard_map/ppermute | solution.py:34
  18.1 4.7 %collective-permute-start.2 = (f32[64,512]{1,0:T(8,128)S(1)}, f32[64,512]{1,0:T(8,128)S(1)}, u32[]{:S(2)}, u32[]{:S(2)}) collective-permute-start(f32[64,512]{1,0:T(8,128)S(1)} %add.107), channel_id=1, source_target_pairs={{0,32},{8,40},{16,48},{24,56},{32,0},{40,8},{48,16},{56,24},{64,96... | collective-permute-start | bytes 393224 | tf_op jit(solution)/shard_map/ppermute | solution.py:34
  22.8 4.5 %collective-permute-done.2 = f32[64,512]{1,0:T(8,128)S(1)} collective-permute-done((f32[64,512]{1,0:T(8,128)S(1)}, f32[64,512]{1,0:T(8,128)S(1)}, u32[]{:S(2)}, u32[]{:S(2)}) %collective-permute-start.2) | collective-permute-done | bytes 131104 | tf_op jit(solution)/shard_map/ppermute | solution.py:34
  27.3 1.7 %collective-permute-start.3 = (f32[64,512]{1,0:T(8,128)S(1)}, f32[64,512]{1,0:T(8,128)S(1)}, u32[]{:S(2)}, u32[]{:S(2)}) collective-permute-start(f32[64,512]{1,0:T(8,128)S(1)} %add.108), channel_id=1, source_target_pairs={{0,64},{8,72},{16,80},{24,88},{32,96},{40,104},{48,112},{56,120},{... | collective-permute-start | bytes 393224 | tf_op jit(solution)/shard_map/ppermute | solution.py:34
  28.9 3.4 %collective-permute-done.3 = f32[64,512]{1,0:T(8,128)S(1)} collective-permute-done((f32[64,512]{1,0:T(8,128)S(1)}, f32[64,512]{1,0:T(8,128)S(1)}, u32[]{:S(2)}, u32[]{:S(2)}) %collective-permute-start.3) | collective-permute-done | bytes 131104 | tf_op jit(solution)/shard_map/ppermute | solution.py:34
  32.4 3.3 %collective-permute-start.4 = (f32[64,512]{1,0:T(8,128)S(1)}, f32[64,512]{1,0:T(8,128)S(1)}, u32[]{:S(2)}, u32[]{:S(2)}) collective-permute-start(f32[64,512]{1,0:T(8,128)S(1)} %add.109), channel_id=1, source_target_pairs={{0,128},{8,136},{16,144},{24,152},{32,160},{40,168},{48,176},{56,1... | collective-permute-start | bytes 393224 | tf_op jit(solution)/shard_map/ppermute | solution.py:34
  35.6 3.3 %collective-permute-done.4 = f32[64,512]{1,0:T(8,128)S(1)} collective-permute-done((f32[64,512]{1,0:T(8,128)S(1)}, f32[64,512]{1,0:T(8,128)S(1)}, u32[]{:S(2)}, u32[]{:S(2)}) %collective-permute-start.4) | collective-permute-done | bytes 131104 | tf_op jit(solution)/shard_map/ppermute | solution.py:34
  39.3 2.8 %collective-permute-start.17 = (f32[64,64]{1,0:T(8,128)S(1)}, f32[64,64]{1,0:T(8,128)S(1)}, u32[]{:S(2)}, u32[]{:S(2)}) collective-permute-start(f32[64,64]{1,0:T(8,128)S(1)} %fusion.19), channel_id=1, source_target_pairs={{0,6},{1,7},{2,4},{3,5},{4,2},{5,3},{6,0},{7,1},{8,14},{9,15},{10,... | collective-permute-start | bytes 49160 | tf_op jit(solution)/shard_map/ppermute | solution.py:34
  42.4 1.7 %collective-permute-start.16 = (f32[64,64]{1,0:T(8,128)S(1)}, f32[64,64]{1,0:T(8,128)S(1)}, u32[]{:S(2)}, u32[]{:S(2)}) collective-permute-start(f32[64,64]{1,0:T(8,128)S(1)} %fusion.19), channel_id=1, source_target_pairs={{0,5},{1,4},{2,7},{3,6},{4,1},{5,0},{6,3},{7,2},{8,13},{9,12},{10,... | collective-permute-start | bytes 49160 | tf_op jit(solution)/shard_map/ppermute | solution.py:34
  44.1 1.7 %collective-permute-start.15 = (f32[64,64]{1,0:T(8,128)S(1)}, f32[64,64]{1,0:T(8,128)S(1)}, u32[]{:S(2)}, u32[]{:S(2)}) collective-permute-start(f32[64,64]{1,0:T(8,128)S(1)} %fusion.19), channel_id=1, source_target_pairs={{0,4},{1,5},{2,6},{3,7},{4,0},{5,1},{6,2},{7,3},{8,12},{9,13},{10,... | collective-permute-start | bytes 49160 | tf_op jit(solution)/shard_map/ppermute | solution.py:34
  45.9 1.6 %collective-permute-start.13 = (f32[64,64]{1,0:T(8,128)S(1)}, f32[64,64]{1,0:T(8,128)}, u32[]{:S(2)}, u32[]{:S(2)}) collective-permute-start(f32[64,64]{1,0:T(8,128)S(1)} %fusion.19), channel_id=1, source_target_pairs={{0,2},{1,3},{2,0},{3,1},{4,6},{5,7},{6,4},{7,5},{8,10},{9,11},{10,... | collective-permute-start | bytes 49160 | tf_op jit(solution)/shard_map/ppermute | solution.py:34
  47.8 1.8 %convolution_bitcast_fusion = f32[32,16,2,64]{3,1,2,0:T(8,128)S(1)} fusion(f32[32,2,16,512]{3,2,1,0:T(8,128)S(1)} %bitcast.40, f32[64,512]{1,0:T(8,128)S(1)} %add.109, f32[64,512]{1,0:T(8,128)S(1)} %collective-permute-done.4), kind=kOutput, calls=%fused_computation.6 | convolution fusion | flops 402718720 | bytes 2621440 | tf_op jit(solution)/shard_map/dot_general | solution.py:24
  50.9 12.9 %all-to-all-start = ((f32[32,16,128]{2,1,0:T(8,128)}), f32[32,16,128]{2,1,0:T(8,128)S(1)}, u32[]{:S(2)}, u32[]{:S(2)}) async-start(f32[32,16,128]{2,1,0:T(8,128)} %reshape.50), calls=%async_computation | async-start | bytes 524288 | tf_op jit(solution)/shard_map/all_to_all | solution.py:69
  66.1 5.8 %cholesky.18 = f32[64,64]{1,0:T(8,128)S(1)} custom-call(f32[64,64]{1,0:T(8,128)S(1)} %fusion.12), custom_call_target="Cholesky" | custom-call | tf_op jit(solution)/shard_map/jit(cholesky)/cholesky | solution.py:19
  73.3 4.9 %custom-call.7 = f32[1,64,64]{1,2,0:T(8,128)S(1)} custom-call(f32[1,64,64]{2,1,0:T(8,128)S(1)} %fusion.9), custom_call_target="InvertDiagBlocksLowerTriangular" | custom-call | tf_op jit(solution)/shard_map/jit(_solve_triangular)/triangular_solve | solution.py:20
  78.2 1.9 %collective-permute-start.11 = (f32[16,128]{1,0:T(8,128)S(1)}, f32[16,128]{1,0:T(8,128)S(1)}, u32[]{:S(2)}, u32[]{:S(2)}) collective-permute-start(f32[16,128]{1,0:T(8,128)S(1)} %reduce_sum.19), channel_id=1, source_target_pairs={{0,7},{1,6},{2,5},{3,4},{4,3},{5,2},{6,1},{7,0},{8,15},{9,14},{10,... | collective-permute-start | bytes 24584 | tf_op jit(solution)/shard_map/ppermute | solution.py:34
  82.7 2.2 %collective-permute-start.8 = (f32[16,128]{1,0:T(8,128)S(1)}, f32[16,128]{1,0:T(8,128)S(1)}, u32[]{:S(2)}, u32[]{:S(2)}) collective-permute-start(f32[16,128]{1,0:T(8,128)S(1)} %reduce_sum.19), channel_id=1, source_target_pairs={{0,4},{1,5},{2,6},{3,7},{4,0},{5,1},{6,2},{7,3},{8,12},{9,13},{10,... | collective-permute-start | bytes 24584 | tf_op jit(solution)/shard_map/ppermute | solution.py:34
  84.8 1.7 %collective-permute-start.6 = (f32[16,128]{1,0:T(8,128)S(1)}, f32[16,128]{1,0:T(8,128)S(1)}, u32[]{:S(2)}, u32[]{:S(2)}) collective-permute-start(f32[16,128]{1,0:T(8,128)S(1)} %reduce_sum.19), channel_id=1, source_target_pairs={{0,2},{1,3},{2,0},{3,1},{4,6},{5,7},{6,4},{7,5},{8,10},{9,11},{10,... | collective-permute-start | bytes 24584 | tf_op jit(solution)/shard_map/ppermute | solution.py:34
  90.0 44.0 %all_to_all.10 = bf16[32,40,512]{2,1,0:T(8,128)(2,1)S(1)} all-to-all(bf16[32,40,512]{2,1,0:T(8,128)(2,1)S(1)} %broadcast_in_dim.16), channel_id=1, replica_groups=mesh['rep'=32,'shard'=8] {'rep'}, dimensions={0} | all-to-all | bytes 2621440 | tf_op jit(solution)/shard_map/all_to_all | solution.py:97
  136.2 2.8 %fusion.3 = bf16[1,1024,512]{2,1,0:T(8,128)(2,1)} fusion(f32[1024,64]{1,0:T(8,128)S(1)} %add.133, f32[64,512]{1,0:T(8,128)S(1)} %fusion.18, bf16[1,1024,512]{2,1,0:T(8,128)(2,1)S(1)} %copy-done.1, bf16[1,1024,512]{2,1,0:T(8,128)(2,1)S(1)} %copy-done.2), kind=kOutput, calls=%fused_computation.5 | convolution fusion | flops 405274624 | bytes 3538944 | tf_op jit(solution)/shard_map/dot_general | solution.py:24
  (68 shorter events, 15.4 us)
Async XLA Ops:
  0.6 41.5 %copy-start.1 = (bf16[1,1024,512]{2,1,0:T(8,128)(2,1)S(1)}, bf16[1,1024,512]{2,1,0:T(8,128)(2,1)}, u32[]{:S(2)}) copy-start(bf16[1,1024,512]{2,1,0:T(8,128)(2,1)} %param.7) | copy-start | bytes 3145732
  0.7 41.5 %copy-start.2 = (bf16[1,1024,512]{2,1,0:T(8,128)(2,1)S(1)}, bf16[1,1024,512]{2,1,0:T(8,128)(2,1)}, u32[]{:S(2)}) copy-start(bf16[1,1024,512]{2,1,0:T(8,128)(2,1)} %param.6) | copy-start | bytes 3145732
  4.8 5.3 %collective-permute-start = (f32[64,512]{1,0:T(8,128)S(1)}, f32[64,512]{1,0:T(8,128)S(1)}, u32[]{:S(2)}, u32[]{:S(2)}) collective-permute-start(f32[64,512]{1,0:T(8,128)S(1)} %fusion.4), channel_id=1, source_target_pairs={{0,8},{8,0},{16,24},{24,16},{32,40},{40,32},{48,56},{56,48},{64,72... | collective-permute-start | bytes 393224 | tf_op jit(solution)/shard_map/ppermute | solution.py:34
  10.1 8.0 %collective-permute-start.1 = (f32[64,512]{1,0:T(8,128)S(1)}, f32[64,512]{1,0:T(8,128)S(1)}, u32[]{:S(2)}, u32[]{:S(2)}) collective-permute-start(f32[64,512]{1,0:T(8,128)S(1)} %add.106), channel_id=1, source_target_pairs={{0,16},{8,24},{16,0},{24,8},{32,48},{40,56},{48,32},{56,40},{64,80... | collective-permute-start | bytes 393224 | tf_op jit(solution)/shard_map/ppermute | solution.py:34
  18.1 9.1 %collective-permute-start.2 = (f32[64,512]{1,0:T(8,128)S(1)}, f32[64,512]{1,0:T(8,128)S(1)}, u32[]{:S(2)}, u32[]{:S(2)}) collective-permute-start(f32[64,512]{1,0:T(8,128)S(1)} %add.107), channel_id=1, source_target_pairs={{0,32},{8,40},{16,48},{24,56},{32,0},{40,8},{48,16},{56,24},{64,96... | collective-permute-start | bytes 393224 | tf_op jit(solution)/shard_map/ppermute | solution.py:34
  27.3 5.1 %collective-permute-start.3 = (f32[64,512]{1,0:T(8,128)S(1)}, f32[64,512]{1,0:T(8,128)S(1)}, u32[]{:S(2)}, u32[]{:S(2)}) collective-permute-start(f32[64,512]{1,0:T(8,128)S(1)} %add.108), channel_id=1, source_target_pairs={{0,64},{8,72},{16,80},{24,88},{32,96},{40,104},{48,112},{56,120},{... | collective-permute-start | bytes 393224 | tf_op jit(solution)/shard_map/ppermute | solution.py:34
  32.4 6.6 %collective-permute-start.4 = (f32[64,512]{1,0:T(8,128)S(1)}, f32[64,512]{1,0:T(8,128)S(1)}, u32[]{:S(2)}, u32[]{:S(2)}) collective-permute-start(f32[64,512]{1,0:T(8,128)S(1)} %add.109), channel_id=1, source_target_pairs={{0,128},{8,136},{16,144},{24,152},{32,160},{40,168},{48,176},{56,1... | collective-permute-start | bytes 393224 | tf_op jit(solution)/shard_map/ppermute | solution.py:34
  39.2 6.7 %collective-permute-start.18 = (f32[64,64]{1,0:T(8,128)S(1)}, f32[64,64]{1,0:T(8,128)S(1)}, u32[]{:S(2)}, u32[]{:S(2)}) collective-permute-start(f32[64,64]{1,0:T(8,128)S(1)} %fusion.19), channel_id=1, source_target_pairs={{0,7},{1,6},{2,5},{3,4},{4,3},{5,2},{6,1},{7,0},{8,15},{9,14},{10,... | collective-permute-start | bytes 49160 | tf_op jit(solution)/shard_map/ppermute | solution.py:34
  39.3 8.2 %collective-permute-start.17 = (f32[64,64]{1,0:T(8,128)S(1)}, f32[64,64]{1,0:T(8,128)S(1)}, u32[]{:S(2)}, u32[]{:S(2)}) collective-permute-start(f32[64,64]{1,0:T(8,128)S(1)} %fusion.19), channel_id=1, source_target_pairs={{0,6},{1,7},{2,4},{3,5},{4,2},{5,3},{6,0},{7,1},{8,14},{9,15},{10,... | collective-permute-start | bytes 49160 | tf_op jit(solution)/shard_map/ppermute | solution.py:34
  42.4 21.4 %collective-permute-start.16 = (f32[64,64]{1,0:T(8,128)S(1)}, f32[64,64]{1,0:T(8,128)S(1)}, u32[]{:S(2)}, u32[]{:S(2)}) collective-permute-start(f32[64,64]{1,0:T(8,128)S(1)} %fusion.19), channel_id=1, source_target_pairs={{0,5},{1,4},{2,7},{3,6},{4,1},{5,0},{6,3},{7,2},{8,13},{9,12},{10,... | collective-permute-start | bytes 49160 | tf_op jit(solution)/shard_map/ppermute | solution.py:34
  44.1 19.7 %collective-permute-start.15 = (f32[64,64]{1,0:T(8,128)S(1)}, f32[64,64]{1,0:T(8,128)S(1)}, u32[]{:S(2)}, u32[]{:S(2)}) collective-permute-start(f32[64,64]{1,0:T(8,128)S(1)} %fusion.19), channel_id=1, source_target_pairs={{0,4},{1,5},{2,6},{3,7},{4,0},{5,1},{6,2},{7,3},{8,12},{9,13},{10,... | collective-permute-start | bytes 49160 | tf_op jit(solution)/shard_map/ppermute | solution.py:34
  45.9 18.0 %collective-permute-start.14 = (f32[64,64]{1,0:T(8,128)S(1)}, f32[64,64]{1,0:T(8,128)S(1)}, u32[]{:S(2)}, u32[]{:S(2)}) collective-permute-start(f32[64,64]{1,0:T(8,128)S(1)} %fusion.19), channel_id=1, source_target_pairs={{0,3},{1,2},{2,1},{3,0},{4,7},{5,6},{6,5},{7,4},{8,11},{9,10},{10,... | collective-permute-start | bytes 49160 | tf_op jit(solution)/shard_map/ppermute | solution.py:34
  45.9 18.0 %collective-permute-start.13 = (f32[64,64]{1,0:T(8,128)S(1)}, f32[64,64]{1,0:T(8,128)}, u32[]{:S(2)}, u32[]{:S(2)}) collective-permute-start(f32[64,64]{1,0:T(8,128)S(1)} %fusion.19), channel_id=1, source_target_pairs={{0,2},{1,3},{2,0},{3,1},{4,6},{5,7},{6,4},{7,5},{8,10},{9,11},{10,... | collective-permute-start | bytes 49160 | tf_op jit(solution)/shard_map/ppermute | solution.py:34
  47.5 16.4 %collective-permute-start.12 = (f32[64,64]{1,0:T(8,128)S(1)}, f32[64,64]{1,0:T(8,128)}, u32[]{:S(2)}, u32[]{:S(2)}) collective-permute-start(f32[64,64]{1,0:T(8,128)S(1)} %fusion.19), channel_id=1, source_target_pairs={{0,1},{1,0},{2,3},{3,2},{4,5},{5,4},{6,7},{7,6},{8,9},{9,8},{10,11... | collective-permute-start | bytes 49160 | tf_op jit(solution)/shard_map/ppermute | solution.py:34
  49.6 39.4 %copy-start.5 = (f32[32,512]{1,0:T(8,128)S(1)}, f32[32,512]{1,0:T(8,128)}, u32[]{:S(2)}) copy-start(f32[32,512]{1,0:T(8,128)} %param.9) | copy-start | bytes 196612
  49.6 39.4 %copy-start.6 = (f32[32,512]{1,0:T(8,128)S(1)}, f32[32,512]{1,0:T(8,128)}, u32[]{:S(2)}) copy-start(f32[32,512]{1,0:T(8,128)} %param.11) | copy-start | bytes 196612
  50.9 27.3 %all-to-all-start = ((f32[32,16,128]{2,1,0:T(8,128)}), f32[32,16,128]{2,1,0:T(8,128)S(1)}, u32[]{:S(2)}, u32[]{:S(2)}) async-start(f32[32,16,128]{2,1,0:T(8,128)} %reshape.50), calls=%async_computation | async-start | bytes 524288 | tf_op jit(solution)/shard_map/all_to_all | solution.py:69
  78.2 6.6 %collective-permute-start.11 = (f32[16,128]{1,0:T(8,128)S(1)}, f32[16,128]{1,0:T(8,128)S(1)}, u32[]{:S(2)}, u32[]{:S(2)}) collective-permute-start(f32[16,128]{1,0:T(8,128)S(1)} %reduce_sum.19), channel_id=1, source_target_pairs={{0,7},{1,6},{2,5},{3,4},{4,3},{5,2},{6,1},{7,0},{8,15},{9,14},{10,... | collective-permute-start | bytes 24584 | tf_op jit(solution)/shard_map/ppermute | solution.py:34
  80.1 6.4 %collective-permute-start.10 = (f32[16,128]{1,0:T(8,128)S(1)}, f32[16,128]{1,0:T(8,128)S(1)}, u32[]{:S(2)}, u32[]{:S(2)}) collective-permute-start(f32[16,128]{1,0:T(8,128)S(1)} %reduce_sum.19), channel_id=1, source_target_pairs={{0,6},{1,7},{2,4},{3,5},{4,2},{5,3},{6,0},{7,1},{8,14},{9,15},{10,... | collective-permute-start | bytes 24584 | tf_op jit(solution)/shard_map/ppermute | solution.py:34
  81.4 5.6 %collective-permute-start.9 = (f32[16,128]{1,0:T(8,128)S(1)}, f32[16,128]{1,0:T(8,128)S(1)}, u32[]{:S(2)}, u32[]{:S(2)}) collective-permute-start(f32[16,128]{1,0:T(8,128)S(1)} %reduce_sum.19), channel_id=1, source_target_pairs={{0,5},{1,4},{2,7},{3,6},{4,1},{5,0},{6,3},{7,2},{8,13},{9,12},{10,... | collective-permute-start | bytes 24584 | tf_op jit(solution)/shard_map/ppermute | solution.py:34
  82.7 5.2 %collective-permute-start.8 = (f32[16,128]{1,0:T(8,128)S(1)}, f32[16,128]{1,0:T(8,128)S(1)}, u32[]{:S(2)}, u32[]{:S(2)}) collective-permute-start(f32[16,128]{1,0:T(8,128)S(1)} %reduce_sum.19), channel_id=1, source_target_pairs={{0,4},{1,5},{2,6},{3,7},{4,0},{5,1},{6,2},{7,3},{8,12},{9,13},{10,... | collective-permute-start | bytes 24584 | tf_op jit(solution)/shard_map/ppermute | solution.py:34
  84.8 3.1 %collective-permute-start.7 = (f32[16,128]{1,0:T(8,128)S(1)}, f32[16,128]{1,0:T(8,128)S(1)}, u32[]{:S(2)}, u32[]{:S(2)}) collective-permute-start(f32[16,128]{1,0:T(8,128)S(1)} %reduce_sum.19), channel_id=1, source_target_pairs={{0,3},{1,2},{2,1},{3,0},{4,7},{5,6},{6,5},{7,4},{8,11},{9,10},{10,... | collective-permute-start | bytes 24584 | tf_op jit(solution)/shard_map/ppermute | solution.py:34
  84.8 3.7 %collective-permute-start.6 = (f32[16,128]{1,0:T(8,128)S(1)}, f32[16,128]{1,0:T(8,128)S(1)}, u32[]{:S(2)}, u32[]{:S(2)}) collective-permute-start(f32[16,128]{1,0:T(8,128)S(1)} %reduce_sum.19), channel_id=1, source_target_pairs={{0,2},{1,3},{2,0},{3,1},{4,6},{5,7},{6,4},{7,5},{8,10},{9,11},{10,... | collective-permute-start | bytes 24584 | tf_op jit(solution)/shard_map/ppermute | solution.py:34
  86.5 2.0 %collective-permute-start.5 = (f32[16,128]{1,0:T(8,128)S(1)}, f32[16,128]{1,0:T(8,128)S(1)}, u32[]{:S(2)}, u32[]{:S(2)}) collective-permute-start(f32[16,128]{1,0:T(8,128)S(1)} %reduce_sum.19), channel_id=1, source_target_pairs={{0,1},{1,0},{2,3},{3,2},{4,5},{5,4},{6,7},{7,6},{8,9},{9,8},{10,11... | collective-permute-start | bytes 24584 | tf_op jit(solution)/shard_map/ppermute | solution.py:34
  (4 other events, 44.3 us)

commit v2 on v0

v2 whole, which is shorter than its diff:
```python
import jax
import jax.numpy as jnp
from jax import lax
from jax.experimental import pallas as pl
from jax.experimental.pallas import tpu as pltpu
from jax.sharding import PartitionSpec as P

HIGHEST = lax.Precision.HIGHEST
beta_one = 0.9
beta_two = 0.95
learn_rate = 0.02
decay_rate = 0.1
adam_eps = 1e-08
ridge_rate = 1e-06

F32 = jnp.float32
BF16 = jnp.bfloat16
Y_SIZE, Z_SIZE = 4, 8
Y_STEPS = (8, 16, 24)
X_STEPS = (2, 4, 6)


def exact(left, right, left_dim, right_dim):
    return lax.dot_general(
        left,
        right,
        (((left_dim,), (right_dim,)), ((), ())),
        precision=HIGHEST,
        preferred_element_type=F32,
    )


def native(left, right, left_dim, right_dim):
    return lax.dot_general(
        left, right, (((left_dim,), (right_dim,)), ((), ())), preferred_element_type=F32
    )


def three_parts(value):
    high = value.astype(BF16)
    rest = value - high.astype(F32)
    middle = rest.astype(BF16)
    return high, middle, (rest - middle.astype(F32)).astype(BF16)


def exchange(value, axis, distance):
    return lax.ppermute(value, axis, [(i, i ^ distance) for i in range(lax.axis_size(axis))])


def sum_four(terms):
    return (terms[0] + terms[1]) + (terms[2] + terms[3])


def shard_sum(value):
    value = value + exchange(value, "shard", 1)
    return sum_four([value] + [exchange(value, "shard", d) for d in X_STEPS])


def whole(shape):
    return pl.BlockSpec(shape, lambda *_: (0,) * len(shape))


def near(*values):
    return [pltpu.with_memory_space_constraint(v, pltpu.VMEM) for v in values]


def factor_kernel(rep_ref, warm_ref, grad_ref, feed_ref, *refs):
    outs, parts_ref = refs[:-1], refs[-1]
    rank = warm_ref.shape[0]
    step = pl.program_id(0)

    @pl.when(step == 0)
    def _():
        for i, part in enumerate(three_parts(warm_ref[...])):
            parts_ref[i * rank : (i + 1) * rank, :] = part

    total = native(parts_ref[...], grad_ref[...], 1, 0) + native(parts_ref[...], feed_ref[...], 1, 0)
    total = (total[2 * rank :] + total[rank : 2 * rank]) + total[:rank]
    for i, out in enumerate(outs):

        @pl.when(step == i)
        def _(out=out):
            out[...] = total


def local_factor(rep, warm_t, gradient, feedback):
    rank, rows = warm_t.shape
    quarter = gradient.shape[1] // Y_SIZE
    column_block = pl.BlockSpec((rows, quarter), lambda d, rep: (0, (rep[0] // Z_SIZE) ^ d))
    return pl.pallas_call(
        factor_kernel,
        out_shape=[pltpu.VMEM((rank, quarter), F32)] * Y_SIZE,
        grid_spec=pltpu.PrefetchScalarGridSpec(
            num_scalar_prefetch=1,
            grid=(Y_SIZE,),
            in_specs=[whole((rank, rows)), column_block, column_block],
            out_specs=[whole((rank, quarter))] * Y_SIZE,
            scratch_shapes=[pltpu.VMEM((3 * rank, rows), BF16)],
        ),
        cost_estimate=pl.CostEstimate(flops=2_000_000_000, bytes_accessed=2_500_000, transcendentals=0),
        name="local_factor",
    )(rep, warm_t, gradient, feedback)


def assemble_kernel(rep_ref, *refs):
    quarters, (factor_ref, parts_ref, gram_ref) = refs[:Y_SIZE], refs[Y_SIZE:]
    rank, quarter = quarters[0].shape
    own = rep_ref[0] // Z_SIZE
    for d, block in enumerate(quarters):
        at = pl.ds(pl.multiple_of((own ^ d) * quarter, quarter), quarter)
        factor_ref[:, at] = block[...]
    factor = factor_ref[...]
    for i, part in enumerate(three_parts(factor)):
        parts_ref[i * rank : (i + 1) * rank, :] = part
    gram_ref[...] = exact(factor, factor, 1, 1)


def assemble(rep, quarters):
    rank, quarter = quarters[0].shape
    columns = quarter * Y_SIZE
    shapes = [(rank, columns), (3 * rank, columns), (rank, rank)]
    types = [F32, BF16, F32]
    return pl.pallas_call(
        assemble_kernel,
        out_shape=[pltpu.VMEM(s, t) for s, t in zip(shapes, types)],
        grid_spec=pltpu.PrefetchScalarGridSpec(
            num_scalar_prefetch=1,
            grid=(1,),
            in_specs=[whole((rank, quarter))] * Y_SIZE,
            out_specs=[whole(s) for s in shapes],
        ),
        cost_estimate=pl.CostEstimate(flops=100_000_000, bytes_accessed=500_000, transcendentals=0),
        name="assemble_factor",
    )(rep, *near(*quarters))


def project_kernel(grad_ref, feed_ref, parts_ref, out_ref):
    groups, half, _ = out_ref.shape
    rank = parts_ref.shape[0] // 3
    parts = parts_ref[...]
    total = native(grad_ref[...], parts, 1, 1) + native(feed_ref[...], parts, 1, 1)
    value = (total[:, 2 * rank :] + total[:, rank : 2 * rank]) + total[:, :rank]
    value = value.reshape(groups, 2, half, rank)
    out_ref[...] = jnp.concatenate([value[:, 0], value[:, 1]], axis=-1)


def project(gradient, feedback, parts, replicas):
    rows, columns = gradient.shape
    rank = parts.shape[0] // 3
    half = rows // replicas // 2
    steps = 4
    row_block = pl.BlockSpec((rows // steps, columns), lambda i: (i, 0))
    return pl.pallas_call(
        project_kernel,
        out_shape=jax.ShapeDtypeStruct((replicas, half, 2 * rank), F32),
        grid=(steps,),
        in_specs=[row_block, row_block, whole(parts.shape)],
        out_specs=pl.BlockSpec((replicas // steps, half, 2 * rank), lambda i: (i, 0, 0)),
        cost_estimate=pl.CostEstimate(flops=2_000_000_000, bytes_accessed=2_500_000, transcendentals=0),
        name="project",
    )(gradient, feedback, *near(parts))


def inverse_kernel(gram_ref, factor_ref, inverse_ref, unit_ref):
    rank = gram_ref.shape[0]
    row = lax.broadcasted_iota(jnp.int32, (rank, rank), 0)
    column = lax.broadcasted_iota(jnp.int32, (rank, rank), 1)
    diagonal = row == column
    gram = gram_ref[...]
    trace = jnp.sum(jnp.where(diagonal, gram, 0.0))
    gram = gram + jnp.where(diagonal, ridge_rate * trace / rank, 0.0)
    table = jnp.concatenate([gram, jnp.where(diagonal, 1.0, 0.0)], axis=1)
    row_index = lax.broadcasted_iota(jnp.int32, (rank, 1), 0)
    pivots = jnp.zeros((rank, 1), F32)
    for k in range(rank):
        pivot_row = table[k : k + 1, :]
        pivot_column = table[:, k : k + 1]
        pivot = table[k : k + 1, k : k + 1]
        scale = jnp.where(row_index > k, pivot_column / pivot, 0.0)
        pivots = jnp.where(row_index == k, pivot, pivots)
        table = table - scale * pivot_row
    inverse = table[:, rank:] / jnp.sqrt(pivots)
    inverse_ref[...] = inverse
    unit_ref[...] = exact(inverse, factor_ref[...], 1, 0)


def invert(gram, factor_t):
    return pl.pallas_call(
        inverse_kernel,
        out_shape=[
            pltpu.VMEM(gram.shape, F32),
            pltpu.VMEM(factor_t.shape, F32),
        ],
        cost_estimate=pl.CostEstimate(flops=4_000_000_000, bytes_accessed=300_000, transcendentals=0),
        name="invert",
    )(*near(gram, factor_t))


def update_kernel(replicas, sum_ref, inverse_ref, unit_ref, master_ref, moment_ref, second_ref,
                  send_ref, master_out, moment_out, second_out):
    rank = inverse_ref.shape[0]
    columns = master_ref.shape[1]
    packed = sum_ref[...]
    own = jnp.concatenate([packed[:, :rank], packed[:, rank:]], axis=0)
    right = exact(own, inverse_ref[...], 1, 1) / replicas
    grad = exact(right, unit_ref[...], 1, 0)
    moment = beta_one * moment_ref[...] + (1.0 - beta_one) * grad
    second = beta_two * second_ref[...] + (1.0 - beta_two) * grad * grad
    master = master_ref[...]
    master = master - learn_rate * (
        moment / (jnp.sqrt(second) + adam_eps) + decay_rate * master
    )
    moment_out[...] = moment
    second_out[...] = second
    master_out[...] = master
    high = right.astype(BF16).astype(F32)
    send_ref[:, :columns] = master.astype(BF16)
    send_ref[:, columns:] = jnp.concatenate([high, right - high], axis=1).astype(BF16)


def update(replicas, own_sum, inverse, unit_t, master, moment, second):
    rows, columns = master.shape
    rank = inverse.shape[0]
    block = jax.ShapeDtypeStruct(master.shape, F32)
    return pl.pallas_call(
        lambda *refs: update_kernel(replicas, *refs),
        out_shape=[pltpu.VMEM((rows, columns + 2 * rank), BF16), block, block, block],
        cost_estimate=pl.CostEstimate(flops=50_000_000, bytes_accessed=600_000, transcendentals=0),
        name="update",
    )(*near(own_sum, inverse, unit_t, master, moment, second))


def finish_kernel(rep_ref, *refs):
    blocks, (unit_ref, grad_ref, feed_ref) = refs[:Y_SIZE], refs[Y_SIZE : Y_SIZE + 3]
    new_ref, weights_ref, right_ref, parts_ref, right_rows = refs[Y_SIZE + 3 :]
    rank, columns = unit_ref.shape
    own_rows = blocks[0].shape[1]
    rep = rep_ref[0]
    own_y, own_z = rep // Z_SIZE, rep % Z_SIZE
    step = pl.program_id(0)

    @pl.when(step == 0)
    def _():
        for i, part in enumerate(three_parts(unit_ref[...])):
            parts_ref[i, :rank, :] = part
            parts_ref[i, rank:, :] = part

    for d, block in enumerate(blocks):

        @pl.when(step == d)
        def _(d=d, block=block):
            first = (own_y ^ d) * (Z_SIZE * own_rows)
            for j in range(Z_SIZE):
                at = pl.multiple_of((own_z ^ j) * own_rows, own_rows)
                rows = pl.ds(at, own_rows)
                right = block[j, :, columns:]
                approx = native(right, parts_ref[2], 1, 0) + native(right, parts_ref[1], 1, 0)
                approx = approx + native(right, parts_ref[0], 1, 0)
                merged = grad_ref[rows, :].astype(F32) + feed_ref[rows, :].astype(F32)
                new_ref[rows, :] = (merged - approx).astype(BF16)
                weights_ref[rows, :] = block[j, :, :columns]
                wide = right.astype(F32)
                all_rows = pl.ds(pl.multiple_of(first + at, own_rows), own_rows)
                right_rows[all_rows, :] = wide[:, :rank] + wide[:, rank:]

    @pl.when(step == Y_SIZE - 1)
    def _():
        right_ref[...] = right_rows[...].T


def finish(rep, blocks, unit_t, gradient, feedback):
    rows, columns = gradient.shape
    rank = unit_t.shape[0]
    quarter = rows // Y_SIZE
    row_block = pl.BlockSpec((quarter, columns), lambda d, rep: ((rep[0] // Z_SIZE) ^ d, 0))
    return pl.pallas_call(
        finish_kernel,
        out_shape=[
            jax.ShapeDtypeStruct((rows, columns), BF16),
            jax.ShapeDtypeStruct((rows, columns), BF16),
            jax.ShapeDtypeStruct((rank, rows), F32),
        ],
        grid_spec=pltpu.PrefetchScalarGridSpec(
            num_scalar_prefetch=1,
            grid=(Y_SIZE,),
            in_specs=[whole(b.shape) for b in blocks] + [whole(unit_t.shape), row_block, row_block],
            out_specs=[row_block, row_block, whole((rank, rows))],
            scratch_shapes=[
                pltpu.VMEM((3, 2 * rank, columns), BF16),
                pltpu.VMEM((rows, rank), F32),
            ],
        ),
        cost_estimate=pl.CostEstimate(flops=1_000_000_000, bytes_accessed=6_000_000, transcendentals=0),
        name="finish",
    )(rep, *near(*blocks, unit_t), gradient, feedback)


def on_device(gradient, feedback, warm_start, master, moment, second):
    replicas = lax.axis_size("rep")
    gradient, feedback = gradient[0], feedback[0]
    rep = lax.axis_index("rep").astype(jnp.int32).reshape(1)

    pieces = local_factor(rep, warm_start.T, gradient, feedback)
    quarter = sum_four([pieces[0]] + [exchange(p, "rep", d) for p, d in zip(pieces[1:], Y_STEPS)])
    for distance in (1, 2, 4):
        quarter = quarter + exchange(quarter, "rep", distance)
    quarter = quarter / replicas
    quarters = [quarter] + [exchange(quarter, "rep", d) for d in Y_STEPS]
    factor_t, parts, gram_term = assemble(rep, quarters)

    packed = project(gradient, feedback, parts, replicas)
    received = lax.all_to_all(packed, "rep", 0, 0, tiled=True)
    inverse, unit_t = invert(shard_sum(gram_term), factor_t)
    received, inverse, unit_t = lax.optimization_barrier((received, inverse, unit_t))
    own_sum = shard_sum(received.sum(0))

    send, master_out, moment_out, second_out = update(
        replicas, own_sum, inverse, unit_t, master, moment, second
    )
    pair = jnp.stack([send, exchange(send, "rep", 1)])
    column = jnp.concatenate([pair] + [exchange(pair, "rep", d) for d in (2, 4, 6)])
    blocks = [column] + [exchange(column, "rep", d) for d in Y_STEPS]
    new_feedback, weights, right_t = finish(rep, blocks, unit_t, gradient, feedback)
    return (new_feedback[None], weights, master_out, moment_out, second_out, right_t.T)


def solution(mesh):
    return jax.shard_map(
        on_device,
        mesh=mesh,
        in_specs=(
            P("rep", None, "shard"),
            P("rep", None, "shard"),
            P(),
            P("rep", "shard"),
            P("rep", "shard"),
            P("rep", "shard"),
        ),
        out_specs=(
            P("rep", None, "shard"),
            P(None, "shard"),
            P("rep", "shard"),
            P("rep", "shard"),
            P("rep", "shard"),
            P(),
        ),
        check_vma=False,
    )
```

time: 534 us -> 117 us (0.22)
  waiting for transfers between devices: 461 us -> 45.2 us
  starting transfers between devices: 0.12 us -> 48.5 us
  blocking collectives: 23.6 us -> 0 us
  Pallas kernels: 0 us -> 20.3 us
  other arithmetic: 17.4 us -> 0.1 us
  between operations: 14.5 us -> 0.81 us
  matrix products: 11.3 us -> 0 us
    psum x2 -> x0, waiting for transfers between devices: 387 us -> none  [the longest x1 244 us: on_device(): right_factor = lax.psum(projected, ('rep', 'shard')) / replicas]
    all_gather x1 -> x0, waiting for transfers between devices: 73.2 us -> none  [on_device(): lax.all_gather(master_out.astype(jnp.bfloat16), 'rep', axis=0, tiled=True)]
    ppermute x0 -> x24, waiting for transfers between devices: none -> 39.7 us  [exchange(): lax.ppermute(value, axis, [(i, i ^ distance) for i in range(lax.axis_size...]
    ppermute x0 -> x24, starting transfers between devices: none -> 37.9 us  [exchange(): lax.ppermute(value, axis, [(i, i ^ distance) for i in range(lax.axis_size...]
    psum x1 -> x0, blocking collectives: 23.6 us -> none  [on_device(): gram = lax.psum(gram_part, 'shard')]
    pallas_call x0 -> x6, Pallas kernels: none -> 20.3 us  [the longest x1 6.17 us: invert(): pl.pallas_call(inverse_kernel, out_shape=[pltpu.VMEM(gram.shape, F32), pl...]
    another operation x5 -> x1, other arithmetic: 12.1 us -> 0.01 us  [on_device(): pair = jnp.stack([send, exchange(send, 'rep', 1)])]
    dot_general x5 -> x0, matrix products: 11.1 us -> none  [the longest x2 5.07 us: contract_first(): lax.dot_general(left, right, (((0,), (0,)), ((), ())), precision=HIGHEST,...]
  transfers between devices with their start and end apart: 3 -> 25, of which waited for: 3 -> 17; matrix products, arithmetic and copies ran while one was open for 1% -> 0% of each run, Pallas kernels for 0% -> 9%
where the time goes in v2:
time: 117 us; the launch traced here: 115 us
  starting transfers between devices  48.5 us (41%)
  waiting for transfers between devices  45.2 us (39%)
  Pallas kernels  20.3 us (17%)
    ppermute x24, waiting for transfers between devices, exchange(): lax.ppermute(value, axis, [(i, i ^ distance) for i in range(lax.axis_size...  39.7 us
    ppermute x24, starting transfers between devices, exchange(): lax.ppermute(value, axis, [(i, i ^ distance) for i in range(lax.axis_size...  37.9 us
    all_to_all x1, starting transfers between devices, on_device(): received = lax.all_to_all(packed, 'rep', 0, 0, tiled=True)  10.6 us
    pallas_call x1, Pallas kernels, invert(): pl.pallas_call(inverse_kernel, out_shape=[pltpu.VMEM(gram.shape, F32), pl...  6.17 us
    all_to_all x1, waiting for transfers between devices, on_device(): received = lax.all_to_all(packed, 'rep', 0, 0, tiled=True)  5.56 us
    pallas_call x1, Pallas kernels, finish(): pl.pallas_call(finish_kernel, out_shape=[jax.ShapeDtypeStruct((rows, colu...  4.9 us
    pallas_call x1, Pallas kernels, project(): pl.pallas_call(project_kernel, out_shape=jax.ShapeDtypeStruct((replicas,...  4.27 us
    pallas_call x1, Pallas kernels, local_factor(): pl.pallas_call(factor_kernel, out_shape=[pltpu.VMEM((rank, quarter), F32)...  3.52 us
  transfers between devices with their start and end apart: 25, of which 17 were waited for; matrix products, arithmetic and copies ran while one was open for 0% of the time, Pallas kernels for 9%

profile of v2, /device:TPU:32, one launch (start us, length us, event | category | flops | bytes accessed | tf_op | source)
XLA Modules:
  0.0 115.0 jit_solution(5208455733104030322)
XLA Ops:
  0.6 3.5 %local_factor.1 = (f32[64,128]{1,0:T(8,128)S(1)}, f32[64,128]{1,0:T(8,128)S(1)}, f32[64,128]{1,0:T(8,128)S(1)}, f32[64,128]{1,0:T(8,128)S(1)}) custom-call(s32[1]{0:T(128)} %bitcast.rep_ref, f32[64,1024]{1,0:T(8,128)} %bitcast.18, bf16[1024,512]{1,0:T(8,128)(2,1)} %bitcast.12, bf16[1024,512]{1,0:T(8,128)(2,1)} %bitcast.15), custom_call_target="tpu_custom_call" | custom-call | flops 2000000000 | bytes 2500000 | tf_op jit(solution)/shard_map/local_factor/pallas_call | solution.py:90
  4.2 1.7 %collective-permute-start = (f32[64,128]{1,0:T(8,128)S(1)}, f32[64,128]{1,0:T(8,128)S(1)}, u32[]{:S(2)}, u32[]{:S(2)}) collective-permute-start(f32[64,128]{1,0:T(8,128)S(1)} %get-tuple-element.26), channel_id=1, source_target_pairs={{0,64},{8,72},{16,80},{24,88},{32,96},{40,104},{48,112},{56,120},{... | collective-permute-start | bytes 98312 | tf_op jit(solution)/shard_map/ppermute | solution.py:47
  5.8 2.9 %collective-permute-start.1 = (f32[64,128]{1,0:T(8,128)S(1)}, f32[64,128]{1,0:T(8,128)S(1)}, u32[]{:S(2)}, u32[]{:S(2)}) collective-permute-start(f32[64,128]{1,0:T(8,128)S(1)} %get-tuple-element.27), channel_id=1, source_target_pairs={{0,128},{8,136},{16,144},{24,152},{32,160},{40,168},{48,176},{56,1... | collective-permute-start | bytes 98312 | tf_op jit(solution)/shard_map/ppermute | solution.py:47
  8.9 2.3 %collective-permute-done.1 = f32[64,128]{1,0:T(8,128)S(1)} collective-permute-done((f32[64,128]{1,0:T(8,128)S(1)}, f32[64,128]{1,0:T(8,128)S(1)}, u32[]{:S(2)}, u32[]{:S(2)}) %collective-permute-start.1) | collective-permute-done | bytes 32800 | tf_op jit(solution)/shard_map/ppermute | solution.py:47
  11.2 2.6 %collective-permute-done.2 = f32[64,128]{1,0:T(8,128)S(1)} collective-permute-done((f32[64,128]{1,0:T(8,128)S(1)}, f32[64,128]{1,0:T(8,128)S(1)}, u32[]{:S(2)}, u32[]{:S(2)}) %collective-permute-start.2) | collective-permute-done | bytes 32800 | tf_op jit(solution)/shard_map/ppermute | solution.py:47
  14.1 3.8 %collective-permute-done.3 = f32[64,128]{1,0:T(8,128)S(1)} collective-permute-done((f32[64,128]{1,0:T(8,128)S(1)}, f32[64,128]{1,0:T(8,128)S(1)}, u32[]{:S(2)}, u32[]{:S(2)}) %collective-permute-start.3) | collective-permute-done | bytes 32800 | tf_op jit(solution)/shard_map/ppermute | solution.py:47
  17.9 3.3 %collective-permute-start.4 = (f32[64,128]{1,0:T(8,128)S(1)}, f32[64,128]{1,0:T(8,128)S(1)}, u32[]{:S(2)}, u32[]{:S(2)}) collective-permute-start(f32[64,128]{1,0:T(8,128)S(1)} %add.45), channel_id=1, source_target_pairs={{0,16},{8,24},{16,0},{24,8},{32,48},{40,56},{48,32},{56,40},{64,80... | collective-permute-start | bytes 98312 | tf_op jit(solution)/shard_map/ppermute | solution.py:47
  21.1 1.9 %collective-permute-done.4 = f32[64,128]{1,0:T(8,128)S(1)} collective-permute-done((f32[64,128]{1,0:T(8,128)S(1)}, f32[64,128]{1,0:T(8,128)S(1)}, u32[]{:S(2)}, u32[]{:S(2)}) %collective-permute-start.4) | collective-permute-done | bytes 32800 | tf_op jit(solution)/shard_map/ppermute | solution.py:47
  23.0 6.1 %collective-permute-start.5 = (f32[64,128]{1,0:T(8,128)S(1)}, f32[64,128]{1,0:T(8,128)S(1)}, u32[]{:S(2)}, u32[]{:S(2)}) collective-permute-start(f32[64,128]{1,0:T(8,128)S(1)} %add.46), channel_id=1, source_target_pairs={{0,32},{8,40},{16,48},{24,56},{32,0},{40,8},{48,16},{56,24},{64,96... | collective-permute-start | bytes 98312 | tf_op jit(solution)/shard_map/ppermute | solution.py:47
  29.2 1.9 %collective-permute-done.5 = f32[64,128]{1,0:T(8,128)S(1)} collective-permute-done((f32[64,128]{1,0:T(8,128)S(1)}, f32[64,128]{1,0:T(8,128)S(1)}, u32[]{:S(2)}, u32[]{:S(2)}) %collective-permute-start.5) | collective-permute-done | bytes 32800 | tf_op jit(solution)/shard_map/ppermute | solution.py:47
  32.1 3.1 %collective-permute-start.6 = (f32[64,128]{1,0:T(8,128)S(1)}, f32[64,128]{1,0:T(8,128)S(1)}, u32[]{:S(2)}, u32[]{:S(2)}) collective-permute-start(f32[64,128]{1,0:T(8,128)S(1)} %add_multiply_fusion.refs_0_), channel_id=1, source_target_pairs={{0,64},{8,72},{16,80},{24,88},{32,96},{40,104},{48,112},{56,120},{... | collective-permute-start | bytes 98312 | tf_op jit(solution)/shard_map/ppermute | solution.py:47
  39.0 2.8 %collective-permute-start.12 = (f32[64,64]{1,0:T(8,128)S(1)}, f32[64,64]{1,0:T(8,128)S(1)}, u32[]{:S(2)}, u32[]{:S(2)}) collective-permute-start(f32[64,64]{1,0:T(8,128)S(1)} %add.48), channel_id=1, source_target_pairs={{0,6},{1,7},{2,4},{3,5},{4,2},{5,3},{6,0},{7,1},{8,14},{9,15},{10,... | collective-permute-start | bytes 49160 | tf_op jit(solution)/shard_map/ppermute | solution.py:47
  43.1 4.3 %project.1 = f32[32,16,128]{2,1,0:T(8,128)} custom-call(bf16[1024,512]{1,0:T(8,128)(2,1)} %bitcast.13, bf16[1024,512]{1,0:T(8,128)(2,1)} %bitcast.16, bf16[192,512]{1,0:T(8,128)(2,1)S(1)} %get-tuple-element.29.parts_ref), custom_call_target="tpu_custom_call" | custom-call | flops 2000000000 | bytes 2500000 | tf_op jit(solution)/shard_map/project/pallas_call | solution.py:153
  47.4 10.6 %all-to-all-start = ((f32[32,16,128]{2,1,0:T(8,128)}), f32[32,16,128]{2,1,0:T(8,128)S(1)}, u32[]{:S(2)}, u32[]{:S(2)}) async-start(f32[32,16,128]{2,1,0:T(8,128)} %project.1), calls=%async_computation | async-start | bytes 524288 | tf_op jit(solution)/shard_map/all_to_all | solution.py:312
  58.1 6.2 %invert.1 = (f32[64,64]{1,0:T(8,128)S(1)}, f32[64,512]{1,0:T(8,128)S(1)}) custom-call(f32[64,64]{1,0:T(8,128)S(1)} %add_add_fusion.gram_ref, f32[64,512]{1,0:T(8,128)S(1)} %get-tuple-element.31.factor_ref), custom_call_target="tpu_custom_call" | custom-call | flops 4000000000 | bytes 300000 | tf_op jit(solution)/shard_map/invert/pallas_call | solution.py:188
  64.2 5.6 %all-to-all-done = f32[32,16,128]{2,1,0:T(8,128)S(1)} async-done(((f32[32,16,128]{2,1,0:T(8,128)}), f32[32,16,128]{2,1,0:T(8,128)S(1)}, u32[]{:S(2)}, u32[]{:S(2)}) %all-to-all-start) | async-done | bytes 262176 | tf_op jit(solution)/shard_map/all_to_all | solution.py:312
  71.1 2.8 %collective-permute-start.16 = (f32[16,128]{1,0:T(8,128)S(1)}, f32[16,128]{1,0:T(8,128)S(1)}, u32[]{:S(2)}, u32[]{:S(2)}) collective-permute-start(f32[16,128]{1,0:T(8,128)S(1)} %add.52), channel_id=1, source_target_pairs={{0,6},{1,7},{2,4},{3,5},{4,2},{5,3},{6,0},{7,1},{8,14},{9,15},{10,... | collective-permute-start | bytes 24584 | tf_op jit(solution)/shard_map/ppermute | solution.py:47
  76.0 3.1 %collective-permute-done.15 = f32[16,128]{1,0:T(8,128)S(1)} collective-permute-done((f32[16,128]{1,0:T(8,128)S(1)}, f32[16,128]{1,0:T(8,128)S(1)}, u32[]{:S(2)}, u32[]{:S(2)}) %collective-permute-start.15) | collective-permute-done | bytes 8224 | tf_op jit(solution)/shard_map/ppermute | solution.py:47
  80.5 3.8 %collective-permute-done.17 = bf16[32,640]{1,0:T(8,128)(2,1)S(1)} collective-permute-done((bf16[32,640]{1,0:T(8,128)(2,1)S(1)}, bf16[32,640]{1,0:T(8,128)(2,1)S(1)}, u32[]{:S(2)}, u32[]{:S(2)}) %collective-permute-start.17) | collective-permute-done | bytes 40992 | tf_op jit(solution)/shard_map/ppermute | solution.py:47
  84.5 4.3 %collective-permute-start.19 = (bf16[2,32,640]{2,1,0:T(8,128)(2,1)S(1)}, bf16[2,32,640]{2,1,0:T(8,128)(2,1)S(1)}, u32[]{:S(2)}, u32[]{:S(2)}) collective-permute-start(bf16[2,32,640]{2,1,0:T(8,128)(2,1)S(1)} %pad_maximum_fusion), channel_id=1, source_target_pairs={{0,32},{8,40},{16,48},{24,56},{32,0},{40,8},{48,16},{56,24},{64,96... | collective-permute-start | bytes 245768 | tf_op jit(solution)/shard_map/ppermute | solution.py:47
  88.8 2.0 %collective-permute-start.18 = (bf16[2,32,640]{2,1,0:T(8,128)(2,1)S(1)}, bf16[2,32,640]{2,1,0:T(8,128)(2,1)S(1)}, u32[]{:S(2)}, u32[]{:S(2)}) collective-permute-start(bf16[2,32,640]{2,1,0:T(8,128)(2,1)S(1)} %pad_maximum_fusion), channel_id=1, source_target_pairs={{0,16},{8,24},{16,0},{24,8},{32,48},{40,56},{48,32},{56,40},{64,80... | collective-permute-start | bytes 245768 | tf_op jit(solution)/shard_map/ppermute | solution.py:47
  90.8 4.5 %collective-permute-done.18 = bf16[2,32,640]{2,1,0:T(8,128)(2,1)S(1)} collective-permute-done((bf16[2,32,640]{2,1,0:T(8,128)(2,1)S(1)}, bf16[2,32,640]{2,1,0:T(8,128)(2,1)S(1)}, u32[]{:S(2)}, u32[]{:S(2)}) %collective-permute-start.18) | collective-permute-done | bytes 81952 | tf_op jit(solution)/shard_map/ppermute | solution.py:47
  99.6 9.8 %collective-permute-done.23.refs_3_ = bf16[8,32,640]{2,1,0:T(8,128)(2,1)S(1)} collective-permute-done((bf16[8,32,640]{2,1,0:T(8,128)(2,1)S(1)}, bf16[8,32,640]{2,1,0:T(8,128)(2,1)S(1)}, u32[]{:S(2)}, u32[]{:S(2)}) %collective-permute-start.23) | collective-permute-done | bytes 327712 | tf_op jit(solution)/shard_map/ppermute | solution.py:47
  110.1 4.9 %finish.1 = (bf16[1024,512]{1,0:T(8,128)(2,1)}, bf16[1024,512]{1,0:T(8,128)(2,1)}, f32[64,1024]{1,0:T(8,128)}) custom-call(s32[1]{0:T(128)} %bitcast.rep_ref, bf16[8,32,640]{2,1,0:T(8,128)(2,1)S(1)} %constant_dynamic-update-slice_fusion.refs_0_, bf16[8,32,640]{2,1,0:T(8,128)(2,1)S(1)} %collective-permute-done.21.refs_1_, ...), custom_call_target="tpu_custom_call" | custom-call | flops 1000000000 | bytes 6000000 | tf_op jit(solution)/shard_map/finish/pallas_call | solution.py:276
  (53 shorter events, 16.6 us)
Async XLA Ops:
  4.2 4.8 %collective-permute-start = (f32[64,128]{1,0:T(8,128)S(1)}, f32[64,128]{1,0:T(8,128)S(1)}, u32[]{:S(2)}, u32[]{:S(2)}) collective-permute-start(f32[64,128]{1,0:T(8,128)S(1)} %get-tuple-element.26), channel_id=1, source_target_pairs={{0,64},{8,72},{16,80},{24,88},{32,96},{40,104},{48,112},{56,120},{... | collective-permute-start | bytes 98312 | tf_op jit(solution)/shard_map/ppermute | solution.py:47
  5.8 5.4 %collective-permute-start.1 = (f32[64,128]{1,0:T(8,128)S(1)}, f32[64,128]{1,0:T(8,128)S(1)}, u32[]{:S(2)}, u32[]{:S(2)}) collective-permute-start(f32[64,128]{1,0:T(8,128)S(1)} %get-tuple-element.27), channel_id=1, source_target_pairs={{0,128},{8,136},{16,144},{24,152},{32,160},{40,168},{48,176},{56,1... | collective-permute-start | bytes 98312 | tf_op jit(solution)/shard_map/ppermute | solution.py:47
  8.7 5.1 %collective-permute-start.2 = (f32[64,128]{1,0:T(8,128)S(1)}, f32[64,128]{1,0:T(8,128)S(1)}, u32[]{:S(2)}, u32[]{:S(2)}) collective-permute-start(f32[64,128]{1,0:T(8,128)S(1)} %get-tuple-element.28), channel_id=1, source_target_pairs={{0,192},{8,200},{16,208},{24,216},{32,224},{40,232},{48,240},{56,2... | collective-permute-start | bytes 98312 | tf_op jit(solution)/shard_map/ppermute | solution.py:47
  13.9 4.0 %collective-permute-start.3 = (f32[64,128]{1,0:T(8,128)S(1)}, f32[64,128]{1,0:T(8,128)S(1)}, u32[]{:S(2)}, u32[]{:S(2)}) collective-permute-start(f32[64,128]{1,0:T(8,128)S(1)} %add_add_fusion.1), channel_id=1, source_target_pairs={{0,8},{8,0},{16,24},{24,16},{32,40},{40,32},{48,56},{56,48},{64,72... | collective-permute-start | bytes 98312 | tf_op jit(solution)/shard_map/ppermute | solution.py:47
  17.9 5.2 %collective-permute-start.4 = (f32[64,128]{1,0:T(8,128)S(1)}, f32[64,128]{1,0:T(8,128)S(1)}, u32[]{:S(2)}, u32[]{:S(2)}) collective-permute-start(f32[64,128]{1,0:T(8,128)S(1)} %add.45), channel_id=1, source_target_pairs={{0,16},{8,24},{16,0},{24,8},{32,48},{40,56},{48,32},{56,40},{64,80... | collective-permute-start | bytes 98312 | tf_op jit(solution)/shard_map/ppermute | solution.py:47
  23.0 8.0 %collective-permute-start.5 = (f32[64,128]{1,0:T(8,128)S(1)}, f32[64,128]{1,0:T(8,128)S(1)}, u32[]{:S(2)}, u32[]{:S(2)}) collective-permute-start(f32[64,128]{1,0:T(8,128)S(1)} %add.46), channel_id=1, source_target_pairs={{0,32},{8,40},{16,48},{24,56},{32,0},{40,8},{48,16},{56,24},{64,96... | collective-permute-start | bytes 98312 | tf_op jit(solution)/shard_map/ppermute | solution.py:47
  31.1 5.1 %collective-permute-start.8 = (f32[64,128]{1,0:T(8,128)S(1)}, f32[64,128]{1,0:T(8,128)S(1)}, u32[]{:S(2)}, u32[]{:S(2)}) collective-permute-start(f32[64,128]{1,0:T(8,128)S(1)} %add_multiply_fusion.refs_0_), channel_id=1, source_target_pairs={{0,192},{8,200},{16,208},{24,216},{32,224},{40,232},{48,240},{56,2... | collective-permute-start | bytes 98312 | tf_op jit(solution)/shard_map/ppermute | solution.py:47
  31.4 5.4 %collective-permute-start.7 = (f32[64,128]{1,0:T(8,128)S(1)}, f32[64,128]{1,0:T(8,128)S(1)}, u32[]{:S(2)}, u32[]{:S(2)}) collective-permute-start(f32[64,128]{1,0:T(8,128)S(1)} %add_multiply_fusion.refs_0_), channel_id=1, source_target_pairs={{0,128},{8,136},{16,144},{24,152},{32,160},{40,168},{48,176},{56,1... | collective-permute-start | bytes 98312 | tf_op jit(solution)/shard_map/ppermute | solution.py:47
  32.1 5.3 %collective-permute-start.6 = (f32[64,128]{1,0:T(8,128)S(1)}, f32[64,128]{1,0:T(8,128)S(1)}, u32[]{:S(2)}, u32[]{:S(2)}) collective-permute-start(f32[64,128]{1,0:T(8,128)S(1)} %add_multiply_fusion.refs_0_), channel_id=1, source_target_pairs={{0,64},{8,72},{16,80},{24,88},{32,96},{40,104},{48,112},{56,120},{... | collective-permute-start | bytes 98312 | tf_op jit(solution)/shard_map/ppermute | solution.py:47
  37.7 1.3 %collective-permute-start.9 = (f32[64,64]{1,0:T(8,128)S(1)}, f32[64,64]{1,0:T(8,128)S(1)}, u32[]{:S(2)}, u32[]{:S(2)}) collective-permute-start(f32[64,64]{1,0:T(8,128)S(1)} %get-tuple-element.30), channel_id=1, source_target_pairs={{0,1},{1,0},{2,3},{3,2},{4,5},{5,4},{6,7},{7,6},{8,9},{9,8},{10,11... | collective-permute-start | bytes 49160 | tf_op jit(solution)/shard_map/ppermute | solution.py:47
  39.0 19.0 %collective-permute-start.12 = (f32[64,64]{1,0:T(8,128)S(1)}, f32[64,64]{1,0:T(8,128)S(1)}, u32[]{:S(2)}, u32[]{:S(2)}) collective-permute-start(f32[64,64]{1,0:T(8,128)S(1)} %add.48), channel_id=1, source_target_pairs={{0,6},{1,7},{2,4},{3,5},{4,2},{5,3},{6,0},{7,1},{8,14},{9,15},{10,... | collective-permute-start | bytes 49160 | tf_op jit(solution)/shard_map/ppermute | solution.py:47
  41.8 16.3 %collective-permute-start.11 = (f32[64,64]{1,0:T(8,128)S(1)}, f32[64,64]{1,0:T(8,128)S(1)}, u32[]{:S(2)}, u32[]{:S(2)}) collective-permute-start(f32[64,64]{1,0:T(8,128)S(1)} %add.48), channel_id=1, source_target_pairs={{0,4},{1,5},{2,6},{3,7},{4,0},{5,1},{6,2},{7,3},{8,12},{9,13},{10,... | collective-permute-start | bytes 49160 | tf_op jit(solution)/shard_map/ppermute | solution.py:47
  42.6 15.5 %collective-permute-start.10 = (f32[64,64]{1,0:T(8,128)S(1)}, f32[64,64]{1,0:T(8,128)S(1)}, u32[]{:S(2)}, u32[]{:S(2)}) collective-permute-start(f32[64,64]{1,0:T(8,128)S(1)} %add.48), channel_id=1, source_target_pairs={{0,2},{1,3},{2,0},{3,1},{4,6},{5,7},{6,4},{7,5},{8,10},{9,11},{10,... | collective-permute-start | bytes 49160 | tf_op jit(solution)/shard_map/ppermute | solution.py:47
  47.4 22.4 %all-to-all-start = ((f32[32,16,128]{2,1,0:T(8,128)}), f32[32,16,128]{2,1,0:T(8,128)S(1)}, u32[]{:S(2)}, u32[]{:S(2)}) async-start(f32[32,16,128]{2,1,0:T(8,128)} %project.1), calls=%async_computation | async-start | bytes 524288 | tf_op jit(solution)/shard_map/all_to_all | solution.py:312
  71.1 4.9 %collective-permute-start.16 = (f32[16,128]{1,0:T(8,128)S(1)}, f32[16,128]{1,0:T(8,128)S(1)}, u32[]{:S(2)}, u32[]{:S(2)}) collective-permute-start(f32[16,128]{1,0:T(8,128)S(1)} %add.52), channel_id=1, source_target_pairs={{0,6},{1,7},{2,4},{3,5},{4,2},{5,3},{6,0},{7,1},{8,14},{9,15},{10,... | collective-permute-start | bytes 24584 | tf_op jit(solution)/shard_map/ppermute | solution.py:47
  73.9 5.2 %collective-permute-start.15 = (f32[16,128]{1,0:T(8,128)S(1)}, f32[16,128]{1,0:T(8,128)S(1)}, u32[]{:S(2)}, u32[]{:S(2)}) collective-permute-start(f32[16,128]{1,0:T(8,128)S(1)} %add.52), channel_id=1, source_target_pairs={{0,4},{1,5},{2,6},{3,7},{4,0},{5,1},{6,2},{7,3},{8,12},{9,13},{10,... | collective-permute-start | bytes 24584 | tf_op jit(solution)/shard_map/ppermute | solution.py:47
  74.7 4.4 %collective-permute-start.14 = (f32[16,128]{1,0:T(8,128)S(1)}, f32[16,128]{1,0:T(8,128)S(1)}, u32[]{:S(2)}, u32[]{:S(2)}) collective-permute-start(f32[16,128]{1,0:T(8,128)S(1)} %add.52), channel_id=1, source_target_pairs={{0,2},{1,3},{2,0},{3,1},{4,6},{5,7},{6,4},{7,5},{8,10},{9,11},{10,... | collective-permute-start | bytes 24584 | tf_op jit(solution)/shard_map/ppermute | solution.py:47
  80.2 4.0 %collective-permute-start.17 = (bf16[32,640]{1,0:T(8,128)(2,1)S(1)}, bf16[32,640]{1,0:T(8,128)(2,1)S(1)}, u32[]{:S(2)}, u32[]{:S(2)}) collective-permute-start(bf16[32,640]{1,0:T(8,128)(2,1)S(1)} %get-tuple-element.37), channel_id=1, source_target_pairs={{0,8},{8,0},{16,24},{24,16},{32,40},{40,32},{48,56},{56,48},{64,72... | collective-permute-start | bytes 122888 | tf_op jit(solution)/shard_map/ppermute | solution.py:47
  84.2 11.1 %collective-permute-start.20 = (bf16[2,32,640]{2,1,0:T(8,128)(2,1)S(1)}, bf16[2,32,640]{2,1,0:T(8,128)(2,1)S(1)}, u32[]{:S(2)}, u32[]{:S(2)}) collective-permute-start(bf16[2,32,640]{2,1,0:T(8,128)(2,1)S(1)} %pad_maximum_fusion), channel_id=1, source_target_pairs={{0,48},{8,56},{16,32},{24,40},{32,16},{40,24},{48,0},{56,8},{64,11... | collective-permute-start | bytes 245768 | tf_op jit(solution)/shard_map/ppermute | solution.py:47
  84.5 10.8 %collective-permute-start.19 = (bf16[2,32,640]{2,1,0:T(8,128)(2,1)S(1)}, bf16[2,32,640]{2,1,0:T(8,128)(2,1)S(1)}, u32[]{:S(2)}, u32[]{:S(2)}) collective-permute-start(bf16[2,32,640]{2,1,0:T(8,128)(2,1)S(1)} %pad_maximum_fusion), channel_id=1, source_target_pairs={{0,32},{8,40},{16,48},{24,56},{32,0},{40,8},{48,16},{56,24},{64,96... | collective-permute-start | bytes 245768 | tf_op jit(solution)/shard_map/ppermute | solution.py:47
  88.8 6.5 %collective-permute-start.18 = (bf16[2,32,640]{2,1,0:T(8,128)(2,1)S(1)}, bf16[2,32,640]{2,1,0:T(8,128)(2,1)S(1)}, u32[]{:S(2)}, u32[]{:S(2)}) collective-permute-start(bf16[2,32,640]{2,1,0:T(8,128)(2,1)S(1)} %pad_maximum_fusion), channel_id=1, source_target_pairs={{0,16},{8,24},{16,0},{24,8},{32,48},{40,56},{48,32},{56,40},{64,80... | collective-permute-start | bytes 245768 | tf_op jit(solution)/shard_map/ppermute | solution.py:47
  95.4 14.0 %collective-permute-start.23 = (bf16[8,32,640]{2,1,0:T(8,128)(2,1)S(1)}, bf16[8,32,640]{2,1,0:T(8,128)(2,1)S(1)}, u32[]{:S(2)}, u32[]{:S(2)}) collective-permute-start(bf16[8,32,640]{2,1,0:T(8,128)(2,1)S(1)} %constant_dynamic-update-slice_fusion.refs_0_), channel_id=1, source_target_pairs={{0,192},{8,200},{16,208},{24,216},{32,224},{40,232},{48,240},{56,2... | collective-permute-start | bytes 983048 | tf_op jit(solution)/shard_map/ppermute | solution.py:47
  96.7 12.8 %collective-permute-start.22 = (bf16[8,32,640]{2,1,0:T(8,128)(2,1)S(1)}, bf16[8,32,640]{2,1,0:T(8,128)(2,1)S(1)}, u32[]{:S(2)}, u32[]{:S(2)}) collective-permute-start(bf16[8,32,640]{2,1,0:T(8,128)(2,1)S(1)} %constant_dynamic-update-slice_fusion.refs_0_), channel_id=1, source_target_pairs={{0,128},{8,136},{16,144},{24,152},{32,160},{40,168},{48,176},{56,1... | collective-permute-start | bytes 983048 | tf_op jit(solution)/shard_map/ppermute | solution.py:47
  98.2 11.9 %collective-permute-start.21 = (bf16[8,32,640]{2,1,0:T(8,128)(2,1)S(1)}, bf16[8,32,640]{2,1,0:T(8,128)(2,1)S(1)}, u32[]{:S(2)}, u32[]{:S(2)}) collective-permute-start(bf16[8,32,640]{2,1,0:T(8,128)(2,1)S(1)} %constant_dynamic-update-slice_fusion.refs_0_), channel_id=1, source_target_pairs={{0,64},{8,72},{16,80},{24,88},{32,96},{40,104},{48,112},{56,120},{... | collective-permute-start | bytes 983048 | tf_op jit(solution)/shard_map/ppermute | solution.py:47
  (4 other events, 29.0 us)

commit v3 on v2

v3 whole, which is shorter than its diff:
```python
import jax
import jax.numpy as jnp
from jax import lax
from jax.experimental import pallas as pl
from jax.experimental.pallas import tpu as pltpu
from jax.sharding import PartitionSpec as P

HIGHEST = lax.Precision.HIGHEST
beta_one = 0.9
beta_two = 0.95
learn_rate = 0.02
decay_rate = 0.1
adam_eps = 1e-08
ridge_rate = 1e-06

F32 = jnp.float32
BF16 = jnp.bfloat16
Y_SIZE, Z_SIZE = 4, 8
Y_STEPS = (8, 16, 24)
X_STEPS = (2, 4, 6)


def exact(left, right, left_dim, right_dim):
    return lax.dot_general(
        left,
        right,
        (((left_dim,), (right_dim,)), ((), ())),
        precision=HIGHEST,
        preferred_element_type=F32,
    )


def native(left, right, left_dim, right_dim):
    return lax.dot_general(
        left, right, (((left_dim,), (right_dim,)), ((), ())), preferred_element_type=F32
    )


def three_parts(value):
    high = value.astype(BF16)
    rest = value - high.astype(F32)
    middle = rest.astype(BF16)
    return high, middle, (rest - middle.astype(F32)).astype(BF16)


def exchange(value, axis, distance):
    return lax.ppermute(value, axis, [(i, i ^ distance) for i in range(lax.axis_size(axis))])


def sum_four(terms):
    return (terms[0] + terms[1]) + (terms[2] + terms[3])


def shard_sum(value):
    value = value + exchange(value, "shard", 1)
    return sum_four([value] + [exchange(value, "shard", d) for d in X_STEPS])


def whole(shape):
    return pl.BlockSpec(shape, lambda *_: (0,) * len(shape))


def call(kernel, outs, args, cost, name, aliases=None, grid=None, out_specs=None, spare=(),
         scratch=()):
    specs = [pl.BlockSpec(memory_space=pltpu.VMEM)] * (len(args) - 1)
    specs += [pl.BlockSpec(memory_space=pl.ANY)] * len(spare)
    flops, traffic = cost
    return pl.pallas_call(
        kernel,
        out_shape=outs,
        grid_spec=pltpu.PrefetchScalarGridSpec(
            num_scalar_prefetch=1,
            grid=grid or (1,),
            in_specs=specs,
            out_specs=out_specs or [pl.BlockSpec(memory_space=pltpu.VMEM)] * len(outs),
            scratch_shapes=scratch,
        ),
        input_output_aliases=aliases or {},
        compiler_params=pltpu.CompilerParams(vmem_limit_bytes=16 * 2**20),
        cost_estimate=pl.CostEstimate(flops=flops, bytes_accessed=traffic, transcendentals=0),
        name=name,
    )(
        args[0],
        *[pltpu.with_memory_space_constraint(v, pltpu.VMEM) for v in args[1:]],
        *spare,
    )


def factor_kernel(rep_ref, warm_ref, grad_ref, feed_ref, *refs):
    outs, parts_ref, total_ref = refs[:-2], refs[-2], refs[-1]
    rank = warm_ref.shape[0]
    width = grad_ref.shape[1]
    quarter = outs[0].shape[1]
    step = pl.program_id(0)

    @pl.when(step == 0)
    def _():
        for i, part in enumerate(three_parts(warm_ref[...])):
            parts_ref[i * rank : (i + 1) * rank, :] = part

    total = native(parts_ref[...], grad_ref[...], 1, 0) + native(parts_ref[...], feed_ref[...], 1, 0)
    total = (total[2 * rank :] + total[rank : 2 * rank]) + total[:rank]
    total_ref[:, pl.ds(pl.multiple_of(step * width, width), width)] = total

    @pl.when(step == pl.num_programs(0) - 1)
    def _():
        own = rep_ref[0] // Z_SIZE
        for d, out in enumerate(outs):
            out[...] = total_ref[:, pl.ds(pl.multiple_of((own ^ d) * quarter, quarter), quarter)]


def local_factor(rep, warm_t, gradient, feedback):
    rank, rows = warm_t.shape
    columns = gradient.shape[1]
    quarter = columns // Y_SIZE
    steps = 2
    column_block = pl.BlockSpec((rows, columns // steps), lambda i, rep: (0, i))
    return pl.pallas_call(
        factor_kernel,
        out_shape=[pltpu.VMEM((rank, quarter), F32)] * Y_SIZE,
        grid_spec=pltpu.PrefetchScalarGridSpec(
            num_scalar_prefetch=1,
            grid=(steps,),
            in_specs=[whole((rank, rows)), column_block, column_block],
            out_specs=[whole((rank, quarter))] * Y_SIZE,
            scratch_shapes=[pltpu.VMEM((3 * rank, rows), BF16), pltpu.VMEM((rank, columns), F32)],
        ),
        compiler_params=pltpu.CompilerParams(vmem_limit_bytes=16 * 2**20),
        cost_estimate=pl.CostEstimate(flops=10**9, bytes_accessed=2_500_000, transcendentals=0),
        name="local_factor",
    )(rep, warm_t, gradient, feedback)


def assemble_kernel(rep_ref, *refs):
    quarters, (factor_ref, parts_ref, gram_ref) = refs[:Y_SIZE], refs[Y_SIZE:]
    rank, quarter = quarters[0].shape
    own = rep_ref[0] // Z_SIZE
    for d, block in enumerate(quarters):
        at = pl.ds(pl.multiple_of((own ^ d) * quarter, quarter), quarter)
        factor_ref[:, at] = block[...]
    factor = factor_ref[...]
    for i, part in enumerate(three_parts(factor)):
        parts_ref[i * rank : (i + 1) * rank, :] = part
    gram_ref[...] = exact(factor, factor, 1, 1)


def assemble(rep, quarters):
    rank, quarter = quarters[0].shape
    columns = quarter * Y_SIZE
    outs = [
        pltpu.VMEM((rank, columns), F32),
        pltpu.VMEM((3 * rank, columns), BF16),
        pltpu.VMEM((rank, rank), F32),
    ]
    return call(assemble_kernel, outs, (rep, *quarters), (10**8, 500_000), "assemble_factor")


def project_kernel(rep_ref, grad_ref, feed_ref, parts_ref, out_ref):
    replicas, half, _ = out_ref.shape
    rows = grad_ref.shape[0]
    rank = parts_ref.shape[0] // 3
    parts = parts_ref[...]
    groups = 8
    size = rows // replicas * groups

    for i in range(replicas // groups):
        at = slice(i * size, (i + 1) * size)
        total = native(grad_ref[at, :], parts, 1, 1) + native(feed_ref[at, :], parts, 1, 1)
        value = (total[:, 2 * rank :] + total[:, rank : 2 * rank]) + total[:, :rank]
        value = value.reshape(groups, 2, half, rank)
        out_ref[i * groups : (i + 1) * groups] = jnp.concatenate([value[:, 0], value[:, 1]], axis=-1)


def project(rep, gradient, feedback, parts, replicas):
    rank = parts.shape[0] // 3
    half = gradient.shape[0] // replicas // 2
    outs = [pltpu.VMEM((replicas, half, 2 * rank), F32)]
    return call(
        project_kernel, outs, (rep, gradient, feedback, parts), (10**9, 2_500_000), "project"
    )[0]


def inverse_kernel(rep_ref, gram_ref, factor_ref, inverse_ref, unit_ref, parts_ref):
    rank = gram_ref.shape[0]
    width = 8
    row = lax.broadcasted_iota(jnp.int32, (rank, rank), 0)
    column = lax.broadcasted_iota(jnp.int32, (rank, rank), 1)
    diagonal = row == column
    gram = gram_ref[...]
    trace = jnp.sum(jnp.where(diagonal, gram, 0.0))
    gram = gram + jnp.where(diagonal, ridge_rate * trace / rank, 0.0)
    table = jnp.concatenate([gram, jnp.where(diagonal, 1.0, 0.0)], axis=1)
    row = lax.broadcasted_iota(jnp.int32, table.shape, 0)
    pivots = jnp.ones(table.shape, F32)
    for k in range(0, rank, width):
        ahead = [jnp.broadcast_to(table[:, c : c + 1], table.shape) for c in range(k, k + width)]
        lines = [table[c : c + 1, :] for c in range(k, k + width)]
        for i in range(width):
            at = k + i
            pivot = ahead[i][at : at + 1, :]
            pivots = jnp.where(row == at, pivot, pivots)
            scale = jnp.where(row > at, ahead[i] * (1.0 / pivot), 0.0)
            for j in range(i + 1, width):
                entry = ahead[j][at : at + 1, :]
                ahead[j] = ahead[j] - scale * entry
                lines[j] = lines[j] - scale[k + j : k + j + 1, :] * lines[i]
            table = table - scale * lines[i]
    inverse = table[:, rank:] / jnp.sqrt(pivots[:, rank:])
    inverse_ref[...] = inverse
    unit = exact(inverse, factor_ref[...], 1, 0)
    unit_ref[...] = unit
    for i, part in enumerate(three_parts(unit)):
        parts_ref[2 * i * rank : (2 * i + 1) * rank, :] = part
        parts_ref[(2 * i + 1) * rank : (2 * i + 2) * rank, :] = part


def invert(rep, gram, factor_t):
    rank, columns = factor_t.shape
    outs = [
        pltpu.VMEM((rank, rank), F32),
        pltpu.VMEM((rank, columns), F32),
        pltpu.VMEM((6 * rank, columns), BF16),
    ]
    return call(inverse_kernel, outs, (rep, gram, factor_t), (2 * 10**9, 500_000), "invert")


def update_kernel(replicas, rep_ref, sum_ref, inverse_ref, unit_ref, master_ref, moment_ref,
                  second_ref, send_ref, master_out, moment_out, second_out):
    rank = inverse_ref.shape[0]
    columns = master_ref.shape[1]
    packed = sum_ref[...]
    own = jnp.concatenate([packed[:, :rank], packed[:, rank:]], axis=0)
    right = exact(own, inverse_ref[...], 1, 1) / replicas
    grad = exact(right, unit_ref[...], 1, 0)
    moment = beta_one * moment_ref[...] + (1.0 - beta_one) * grad
    second = beta_two * second_ref[...] + (1.0 - beta_two) * grad * grad
    master = master_ref[...]
    master = master - learn_rate * (
        moment / (jnp.sqrt(second) + adam_eps) + decay_rate * master
    )
    moment_out[...] = moment
    second_out[...] = second
    master_out[...] = master
    high = right.astype(BF16).astype(F32)
    send_ref[:, :columns] = master.astype(BF16)
    send_ref[:, columns:] = jnp.concatenate([high, right - high], axis=1).astype(BF16)


def update(replicas, rep, own_sum, inverse, unit_t, master, moment, second):
    rows, columns = master.shape
    rank = inverse.shape[0]
    block = pltpu.VMEM(master.shape, F32)
    outs = [pltpu.VMEM((rows, columns + 2 * rank), BF16), block, block, block]
    args = (rep, own_sum, inverse, unit_t, master, moment, second)
    kernel = lambda *refs: update_kernel(replicas, *refs)
    return call(kernel, outs, args, (5 * 10**7, 600_000), "update")


def finish_rows(own_y, own_z, d, block, parts_ref, grad_ref, feed_ref, new_ref, weights_ref):
    columns = grad_ref.shape[1]
    groups, own_rows, width = block.shape
    right = block[:, :, columns:].reshape(groups * own_rows, width - columns)
    approx = native(jnp.concatenate([right] * 3, axis=1), parts_ref[...], 1, 0)
    first = (own_y ^ d) * (groups * own_rows)
    for j in range(groups):
        at = pl.multiple_of((own_z ^ j) * own_rows, own_rows)
        source = pl.ds(pl.multiple_of(first + at, own_rows), own_rows)
        merged = grad_ref[source, :].astype(F32) + feed_ref[source, :].astype(F32)
        rows = pl.ds(at, own_rows)
        piece = approx[j * own_rows : (j + 1) * own_rows]
        new_ref[rows, :] = (merged - piece).astype(BF16)
        weights_ref[rows, :] = block[j, :, :columns]


def finish_own_kernel(rep_ref, block, parts_ref, grad_ref, feed_ref, new_ref, weights_ref):
    own_y, own_z = rep_ref[0] // Z_SIZE, rep_ref[0] % Z_SIZE
    finish_rows(own_y, own_z, 0, block, parts_ref, grad_ref, feed_ref, new_ref, weights_ref)


def finish_rest_kernel(rep_ref, *refs):
    blocks, (parts_ref, grad_ref, feed_ref) = refs[:Y_SIZE], refs[Y_SIZE : Y_SIZE + 3]
    new_ref, weights_ref, right_ref, right_rows = refs[Y_SIZE + 5 :]
    columns = grad_ref.shape[1]
    groups, own_rows, width = blocks[0].shape
    rank = (width - columns) // 2
    own_y, own_z = rep_ref[0] // Z_SIZE, rep_ref[0] % Z_SIZE
    step = pl.program_id(0)
    for d in range(1, Y_SIZE):

        @pl.when(step == d - 1)
        def _(d=d):
            finish_rows(
                own_y, own_z, d, blocks[d], parts_ref, grad_ref, feed_ref, new_ref, weights_ref
            )

    @pl.when(step == 0)
    def _():
        for d, block in enumerate(blocks):
            for j in range(groups):
                at = (own_y ^ d) * (groups * own_rows) + (own_z ^ j) * own_rows
                wide = block[j, :, columns:].astype(F32)
                rows = pl.ds(pl.multiple_of(at, own_rows), own_rows)
                right_rows[rows, :] = wide[:, :rank] + wide[:, rank:]
        right_ref[...] = right_rows[...].T


def finish_own(rep, block, parts, gradient, feedback):
    rows, columns = gradient.shape
    row_block = pl.BlockSpec((rows // Y_SIZE, columns), lambda i, rep: (rep[0] // Z_SIZE, 0))
    return call(
        finish_own_kernel,
        [jax.ShapeDtypeStruct((rows, columns), BF16)] * 2,
        (rep, block, parts, gradient, feedback),
        (10**9, 1_500_000),
        "finish_own",
        out_specs=[row_block, row_block],
    )


def finish_rest(rep, blocks, parts, gradient, feedback, begun):
    rows, columns = gradient.shape
    rank = (blocks[0].shape[2] - columns) // 2
    row_block = pl.BlockSpec(
        (rows // Y_SIZE, columns), lambda i, rep: ((rep[0] // Z_SIZE) ^ (i + 1), 0)
    )
    return call(
        finish_rest_kernel,
        [jax.ShapeDtypeStruct((rows, columns), BF16)] * 2
        + [jax.ShapeDtypeStruct((rank, rows), F32)],
        (rep, *blocks, parts, gradient, feedback),
        (10**9, 4_500_000),
        "finish_rest",
        aliases={Y_SIZE + 4: 0, Y_SIZE + 5: 1},
        grid=(Y_SIZE - 1,),
        out_specs=[row_block, row_block, whole((rank, rows))],
        spare=begun,
        scratch=[pltpu.VMEM((rows, rank), F32)],
    )


def on_device(gradient, feedback, warm_start, master, moment, second):
    replicas = lax.axis_size("rep")
    gradient, feedback = gradient[0], feedback[0]
    rep = lax.axis_index("rep").astype(jnp.int32).reshape(1)

    pieces = local_factor(rep, warm_start.T, gradient, feedback)
    quarter = sum_four([pieces[0]] + [exchange(p, "rep", d) for p, d in zip(pieces[1:], Y_STEPS)])
    for distance in (1, 2, 4):
        quarter = quarter + exchange(quarter, "rep", distance)
    quarter = quarter / replicas
    quarters = [quarter] + [exchange(quarter, "rep", d) for d in Y_STEPS]
    factor_t, parts, gram_term = assemble(rep, quarters)

    gram_pair = gram_term + exchange(gram_term, "shard", 1)
    packed = project(rep, gradient, feedback, parts, replicas)
    gram_pair, packed = lax.optimization_barrier((gram_pair, packed))
    received = lax.all_to_all(packed, "rep", 0, 0, tiled=True)
    gram = sum_four([gram_pair] + [exchange(gram_pair, "shard", d) for d in X_STEPS])
    inverse, unit_t, unit_parts = invert(rep, gram, factor_t)
    received, inverse, unit_t, unit_parts = lax.optimization_barrier(
        (received, inverse, unit_t, unit_parts)
    )
    own_sum = shard_sum(received.sum(0))

    send, master_out, moment_out, second_out = update(
        replicas, rep, own_sum, inverse, unit_t, master, moment, second
    )
    pair = jnp.stack([send, exchange(send, "rep", 1)])
    column = jnp.concatenate([pair] + [exchange(pair, "rep", d) for d in (2, 4, 6)])
    others = [exchange(column, "rep", d) for d in Y_STEPS]
    begun = finish_own(rep, column, unit_parts, gradient, feedback)
    new_feedback, weights, right_t = finish_rest(
        rep, [column] + others, unit_parts, gradient, feedback, begun
    )
    return (new_feedback[None], weights, master_out, moment_out, second_out, right_t.T)


def solution(mesh):
    return jax.shard_map(
        on_device,
        mesh=mesh,
        in_specs=(
            P("rep", None, "shard"),
            P("rep", None, "shard"),
            P(),
            P("rep", "shard"),
            P("rep", "shard"),
            P("rep", "shard"),
        ),
        out_specs=(
            P("rep", None, "shard"),
            P(None, "shard"),
            P("rep", "shard"),
            P("rep", "shard"),
            P("rep", "shard"),
            P(),
        ),
        check_vma=False,
    )
```

time: 117 us -> 108 us (0.923)
  Pallas kernels: 20.3 us -> 9.2 us
  local copies, waits for them, and re-layouts: 0.07 us -> 5.36 us
  waiting for transfers between devices: 45.2 us -> 42.3 us
    pallas_call x5 -> x6, Pallas kernels: 16.8 us -> 8.16 us  [call(): pl.pallas_call(kernel, out_shape=outs, grid_spec=pltpu.PrefetchScalarGrid...]
    unnamed x10 -> x23, local copies, waits for them, and re-layouts: 0.06 us -> 5.34 us
    all_to_all x1, waiting for transfers between devices: 5.56 us -> 2.46 us  [on_device(): received = lax.all_to_all(packed, 'rep', 0, 0, tiled=True)]
    pallas_call x1, Pallas kernels: 3.52 us -> 1.04 us  [local_factor(): pl.pallas_call(factor_kernel, out_shape=[pltpu.VMEM((rank, quarter), F32)...]
  transfers between devices with their start and end apart: 25 -> 25, of which waited for: 17 -> 18; matrix products, arithmetic and copies ran while one was open for 0% -> 2% of each run, Pallas kernels for 9% -> 4%
where the time goes in v3:
time: 108 us; the launch traced here: 106 us
  starting transfers between devices  48.5 us (45%)
  waiting for transfers between devices  42.3 us (39%)
  Pallas kernels  9.2 us (9%)
  local copies, waits for them, and re-layouts  5.36 us (5%)
    ppermute x24, waiting for transfers between devices, exchange(): lax.ppermute(value, axis, [(i, i ^ distance) for i in range(lax.axis_size...  39.9 us
    ppermute x24, starting transfers between devices, exchange(): lax.ppermute(value, axis, [(i, i ^ distance) for i in range(lax.axis_size...  37.8 us
    all_to_all x1, starting transfers between devices, on_device(): received = lax.all_to_all(packed, 'rep', 0, 0, tiled=True)  10.7 us
    pallas_call x6, Pallas kernels, call(): pl.pallas_call(kernel, out_shape=outs, grid_spec=pltpu.PrefetchScalarGrid...  8.16 us
    unnamed x23, local copies, waits for them, and re-layouts  5.34 us
    all_to_all x1, waiting for transfers between devices, on_device(): received = lax.all_to_all(packed, 'rep', 0, 0, tiled=True)  2.46 us
  transfers between devices with their start and end apart: 25, of which 18 were waited for; matrix products, arithmetic and copies ran while one was open for 2% of the time, Pallas kernels for 4%

profile of v3, /device:TPU:32, one launch (start us, length us, event | category | flops | bytes accessed | tf_op | source)
XLA Modules:
  0.0 106.3 jit_solution(10874123465061540443)
XLA Ops:
  5.1 1.7 %collective-permute-start = (f32[64,128]{1,0:T(8,128)S(1)}, f32[64,128]{1,0:T(8,128)S(1)}, u32[]{:S(2)}, u32[]{:S(2)}) collective-permute-start(f32[64,128]{1,0:T(8,128)S(1)} %get-tuple-element.32), channel_id=1, source_target_pairs={{0,64},{8,72},{16,80},{24,88},{32,96},{40,104},{48,112},{56,120},{... | collective-permute-start | bytes 98312 | tf_op jit(solution)/shard_map/ppermute | solution.py:47
  6.8 2.9 %collective-permute-start.1 = (f32[64,128]{1,0:T(8,128)S(1)}, f32[64,128]{1,0:T(8,128)S(1)}, u32[]{:S(2)}, u32[]{:S(2)}) collective-permute-start(f32[64,128]{1,0:T(8,128)S(1)} %get-tuple-element.33), channel_id=1, source_target_pairs={{0,128},{8,136},{16,144},{24,152},{32,160},{40,168},{48,176},{56,1... | collective-permute-start | bytes 98312 | tf_op jit(solution)/shard_map/ppermute | solution.py:47
  9.9 2.3 %collective-permute-done.1 = f32[64,128]{1,0:T(8,128)S(1)} collective-permute-done((f32[64,128]{1,0:T(8,128)S(1)}, f32[64,128]{1,0:T(8,128)S(1)}, u32[]{:S(2)}, u32[]{:S(2)}) %collective-permute-start.1) | collective-permute-done | bytes 32800 | tf_op jit(solution)/shard_map/ppermute | solution.py:47
  12.2 2.6 %collective-permute-done.2 = f32[64,128]{1,0:T(8,128)S(1)} collective-permute-done((f32[64,128]{1,0:T(8,128)S(1)}, f32[64,128]{1,0:T(8,128)S(1)}, u32[]{:S(2)}, u32[]{:S(2)}) %collective-permute-start.2) | collective-permute-done | bytes 32800 | tf_op jit(solution)/shard_map/ppermute | solution.py:47
  15.0 3.8 %collective-permute-done.3 = f32[64,128]{1,0:T(8,128)S(1)} collective-permute-done((f32[64,128]{1,0:T(8,128)S(1)}, f32[64,128]{1,0:T(8,128)S(1)}, u32[]{:S(2)}, u32[]{:S(2)}) %collective-permute-start.3) | collective-permute-done | bytes 32800 | tf_op jit(solution)/shard_map/ppermute | solution.py:47
  18.8 3.3 %collective-permute-start.4 = (f32[64,128]{1,0:T(8,128)S(1)}, f32[64,128]{1,0:T(8,128)S(1)}, u32[]{:S(2)}, u32[]{:S(2)}) collective-permute-start(f32[64,128]{1,0:T(8,128)S(1)} %add.45), channel_id=1, source_target_pairs={{0,16},{8,24},{16,0},{24,8},{32,48},{40,56},{48,32},{56,40},{64,80... | collective-permute-start | bytes 98312 | tf_op jit(solution)/shard_map/ppermute | solution.py:47
  22.1 1.9 %collective-permute-done.4 = f32[64,128]{1,0:T(8,128)S(1)} collective-permute-done((f32[64,128]{1,0:T(8,128)S(1)}, f32[64,128]{1,0:T(8,128)S(1)}, u32[]{:S(2)}, u32[]{:S(2)}) %collective-permute-start.4) | collective-permute-done | bytes 32800 | tf_op jit(solution)/shard_map/ppermute | solution.py:47
  24.0 6.1 %collective-permute-start.5 = (f32[64,128]{1,0:T(8,128)S(1)}, f32[64,128]{1,0:T(8,128)S(1)}, u32[]{:S(2)}, u32[]{:S(2)}) collective-permute-start(f32[64,128]{1,0:T(8,128)S(1)} %add.46), channel_id=1, source_target_pairs={{0,32},{8,40},{16,48},{24,56},{32,0},{40,8},{48,16},{56,24},{64,96... | collective-permute-start | bytes 98312 | tf_op jit(solution)/shard_map/ppermute | solution.py:47
  30.1 1.9 %collective-permute-done.5 = f32[64,128]{1,0:T(8,128)S(1)} collective-permute-done((f32[64,128]{1,0:T(8,128)S(1)}, f32[64,128]{1,0:T(8,128)S(1)}, u32[]{:S(2)}, u32[]{:S(2)}) %collective-permute-start.5) | collective-permute-done | bytes 32800 | tf_op jit(solution)/shard_map/ppermute | solution.py:47
  33.0 3.1 %collective-permute-start.6 = (f32[64,128]{1,0:T(8,128)S(1)}, f32[64,128]{1,0:T(8,128)S(1)}, u32[]{:S(2)}, u32[]{:S(2)}) collective-permute-start(f32[64,128]{1,0:T(8,128)S(1)} %add_multiply_fusion.refs_0_), channel_id=1, source_target_pairs={{0,64},{8,72},{16,80},{24,88},{32,96},{40,104},{48,112},{56,120},{... | collective-permute-start | bytes 98312 | tf_op jit(solution)/shard_map/ppermute | solution.py:47
  38.7 1.6 %project.1 = f32[32,16,128]{2,1,0:T(8,128)} custom-call(s32[1]{0:T(128)} %bitcast.rep_ref.refs_0_, bf16[1024,512]{1,0:T(8,128)(2,1)S(1)} %bitcast.11, bf16[1024,512]{1,0:T(8,128)(2,1)S(1)} %bitcast.15, bf16[192,512]{1,0:T(8,128)(2,1)S(1)} %get-tuple-element.36.parts_ref), custom_call_target="tpu_custom_call" | custom-call | flops 1000000000 | bytes 2500000 | tf_op jit(solution)/shard_map/project/pallas_call | solution.py:68
  40.3 10.7 %all-to-all-start = ((f32[32,16,128]{2,1,0:T(8,128)}), f32[32,16,128]{2,1,0:T(8,128)S(1)}, u32[]{:S(2)}, u32[]{:S(2)}) async-start(f32[32,16,128]{2,1,0:T(8,128)} %project.1), calls=%async_computation | async-start | bytes 524288 | tf_op jit(solution)/shard_map/all_to_all | solution.py:357
  51.0 2.8 %collective-permute-start.12 = (f32[64,64]{1,0:T(8,128)S(1)}, f32[64,64]{1,0:T(8,128)S(1)}, u32[]{:S(2)}, u32[]{:S(2)}) collective-permute-start(f32[64,64]{1,0:T(8,128)S(1)} %add.48), channel_id=1, source_target_pairs={{0,6},{1,7},{2,4},{3,5},{4,2},{5,3},{6,0},{7,1},{8,14},{9,15},{10,... | collective-permute-start | bytes 49160 | tf_op jit(solution)/shard_map/ppermute | solution.py:47
  56.2 3.1 %collective-permute-done.11 = f32[64,64]{1,0:T(8,128)S(1)} collective-permute-done((f32[64,64]{1,0:T(8,128)S(1)}, f32[64,64]{1,0:T(8,128)S(1)}, u32[]{:S(2)}, u32[]{:S(2)}) %collective-permute-start.11) | collective-permute-done | bytes 16416 | tf_op jit(solution)/shard_map/ppermute | solution.py:47
  59.3 2.2 %invert.1 = (f32[64,64]{1,0:T(8,128)S(1)}, f32[64,512]{1,0:T(8,128)S(1)}, bf16[384,512]{1,0:T(8,128)(2,1)S(1)}) custom-call(s32[1]{0:T(128)} %bitcast.rep_ref.refs_0_, f32[64,64]{1,0:T(8,128)S(1)} %add_add_fusion.gram_ref, f32[64,512]{1,0:T(8,128)S(1)} %get-tuple-element.39.factor_ref), custom_call_target="tpu_custom_call" | custom-call | flops 2000000000 | bytes 500000 | tf_op jit(solution)/shard_map/invert/pallas_call | solution.py:68
  61.5 2.5 %all-to-all-done = f32[32,16,128]{2,1,0:T(8,128)S(1)} async-done(((f32[32,16,128]{2,1,0:T(8,128)}), f32[32,16,128]{2,1,0:T(8,128)S(1)}, u32[]{:S(2)}, u32[]{:S(2)}) %all-to-all-start) | async-done | bytes 262176 | tf_op jit(solution)/shard_map/all_to_all | solution.py:357
  65.3 2.8 %collective-permute-start.16 = (f32[16,128]{1,0:T(8,128)S(1)}, f32[16,128]{1,0:T(8,128)S(1)}, u32[]{:S(2)}, u32[]{:S(2)}) collective-permute-start(f32[16,128]{1,0:T(8,128)S(1)} %add.52), channel_id=1, source_target_pairs={{0,6},{1,7},{2,4},{3,5},{4,2},{5,3},{6,0},{7,1},{8,14},{9,15},{10,... | collective-permute-start | bytes 24584 | tf_op jit(solution)/shard_map/ppermute | solution.py:47
  70.1 3.1 %collective-permute-done.15 = f32[16,128]{1,0:T(8,128)S(1)} collective-permute-done((f32[16,128]{1,0:T(8,128)S(1)}, f32[16,128]{1,0:T(8,128)S(1)}, u32[]{:S(2)}, u32[]{:S(2)}) %collective-permute-start.15) | collective-permute-done | bytes 8224 | tf_op jit(solution)/shard_map/ppermute | solution.py:47
  73.8 4.0 %collective-permute-done.17 = bf16[32,640]{1,0:T(8,128)(2,1)S(1)} collective-permute-done((bf16[32,640]{1,0:T(8,128)(2,1)S(1)}, bf16[32,640]{1,0:T(8,128)(2,1)S(1)}, u32[]{:S(2)}, u32[]{:S(2)}) %collective-permute-start.17) | collective-permute-done | bytes 40992 | tf_op jit(solution)/shard_map/ppermute | solution.py:47
  78.0 4.3 %collective-permute-start.19 = (bf16[2,32,640]{2,1,0:T(8,128)(2,1)S(1)}, bf16[2,32,640]{2,1,0:T(8,128)(2,1)S(1)}, u32[]{:S(2)}, u32[]{:S(2)}) collective-permute-start(bf16[2,32,640]{2,1,0:T(8,128)(2,1)S(1)} %pad_maximum_fusion), channel_id=1, source_target_pairs={{0,32},{8,40},{16,48},{24,56},{32,0},{40,8},{48,16},{56,24},{64,96... | collective-permute-start | bytes 245768 | tf_op jit(solution)/shard_map/ppermute | solution.py:47
  82.3 2.1 %collective-permute-start.18 = (bf16[2,32,640]{2,1,0:T(8,128)(2,1)S(1)}, bf16[2,32,640]{2,1,0:T(8,128)(2,1)S(1)}, u32[]{:S(2)}, u32[]{:S(2)}) collective-permute-start(bf16[2,32,640]{2,1,0:T(8,128)(2,1)S(1)} %pad_maximum_fusion), channel_id=1, source_target_pairs={{0,16},{8,24},{16,0},{24,8},{32,48},{40,56},{48,32},{56,40},{64,80... | collective-permute-start | bytes 245768 | tf_op jit(solution)/shard_map/ppermute | solution.py:47
  84.4 4.4 %collective-permute-done.18 = bf16[2,32,640]{2,1,0:T(8,128)(2,1)S(1)} collective-permute-done((bf16[2,32,640]{2,1,0:T(8,128)(2,1)S(1)}, bf16[2,32,640]{2,1,0:T(8,128)(2,1)S(1)}, u32[]{:S(2)}, u32[]{:S(2)}) %collective-permute-start.18) | collective-permute-done | bytes 81952 | tf_op jit(solution)/shard_map/ppermute | solution.py:47
  96.0 7.0 %collective-permute-done.23.refs_3_ = bf16[8,32,640]{2,1,0:T(8,128)(2,1)S(1)} collective-permute-done((bf16[8,32,640]{2,1,0:T(8,128)(2,1)S(1)}, bf16[8,32,640]{2,1,0:T(8,128)(2,1)S(1)}, u32[]{:S(2)}, u32[]{:S(2)}) %collective-permute-start.23) | collective-permute-done | bytes 327712 | tf_op jit(solution)/shard_map/ppermute | solution.py:47
  103.6 2.6 %finish_rest.1 = (bf16[1024,512]{1,0:T(8,128)(2,1)}, bf16[1024,512]{1,0:T(8,128)(2,1)}, f32[64,1024]{1,0:T(8,128)}) custom-call(s32[1]{0:T(128)} %bitcast.rep_ref.refs_0_, bf16[8,32,640]{2,1,0:T(8,128)(2,1)S(1)} %constant_dynamic-update-slice_fusion.block.refs_0_, ...), custom_call_target="tpu_custom_call", output_to_operand_aliasing={{0}: (8, {}), {1}: (9, {})} | custom-call | flops 1000000000 | bytes 4500000 | tf_op jit(solution)/shard_map/finish_rest/pallas_call | solution.py:68
  (67 shorter events, 22.9 us)
Async XLA Ops:
  5.1 4.8 %collective-permute-start = (f32[64,128]{1,0:T(8,128)S(1)}, f32[64,128]{1,0:T(8,128)S(1)}, u32[]{:S(2)}, u32[]{:S(2)}) collective-permute-start(f32[64,128]{1,0:T(8,128)S(1)} %get-tuple-element.32), channel_id=1, source_target_pairs={{0,64},{8,72},{16,80},{24,88},{32,96},{40,104},{48,112},{56,120},{... | collective-permute-start | bytes 98312 | tf_op jit(solution)/shard_map/ppermute | solution.py:47
  6.8 5.4 %collective-permute-start.1 = (f32[64,128]{1,0:T(8,128)S(1)}, f32[64,128]{1,0:T(8,128)S(1)}, u32[]{:S(2)}, u32[]{:S(2)}) collective-permute-start(f32[64,128]{1,0:T(8,128)S(1)} %get-tuple-element.33), channel_id=1, source_target_pairs={{0,128},{8,136},{16,144},{24,152},{32,160},{40,168},{48,176},{56,1... | collective-permute-start | bytes 98312 | tf_op jit(solution)/shard_map/ppermute | solution.py:47
  9.7 5.1 %collective-permute-start.2 = (f32[64,128]{1,0:T(8,128)S(1)}, f32[64,128]{1,0:T(8,128)S(1)}, u32[]{:S(2)}, u32[]{:S(2)}) collective-permute-start(f32[64,128]{1,0:T(8,128)S(1)} %get-tuple-element.34), channel_id=1, source_target_pairs={{0,192},{8,200},{16,208},{24,216},{32,224},{40,232},{48,240},{56,2... | collective-permute-start | bytes 98312 | tf_op jit(solution)/shard_map/ppermute | solution.py:47
  14.8 4.0 %collective-permute-start.3 = (f32[64,128]{1,0:T(8,128)S(1)}, f32[64,128]{1,0:T(8,128)S(1)}, u32[]{:S(2)}, u32[]{:S(2)}) collective-permute-start(f32[64,128]{1,0:T(8,128)S(1)} %add_add_fusion.1), channel_id=1, source_target_pairs={{0,8},{8,0},{16,24},{24,16},{32,40},{40,32},{48,56},{56,48},{64,72... | collective-permute-start | bytes 98312 | tf_op jit(solution)/shard_map/ppermute | solution.py:47
  18.8 5.2 %collective-permute-start.4 = (f32[64,128]{1,0:T(8,128)S(1)}, f32[64,128]{1,0:T(8,128)S(1)}, u32[]{:S(2)}, u32[]{:S(2)}) collective-permute-start(f32[64,128]{1,0:T(8,128)S(1)} %add.45), channel_id=1, source_target_pairs={{0,16},{8,24},{16,0},{24,8},{32,48},{40,56},{48,32},{56,40},{64,80... | collective-permute-start | bytes 98312 | tf_op jit(solution)/shard_map/ppermute | solution.py:47
  24.0 8.0 %collective-permute-start.5 = (f32[64,128]{1,0:T(8,128)S(1)}, f32[64,128]{1,0:T(8,128)S(1)}, u32[]{:S(2)}, u32[]{:S(2)}) collective-permute-start(f32[64,128]{1,0:T(8,128)S(1)} %add.46), channel_id=1, source_target_pairs={{0,32},{8,40},{16,48},{24,56},{32,0},{40,8},{48,16},{56,24},{64,96... | collective-permute-start | bytes 98312 | tf_op jit(solution)/shard_map/ppermute | solution.py:47
  32.0 5.1 %collective-permute-start.8 = (f32[64,128]{1,0:T(8,128)S(1)}, f32[64,128]{1,0:T(8,128)S(1)}, u32[]{:S(2)}, u32[]{:S(2)}) collective-permute-start(f32[64,128]{1,0:T(8,128)S(1)} %add_multiply_fusion.refs_0_), channel_id=1, source_target_pairs={{0,192},{8,200},{16,208},{24,216},{32,224},{40,232},{48,240},{56,2... | collective-permute-start | bytes 98312 | tf_op jit(solution)/shard_map/ppermute | solution.py:47
  32.3 5.4 %collective-permute-start.7 = (f32[64,128]{1,0:T(8,128)S(1)}, f32[64,128]{1,0:T(8,128)S(1)}, u32[]{:S(2)}, u32[]{:S(2)}) collective-permute-start(f32[64,128]{1,0:T(8,128)S(1)} %add_multiply_fusion.refs_0_), channel_id=1, source_target_pairs={{0,128},{8,136},{16,144},{24,152},{32,160},{40,168},{48,176},{56,1... | collective-permute-start | bytes 98312 | tf_op jit(solution)/shard_map/ppermute | solution.py:47
  33.0 5.3 %collective-permute-start.6 = (f32[64,128]{1,0:T(8,128)S(1)}, f32[64,128]{1,0:T(8,128)S(1)}, u32[]{:S(2)}, u32[]{:S(2)}) collective-permute-start(f32[64,128]{1,0:T(8,128)S(1)} %add_multiply_fusion.refs_0_), channel_id=1, source_target_pairs={{0,64},{8,72},{16,80},{24,88},{32,96},{40,104},{48,112},{56,120},{... | collective-permute-start | bytes 98312 | tf_op jit(solution)/shard_map/ppermute | solution.py:47
  38.6 1.7 %collective-permute-start.9 = (f32[64,64]{1,0:T(8,128)S(1)}, f32[64,64]{1,0:T(8,128)S(1)}, u32[]{:S(2)}, u32[]{:S(2)}) collective-permute-start(f32[64,64]{1,0:T(8,128)S(1)} %get-tuple-element.35), channel_id=1, source_target_pairs={{0,1},{1,0},{2,3},{3,2},{4,5},{5,4},{6,7},{7,6},{8,9},{9,8},{10,11... | collective-permute-start | bytes 49160 | tf_op jit(solution)/shard_map/ppermute | solution.py:47
  40.3 23.6 %all-to-all-start = ((f32[32,16,128]{2,1,0:T(8,128)}), f32[32,16,128]{2,1,0:T(8,128)S(1)}, u32[]{:S(2)}, u32[]{:S(2)}) async-start(f32[32,16,128]{2,1,0:T(8,128)} %project.1), calls=%async_computation | async-start | bytes 524288 | tf_op jit(solution)/shard_map/all_to_all | solution.py:357
  51.0 5.2 %collective-permute-start.12 = (f32[64,64]{1,0:T(8,128)S(1)}, f32[64,64]{1,0:T(8,128)S(1)}, u32[]{:S(2)}, u32[]{:S(2)}) collective-permute-start(f32[64,64]{1,0:T(8,128)S(1)} %add.48), channel_id=1, source_target_pairs={{0,6},{1,7},{2,4},{3,5},{4,2},{5,3},{6,0},{7,1},{8,14},{9,15},{10,... | collective-permute-start | bytes 49160 | tf_op jit(solution)/shard_map/ppermute | solution.py:47
  53.9 5.4 %collective-permute-start.11 = (f32[64,64]{1,0:T(8,128)S(1)}, f32[64,64]{1,0:T(8,128)S(1)}, u32[]{:S(2)}, u32[]{:S(2)}) collective-permute-start(f32[64,64]{1,0:T(8,128)S(1)} %add.48), channel_id=1, source_target_pairs={{0,4},{1,5},{2,6},{3,7},{4,0},{5,1},{6,2},{7,3},{8,12},{9,13},{10,... | collective-permute-start | bytes 49160 | tf_op jit(solution)/shard_map/ppermute | solution.py:47
  54.7 4.6 %collective-permute-start.10 = (f32[64,64]{1,0:T(8,128)S(1)}, f32[64,64]{1,0:T(8,128)S(1)}, u32[]{:S(2)}, u32[]{:S(2)}) collective-permute-start(f32[64,64]{1,0:T(8,128)S(1)} %add.48), channel_id=1, source_target_pairs={{0,2},{1,3},{2,0},{3,1},{4,6},{5,7},{6,4},{7,5},{8,10},{9,11},{10,... | collective-permute-start | bytes 49160 | tf_op jit(solution)/shard_map/ppermute | solution.py:47
  65.3 4.9 %collective-permute-start.16 = (f32[16,128]{1,0:T(8,128)S(1)}, f32[16,128]{1,0:T(8,128)S(1)}, u32[]{:S(2)}, u32[]{:S(2)}) collective-permute-start(f32[16,128]{1,0:T(8,128)S(1)} %add.52), channel_id=1, source_target_pairs={{0,6},{1,7},{2,4},{3,5},{4,2},{5,3},{6,0},{7,1},{8,14},{9,15},{10,... | collective-permute-start | bytes 24584 | tf_op jit(solution)/shard_map/ppermute | solution.py:47
  68.0 5.2 %collective-permute-start.15 = (f32[16,128]{1,0:T(8,128)S(1)}, f32[16,128]{1,0:T(8,128)S(1)}, u32[]{:S(2)}, u32[]{:S(2)}) collective-permute-start(f32[16,128]{1,0:T(8,128)S(1)} %add.52), channel_id=1, source_target_pairs={{0,4},{1,5},{2,6},{3,7},{4,0},{5,1},{6,2},{7,3},{8,12},{9,13},{10,... | collective-permute-start | bytes 24584 | tf_op jit(solution)/shard_map/ppermute | solution.py:47
  68.8 4.4 %collective-permute-start.14 = (f32[16,128]{1,0:T(8,128)S(1)}, f32[16,128]{1,0:T(8,128)S(1)}, u32[]{:S(2)}, u32[]{:S(2)}) collective-permute-start(f32[16,128]{1,0:T(8,128)S(1)} %add.52), channel_id=1, source_target_pairs={{0,2},{1,3},{2,0},{3,1},{4,6},{5,7},{6,4},{7,5},{8,10},{9,11},{10,... | collective-permute-start | bytes 24584 | tf_op jit(solution)/shard_map/ppermute | solution.py:47
  73.7 4.1 %collective-permute-start.17 = (bf16[32,640]{1,0:T(8,128)(2,1)S(1)}, bf16[32,640]{1,0:T(8,128)(2,1)S(1)}, u32[]{:S(2)}, u32[]{:S(2)}) collective-permute-start(bf16[32,640]{1,0:T(8,128)(2,1)S(1)} %get-tuple-element.46), channel_id=1, source_target_pairs={{0,8},{8,0},{16,24},{24,16},{32,40},{40,32},{48,56},{56,48},{64,72... | collective-permute-start | bytes 122888 | tf_op jit(solution)/shard_map/ppermute | solution.py:47
  77.8 11.1 %collective-permute-start.20 = (bf16[2,32,640]{2,1,0:T(8,128)(2,1)S(1)}, bf16[2,32,640]{2,1,0:T(8,128)(2,1)S(1)}, u32[]{:S(2)}, u32[]{:S(2)}) collective-permute-start(bf16[2,32,640]{2,1,0:T(8,128)(2,1)S(1)} %pad_maximum_fusion), channel_id=1, source_target_pairs={{0,48},{8,56},{16,32},{24,40},{32,16},{40,24},{48,0},{56,8},{64,11... | collective-permute-start | bytes 245768 | tf_op jit(solution)/shard_map/ppermute | solution.py:47
  78.0 10.8 %collective-permute-start.19 = (bf16[2,32,640]{2,1,0:T(8,128)(2,1)S(1)}, bf16[2,32,640]{2,1,0:T(8,128)(2,1)S(1)}, u32[]{:S(2)}, u32[]{:S(2)}) collective-permute-start(bf16[2,32,640]{2,1,0:T(8,128)(2,1)S(1)} %pad_maximum_fusion), channel_id=1, source_target_pairs={{0,32},{8,40},{16,48},{24,56},{32,0},{40,8},{48,16},{56,24},{64,96... | collective-permute-start | bytes 245768 | tf_op jit(solution)/shard_map/ppermute | solution.py:47
  82.3 6.5 %collective-permute-start.18 = (bf16[2,32,640]{2,1,0:T(8,128)(2,1)S(1)}, bf16[2,32,640]{2,1,0:T(8,128)(2,1)S(1)}, u32[]{:S(2)}, u32[]{:S(2)}) collective-permute-start(bf16[2,32,640]{2,1,0:T(8,128)(2,1)S(1)} %pad_maximum_fusion), channel_id=1, source_target_pairs={{0,16},{8,24},{16,0},{24,8},{32,48},{40,56},{48,32},{56,40},{64,80... | collective-permute-start | bytes 245768 | tf_op jit(solution)/shard_map/ppermute | solution.py:47
  88.9 14.1 %collective-permute-start.23 = (bf16[8,32,640]{2,1,0:T(8,128)(2,1)S(1)}, bf16[8,32,640]{2,1,0:T(8,128)(2,1)S(1)}, u32[]{:S(2)}, u32[]{:S(2)}) collective-permute-start(bf16[8,32,640]{2,1,0:T(8,128)(2,1)S(1)} %constant_dynamic-update-slice_fusion.block.refs_0_), channel_id=1, source_target_pairs={{0,192},{8,200},{16,208},{24,216},{32,224},{40,232},{48,240},{56,2... | collective-permute-start | bytes 983048 | tf_op jit(solution)/shard_map/ppermute | solution.py:47
  90.5 12.5 %collective-permute-start.22 = (bf16[8,32,640]{2,1,0:T(8,128)(2,1)S(1)}, bf16[8,32,640]{2,1,0:T(8,128)(2,1)S(1)}, u32[]{:S(2)}, u32[]{:S(2)}) collective-permute-start(bf16[8,32,640]{2,1,0:T(8,128)(2,1)S(1)} %constant_dynamic-update-slice_fusion.block.refs_0_), channel_id=1, source_target_pairs={{0,128},{8,136},{16,144},{24,152},{32,160},{40,168},{48,176},{56,1... | collective-permute-start | bytes 983048 | tf_op jit(solution)/shard_map/ppermute | solution.py:47
  91.7 12.0 %collective-permute-start.21 = (bf16[8,32,640]{2,1,0:T(8,128)(2,1)S(1)}, bf16[8,32,640]{2,1,0:T(8,128)(2,1)S(1)}, u32[]{:S(2)}, u32[]{:S(2)}) collective-permute-start(bf16[8,32,640]{2,1,0:T(8,128)(2,1)S(1)} %constant_dynamic-update-slice_fusion.block.refs_0_), channel_id=1, source_target_pairs={{0,64},{8,72},{16,80},{24,88},{32,96},{40,104},{48,112},{56,120},{... | collective-permute-start | bytes 983048 | tf_op jit(solution)/shard_map/ppermute | solution.py:47
  (9 other events, 101.8 us)

commit v4 on v3

--- a/solution.py
+++ b/solution.py
@@ -18,6 +18,7 @@
 Y_SIZE, Z_SIZE = 4, 8
 Y_STEPS = (8, 16, 24)
 X_STEPS = (2, 4, 6)
+ROW_BLOCKS = 4
 
 
 def exact(left, right, left_dim, right_dim):
@@ -86,49 +87,61 @@
     )
 
 
-def factor_kernel(rep_ref, warm_ref, grad_ref, feed_ref, *refs):
-    outs, parts_ref, total_ref = refs[:-2], refs[-2], refs[-1]
-    rank = warm_ref.shape[0]
-    width = grad_ref.shape[1]
+def factor_kernel(rep_ref, warm_far, grad_far, feed_far, *refs):
+    outs, (grad_ref, feed_ref, warm_ref, parts_ref, total_ref, sems) = refs[:Y_SIZE], refs[Y_SIZE:]
+    rank, rows = warm_ref.shape
     quarter = outs[0].shape[1]
-    step = pl.program_id(0)
-
-    @pl.when(step == 0)
-    def _():
-        for i, part in enumerate(three_parts(warm_ref[...])):
-            parts_ref[i * rank : (i + 1) * rank, :] = part
-
-    total = native(parts_ref[...], grad_ref[...], 1, 0) + native(parts_ref[...], feed_ref[...], 1, 0)
-    total = (total[2 * rank :] + total[rank : 2 * rank]) + total[:rank]
-    total_ref[:, pl.ds(pl.multiple_of(step * width, width), width)] = total
-
-    @pl.when(step == pl.num_programs(0) - 1)
-    def _():
-        own = rep_ref[0] // Z_SIZE
-        for d, out in enumerate(outs):
-            out[...] = total_ref[:, pl.ds(pl.multiple_of((own ^ d) * quarter, quarter), quarter)]
+    size = rows // ROW_BLOCKS
+    warm_copy = pltpu.make_async_copy(warm_far, warm_ref, sems.at[2 * ROW_BLOCKS])
+    warm_copy.start()
+    copies = []
+    for i in range(ROW_BLOCKS):
+        at = pl.ds(i * size, size)
+        for k, (far, ref) in enumerate([(grad_far, grad_ref), (feed_far, feed_ref)]):
+            copies.append(pltpu.make_async_copy(far.at[at], ref.at[at], sems.at[2 * i + k]))
+            copies[-1].start()
+    warm_copy.wait()
+    for i, part in enumerate(three_parts(warm_ref[...])):
+        parts_ref[i * rank : (i + 1) * rank, :] = part
+    total = None
+    for i in range(ROW_BLOCKS):
+        at = slice(i * size, (i + 1) * size)
+        copies[2 * i].wait()
+        copies[2 * i + 1].wait()
+        parts = parts_ref[:, at]
+        term = native(parts, grad_ref[at, :], 1, 0) + native(parts, feed_ref[at, :], 1, 0)
+        total = term if total is None else total + term
+    total_ref[...] = (total[2 * rank :] + total[rank : 2 * rank]) + total[:rank]
+    own = rep_ref[0] // Z_SIZE
+    for d, out in enumerate(outs):
+        out[...] = total_ref[:, pl.ds(pl.multiple_of((own ^ d) * quarter, quarter), quarter)]
 
 
 def local_factor(rep, warm_t, gradient, feedback):
     rank, rows = warm_t.shape
     columns = gradient.shape[1]
-    quarter = columns // Y_SIZE
-    steps = 2
-    column_block = pl.BlockSpec((rows, columns // steps), lambda i, rep: (0, i))
-    return pl.pallas_call(
+    near = pltpu.VMEM((rows, columns), BF16)
+    args = [pltpu.with_memory_space_constraint(v, pltpu.HBM) for v in (warm_t, gradient, feedback)]
+    outs = pl.pallas_call(
         factor_kernel,
-        out_shape=[pltpu.VMEM((rank, quarter), F32)] * Y_SIZE,
+        out_shape=[pltpu.VMEM((rank, columns // Y_SIZE), F32)] * Y_SIZE + [near] * 2,
         grid_spec=pltpu.PrefetchScalarGridSpec(
             num_scalar_prefetch=1,
-            grid=(steps,),
-            in_specs=[whole((rank, rows)), column_block, column_block],
-            out_specs=[whole((rank, quarter))] * Y_SIZE,
-            scratch_shapes=[pltpu.VMEM((3 * rank, rows), BF16), pltpu.VMEM((rank, columns), F32)],
+            grid=(1,),
+            in_specs=[pl.BlockSpec(memory_space=pl.ANY)] * 3,
+            out_specs=[pl.BlockSpec(memory_space=pltpu.VMEM)] * (Y_SIZE + 2),
+            scratch_shapes=[
+                pltpu.VMEM((rank, rows), F32),
+                pltpu.VMEM((3 * rank, rows), BF16),
+                pltpu.VMEM((rank, columns), F32),
+                pltpu.SemaphoreType.DMA((2 * ROW_BLOCKS + 1,)),
+            ],
         ),
         compiler_params=pltpu.CompilerParams(vmem_limit_bytes=16 * 2**20),
         cost_estimate=pl.CostEstimate(flops=10**9, bytes_accessed=2_500_000, transcendentals=0),
         name="local_factor",
-    )(rep, warm_t, gradient, feedback)
+    )(rep, *args)
+    return outs[:Y_SIZE], outs[Y_SIZE], outs[Y_SIZE + 1]
 
 
 def assemble_kernel(rep_ref, *refs):
@@ -256,7 +269,7 @@
     return call(kernel, outs, args, (5 * 10**7, 600_000), "update")
 
 
-def finish_rows(own_y, own_z, d, block, parts_ref, grad_ref, feed_ref, new_ref, weights_ref):
+def new_rows(own_y, own_z, d, block, parts_ref, grad_ref, feed_ref, out_ref):
     columns = grad_ref.shape[1]
     groups, own_rows, width = block.shape
     right = block[:, :, columns:].reshape(groups * own_rows, width - columns)
@@ -266,75 +279,71 @@
         at = pl.multiple_of((own_z ^ j) * own_rows, own_rows)
         source = pl.ds(pl.multiple_of(first + at, own_rows), own_rows)
         merged = grad_ref[source, :].astype(F32) + feed_ref[source, :].astype(F32)
-        rows = pl.ds(at, own_rows)
         piece = approx[j * own_rows : (j + 1) * own_rows]
-        new_ref[rows, :] = (merged - piece).astype(BF16)
-        weights_ref[rows, :] = block[j, :, :columns]
-
-
-def finish_own_kernel(rep_ref, block, parts_ref, grad_ref, feed_ref, new_ref, weights_ref):
-    own_y, own_z = rep_ref[0] // Z_SIZE, rep_ref[0] % Z_SIZE
-    finish_rows(own_y, own_z, 0, block, parts_ref, grad_ref, feed_ref, new_ref, weights_ref)
-
-
-def finish_rest_kernel(rep_ref, *refs):
-    blocks, (parts_ref, grad_ref, feed_ref) = refs[:Y_SIZE], refs[Y_SIZE : Y_SIZE + 3]
-    new_ref, weights_ref, right_ref, right_rows = refs[Y_SIZE + 5 :]
+        out_ref[pl.ds(at, own_rows), :] = (merged - piece).astype(BF16)
+
+
+def finish_kernel(begins, ds, rep_ref, *refs):
+    count = Y_SIZE if not begins else len(ds)
+    blocks, (parts_ref, grad_ref, feed_ref) = refs[:count], refs[count : count + 3]
+    rest = refs[count + 3 :] if begins else refs[count + 5 :]
+    if begins:
+        new_far, weights_far, new_near, sems = rest
+    else:
+        new_far, weights_far, right_ref, new_near, right_rows, sems = rest
     columns = grad_ref.shape[1]
     groups, own_rows, width = blocks[0].shape
+    size = groups * own_rows
     rank = (width - columns) // 2
     own_y, own_z = rep_ref[0] // Z_SIZE, rep_ref[0] % Z_SIZE
-    step = pl.program_id(0)
-    for d in range(1, Y_SIZE):
-
-        @pl.when(step == d - 1)
-        def _(d=d):
-            finish_rows(
-                own_y, own_z, d, blocks[d], parts_ref, grad_ref, feed_ref, new_ref, weights_ref
-            )
-
-    @pl.when(step == 0)
-    def _():
+    copies = []
+
+    def send(source, target):
+        copies.append(pltpu.make_async_copy(source, target, sems.at[len(copies)]))
+        copies[-1].start()
+
+    def rows_of(d, j):
+        at = (own_y ^ d) * size + (own_z ^ j) * own_rows
+        return pl.ds(pl.multiple_of(at, own_rows), own_rows)
+
+    for i, d in enumerate(ds):
+        for j in range(groups):
+            send(blocks[d].at[j, :, pl.ds(0, columns)], weights_far.at[rows_of(d, j)])
+        new_rows(own_y, own_z, d, blocks[d], parts_ref, grad_ref, feed_ref, new_near.at[i])
+        target = pl.ds(pl.multiple_of((own_y ^ d) * size, size), size)
+        send(new_near.at[i], new_far.at[target])
+    if not begins:
         for d, block in enumerate(blocks):
             for j in range(groups):
-                at = (own_y ^ d) * (groups * own_rows) + (own_z ^ j) * own_rows
                 wide = block[j, :, columns:].astype(F32)
-                rows = pl.ds(pl.multiple_of(at, own_rows), own_rows)
-                right_rows[rows, :] = wide[:, :rank] + wide[:, rank:]
+                right_rows[rows_of(d, j), :] = wide[:, :rank] + wide[:, rank:]
         right_ref[...] = right_rows[...].T
-
-
-def finish_own(rep, block, parts, gradient, feedback):
+    for copy in copies:
+        copy.wait()
+
+
+def finish(begins, ds, rep, blocks, parts, gradient, feedback, begun=()):
     rows, columns = gradient.shape
-    row_block = pl.BlockSpec((rows // Y_SIZE, columns), lambda i, rep: (rep[0] // Z_SIZE, 0))
+    groups, own_rows, width = blocks[0].shape
+    rank = (width - columns) // 2
+    far = pl.BlockSpec(memory_space=pl.ANY)
+    outs = [jax.ShapeDtypeStruct((rows, columns), BF16)] * 2
+    out_specs = [far, far]
+    scratch = [pltpu.VMEM((len(ds), groups * own_rows, columns), BF16)]
+    if not begins:
+        outs = outs + [jax.ShapeDtypeStruct((rank, rows), F32)]
+        out_specs = out_specs + [whole((rank, rows))]
+        scratch = scratch + [pltpu.VMEM((rows, rank), F32)]
     return call(
-        finish_own_kernel,
-        [jax.ShapeDtypeStruct((rows, columns), BF16)] * 2,
-        (rep, block, parts, gradient, feedback),
-        (10**9, 1_500_000),
-        "finish_own",
-        out_specs=[row_block, row_block],
-    )
-
-
-def finish_rest(rep, blocks, parts, gradient, feedback, begun):
-    rows, columns = gradient.shape
-    rank = (blocks[0].shape[2] - columns) // 2
-    row_block = pl.BlockSpec(
-        (rows // Y_SIZE, columns), lambda i, rep: ((rep[0] // Z_SIZE) ^ (i + 1), 0)
-    )
-    return call(
-        finish_rest_kernel,
-        [jax.ShapeDtypeStruct((rows, columns), BF16)] * 2
-        + [jax.ShapeDtypeStruct((rank, rows), F32)],
+        lambda *refs: finish_kernel(begins, ds, *refs),
+        outs,
         (rep, *blocks, parts, gradient, feedback),
-        (10**9, 4_500_000),
-        "finish_rest",
-        aliases={Y_SIZE + 4: 0, Y_SIZE + 5: 1},
-        grid=(Y_SIZE - 1,),
-        out_specs=[row_block, row_block, whole((rank, rows))],
+        (len(ds) * 3 * 10**8, len(ds) * 1_500_000),
+        "finish_own" if begins else "finish_rest",
+        aliases={} if begins else {Y_SIZE + 4: 0, Y_SIZE + 5: 1},
+        out_specs=out_specs,
         spare=begun,
-        scratch=[pltpu.VMEM((rows, rank), F32)],
+        scratch=scratch + [pltpu.SemaphoreType.DMA((len(ds) * (groups + 1),))],
     )
 
 
@@ -343,7 +352,7 @@
     gradient, feedback = gradient[0], feedback[0]
     rep = lax.axis_index("rep").astype(jnp.int32).reshape(1)
 
-    pieces = local_factor(rep, warm_start.T, gradient, feedback)
+    pieces, gradient, feedback = local_factor(rep, warm_start.T, gradient, feedback)
     quarter = sum_four([pieces[0]] + [exchange(p, "rep", d) for p, d in zip(pieces[1:], Y_STEPS)])
     for distance in (1, 2, 4):
         quarter = quarter + exchange(quarter, "rep", distance)
@@ -368,9 +377,10 @@
     pair = jnp.stack([send, exchange(send, "rep", 1)])
     column = jnp.concatenate([pair] + [exchange(pair, "rep", d) for d in (2, 4, 6)])
     others = [exchange(column, "rep", d) for d in Y_STEPS]
-    begun = finish_own(rep, column, unit_parts, gradient, feedback)
-    new_feedback, weights, right_t = finish_rest(
-        rep, [column] + others, unit_parts, gradient, feedback, begun
+    begun = finish(True, (0,), rep, [column], unit_parts, gradient, feedback)
+    blocks = [column] + others
+    new_feedback, weights, right_t = finish(
+        False, (1, 2, 3), rep, blocks, unit_parts, gradient, feedback, begun
     )
     return (new_feedback[None], weights, master_out, moment_out, second_out, right_t.T)
 

time: 108 us -> 105 us (0.972)
  local copies, waits for them, and re-layouts: 5.36 us -> 1.96 us
    unnamed x23 -> x13, local copies, waits for them, and re-layouts: 5.34 us -> 1.95 us
  transfers between devices with their start and end apart: 25 -> 25, of which waited for: 18 -> 18; matrix products, arithmetic and copies ran while one was open for 2% -> 2% of each run, Pallas kernels for 4% -> 5%
where the time goes in v4:
time: 105 us; the launch traced here: 104 us
  starting transfers between devices  48.4 us (46%)
  waiting for transfers between devices  42.3 us (40%)
  Pallas kernels  9.95 us (9%)
  local copies, waits for them, and re-layouts  1.96 us (2%)
    ppermute x24, waiting for transfers between devices, exchange(): lax.ppermute(value, axis, [(i, i ^ distance) for i in range(lax.axis_size...  39.8 us
    ppermute x24, starting transfers between devices, exchange(): lax.ppermute(value, axis, [(i, i ^ distance) for i in range(lax.axis_size...  37.8 us
    all_to_all x1, starting transfers between devices, on_device(): received = lax.all_to_all(packed, 'rep', 0, 0, tiled=True)  10.7 us
    pallas_call x6, Pallas kernels, call(): pl.pallas_call(kernel, out_shape=outs, grid_spec=pltpu.PrefetchScalarGrid...  8.01 us
    all_to_all x1, waiting for transfers between devices, on_device(): received = lax.all_to_all(packed, 'rep', 0, 0, tiled=True)  2.45 us
  transfers between devices with their start and end apart: 25, of which 18 were waited for; matrix products, arithmetic and copies ran while one was open for 2% of the time, Pallas kernels for 5%

profile of v4, /device:TPU:32, one launch (start us, length us, event | category | flops | bytes accessed | tf_op | source)
XLA Modules:
  0.0 103.7 jit_solution(849797196931820213)
XLA Ops:
  0.6 1.9 %local_factor.1 = (f32[64,128]{1,0:T(8,128)S(1)}, f32[64,128]{1,0:T(8,128)S(1)}, f32[64,128]{1,0:T(8,128)S(1)}, f32[64,128]{1,0:T(8,128)S(1)}, bf16[1024,512]{1,...) custom-call(s32[1]{0:T(128)} %bitcast.rep_ref.refs_0_, f32[64,1024]{1,0:T(8,128)} %bitcast.15, bf16[1024,512]{1,0:T(8,128)(2,1)} %bitcast.13, ...), custom_call_target="tpu_custom_call" | custom-call | flops 1000000000 | bytes 2500000 | tf_op jit(solution)/shard_map/local_factor/pallas_call | solution.py:125
  2.6 1.7 %collective-permute-start = (f32[64,128]{1,0:T(8,128)S(1)}, f32[64,128]{1,0:T(8,128)S(1)}, u32[]{:S(2)}, u32[]{:S(2)}) collective-permute-start(f32[64,128]{1,0:T(8,128)S(1)} %get-tuple-element.34), channel_id=1, source_target_pairs={{0,64},{8,72},{16,80},{24,88},{32,96},{40,104},{48,112},{56,120},{... | collective-permute-start | bytes 98312 | tf_op jit(solution)/shard_map/ppermute | solution.py:48
  4.3 2.9 %collective-permute-start.1 = (f32[64,128]{1,0:T(8,128)S(1)}, f32[64,128]{1,0:T(8,128)S(1)}, u32[]{:S(2)}, u32[]{:S(2)}) collective-permute-start(f32[64,128]{1,0:T(8,128)S(1)} %get-tuple-element.35), channel_id=1, source_target_pairs={{0,128},{8,136},{16,144},{24,152},{32,160},{40,168},{48,176},{56,1... | collective-permute-start | bytes 98312 | tf_op jit(solution)/shard_map/ppermute | solution.py:48
  7.4 2.3 %collective-permute-done.1 = f32[64,128]{1,0:T(8,128)S(1)} collective-permute-done((f32[64,128]{1,0:T(8,128)S(1)}, f32[64,128]{1,0:T(8,128)S(1)}, u32[]{:S(2)}, u32[]{:S(2)}) %collective-permute-start.1) | collective-permute-done | bytes 32800 | tf_op jit(solution)/shard_map/ppermute | solution.py:48
  9.7 2.6 %collective-permute-done.2 = f32[64,128]{1,0:T(8,128)S(1)} collective-permute-done((f32[64,128]{1,0:T(8,128)S(1)}, f32[64,128]{1,0:T(8,128)S(1)}, u32[]{:S(2)}, u32[]{:S(2)}) %collective-permute-start.2) | collective-permute-done | bytes 32800 | tf_op jit(solution)/shard_map/ppermute | solution.py:48
  12.5 3.8 %collective-permute-done.3 = f32[64,128]{1,0:T(8,128)S(1)} collective-permute-done((f32[64,128]{1,0:T(8,128)S(1)}, f32[64,128]{1,0:T(8,128)S(1)}, u32[]{:S(2)}, u32[]{:S(2)}) %collective-permute-start.3) | collective-permute-done | bytes 32800 | tf_op jit(solution)/shard_map/ppermute | solution.py:48
  16.3 3.3 %collective-permute-start.4 = (f32[64,128]{1,0:T(8,128)S(1)}, f32[64,128]{1,0:T(8,128)S(1)}, u32[]{:S(2)}, u32[]{:S(2)}) collective-permute-start(f32[64,128]{1,0:T(8,128)S(1)} %add.45), channel_id=1, source_target_pairs={{0,16},{8,24},{16,0},{24,8},{32,48},{40,56},{48,32},{56,40},{64,80... | collective-permute-start | bytes 98312 | tf_op jit(solution)/shard_map/ppermute | solution.py:48
  19.6 1.9 %collective-permute-done.4 = f32[64,128]{1,0:T(8,128)S(1)} collective-permute-done((f32[64,128]{1,0:T(8,128)S(1)}, f32[64,128]{1,0:T(8,128)S(1)}, u32[]{:S(2)}, u32[]{:S(2)}) %collective-permute-start.4) | collective-permute-done | bytes 32800 | tf_op jit(solution)/shard_map/ppermute | solution.py:48
  21.5 6.1 %collective-permute-start.5 = (f32[64,128]{1,0:T(8,128)S(1)}, f32[64,128]{1,0:T(8,128)S(1)}, u32[]{:S(2)}, u32[]{:S(2)}) collective-permute-start(f32[64,128]{1,0:T(8,128)S(1)} %add.46), channel_id=1, source_target_pairs={{0,32},{8,40},{16,48},{24,56},{32,0},{40,8},{48,16},{56,24},{64,96... | collective-permute-start | bytes 98312 | tf_op jit(solution)/shard_map/ppermute | solution.py:48
  27.6 1.9 %collective-permute-done.5 = f32[64,128]{1,0:T(8,128)S(1)} collective-permute-done((f32[64,128]{1,0:T(8,128)S(1)}, f32[64,128]{1,0:T(8,128)S(1)}, u32[]{:S(2)}, u32[]{:S(2)}) %collective-permute-start.5) | collective-permute-done | bytes 32800 | tf_op jit(solution)/shard_map/ppermute | solution.py:48
  30.5 3.1 %collective-permute-start.6 = (f32[64,128]{1,0:T(8,128)S(1)}, f32[64,128]{1,0:T(8,128)S(1)}, u32[]{:S(2)}, u32[]{:S(2)}) collective-permute-start(f32[64,128]{1,0:T(8,128)S(1)} %add_multiply_fusion.refs_0_), channel_id=1, source_target_pairs={{0,64},{8,72},{16,80},{24,88},{32,96},{40,104},{48,112},{56,120},{... | collective-permute-start | bytes 98312 | tf_op jit(solution)/shard_map/ppermute | solution.py:48
  37.8 10.7 %all-to-all-start = ((f32[32,16,128]{2,1,0:T(8,128)}), f32[32,16,128]{2,1,0:T(8,128)S(1)}, u32[]{:S(2)}, u32[]{:S(2)}) async-start(f32[32,16,128]{2,1,0:T(8,128)} %project.1), calls=%async_computation | async-start | bytes 524288 | tf_op jit(solution)/shard_map/all_to_all | solution.py:366
  48.5 2.9 %collective-permute-start.12 = (f32[64,64]{1,0:T(8,128)S(1)}, f32[64,64]{1,0:T(8,128)S(1)}, u32[]{:S(2)}, u32[]{:S(2)}) collective-permute-start(f32[64,64]{1,0:T(8,128)S(1)} %add.48), channel_id=1, source_target_pairs={{0,6},{1,7},{2,4},{3,5},{4,2},{5,3},{6,0},{7,1},{8,14},{9,15},{10,... | collective-permute-start | bytes 49160 | tf_op jit(solution)/shard_map/ppermute | solution.py:48
  53.7 3.1 %collective-permute-done.11 = f32[64,64]{1,0:T(8,128)S(1)} collective-permute-done((f32[64,64]{1,0:T(8,128)S(1)}, f32[64,64]{1,0:T(8,128)S(1)}, u32[]{:S(2)}, u32[]{:S(2)}) %collective-permute-start.11) | collective-permute-done | bytes 16416 | tf_op jit(solution)/shard_map/ppermute | solution.py:48
  56.8 2.2 %invert.1 = (f32[64,64]{1,0:T(8,128)S(1)}, f32[64,512]{1,0:T(8,128)S(1)}, bf16[384,512]{1,0:T(8,128)(2,1)S(1)}) custom-call(s32[1]{0:T(128)} %bitcast.rep_ref.refs_0_, f32[64,64]{1,0:T(8,128)S(1)} %add_add_fusion.gram_ref, f32[64,512]{1,0:T(8,128)S(1)} %get-tuple-element.43.factor_ref), custom_call_target="tpu_custom_call" | custom-call | flops 2000000000 | bytes 500000 | tf_op jit(solution)/shard_map/invert/pallas_call | solution.py:69
  59.0 2.4 %all-to-all-done = f32[32,16,128]{2,1,0:T(8,128)S(1)} async-done(((f32[32,16,128]{2,1,0:T(8,128)}), f32[32,16,128]{2,1,0:T(8,128)S(1)}, u32[]{:S(2)}, u32[]{:S(2)}) %all-to-all-start) | async-done | bytes 262176 | tf_op jit(solution)/shard_map/all_to_all | solution.py:366
  62.7 2.8 %collective-permute-start.16 = (f32[16,128]{1,0:T(8,128)S(1)}, f32[16,128]{1,0:T(8,128)S(1)}, u32[]{:S(2)}, u32[]{:S(2)}) collective-permute-start(f32[16,128]{1,0:T(8,128)S(1)} %add.52), channel_id=1, source_target_pairs={{0,6},{1,7},{2,4},{3,5},{4,2},{5,3},{6,0},{7,1},{8,14},{9,15},{10,... | collective-permute-start | bytes 24584 | tf_op jit(solution)/shard_map/ppermute | solution.py:48
  67.6 3.1 %collective-permute-done.15 = f32[16,128]{1,0:T(8,128)S(1)} collective-permute-done((f32[16,128]{1,0:T(8,128)S(1)}, f32[16,128]{1,0:T(8,128)S(1)}, u32[]{:S(2)}, u32[]{:S(2)}) %collective-permute-start.15) | collective-permute-done | bytes 8224 | tf_op jit(solution)/shard_map/ppermute | solution.py:48
  71.3 4.0 %collective-permute-done.17 = bf16[32,640]{1,0:T(8,128)(2,1)S(1)} collective-permute-done((bf16[32,640]{1,0:T(8,128)(2,1)S(1)}, bf16[32,640]{1,0:T(8,128)(2,1)S(1)}, u32[]{:S(2)}, u32[]{:S(2)}) %collective-permute-start.17) | collective-permute-done | bytes 40992 | tf_op jit(solution)/shard_map/ppermute | solution.py:48
  75.5 4.3 %collective-permute-start.19 = (bf16[2,32,640]{2,1,0:T(8,128)(2,1)S(1)}, bf16[2,32,640]{2,1,0:T(8,128)(2,1)S(1)}, u32[]{:S(2)}, u32[]{:S(2)}) collective-permute-start(bf16[2,32,640]{2,1,0:T(8,128)(2,1)S(1)} %pad_maximum_fusion), channel_id=1, source_target_pairs={{0,32},{8,40},{16,48},{24,56},{32,0},{40,8},{48,16},{56,24},{64,96... | collective-permute-start | bytes 245768 | tf_op jit(solution)/shard_map/ppermute | solution.py:48
  79.8 2.0 %collective-permute-start.18 = (bf16[2,32,640]{2,1,0:T(8,128)(2,1)S(1)}, bf16[2,32,640]{2,1,0:T(8,128)(2,1)S(1)}, u32[]{:S(2)}, u32[]{:S(2)}) collective-permute-start(bf16[2,32,640]{2,1,0:T(8,128)(2,1)S(1)} %pad_maximum_fusion), channel_id=1, source_target_pairs={{0,16},{8,24},{16,0},{24,8},{32,48},{40,56},{48,32},{56,40},{64,80... | collective-permute-start | bytes 245768 | tf_op jit(solution)/shard_map/ppermute | solution.py:48
  81.9 4.4 %collective-permute-done.18 = bf16[2,32,640]{2,1,0:T(8,128)(2,1)S(1)} collective-permute-done((bf16[2,32,640]{2,1,0:T(8,128)(2,1)S(1)}, bf16[2,32,640]{2,1,0:T(8,128)(2,1)S(1)}, u32[]{:S(2)}, u32[]{:S(2)}) %collective-permute-start.18) | collective-permute-done | bytes 81952 | tf_op jit(solution)/shard_map/ppermute | solution.py:48
  93.6 6.9 %collective-permute-done.23.refs_4_ = bf16[8,32,640]{2,1,0:T(8,128)(2,1)S(1)} collective-permute-done((bf16[8,32,640]{2,1,0:T(8,128)(2,1)S(1)}, bf16[8,32,640]{2,1,0:T(8,128)(2,1)S(1)}, u32[]{:S(2)}, u32[]{:S(2)}) %collective-permute-start.23) | collective-permute-done | bytes 327712 | tf_op jit(solution)/shard_map/ppermute | solution.py:48
  101.2 2.4 %finish_rest.1 = (bf16[1024,512]{1,0:T(8,128)(2,1)}, bf16[1024,512]{1,0:T(8,128)(2,1)}, f32[64,1024]{1,0:T(8,128)}) custom-call(s32[1]{0:T(128)} %bitcast.rep_ref.refs_0_, bf16[8,32,640]{2,1,0:T(8,128)(2,1)S(1)} %constant_dynamic-update-slice_fusion.refs_1_, ...), custom_call_target="tpu_custom_call", output_to_operand_aliasing={{0}: (8, {}), {1}: (9, {})} | custom-call | flops 900000000 | bytes 4500000 | tf_op jit(solution)/shard_map/finish_rest/pallas_call | solution.py:69
  (57 shorter events, 20.1 us)
Async XLA Ops:
  2.6 4.8 %collective-permute-start = (f32[64,128]{1,0:T(8,128)S(1)}, f32[64,128]{1,0:T(8,128)S(1)}, u32[]{:S(2)}, u32[]{:S(2)}) collective-permute-start(f32[64,128]{1,0:T(8,128)S(1)} %get-tuple-element.34), channel_id=1, source_target_pairs={{0,64},{8,72},{16,80},{24,88},{32,96},{40,104},{48,112},{56,120},{... | collective-permute-start | bytes 98312 | tf_op jit(solution)/shard_map/ppermute | solution.py:48
  4.3 5.4 %collective-permute-start.1 = (f32[64,128]{1,0:T(8,128)S(1)}, f32[64,128]{1,0:T(8,128)S(1)}, u32[]{:S(2)}, u32[]{:S(2)}) collective-permute-start(f32[64,128]{1,0:T(8,128)S(1)} %get-tuple-element.35), channel_id=1, source_target_pairs={{0,128},{8,136},{16,144},{24,152},{32,160},{40,168},{48,176},{56,1... | collective-permute-start | bytes 98312 | tf_op jit(solution)/shard_map/ppermute | solution.py:48
  7.2 5.1 %collective-permute-start.2 = (f32[64,128]{1,0:T(8,128)S(1)}, f32[64,128]{1,0:T(8,128)S(1)}, u32[]{:S(2)}, u32[]{:S(2)}) collective-permute-start(f32[64,128]{1,0:T(8,128)S(1)} %get-tuple-element.36), channel_id=1, source_target_pairs={{0,192},{8,200},{16,208},{24,216},{32,224},{40,232},{48,240},{56,2... | collective-permute-start | bytes 98312 | tf_op jit(solution)/shard_map/ppermute | solution.py:48
  12.3 4.0 %collective-permute-start.3 = (f32[64,128]{1,0:T(8,128)S(1)}, f32[64,128]{1,0:T(8,128)S(1)}, u32[]{:S(2)}, u32[]{:S(2)}) collective-permute-start(f32[64,128]{1,0:T(8,128)S(1)} %add_add_fusion.1), channel_id=1, source_target_pairs={{0,8},{8,0},{16,24},{24,16},{32,40},{40,32},{48,56},{56,48},{64,72... | collective-permute-start | bytes 98312 | tf_op jit(solution)/shard_map/ppermute | solution.py:48
  16.3 5.2 %collective-permute-start.4 = (f32[64,128]{1,0:T(8,128)S(1)}, f32[64,128]{1,0:T(8,128)S(1)}, u32[]{:S(2)}, u32[]{:S(2)}) collective-permute-start(f32[64,128]{1,0:T(8,128)S(1)} %add.45), channel_id=1, source_target_pairs={{0,16},{8,24},{16,0},{24,8},{32,48},{40,56},{48,32},{56,40},{64,80... | collective-permute-start | bytes 98312 | tf_op jit(solution)/shard_map/ppermute | solution.py:48
  21.5 8.0 %collective-permute-start.5 = (f32[64,128]{1,0:T(8,128)S(1)}, f32[64,128]{1,0:T(8,128)S(1)}, u32[]{:S(2)}, u32[]{:S(2)}) collective-permute-start(f32[64,128]{1,0:T(8,128)S(1)} %add.46), channel_id=1, source_target_pairs={{0,32},{8,40},{16,48},{24,56},{32,0},{40,8},{48,16},{56,24},{64,96... | collective-permute-start | bytes 98312 | tf_op jit(solution)/shard_map/ppermute | solution.py:48
  29.5 5.1 %collective-permute-start.8 = (f32[64,128]{1,0:T(8,128)S(1)}, f32[64,128]{1,0:T(8,128)S(1)}, u32[]{:S(2)}, u32[]{:S(2)}) collective-permute-start(f32[64,128]{1,0:T(8,128)S(1)} %add_multiply_fusion.refs_0_), channel_id=1, source_target_pairs={{0,192},{8,200},{16,208},{24,216},{32,224},{40,232},{48,240},{56,2... | collective-permute-start | bytes 98312 | tf_op jit(solution)/shard_map/ppermute | solution.py:48
  29.8 5.4 %collective-permute-start.7 = (f32[64,128]{1,0:T(8,128)S(1)}, f32[64,128]{1,0:T(8,128)S(1)}, u32[]{:S(2)}, u32[]{:S(2)}) collective-permute-start(f32[64,128]{1,0:T(8,128)S(1)} %add_multiply_fusion.refs_0_), channel_id=1, source_target_pairs={{0,128},{8,136},{16,144},{24,152},{32,160},{40,168},{48,176},{56,1... | collective-permute-start | bytes 98312 | tf_op jit(solution)/shard_map/ppermute | solution.py:48
  30.5 5.3 %collective-permute-start.6 = (f32[64,128]{1,0:T(8,128)S(1)}, f32[64,128]{1,0:T(8,128)S(1)}, u32[]{:S(2)}, u32[]{:S(2)}) collective-permute-start(f32[64,128]{1,0:T(8,128)S(1)} %add_multiply_fusion.refs_0_), channel_id=1, source_target_pairs={{0,64},{8,72},{16,80},{24,88},{32,96},{40,104},{48,112},{56,120},{... | collective-permute-start | bytes 98312 | tf_op jit(solution)/shard_map/ppermute | solution.py:48
  36.1 1.7 %collective-permute-start.9 = (f32[64,64]{1,0:T(8,128)S(1)}, f32[64,64]{1,0:T(8,128)S(1)}, u32[]{:S(2)}, u32[]{:S(2)}) collective-permute-start(f32[64,64]{1,0:T(8,128)S(1)} %get-tuple-element.37), channel_id=1, source_target_pairs={{0,1},{1,0},{2,3},{3,2},{4,5},{5,4},{6,7},{7,6},{8,9},{9,8},{10,11... | collective-permute-start | bytes 49160 | tf_op jit(solution)/shard_map/ppermute | solution.py:48
  37.8 23.6 %all-to-all-start = ((f32[32,16,128]{2,1,0:T(8,128)}), f32[32,16,128]{2,1,0:T(8,128)S(1)}, u32[]{:S(2)}, u32[]{:S(2)}) async-start(f32[32,16,128]{2,1,0:T(8,128)} %project.1), calls=%async_computation | async-start | bytes 524288 | tf_op jit(solution)/shard_map/all_to_all | solution.py:366
  48.5 5.2 %collective-permute-start.12 = (f32[64,64]{1,0:T(8,128)S(1)}, f32[64,64]{1,0:T(8,128)S(1)}, u32[]{:S(2)}, u32[]{:S(2)}) collective-permute-start(f32[64,64]{1,0:T(8,128)S(1)} %add.48), channel_id=1, source_target_pairs={{0,6},{1,7},{2,4},{3,5},{4,2},{5,3},{6,0},{7,1},{8,14},{9,15},{10,... | collective-permute-start | bytes 49160 | tf_op jit(solution)/shard_map/ppermute | solution.py:48
  51.3 5.4 %collective-permute-start.11 = (f32[64,64]{1,0:T(8,128)S(1)}, f32[64,64]{1,0:T(8,128)S(1)}, u32[]{:S(2)}, u32[]{:S(2)}) collective-permute-start(f32[64,64]{1,0:T(8,128)S(1)} %add.48), channel_id=1, source_target_pairs={{0,4},{1,5},{2,6},{3,7},{4,0},{5,1},{6,2},{7,3},{8,12},{9,13},{10,... | collective-permute-start | bytes 49160 | tf_op jit(solution)/shard_map/ppermute | solution.py:48
  52.1 4.6 %collective-permute-start.10 = (f32[64,64]{1,0:T(8,128)S(1)}, f32[64,64]{1,0:T(8,128)S(1)}, u32[]{:S(2)}, u32[]{:S(2)}) collective-permute-start(f32[64,64]{1,0:T(8,128)S(1)} %add.48), channel_id=1, source_target_pairs={{0,2},{1,3},{2,0},{3,1},{4,6},{5,7},{6,4},{7,5},{8,10},{9,11},{10,... | collective-permute-start | bytes 49160 | tf_op jit(solution)/shard_map/ppermute | solution.py:48
  62.7 4.9 %collective-permute-start.16 = (f32[16,128]{1,0:T(8,128)S(1)}, f32[16,128]{1,0:T(8,128)S(1)}, u32[]{:S(2)}, u32[]{:S(2)}) collective-permute-start(f32[16,128]{1,0:T(8,128)S(1)} %add.52), channel_id=1, source_target_pairs={{0,6},{1,7},{2,4},{3,5},{4,2},{5,3},{6,0},{7,1},{8,14},{9,15},{10,... | collective-permute-start | bytes 24584 | tf_op jit(solution)/shard_map/ppermute | solution.py:48
  65.5 5.2 %collective-permute-start.15 = (f32[16,128]{1,0:T(8,128)S(1)}, f32[16,128]{1,0:T(8,128)S(1)}, u32[]{:S(2)}, u32[]{:S(2)}) collective-permute-start(f32[16,128]{1,0:T(8,128)S(1)} %add.52), channel_id=1, source_target_pairs={{0,4},{1,5},{2,6},{3,7},{4,0},{5,1},{6,2},{7,3},{8,12},{9,13},{10,... | collective-permute-start | bytes 24584 | tf_op jit(solution)/shard_map/ppermute | solution.py:48
  66.3 4.4 %collective-permute-start.14 = (f32[16,128]{1,0:T(8,128)S(1)}, f32[16,128]{1,0:T(8,128)S(1)}, u32[]{:S(2)}, u32[]{:S(2)}) collective-permute-start(f32[16,128]{1,0:T(8,128)S(1)} %add.52), channel_id=1, source_target_pairs={{0,2},{1,3},{2,0},{3,1},{4,6},{5,7},{6,4},{7,5},{8,10},{9,11},{10,... | collective-permute-start | bytes 24584 | tf_op jit(solution)/shard_map/ppermute | solution.py:48
  71.2 4.1 %collective-permute-start.17 = (bf16[32,640]{1,0:T(8,128)(2,1)S(1)}, bf16[32,640]{1,0:T(8,128)(2,1)S(1)}, u32[]{:S(2)}, u32[]{:S(2)}) collective-permute-start(bf16[32,640]{1,0:T(8,128)(2,1)S(1)} %get-tuple-element.50), channel_id=1, source_target_pairs={{0,8},{8,0},{16,24},{24,16},{32,40},{40,32},{48,56},{56,48},{64,72... | collective-permute-start | bytes 122888 | tf_op jit(solution)/shard_map/ppermute | solution.py:48
  75.3 11.1 %collective-permute-start.20 = (bf16[2,32,640]{2,1,0:T(8,128)(2,1)S(1)}, bf16[2,32,640]{2,1,0:T(8,128)(2,1)S(1)}, u32[]{:S(2)}, u32[]{:S(2)}) collective-permute-start(bf16[2,32,640]{2,1,0:T(8,128)(2,1)S(1)} %pad_maximum_fusion), channel_id=1, source_target_pairs={{0,48},{8,56},{16,32},{24,40},{32,16},{40,24},{48,0},{56,8},{64,11... | collective-permute-start | bytes 245768 | tf_op jit(solution)/shard_map/ppermute | solution.py:48
  75.5 10.8 %collective-permute-start.19 = (bf16[2,32,640]{2,1,0:T(8,128)(2,1)S(1)}, bf16[2,32,640]{2,1,0:T(8,128)(2,1)S(1)}, u32[]{:S(2)}, u32[]{:S(2)}) collective-permute-start(bf16[2,32,640]{2,1,0:T(8,128)(2,1)S(1)} %pad_maximum_fusion), channel_id=1, source_target_pairs={{0,32},{8,40},{16,48},{24,56},{32,0},{40,8},{48,16},{56,24},{64,96... | collective-permute-start | bytes 245768 | tf_op jit(solution)/shard_map/ppermute | solution.py:48
  79.8 6.5 %collective-permute-start.18 = (bf16[2,32,640]{2,1,0:T(8,128)(2,1)S(1)}, bf16[2,32,640]{2,1,0:T(8,128)(2,1)S(1)}, u32[]{:S(2)}, u32[]{:S(2)}) collective-permute-start(bf16[2,32,640]{2,1,0:T(8,128)(2,1)S(1)} %pad_maximum_fusion), channel_id=1, source_target_pairs={{0,16},{8,24},{16,0},{24,8},{32,48},{40,56},{48,32},{56,40},{64,80... | collective-permute-start | bytes 245768 | tf_op jit(solution)/shard_map/ppermute | solution.py:48
  86.4 14.1 %collective-permute-start.23 = (bf16[8,32,640]{2,1,0:T(8,128)(2,1)S(1)}, bf16[8,32,640]{2,1,0:T(8,128)(2,1)S(1)}, u32[]{:S(2)}, u32[]{:S(2)}) collective-permute-start(bf16[8,32,640]{2,1,0:T(8,128)(2,1)S(1)} %constant_dynamic-update-slice_fusion.refs_1_), channel_id=1, source_target_pairs={{0,192},{8,200},{16,208},{24,216},{32,224},{40,232},{48,240},{56,2... | collective-permute-start | bytes 983048 | tf_op jit(solution)/shard_map/ppermute | solution.py:48
  88.0 12.5 %collective-permute-start.22 = (bf16[8,32,640]{2,1,0:T(8,128)(2,1)S(1)}, bf16[8,32,640]{2,1,0:T(8,128)(2,1)S(1)}, u32[]{:S(2)}, u32[]{:S(2)}) collective-permute-start(bf16[8,32,640]{2,1,0:T(8,128)(2,1)S(1)} %constant_dynamic-update-slice_fusion.refs_1_), channel_id=1, source_target_pairs={{0,128},{8,136},{16,144},{24,152},{32,160},{40,168},{48,176},{56,1... | collective-permute-start | bytes 983048 | tf_op jit(solution)/shard_map/ppermute | solution.py:48
  89.2 12.0 %collective-permute-start.21 = (bf16[8,32,640]{2,1,0:T(8,128)(2,1)S(1)}, bf16[8,32,640]{2,1,0:T(8,128)(2,1)S(1)}, u32[]{:S(2)}, u32[]{:S(2)}) collective-permute-start(bf16[8,32,640]{2,1,0:T(8,128)(2,1)S(1)} %constant_dynamic-update-slice_fusion.refs_1_), channel_id=1, source_target_pairs={{0,64},{8,72},{16,80},{24,88},{32,96},{40,104},{48,112},{56,120},{... | collective-permute-start | bytes 983048 | tf_op jit(solution)/shard_map/ppermute | solution.py:48
  (4 other events, 29.0 us)

commit v5 on v4

--- a/solution.py
+++ b/solution.py
@@ -18,6 +18,9 @@
 Y_SIZE, Z_SIZE = 4, 8
 Y_STEPS = (8, 16, 24)
 X_STEPS = (2, 4, 6)
+Z_SUM_STEPS = (1, 3, 7)
+Z_PAIRS = (2, 5, 6)
+Z_ORDER = tuple(pair ^ bit for pair in (0,) + Z_PAIRS for bit in (0, 1))
 ROW_BLOCKS = 4
 
 
@@ -276,7 +279,7 @@
     approx = native(jnp.concatenate([right] * 3, axis=1), parts_ref[...], 1, 0)
     first = (own_y ^ d) * (groups * own_rows)
     for j in range(groups):
-        at = pl.multiple_of((own_z ^ j) * own_rows, own_rows)
+        at = pl.multiple_of((own_z ^ Z_ORDER[j]) * own_rows, own_rows)
         source = pl.ds(pl.multiple_of(first + at, own_rows), own_rows)
         merged = grad_ref[source, :].astype(F32) + feed_ref[source, :].astype(F32)
         piece = approx[j * own_rows : (j + 1) * own_rows]
@@ -303,7 +306,7 @@
         copies[-1].start()
 
     def rows_of(d, j):
-        at = (own_y ^ d) * size + (own_z ^ j) * own_rows
+        at = (own_y ^ d) * size + (own_z ^ Z_ORDER[j]) * own_rows
         return pl.ds(pl.multiple_of(at, own_rows), own_rows)
 
     for i, d in enumerate(ds):
@@ -354,7 +357,7 @@
 
     pieces, gradient, feedback = local_factor(rep, warm_start.T, gradient, feedback)
     quarter = sum_four([pieces[0]] + [exchange(p, "rep", d) for p, d in zip(pieces[1:], Y_STEPS)])
-    for distance in (1, 2, 4):
+    for distance in Z_SUM_STEPS:
         quarter = quarter + exchange(quarter, "rep", distance)
     quarter = quarter / replicas
     quarters = [quarter] + [exchange(quarter, "rep", d) for d in Y_STEPS]
@@ -375,7 +378,7 @@
         replicas, rep, own_sum, inverse, unit_t, master, moment, second
     )
     pair = jnp.stack([send, exchange(send, "rep", 1)])
-    column = jnp.concatenate([pair] + [exchange(pair, "rep", d) for d in (2, 4, 6)])
+    column = jnp.concatenate([pair] + [exchange(pair, "rep", d) for d in Z_PAIRS])
     others = [exchange(column, "rep", d) for d in Y_STEPS]
     begun = finish(True, (0,), rep, [column], unit_parts, gradient, feedback)
     blocks = [column] + others

time: 105 us -> 102 us (0.971)
  starting transfers between devices: 48.4 us -> 44.5 us
  waiting for transfers between devices: 42.3 us -> 43.9 us
    ppermute x24, starting transfers between devices: 37.8 us -> 34.8 us  [exchange(): lax.ppermute(value, axis, [(i, i ^ distance) for i in range(lax.axis_size...]
    ppermute x24, waiting for transfers between devices: 39.8 us -> 41.4 us  [exchange(): lax.ppermute(value, axis, [(i, i ^ distance) for i in range(lax.axis_size...]
where the time goes in v5:
time: 102 us; the launch traced here: 101 us
  starting transfers between devices  44.5 us (44%)
  waiting for transfers between devices  43.9 us (43%)
  Pallas kernels  9.96 us (10%)
  local copies, waits for them, and re-layouts  1.96 us (2%)
    ppermute x24, waiting for transfers between devices, exchange(): lax.ppermute(value, axis, [(i, i ^ distance) for i in range(lax.axis_size...  41.4 us
    ppermute x24, starting transfers between devices, exchange(): lax.ppermute(value, axis, [(i, i ^ distance) for i in range(lax.axis_size...  34.8 us
    all_to_all x1, starting transfers between devices, on_device(): received = lax.all_to_all(packed, 'rep', 0, 0, tiled=True)  9.68 us
    pallas_call x6, Pallas kernels, call(): pl.pallas_call(kernel, out_shape=outs, grid_spec=pltpu.PrefetchScalarGrid...  8.01 us
    all_to_all x1, waiting for transfers between devices, on_device(): received = lax.all_to_all(packed, 'rep', 0, 0, tiled=True)  2.46 us
  transfers between devices with their start and end apart: 25, of which 18 were waited for; matrix products, arithmetic and copies ran while one was open for 2% of the time, Pallas kernels for 5%

profile of v5, /device:TPU:32, one launch (start us, length us, event | category | flops | bytes accessed | tf_op | source)
XLA Modules:
  0.0 101.4 jit_solution(11666720143476045698)
XLA Ops:
  0.6 1.9 %local_factor.1 = (f32[64,128]{1,0:T(8,128)S(1)}, f32[64,128]{1,0:T(8,128)S(1)}, f32[64,128]{1,0:T(8,128)S(1)}, f32[64,128]{1,0:T(8,128)S(1)}, bf16[1024,512]{1,...) custom-call(s32[1]{0:T(128)} %bitcast.rep_ref.refs_0_, f32[64,1024]{1,0:T(8,128)} %bitcast.15, bf16[1024,512]{1,0:T(8,128)(2,1)} %bitcast.13, ...), custom_call_target="tpu_custom_call" | custom-call | flops 1000000000 | bytes 2500000 | tf_op jit(solution)/shard_map/local_factor/pallas_call | solution.py:128
  2.6 1.7 %collective-permute-start = (f32[64,128]{1,0:T(8,128)S(1)}, f32[64,128]{1,0:T(8,128)S(1)}, u32[]{:S(2)}, u32[]{:S(2)}) collective-permute-start(f32[64,128]{1,0:T(8,128)S(1)} %get-tuple-element.34), channel_id=1, source_target_pairs={{0,64},{8,72},{16,80},{24,88},{32,96},{40,104},{48,112},{56,120},{... | collective-permute-start | bytes 98312 | tf_op jit(solution)/shard_map/ppermute | solution.py:51
  4.3 2.9 %collective-permute-start.1 = (f32[64,128]{1,0:T(8,128)S(1)}, f32[64,128]{1,0:T(8,128)S(1)}, u32[]{:S(2)}, u32[]{:S(2)}) collective-permute-start(f32[64,128]{1,0:T(8,128)S(1)} %get-tuple-element.35), channel_id=1, source_target_pairs={{0,128},{8,136},{16,144},{24,152},{32,160},{40,168},{48,176},{56,1... | collective-permute-start | bytes 98312 | tf_op jit(solution)/shard_map/ppermute | solution.py:51
  7.4 2.3 %collective-permute-done.1 = f32[64,128]{1,0:T(8,128)S(1)} collective-permute-done((f32[64,128]{1,0:T(8,128)S(1)}, f32[64,128]{1,0:T(8,128)S(1)}, u32[]{:S(2)}, u32[]{:S(2)}) %collective-permute-start.1) | collective-permute-done | bytes 32800 | tf_op jit(solution)/shard_map/ppermute | solution.py:51
  9.7 2.6 %collective-permute-done.2 = f32[64,128]{1,0:T(8,128)S(1)} collective-permute-done((f32[64,128]{1,0:T(8,128)S(1)}, f32[64,128]{1,0:T(8,128)S(1)}, u32[]{:S(2)}, u32[]{:S(2)}) %collective-permute-start.2) | collective-permute-done | bytes 32800 | tf_op jit(solution)/shard_map/ppermute | solution.py:51
  12.5 3.8 %collective-permute-done.3 = f32[64,128]{1,0:T(8,128)S(1)} collective-permute-done((f32[64,128]{1,0:T(8,128)S(1)}, f32[64,128]{1,0:T(8,128)S(1)}, u32[]{:S(2)}, u32[]{:S(2)}) %collective-permute-start.3) | collective-permute-done | bytes 32800 | tf_op jit(solution)/shard_map/ppermute | solution.py:51
  16.3 2.2 %collective-permute-start.4 = (f32[64,128]{1,0:T(8,128)S(1)}, f32[64,128]{1,0:T(8,128)S(1)}, u32[]{:S(2)}, u32[]{:S(2)}) collective-permute-start(f32[64,128]{1,0:T(8,128)S(1)} %add.45), channel_id=1, source_target_pairs={{0,24},{8,16},{16,8},{24,0},{32,56},{40,48},{48,40},{56,32},{64,88... | collective-permute-start | bytes 98312 | tf_op jit(solution)/shard_map/ppermute | solution.py:51
  18.5 1.9 %collective-permute-done.4 = f32[64,128]{1,0:T(8,128)S(1)} collective-permute-done((f32[64,128]{1,0:T(8,128)S(1)}, f32[64,128]{1,0:T(8,128)S(1)}, u32[]{:S(2)}, u32[]{:S(2)}) %collective-permute-start.4) | collective-permute-done | bytes 32800 | tf_op jit(solution)/shard_map/ppermute | solution.py:51
  20.4 5.7 %collective-permute-start.5 = (f32[64,128]{1,0:T(8,128)S(1)}, f32[64,128]{1,0:T(8,128)S(1)}, u32[]{:S(2)}, u32[]{:S(2)}) collective-permute-start(f32[64,128]{1,0:T(8,128)S(1)} %add.46), channel_id=1, source_target_pairs={{0,56},{8,48},{16,40},{24,32},{32,24},{40,16},{48,8},{56,0},{64,12... | collective-permute-start | bytes 98312 | tf_op jit(solution)/shard_map/ppermute | solution.py:51
  26.1 1.9 %collective-permute-done.5 = f32[64,128]{1,0:T(8,128)S(1)} collective-permute-done((f32[64,128]{1,0:T(8,128)S(1)}, f32[64,128]{1,0:T(8,128)S(1)}, u32[]{:S(2)}, u32[]{:S(2)}) %collective-permute-start.5) | collective-permute-done | bytes 32800 | tf_op jit(solution)/shard_map/ppermute | solution.py:51
  29.0 3.1 %collective-permute-start.6 = (f32[64,128]{1,0:T(8,128)S(1)}, f32[64,128]{1,0:T(8,128)S(1)}, u32[]{:S(2)}, u32[]{:S(2)}) collective-permute-start(f32[64,128]{1,0:T(8,128)S(1)} %add_multiply_fusion.refs_0_), channel_id=1, source_target_pairs={{0,64},{8,72},{16,80},{24,88},{32,96},{40,104},{48,112},{56,120},{... | collective-permute-start | bytes 98312 | tf_op jit(solution)/shard_map/ppermute | solution.py:51
  36.3 9.7 %all-to-all-start = ((f32[32,16,128]{2,1,0:T(8,128)}), f32[32,16,128]{2,1,0:T(8,128)S(1)}, u32[]{:S(2)}, u32[]{:S(2)}) async-start(f32[32,16,128]{2,1,0:T(8,128)} %project.1), calls=%async_computation | async-start | bytes 524288 | tf_op jit(solution)/shard_map/all_to_all | solution.py:369
  46.0 2.8 %collective-permute-start.12 = (f32[64,64]{1,0:T(8,128)S(1)}, f32[64,64]{1,0:T(8,128)S(1)}, u32[]{:S(2)}, u32[]{:S(2)}) collective-permute-start(f32[64,64]{1,0:T(8,128)S(1)} %add.48), channel_id=1, source_target_pairs={{0,6},{1,7},{2,4},{3,5},{4,2},{5,3},{6,0},{7,1},{8,14},{9,15},{10,... | collective-permute-start | bytes 49160 | tf_op jit(solution)/shard_map/ppermute | solution.py:51
  51.2 3.1 %collective-permute-done.11 = f32[64,64]{1,0:T(8,128)S(1)} collective-permute-done((f32[64,64]{1,0:T(8,128)S(1)}, f32[64,64]{1,0:T(8,128)S(1)}, u32[]{:S(2)}, u32[]{:S(2)}) %collective-permute-start.11) | collective-permute-done | bytes 16416 | tf_op jit(solution)/shard_map/ppermute | solution.py:51
  54.3 2.2 %invert.1 = (f32[64,64]{1,0:T(8,128)S(1)}, f32[64,512]{1,0:T(8,128)S(1)}, bf16[384,512]{1,0:T(8,128)(2,1)S(1)}) custom-call(s32[1]{0:T(128)} %bitcast.rep_ref.refs_0_, f32[64,64]{1,0:T(8,128)S(1)} %add_add_fusion.gram_ref, f32[64,512]{1,0:T(8,128)S(1)} %get-tuple-element.43.factor_ref), custom_call_target="tpu_custom_call" | custom-call | flops 2000000000 | bytes 500000 | tf_op jit(solution)/shard_map/invert/pallas_call | solution.py:72
  56.4 2.5 %all-to-all-done = f32[32,16,128]{2,1,0:T(8,128)S(1)} async-done(((f32[32,16,128]{2,1,0:T(8,128)}), f32[32,16,128]{2,1,0:T(8,128)S(1)}, u32[]{:S(2)}, u32[]{:S(2)}) %all-to-all-start) | async-done | bytes 262176 | tf_op jit(solution)/shard_map/all_to_all | solution.py:369
  60.2 2.8 %collective-permute-start.16 = (f32[16,128]{1,0:T(8,128)S(1)}, f32[16,128]{1,0:T(8,128)S(1)}, u32[]{:S(2)}, u32[]{:S(2)}) collective-permute-start(f32[16,128]{1,0:T(8,128)S(1)} %add.52), channel_id=1, source_target_pairs={{0,6},{1,7},{2,4},{3,5},{4,2},{5,3},{6,0},{7,1},{8,14},{9,15},{10,... | collective-permute-start | bytes 24584 | tf_op jit(solution)/shard_map/ppermute | solution.py:51
  65.1 3.1 %collective-permute-done.15 = f32[16,128]{1,0:T(8,128)S(1)} collective-permute-done((f32[16,128]{1,0:T(8,128)S(1)}, f32[16,128]{1,0:T(8,128)S(1)}, u32[]{:S(2)}, u32[]{:S(2)}) %collective-permute-start.15) | collective-permute-done | bytes 8224 | tf_op jit(solution)/shard_map/ppermute | solution.py:51
  68.8 4.0 %collective-permute-done.17 = bf16[32,640]{1,0:T(8,128)(2,1)S(1)} collective-permute-done((bf16[32,640]{1,0:T(8,128)(2,1)S(1)}, bf16[32,640]{1,0:T(8,128)(2,1)S(1)}, u32[]{:S(2)}, u32[]{:S(2)}) %collective-permute-start.17) | collective-permute-done | bytes 40992 | tf_op jit(solution)/shard_map/ppermute | solution.py:51
  73.0 4.3 %collective-permute-start.19 = (bf16[2,32,640]{2,1,0:T(8,128)(2,1)S(1)}, bf16[2,32,640]{2,1,0:T(8,128)(2,1)S(1)}, u32[]{:S(2)}, u32[]{:S(2)}) collective-permute-start(bf16[2,32,640]{2,1,0:T(8,128)(2,1)S(1)} %pad_maximum_fusion), channel_id=1, source_target_pairs={{0,40},{8,32},{16,56},{24,48},{32,8},{40,0},{48,24},{56,16},{64,10... | collective-permute-start | bytes 245768 | tf_op jit(solution)/shard_map/ppermute | solution.py:51
  77.9 5.5 %collective-permute-done.18 = bf16[2,32,640]{2,1,0:T(8,128)(2,1)S(1)} collective-permute-done((bf16[2,32,640]{2,1,0:T(8,128)(2,1)S(1)}, bf16[2,32,640]{2,1,0:T(8,128)(2,1)S(1)}, u32[]{:S(2)}, u32[]{:S(2)}) %collective-permute-start.18) | collective-permute-done | bytes 81952 | tf_op jit(solution)/shard_map/ppermute | solution.py:51
  83.9 2.2 %collective-permute-start.22 = (bf16[8,32,640]{2,1,0:T(8,128)(2,1)S(1)}, bf16[8,32,640]{2,1,0:T(8,128)(2,1)S(1)}, u32[]{:S(2)}, u32[]{:S(2)}) collective-permute-start(bf16[8,32,640]{2,1,0:T(8,128)(2,1)S(1)} %constant_dynamic-update-slice_fusion.refs_1_), channel_id=1, source_target_pairs={{0,128},{8,136},{16,144},{24,152},{32,160},{40,168},{48,176},{56,1... | collective-permute-start | bytes 983048 | tf_op jit(solution)/shard_map/ppermute | solution.py:51
  90.7 7.6 %collective-permute-done.23.refs_4_ = bf16[8,32,640]{2,1,0:T(8,128)(2,1)S(1)} collective-permute-done((bf16[8,32,640]{2,1,0:T(8,128)(2,1)S(1)}, bf16[8,32,640]{2,1,0:T(8,128)(2,1)S(1)}, u32[]{:S(2)}, u32[]{:S(2)}) %collective-permute-start.23) | collective-permute-done | bytes 327712 | tf_op jit(solution)/shard_map/ppermute | solution.py:51
  98.8 2.4 %finish_rest.1 = (bf16[1024,512]{1,0:T(8,128)(2,1)}, bf16[1024,512]{1,0:T(8,128)(2,1)}, f32[64,1024]{1,0:T(8,128)}) custom-call(s32[1]{0:T(128)} %bitcast.rep_ref.refs_0_, bf16[8,32,640]{2,1,0:T(8,128)(2,1)S(1)} %constant_dynamic-update-slice_fusion.refs_1_, ...), custom_call_target="tpu_custom_call", output_to_operand_aliasing={{0}: (8, {}), {1}: (9, {})} | custom-call | flops 900000000 | bytes 4500000 | tf_op jit(solution)/shard_map/finish_rest/pallas_call | solution.py:72
  (57 shorter events, 18.6 us)
Async XLA Ops:
  2.6 4.8 %collective-permute-start = (f32[64,128]{1,0:T(8,128)S(1)}, f32[64,128]{1,0:T(8,128)S(1)}, u32[]{:S(2)}, u32[]{:S(2)}) collective-permute-start(f32[64,128]{1,0:T(8,128)S(1)} %get-tuple-element.34), channel_id=1, source_target_pairs={{0,64},{8,72},{16,80},{24,88},{32,96},{40,104},{48,112},{56,120},{... | collective-permute-start | bytes 98312 | tf_op jit(solution)/shard_map/ppermute | solution.py:51
  4.3 5.4 %collective-permute-start.1 = (f32[64,128]{1,0:T(8,128)S(1)}, f32[64,128]{1,0:T(8,128)S(1)}, u32[]{:S(2)}, u32[]{:S(2)}) collective-permute-start(f32[64,128]{1,0:T(8,128)S(1)} %get-tuple-element.35), channel_id=1, source_target_pairs={{0,128},{8,136},{16,144},{24,152},{32,160},{40,168},{48,176},{56,1... | collective-permute-start | bytes 98312 | tf_op jit(solution)/shard_map/ppermute | solution.py:51
  7.2 5.1 %collective-permute-start.2 = (f32[64,128]{1,0:T(8,128)S(1)}, f32[64,128]{1,0:T(8,128)S(1)}, u32[]{:S(2)}, u32[]{:S(2)}) collective-permute-start(f32[64,128]{1,0:T(8,128)S(1)} %get-tuple-element.36), channel_id=1, source_target_pairs={{0,192},{8,200},{16,208},{24,216},{32,224},{40,232},{48,240},{56,2... | collective-permute-start | bytes 98312 | tf_op jit(solution)/shard_map/ppermute | solution.py:51
  12.3 4.0 %collective-permute-start.3 = (f32[64,128]{1,0:T(8,128)S(1)}, f32[64,128]{1,0:T(8,128)S(1)}, u32[]{:S(2)}, u32[]{:S(2)}) collective-permute-start(f32[64,128]{1,0:T(8,128)S(1)} %add_add_fusion.1), channel_id=1, source_target_pairs={{0,8},{8,0},{16,24},{24,16},{32,40},{40,32},{48,56},{56,48},{64,72... | collective-permute-start | bytes 98312 | tf_op jit(solution)/shard_map/ppermute | solution.py:51
  16.3 4.1 %collective-permute-start.4 = (f32[64,128]{1,0:T(8,128)S(1)}, f32[64,128]{1,0:T(8,128)S(1)}, u32[]{:S(2)}, u32[]{:S(2)}) collective-permute-start(f32[64,128]{1,0:T(8,128)S(1)} %add.45), channel_id=1, source_target_pairs={{0,24},{8,16},{16,8},{24,0},{32,56},{40,48},{48,40},{56,32},{64,88... | collective-permute-start | bytes 98312 | tf_op jit(solution)/shard_map/ppermute | solution.py:51
  20.4 7.6 %collective-permute-start.5 = (f32[64,128]{1,0:T(8,128)S(1)}, f32[64,128]{1,0:T(8,128)S(1)}, u32[]{:S(2)}, u32[]{:S(2)}) collective-permute-start(f32[64,128]{1,0:T(8,128)S(1)} %add.46), channel_id=1, source_target_pairs={{0,56},{8,48},{16,40},{24,32},{32,24},{40,16},{48,8},{56,0},{64,12... | collective-permute-start | bytes 98312 | tf_op jit(solution)/shard_map/ppermute | solution.py:51
  28.0 5.1 %collective-permute-start.8 = (f32[64,128]{1,0:T(8,128)S(1)}, f32[64,128]{1,0:T(8,128)S(1)}, u32[]{:S(2)}, u32[]{:S(2)}) collective-permute-start(f32[64,128]{1,0:T(8,128)S(1)} %add_multiply_fusion.refs_0_), channel_id=1, source_target_pairs={{0,192},{8,200},{16,208},{24,216},{32,224},{40,232},{48,240},{56,2... | collective-permute-start | bytes 98312 | tf_op jit(solution)/shard_map/ppermute | solution.py:51
  28.2 5.4 %collective-permute-start.7 = (f32[64,128]{1,0:T(8,128)S(1)}, f32[64,128]{1,0:T(8,128)S(1)}, u32[]{:S(2)}, u32[]{:S(2)}) collective-permute-start(f32[64,128]{1,0:T(8,128)S(1)} %add_multiply_fusion.refs_0_), channel_id=1, source_target_pairs={{0,128},{8,136},{16,144},{24,152},{32,160},{40,168},{48,176},{56,1... | collective-permute-start | bytes 98312 | tf_op jit(solution)/shard_map/ppermute | solution.py:51
  29.0 5.3 %collective-permute-start.6 = (f32[64,128]{1,0:T(8,128)S(1)}, f32[64,128]{1,0:T(8,128)S(1)}, u32[]{:S(2)}, u32[]{:S(2)}) collective-permute-start(f32[64,128]{1,0:T(8,128)S(1)} %add_multiply_fusion.refs_0_), channel_id=1, source_target_pairs={{0,64},{8,72},{16,80},{24,88},{32,96},{40,104},{48,112},{56,120},{... | collective-permute-start | bytes 98312 | tf_op jit(solution)/shard_map/ppermute | solution.py:51
  34.6 1.7 %collective-permute-start.9 = (f32[64,64]{1,0:T(8,128)S(1)}, f32[64,64]{1,0:T(8,128)S(1)}, u32[]{:S(2)}, u32[]{:S(2)}) collective-permute-start(f32[64,64]{1,0:T(8,128)S(1)} %get-tuple-element.37), channel_id=1, source_target_pairs={{0,1},{1,0},{2,3},{3,2},{4,5},{5,4},{6,7},{7,6},{8,9},{9,8},{10,11... | collective-permute-start | bytes 49160 | tf_op jit(solution)/shard_map/ppermute | solution.py:51
  36.3 22.6 %all-to-all-start = ((f32[32,16,128]{2,1,0:T(8,128)}), f32[32,16,128]{2,1,0:T(8,128)S(1)}, u32[]{:S(2)}, u32[]{:S(2)}) async-start(f32[32,16,128]{2,1,0:T(8,128)} %project.1), calls=%async_computation | async-start | bytes 524288 | tf_op jit(solution)/shard_map/all_to_all | solution.py:369
  46.0 5.2 %collective-permute-start.12 = (f32[64,64]{1,0:T(8,128)S(1)}, f32[64,64]{1,0:T(8,128)S(1)}, u32[]{:S(2)}, u32[]{:S(2)}) collective-permute-start(f32[64,64]{1,0:T(8,128)S(1)} %add.48), channel_id=1, source_target_pairs={{0,6},{1,7},{2,4},{3,5},{4,2},{5,3},{6,0},{7,1},{8,14},{9,15},{10,... | collective-permute-start | bytes 49160 | tf_op jit(solution)/shard_map/ppermute | solution.py:51
  48.8 5.4 %collective-permute-start.11 = (f32[64,64]{1,0:T(8,128)S(1)}, f32[64,64]{1,0:T(8,128)S(1)}, u32[]{:S(2)}, u32[]{:S(2)}) collective-permute-start(f32[64,64]{1,0:T(8,128)S(1)} %add.48), channel_id=1, source_target_pairs={{0,4},{1,5},{2,6},{3,7},{4,0},{5,1},{6,2},{7,3},{8,12},{9,13},{10,... | collective-permute-start | bytes 49160 | tf_op jit(solution)/shard_map/ppermute | solution.py:51
  49.6 4.6 %collective-permute-start.10 = (f32[64,64]{1,0:T(8,128)S(1)}, f32[64,64]{1,0:T(8,128)S(1)}, u32[]{:S(2)}, u32[]{:S(2)}) collective-permute-start(f32[64,64]{1,0:T(8,128)S(1)} %add.48), channel_id=1, source_target_pairs={{0,2},{1,3},{2,0},{3,1},{4,6},{5,7},{6,4},{7,5},{8,10},{9,11},{10,... | collective-permute-start | bytes 49160 | tf_op jit(solution)/shard_map/ppermute | solution.py:51
  60.2 4.9 %collective-permute-start.16 = (f32[16,128]{1,0:T(8,128)S(1)}, f32[16,128]{1,0:T(8,128)S(1)}, u32[]{:S(2)}, u32[]{:S(2)}) collective-permute-start(f32[16,128]{1,0:T(8,128)S(1)} %add.52), channel_id=1, source_target_pairs={{0,6},{1,7},{2,4},{3,5},{4,2},{5,3},{6,0},{7,1},{8,14},{9,15},{10,... | collective-permute-start | bytes 24584 | tf_op jit(solution)/shard_map/ppermute | solution.py:51
  63.0 5.2 %collective-permute-start.15 = (f32[16,128]{1,0:T(8,128)S(1)}, f32[16,128]{1,0:T(8,128)S(1)}, u32[]{:S(2)}, u32[]{:S(2)}) collective-permute-start(f32[16,128]{1,0:T(8,128)S(1)} %add.52), channel_id=1, source_target_pairs={{0,4},{1,5},{2,6},{3,7},{4,0},{5,1},{6,2},{7,3},{8,12},{9,13},{10,... | collective-permute-start | bytes 24584 | tf_op jit(solution)/shard_map/ppermute | solution.py:51
  63.8 4.4 %collective-permute-start.14 = (f32[16,128]{1,0:T(8,128)S(1)}, f32[16,128]{1,0:T(8,128)S(1)}, u32[]{:S(2)}, u32[]{:S(2)}) collective-permute-start(f32[16,128]{1,0:T(8,128)S(1)} %add.52), channel_id=1, source_target_pairs={{0,2},{1,3},{2,0},{3,1},{4,6},{5,7},{6,4},{7,5},{8,10},{9,11},{10,... | collective-permute-start | bytes 24584 | tf_op jit(solution)/shard_map/ppermute | solution.py:51
  68.7 4.1 %collective-permute-start.17 = (bf16[32,640]{1,0:T(8,128)(2,1)S(1)}, bf16[32,640]{1,0:T(8,128)(2,1)S(1)}, u32[]{:S(2)}, u32[]{:S(2)}) collective-permute-start(bf16[32,640]{1,0:T(8,128)(2,1)S(1)} %get-tuple-element.50), channel_id=1, source_target_pairs={{0,8},{8,0},{16,24},{24,16},{32,40},{40,32},{48,56},{56,48},{64,72... | collective-permute-start | bytes 122888 | tf_op jit(solution)/shard_map/ppermute | solution.py:51
  72.8 10.7 %collective-permute-start.20 = (bf16[2,32,640]{2,1,0:T(8,128)(2,1)S(1)}, bf16[2,32,640]{2,1,0:T(8,128)(2,1)S(1)}, u32[]{:S(2)}, u32[]{:S(2)}) collective-permute-start(bf16[2,32,640]{2,1,0:T(8,128)(2,1)S(1)} %pad_maximum_fusion), channel_id=1, source_target_pairs={{0,48},{8,56},{16,32},{24,40},{32,16},{40,24},{48,0},{56,8},{64,11... | collective-permute-start | bytes 245768 | tf_op jit(solution)/shard_map/ppermute | solution.py:51
  73.0 10.4 %collective-permute-start.19 = (bf16[2,32,640]{2,1,0:T(8,128)(2,1)S(1)}, bf16[2,32,640]{2,1,0:T(8,128)(2,1)S(1)}, u32[]{:S(2)}, u32[]{:S(2)}) collective-permute-start(bf16[2,32,640]{2,1,0:T(8,128)(2,1)S(1)} %pad_maximum_fusion), channel_id=1, source_target_pairs={{0,40},{8,32},{16,56},{24,48},{32,8},{40,0},{48,24},{56,16},{64,10... | collective-permute-start | bytes 245768 | tf_op jit(solution)/shard_map/ppermute | solution.py:51
  77.3 6.2 %collective-permute-start.18 = (bf16[2,32,640]{2,1,0:T(8,128)(2,1)S(1)}, bf16[2,32,640]{2,1,0:T(8,128)(2,1)S(1)}, u32[]{:S(2)}, u32[]{:S(2)}) collective-permute-start(bf16[2,32,640]{2,1,0:T(8,128)(2,1)S(1)} %pad_maximum_fusion), channel_id=1, source_target_pairs={{0,16},{8,24},{16,0},{24,8},{32,48},{40,56},{48,32},{56,40},{64,80... | collective-permute-start | bytes 245768 | tf_op jit(solution)/shard_map/ppermute | solution.py:51
  83.5 14.7 %collective-permute-start.23 = (bf16[8,32,640]{2,1,0:T(8,128)(2,1)S(1)}, bf16[8,32,640]{2,1,0:T(8,128)(2,1)S(1)}, u32[]{:S(2)}, u32[]{:S(2)}) collective-permute-start(bf16[8,32,640]{2,1,0:T(8,128)(2,1)S(1)} %constant_dynamic-update-slice_fusion.refs_1_), channel_id=1, source_target_pairs={{0,192},{8,200},{16,208},{24,216},{32,224},{40,232},{48,240},{56,2... | collective-permute-start | bytes 983048 | tf_op jit(solution)/shard_map/ppermute | solution.py:51
  83.9 14.3 %collective-permute-start.22 = (bf16[8,32,640]{2,1,0:T(8,128)(2,1)S(1)}, bf16[8,32,640]{2,1,0:T(8,128)(2,1)S(1)}, u32[]{:S(2)}, u32[]{:S(2)}) collective-permute-start(bf16[8,32,640]{2,1,0:T(8,128)(2,1)S(1)} %constant_dynamic-update-slice_fusion.refs_1_), channel_id=1, source_target_pairs={{0,128},{8,136},{16,144},{24,152},{32,160},{40,168},{48,176},{56,1... | collective-permute-start | bytes 983048 | tf_op jit(solution)/shard_map/ppermute | solution.py:51
  86.1 12.7 %collective-permute-start.21 = (bf16[8,32,640]{2,1,0:T(8,128)(2,1)S(1)}, bf16[8,32,640]{2,1,0:T(8,128)(2,1)S(1)}, u32[]{:S(2)}, u32[]{:S(2)}) collective-permute-start(bf16[8,32,640]{2,1,0:T(8,128)(2,1)S(1)} %constant_dynamic-update-slice_fusion.refs_1_), channel_id=1, source_target_pairs={{0,64},{8,72},{16,80},{24,88},{32,96},{40,104},{48,112},{56,120},{... | collective-permute-start | bytes 983048 | tf_op jit(solution)/shard_map/ppermute | solution.py:51
  (4 other events, 29.0 us)

commit v6 on v5

--- a/solution.py
+++ b/solution.py
@@ -60,37 +60,24 @@
     return sum_four([value] + [exchange(value, "shard", d) for d in X_STEPS])
 
 
-def whole(shape):
-    return pl.BlockSpec(shape, lambda *_: (0,) * len(shape))
-
-
-def call(kernel, outs, args, cost, name, aliases=None, grid=None, out_specs=None, spare=(),
-         scratch=()):
-    specs = [pl.BlockSpec(memory_space=pltpu.VMEM)] * (len(args) - 1)
+def call(kernel, outs, args, cost, name, aliases=None, out_specs=None, spare=(), scratch=()):
+    specs = [pl.BlockSpec(memory_space=pltpu.VMEM)] * len(args)
     specs += [pl.BlockSpec(memory_space=pl.ANY)] * len(spare)
     flops, traffic = cost
     return pl.pallas_call(
         kernel,
         out_shape=outs,
-        grid_spec=pltpu.PrefetchScalarGridSpec(
-            num_scalar_prefetch=1,
-            grid=grid or (1,),
-            in_specs=specs,
-            out_specs=out_specs or [pl.BlockSpec(memory_space=pltpu.VMEM)] * len(outs),
-            scratch_shapes=scratch,
-        ),
+        in_specs=specs,
+        out_specs=out_specs or [pl.BlockSpec(memory_space=pltpu.VMEM)] * len(outs),
+        scratch_shapes=scratch,
         input_output_aliases=aliases or {},
         compiler_params=pltpu.CompilerParams(vmem_limit_bytes=16 * 2**20),
         cost_estimate=pl.CostEstimate(flops=flops, bytes_accessed=traffic, transcendentals=0),
         name=name,
-    )(
-        args[0],
-        *[pltpu.with_memory_space_constraint(v, pltpu.VMEM) for v in args[1:]],
-        *spare,
-    )
-
-
-def factor_kernel(rep_ref, warm_far, grad_far, feed_far, *refs):
+    )(*[pltpu.with_memory_space_constraint(v, pltpu.VMEM) for v in args], *spare)
+
+
+def factor_kernel(warm_far, grad_far, feed_far, *refs):
     outs, (grad_ref, feed_ref, warm_ref, parts_ref, total_ref, sems) = refs[:Y_SIZE], refs[Y_SIZE:]
     rank, rows = warm_ref.shape
     quarter = outs[0].shape[1]
@@ -115,12 +102,12 @@
         term = native(parts, grad_ref[at, :], 1, 0) + native(parts, feed_ref[at, :], 1, 0)
         total = term if total is None else total + term
     total_ref[...] = (total[2 * rank :] + total[rank : 2 * rank]) + total[:rank]
-    own = rep_ref[0] // Z_SIZE
+    own = lax.axis_index("rep") // Z_SIZE
     for d, out in enumerate(outs):
         out[...] = total_ref[:, pl.ds(pl.multiple_of((own ^ d) * quarter, quarter), quarter)]
 
 
-def local_factor(rep, warm_t, gradient, feedback):
+def local_factor(warm_t, gradient, feedback):
     rank, rows = warm_t.shape
     columns = gradient.shape[1]
     near = pltpu.VMEM((rows, columns), BF16)
@@ -128,29 +115,25 @@
     outs = pl.pallas_call(
         factor_kernel,
         out_shape=[pltpu.VMEM((rank, columns // Y_SIZE), F32)] * Y_SIZE + [near] * 2,
-        grid_spec=pltpu.PrefetchScalarGridSpec(
-            num_scalar_prefetch=1,
-            grid=(1,),
-            in_specs=[pl.BlockSpec(memory_space=pl.ANY)] * 3,
-            out_specs=[pl.BlockSpec(memory_space=pltpu.VMEM)] * (Y_SIZE + 2),
-            scratch_shapes=[
-                pltpu.VMEM((rank, rows), F32),
-                pltpu.VMEM((3 * rank, rows), BF16),
-                pltpu.VMEM((rank, columns), F32),
-                pltpu.SemaphoreType.DMA((2 * ROW_BLOCKS + 1,)),
-            ],
-        ),
+        in_specs=[pl.BlockSpec(memory_space=pl.ANY)] * 3,
+        out_specs=[pl.BlockSpec(memory_space=pltpu.VMEM)] * (Y_SIZE + 2),
+        scratch_shapes=[
+            pltpu.VMEM((rank, rows), F32),
+            pltpu.VMEM((3 * rank, rows), BF16),
+            pltpu.VMEM((rank, columns), F32),
+            pltpu.SemaphoreType.DMA((2 * ROW_BLOCKS + 1,)),
+        ],
         compiler_params=pltpu.CompilerParams(vmem_limit_bytes=16 * 2**20),
         cost_estimate=pl.CostEstimate(flops=10**9, bytes_accessed=2_500_000, transcendentals=0),
         name="local_factor",
-    )(rep, *args)
+    )(*args)
     return outs[:Y_SIZE], outs[Y_SIZE], outs[Y_SIZE + 1]
 
 
-def assemble_kernel(rep_ref, *refs):
+def assemble_kernel(*refs):
     quarters, (factor_ref, parts_ref, gram_ref) = refs[:Y_SIZE], refs[Y_SIZE:]
     rank, quarter = quarters[0].shape
-    own = rep_ref[0] // Z_SIZE
+    own = lax.axis_index("rep") // Z_SIZE
     for d, block in enumerate(quarters):
         at = pl.ds(pl.multiple_of((own ^ d) * quarter, quarter), quarter)
         factor_ref[:, at] = block[...]
@@ -160,7 +143,7 @@
     gram_ref[...] = exact(factor, factor, 1, 1)
 
 
-def assemble(rep, quarters):
+def assemble(quarters):
     rank, quarter = quarters[0].shape
     columns = quarter * Y_SIZE
     outs = [
@@ -168,10 +151,10 @@
         pltpu.VMEM((3 * rank, columns), BF16),
         pltpu.VMEM((rank, rank), F32),
     ]
-    return call(assemble_kernel, outs, (rep, *quarters), (10**8, 500_000), "assemble_factor")
-
-
-def project_kernel(rep_ref, grad_ref, feed_ref, parts_ref, out_ref):
+    return call(assemble_kernel, outs, tuple(quarters), (10**8, 500_000), "assemble_factor")
+
+
+def project_kernel(grad_ref, feed_ref, parts_ref, out_ref):
     replicas, half, _ = out_ref.shape
     rows = grad_ref.shape[0]
     rank = parts_ref.shape[0] // 3
@@ -187,16 +170,16 @@
         out_ref[i * groups : (i + 1) * groups] = jnp.concatenate([value[:, 0], value[:, 1]], axis=-1)
 
 
-def project(rep, gradient, feedback, parts, replicas):
+def project(gradient, feedback, parts, replicas):
     rank = parts.shape[0] // 3
     half = gradient.shape[0] // replicas // 2
     outs = [pltpu.VMEM((replicas, half, 2 * rank), F32)]
     return call(
-        project_kernel, outs, (rep, gradient, feedback, parts), (10**9, 2_500_000), "project"
+        project_kernel, outs, (gradient, feedback, parts), (10**9, 2_500_000), "project"
     )[0]
 
 
-def inverse_kernel(rep_ref, gram_ref, factor_ref, inverse_ref, unit_ref, parts_ref):
+def inverse_kernel(gram_ref, factor_ref, inverse_ref, unit_ref, parts_ref):
     rank = gram_ref.shape[0]
     width = 8
     row = lax.broadcasted_iota(jnp.int32, (rank, rank), 0)
@@ -230,17 +213,17 @@
         parts_ref[(2 * i + 1) * rank : (2 * i + 2) * rank, :] = part
 
 
-def invert(rep, gram, factor_t):
+def invert(gram, factor_t):
     rank, columns = factor_t.shape
     outs = [
         pltpu.VMEM((rank, rank), F32),
         pltpu.VMEM((rank, columns), F32),
         pltpu.VMEM((6 * rank, columns), BF16),
     ]
-    return call(inverse_kernel, outs, (rep, gram, factor_t), (2 * 10**9, 500_000), "invert")
-
-
-def update_kernel(replicas, rep_ref, sum_ref, inverse_ref, unit_ref, master_ref, moment_ref,
+    return call(inverse_kernel, outs, (gram, factor_t), (2 * 10**9, 500_000), "invert")
+
+
+def update_kernel(replicas, sum_ref, inverse_ref, unit_ref, master_ref, moment_ref,
                   second_ref, send_ref, master_out, moment_out, second_out):
     rank = inverse_ref.shape[0]
     columns = master_ref.shape[1]
@@ -262,70 +245,68 @@
     send_ref[:, columns:] = jnp.concatenate([high, right - high], axis=1).astype(BF16)
 
 
-def update(replicas, rep, own_sum, inverse, unit_t, master, moment, second):
+def update(replicas, own_sum, inverse, unit_t, master, moment, second):
     rows, columns = master.shape
     rank = inverse.shape[0]
     block = pltpu.VMEM(master.shape, F32)
     outs = [pltpu.VMEM((rows, columns + 2 * rank), BF16), block, block, block]
-    args = (rep, own_sum, inverse, unit_t, master, moment, second)
+    args = (own_sum, inverse, unit_t, master, moment, second)
     kernel = lambda *refs: update_kernel(replicas, *refs)
     return call(kernel, outs, args, (5 * 10**7, 600_000), "update")
 
 
-def new_rows(own_y, own_z, d, block, parts_ref, grad_ref, feed_ref, out_ref):
-    columns = grad_ref.shape[1]
-    groups, own_rows, width = block.shape
-    right = block[:, :, columns:].reshape(groups * own_rows, width - columns)
-    approx = native(jnp.concatenate([right] * 3, axis=1), parts_ref[...], 1, 0)
-    first = (own_y ^ d) * (groups * own_rows)
-    for j in range(groups):
-        at = pl.multiple_of((own_z ^ Z_ORDER[j]) * own_rows, own_rows)
-        source = pl.ds(pl.multiple_of(first + at, own_rows), own_rows)
-        merged = grad_ref[source, :].astype(F32) + feed_ref[source, :].astype(F32)
-        piece = approx[j * own_rows : (j + 1) * own_rows]
-        out_ref[pl.ds(at, own_rows), :] = (merged - piece).astype(BF16)
-
-
-def finish_kernel(begins, ds, rep_ref, *refs):
+def finish_kernel(begins, ds, *refs):
     count = Y_SIZE if not begins else len(ds)
     blocks, (parts_ref, grad_ref, feed_ref) = refs[:count], refs[count : count + 3]
     rest = refs[count + 3 :] if begins else refs[count + 5 :]
     if begins:
         new_far, weights_far, new_near, sems = rest
     else:
-        new_far, weights_far, right_ref, new_near, right_rows, sems = rest
+        new_far, weights_far, right_far, new_near, right_near, sems = rest
     columns = grad_ref.shape[1]
     groups, own_rows, width = blocks[0].shape
     size = groups * own_rows
     rank = (width - columns) // 2
-    own_y, own_z = rep_ref[0] // Z_SIZE, rep_ref[0] % Z_SIZE
+    own_y, own_z = lax.axis_index("rep") // Z_SIZE, lax.axis_index("rep") % Z_SIZE
     copies = []
 
     def send(source, target):
         copies.append(pltpu.make_async_copy(source, target, sems.at[len(copies)]))
         copies[-1].start()
 
-    def rows_of(d, j):
-        at = (own_y ^ d) * size + (own_z ^ Z_ORDER[j]) * own_rows
-        return pl.ds(pl.multiple_of(at, own_rows), own_rows)
-
+    def piece_of(z):
+        step = own_z ^ z
+        return step ^ ((step >> 2) & (1 - ((step >> 1) & 1)))
+
+    def rights_of(block):
+        return jnp.concatenate([block[piece_of(z), :, columns:] for z in range(groups)], axis=0)
+
+    def rows_of(d):
+        return pl.ds(pl.multiple_of((own_y ^ d) * size, size), size)
+
+    for d in ds:
+        for j in range(groups):
+            at = (own_y ^ d) * size + (own_z ^ Z_ORDER[j]) * own_rows
+            target = weights_far.at[pl.ds(pl.multiple_of(at, own_rows), own_rows)]
+            send(blocks[d].at[j, :, pl.ds(0, columns)], target)
+    if not begins:
+        row = lax.broadcasted_iota(jnp.int32, (rank, 2 * rank), 0)
+        column = lax.broadcasted_iota(jnp.int32, (rank, 2 * rank), 1)
+        both = jnp.where((row == column) | (row + rank == column), 1.0, 0.0).astype(BF16)
+        for d, block in enumerate(blocks):
+            right_near[:, rows_of(d)] = native(both, rights_of(block), 1, 1)
+        send(right_near, right_far)
     for i, d in enumerate(ds):
-        for j in range(groups):
-            send(blocks[d].at[j, :, pl.ds(0, columns)], weights_far.at[rows_of(d, j)])
-        new_rows(own_y, own_z, d, blocks[d], parts_ref, grad_ref, feed_ref, new_near.at[i])
-        target = pl.ds(pl.multiple_of((own_y ^ d) * size, size), size)
-        send(new_near.at[i], new_far.at[target])
-    if not begins:
-        for d, block in enumerate(blocks):
-            for j in range(groups):
-                wide = block[j, :, columns:].astype(F32)
-                right_rows[rows_of(d, j), :] = wide[:, :rank] + wide[:, rank:]
-        right_ref[...] = right_rows[...].T
+        right = rights_of(blocks[d])
+        approx = native(jnp.concatenate([right] * 3, axis=1), parts_ref[...], 1, 0)
+        merged = grad_ref[rows_of(d), :].astype(F32) + feed_ref[rows_of(d), :].astype(F32)
+        new_near[i] = (merged - approx).astype(BF16)
+        send(new_near.at[i], new_far.at[rows_of(d)])
     for copy in copies:
         copy.wait()
 
 
-def finish(begins, ds, rep, blocks, parts, gradient, feedback, begun=()):
+def finish(begins, ds, blocks, parts, gradient, feedback, begun=()):
     rows, columns = gradient.shape
     groups, own_rows, width = blocks[0].shape
     rank = (width - columns) // 2
@@ -335,55 +316,54 @@
     scratch = [pltpu.VMEM((len(ds), groups * own_rows, columns), BF16)]
     if not begins:
         outs = outs + [jax.ShapeDtypeStruct((rank, rows), F32)]
-        out_specs = out_specs + [whole((rank, rows))]
-        scratch = scratch + [pltpu.VMEM((rows, rank), F32)]
+        out_specs = out_specs + [far]
+        scratch = scratch + [pltpu.VMEM((rank, rows), F32)]
     return call(
         lambda *refs: finish_kernel(begins, ds, *refs),
         outs,
-        (rep, *blocks, parts, gradient, feedback),
+        (*blocks, parts, gradient, feedback),
         (len(ds) * 3 * 10**8, len(ds) * 1_500_000),
         "finish_own" if begins else "finish_rest",
-        aliases={} if begins else {Y_SIZE + 4: 0, Y_SIZE + 5: 1},
+        aliases={} if begins else {Y_SIZE + 3: 0, Y_SIZE + 4: 1},
         out_specs=out_specs,
         spare=begun,
-        scratch=scratch + [pltpu.SemaphoreType.DMA((len(ds) * (groups + 1),))],
+        scratch=scratch + [pltpu.SemaphoreType.DMA((len(ds) * (groups + 1) + 1,))],
     )
 
 
 def on_device(gradient, feedback, warm_start, master, moment, second):
     replicas = lax.axis_size("rep")
     gradient, feedback = gradient[0], feedback[0]
-    rep = lax.axis_index("rep").astype(jnp.int32).reshape(1)
-
-    pieces, gradient, feedback = local_factor(rep, warm_start.T, gradient, feedback)
+
+    pieces, gradient, feedback = local_factor(warm_start.T, gradient, feedback)
     quarter = sum_four([pieces[0]] + [exchange(p, "rep", d) for p, d in zip(pieces[1:], Y_STEPS)])
     for distance in Z_SUM_STEPS:
         quarter = quarter + exchange(quarter, "rep", distance)
     quarter = quarter / replicas
     quarters = [quarter] + [exchange(quarter, "rep", d) for d in Y_STEPS]
-    factor_t, parts, gram_term = assemble(rep, quarters)
+    factor_t, parts, gram_term = assemble(quarters)
 
     gram_pair = gram_term + exchange(gram_term, "shard", 1)
-    packed = project(rep, gradient, feedback, parts, replicas)
+    packed = project(gradient, feedback, parts, replicas)
     gram_pair, packed = lax.optimization_barrier((gram_pair, packed))
     received = lax.all_to_all(packed, "rep", 0, 0, tiled=True)
     gram = sum_four([gram_pair] + [exchange(gram_pair, "shard", d) for d in X_STEPS])
-    inverse, unit_t, unit_parts = invert(rep, gram, factor_t)
+    inverse, unit_t, unit_parts = invert(gram, factor_t)
     received, inverse, unit_t, unit_parts = lax.optimization_barrier(
         (received, inverse, unit_t, unit_parts)
     )
     own_sum = shard_sum(received.sum(0))
 
     send, master_out, moment_out, second_out = update(
-        replicas, rep, own_sum, inverse, unit_t, master, moment, second
+        replicas, own_sum, inverse, unit_t, master, moment, second
     )
     pair = jnp.stack([send, exchange(send, "rep", 1)])
     column = jnp.concatenate([pair] + [exchange(pair, "rep", d) for d in Z_PAIRS])
     others = [exchange(column, "rep", d) for d in Y_STEPS]
-    begun = finish(True, (0,), rep, [column], unit_parts, gradient, feedback)
+    begun = finish(True, (0,), [column], unit_parts, gradient, feedback)
     blocks = [column] + others
     new_feedback, weights, right_t = finish(
-        False, (1, 2, 3), rep, blocks, unit_parts, gradient, feedback, begun
+        False, (1, 2, 3), blocks, unit_parts, gradient, feedback, begun
     )
     return (new_feedback[None], weights, master_out, moment_out, second_out, right_t.T)
 

time: 102 us -> 101 us (level)
  no operation moved by 1% of the time
where the time goes in v6:
time: 101 us
  starting transfers between devices  44.5 us (44%)
  waiting for transfers between devices  43.9 us (43%)
  Pallas kernels  9.42 us (9%)
  local copies, waits for them, and re-layouts  1.96 us (2%)
    ppermute x24, waiting for transfers between devices, exchange(): lax.ppermute(value, axis, [(i, i ^ distance) for i in range(lax.axis_size...  41.4 us
    ppermute x24, starting transfers between devices, exchange(): lax.ppermute(value, axis, [(i, i ^ distance) for i in range(lax.axis_size...  34.8 us
    all_to_all x1, starting transfers between devices, on_device(): received = lax.all_to_all(packed, 'rep', 0, 0, tiled=True)  9.69 us
    pallas_call x6, Pallas kernels, call(): pl.pallas_call(kernel, out_shape=outs, in_specs=specs, out_specs=out_spec...  7.47 us
    all_to_all x1, waiting for transfers between devices, on_device(): received = lax.all_to_all(packed, 'rep', 0, 0, tiled=True)  2.46 us
  transfers between devices with their start and end apart: 25, of which 18 were waited for; matrix products, arithmetic and copies ran while one was open for 2% of the time, Pallas kernels for 5%

profile of v6, /device:TPU:32, one launch (start us, length us, event | category | flops | bytes accessed | tf_op | source)
XLA Modules:
  0.0 100.8 jit_solution(8635607268887672933)
XLA Ops:
  0.6 1.9 %local_factor.1 = (f32[64,128]{1,0:T(8,128)S(1)}, f32[64,128]{1,0:T(8,128)S(1)}, f32[64,128]{1,0:T(8,128)S(1)}, f32[64,128]{1,0:T(8,128)S(1)}, bf16[1024,512]{1,...) custom-call(f32[64,1024]{1,0:T(8,128)} %bitcast.14, bf16[1024,512]{1,0:T(8,128)(2,1)} %bitcast.12, bf16[1024,512]{1,0:T(8,128)(2,1)} %bitcast.13), custom_call_target="tpu_custom_call" | custom-call | flops 1000000000 | bytes 2500000 | tf_op jit(solution)/shard_map/local_factor/pallas_call | solution.py:115
  2.6 1.7 %collective-permute-start = (f32[64,128]{1,0:T(8,128)S(1)}, f32[64,128]{1,0:T(8,128)S(1)}, u32[]{:S(2)}, u32[]{:S(2)}) collective-permute-start(f32[64,128]{1,0:T(8,128)S(1)} %get-tuple-element.34), channel_id=1, source_target_pairs={{0,64},{8,72},{16,80},{24,88},{32,96},{40,104},{48,112},{56,120},{... | collective-permute-start | bytes 98312 | tf_op jit(solution)/shard_map/ppermute | solution.py:51
  4.3 2.9 %collective-permute-start.1 = (f32[64,128]{1,0:T(8,128)S(1)}, f32[64,128]{1,0:T(8,128)S(1)}, u32[]{:S(2)}, u32[]{:S(2)}) collective-permute-start(f32[64,128]{1,0:T(8,128)S(1)} %get-tuple-element.35), channel_id=1, source_target_pairs={{0,128},{8,136},{16,144},{24,152},{32,160},{40,168},{48,176},{56,1... | collective-permute-start | bytes 98312 | tf_op jit(solution)/shard_map/ppermute | solution.py:51
  7.4 2.3 %collective-permute-done.1 = f32[64,128]{1,0:T(8,128)S(1)} collective-permute-done((f32[64,128]{1,0:T(8,128)S(1)}, f32[64,128]{1,0:T(8,128)S(1)}, u32[]{:S(2)}, u32[]{:S(2)}) %collective-permute-start.1) | collective-permute-done | bytes 32800 | tf_op jit(solution)/shard_map/ppermute | solution.py:51
  9.7 2.6 %collective-permute-done.2 = f32[64,128]{1,0:T(8,128)S(1)} collective-permute-done((f32[64,128]{1,0:T(8,128)S(1)}, f32[64,128]{1,0:T(8,128)S(1)}, u32[]{:S(2)}, u32[]{:S(2)}) %collective-permute-start.2) | collective-permute-done | bytes 32800 | tf_op jit(solution)/shard_map/ppermute | solution.py:51
  12.5 3.8 %collective-permute-done.3 = f32[64,128]{1,0:T(8,128)S(1)} collective-permute-done((f32[64,128]{1,0:T(8,128)S(1)}, f32[64,128]{1,0:T(8,128)S(1)}, u32[]{:S(2)}, u32[]{:S(2)}) %collective-permute-start.3) | collective-permute-done | bytes 32800 | tf_op jit(solution)/shard_map/ppermute | solution.py:51
  16.3 2.2 %collective-permute-start.4 = (f32[64,128]{1,0:T(8,128)S(1)}, f32[64,128]{1,0:T(8,128)S(1)}, u32[]{:S(2)}, u32[]{:S(2)}) collective-permute-start(f32[64,128]{1,0:T(8,128)S(1)} %add.45), channel_id=1, source_target_pairs={{0,24},{8,16},{16,8},{24,0},{32,56},{40,48},{48,40},{56,32},{64,88... | collective-permute-start | bytes 98312 | tf_op jit(solution)/shard_map/ppermute | solution.py:51
  18.5 1.9 %collective-permute-done.4 = f32[64,128]{1,0:T(8,128)S(1)} collective-permute-done((f32[64,128]{1,0:T(8,128)S(1)}, f32[64,128]{1,0:T(8,128)S(1)}, u32[]{:S(2)}, u32[]{:S(2)}) %collective-permute-start.4) | collective-permute-done | bytes 32800 | tf_op jit(solution)/shard_map/ppermute | solution.py:51
  20.4 5.7 %collective-permute-start.5 = (f32[64,128]{1,0:T(8,128)S(1)}, f32[64,128]{1,0:T(8,128)S(1)}, u32[]{:S(2)}, u32[]{:S(2)}) collective-permute-start(f32[64,128]{1,0:T(8,128)S(1)} %add.46), channel_id=1, source_target_pairs={{0,56},{8,48},{16,40},{24,32},{32,24},{40,16},{48,8},{56,0},{64,12... | collective-permute-start | bytes 98312 | tf_op jit(solution)/shard_map/ppermute | solution.py:51
  26.1 1.9 %collective-permute-done.5 = f32[64,128]{1,0:T(8,128)S(1)} collective-permute-done((f32[64,128]{1,0:T(8,128)S(1)}, f32[64,128]{1,0:T(8,128)S(1)}, u32[]{:S(2)}, u32[]{:S(2)}) %collective-permute-start.5) | collective-permute-done | bytes 32800 | tf_op jit(solution)/shard_map/ppermute | solution.py:51
  29.0 3.1 %collective-permute-start.6 = (f32[64,128]{1,0:T(8,128)S(1)}, f32[64,128]{1,0:T(8,128)S(1)}, u32[]{:S(2)}, u32[]{:S(2)}) collective-permute-start(f32[64,128]{1,0:T(8,128)S(1)} %add_multiply_fusion.refs_0_), channel_id=1, source_target_pairs={{0,64},{8,72},{16,80},{24,88},{32,96},{40,104},{48,112},{56,120},{... | collective-permute-start | bytes 98312 | tf_op jit(solution)/shard_map/ppermute | solution.py:51
  36.3 9.7 %all-to-all-start = ((f32[32,16,128]{2,1,0:T(8,128)}), f32[32,16,128]{2,1,0:T(8,128)S(1)}, u32[]{:S(2)}, u32[]{:S(2)}) async-start(f32[32,16,128]{2,1,0:T(8,128)} %project.1), calls=%async_computation | async-start | bytes 524288 | tf_op jit(solution)/shard_map/all_to_all | solution.py:349
  46.0 2.8 %collective-permute-start.12 = (f32[64,64]{1,0:T(8,128)S(1)}, f32[64,64]{1,0:T(8,128)S(1)}, u32[]{:S(2)}, u32[]{:S(2)}) collective-permute-start(f32[64,64]{1,0:T(8,128)S(1)} %add.48), channel_id=1, source_target_pairs={{0,6},{1,7},{2,4},{3,5},{4,2},{5,3},{6,0},{7,1},{8,14},{9,15},{10,... | collective-permute-start | bytes 49160 | tf_op jit(solution)/shard_map/ppermute | solution.py:51
  51.2 3.1 %collective-permute-done.11 = f32[64,64]{1,0:T(8,128)S(1)} collective-permute-done((f32[64,64]{1,0:T(8,128)S(1)}, f32[64,64]{1,0:T(8,128)S(1)}, u32[]{:S(2)}, u32[]{:S(2)}) %collective-permute-start.11) | collective-permute-done | bytes 16416 | tf_op jit(solution)/shard_map/ppermute | solution.py:51
  54.3 2.2 %invert.1 = (f32[64,64]{1,0:T(8,128)S(1)}, f32[64,512]{1,0:T(8,128)S(1)}, bf16[384,512]{1,0:T(8,128)(2,1)S(1)}) custom-call(f32[64,64]{1,0:T(8,128)S(1)} %add_add_fusion.gram_ref, f32[64,512]{1,0:T(8,128)S(1)} %get-tuple-element.43.factor_ref), custom_call_target="tpu_custom_call" | custom-call | flops 2000000000 | bytes 500000 | tf_op jit(solution)/shard_map/invert/pallas_call | solution.py:67
  56.4 2.5 %all-to-all-done = f32[32,16,128]{2,1,0:T(8,128)S(1)} async-done(((f32[32,16,128]{2,1,0:T(8,128)}), f32[32,16,128]{2,1,0:T(8,128)S(1)}, u32[]{:S(2)}, u32[]{:S(2)}) %all-to-all-start) | async-done | bytes 262176 | tf_op jit(solution)/shard_map/all_to_all | solution.py:349
  60.2 2.8 %collective-permute-start.16 = (f32[16,128]{1,0:T(8,128)S(1)}, f32[16,128]{1,0:T(8,128)S(1)}, u32[]{:S(2)}, u32[]{:S(2)}) collective-permute-start(f32[16,128]{1,0:T(8,128)S(1)} %add.52), channel_id=1, source_target_pairs={{0,6},{1,7},{2,4},{3,5},{4,2},{5,3},{6,0},{7,1},{8,14},{9,15},{10,... | collective-permute-start | bytes 24584 | tf_op jit(solution)/shard_map/ppermute | solution.py:51
  65.1 3.1 %collective-permute-done.15 = f32[16,128]{1,0:T(8,128)S(1)} collective-permute-done((f32[16,128]{1,0:T(8,128)S(1)}, f32[16,128]{1,0:T(8,128)S(1)}, u32[]{:S(2)}, u32[]{:S(2)}) %collective-permute-start.15) | collective-permute-done | bytes 8224 | tf_op jit(solution)/shard_map/ppermute | solution.py:51
  68.8 4.0 %collective-permute-done.17 = bf16[32,640]{1,0:T(8,128)(2,1)S(1)} collective-permute-done((bf16[32,640]{1,0:T(8,128)(2,1)S(1)}, bf16[32,640]{1,0:T(8,128)(2,1)S(1)}, u32[]{:S(2)}, u32[]{:S(2)}) %collective-permute-start.17) | collective-permute-done | bytes 40992 | tf_op jit(solution)/shard_map/ppermute | solution.py:51
  73.0 4.3 %collective-permute-start.19 = (bf16[2,32,640]{2,1,0:T(8,128)(2,1)S(1)}, bf16[2,32,640]{2,1,0:T(8,128)(2,1)S(1)}, u32[]{:S(2)}, u32[]{:S(2)}) collective-permute-start(bf16[2,32,640]{2,1,0:T(8,128)(2,1)S(1)} %pad_maximum_fusion), channel_id=1, source_target_pairs={{0,40},{8,32},{16,56},{24,48},{32,8},{40,0},{48,24},{56,16},{64,10... | collective-permute-start | bytes 245768 | tf_op jit(solution)/shard_map/ppermute | solution.py:51
  77.9 5.5 %collective-permute-done.18 = bf16[2,32,640]{2,1,0:T(8,128)(2,1)S(1)} collective-permute-done((bf16[2,32,640]{2,1,0:T(8,128)(2,1)S(1)}, bf16[2,32,640]{2,1,0:T(8,128)(2,1)S(1)}, u32[]{:S(2)}, u32[]{:S(2)}) %collective-permute-start.18) | collective-permute-done | bytes 81952 | tf_op jit(solution)/shard_map/ppermute | solution.py:51
  83.9 2.2 %collective-permute-start.22 = (bf16[8,32,640]{2,1,0:T(8,128)(2,1)S(1)}, bf16[8,32,640]{2,1,0:T(8,128)(2,1)S(1)}, u32[]{:S(2)}, u32[]{:S(2)}) collective-permute-start(bf16[8,32,640]{2,1,0:T(8,128)(2,1)S(1)} %constant_dynamic-update-slice_fusion.refs_0_), channel_id=1, source_target_pairs={{0,128},{8,136},{16,144},{24,152},{32,160},{40,168},{48,176},{56,1... | collective-permute-start | bytes 983048 | tf_op jit(solution)/shard_map/ppermute | solution.py:51
  90.7 7.5 %collective-permute-done.23.refs_3_ = bf16[8,32,640]{2,1,0:T(8,128)(2,1)S(1)} collective-permute-done((bf16[8,32,640]{2,1,0:T(8,128)(2,1)S(1)}, bf16[8,32,640]{2,1,0:T(8,128)(2,1)S(1)}, u32[]{:S(2)}, u32[]{:S(2)}) %collective-permute-start.23) | collective-permute-done | bytes 327712 | tf_op jit(solution)/shard_map/ppermute | solution.py:51
  98.8 1.9 %finish_rest.1 = (bf16[1024,512]{1,0:T(8,128)(2,1)}, bf16[1024,512]{1,0:T(8,128)(2,1)}, f32[64,1024]{1,0:T(8,128)}) custom-call(bf16[8,32,640]{2,1,0:T(8,128)(2,1)S(1)} %constant_dynamic-update-slice_fusion.refs_0_, bf16[8,32,640]{2,1,0:T(8,128)(2,1)S(1)} %collective-permute-done.21.refs_1_, ...), custom_call_target="tpu_custom_call", output_to_operand_aliasing={{0}: (7, {}), {1}: (8, {})} | custom-call | flops 900000000 | bytes 4500000 | tf_op jit(solution)/shard_map/finish_rest/pallas_call | solution.py:67
  (57 shorter events, 18.5 us)
Async XLA Ops:
  2.6 4.8 %collective-permute-start = (f32[64,128]{1,0:T(8,128)S(1)}, f32[64,128]{1,0:T(8,128)S(1)}, u32[]{:S(2)}, u32[]{:S(2)}) collective-permute-start(f32[64,128]{1,0:T(8,128)S(1)} %get-tuple-element.34), channel_id=1, source_target_pairs={{0,64},{8,72},{16,80},{24,88},{32,96},{40,104},{48,112},{56,120},{... | collective-permute-start | bytes 98312 | tf_op jit(solution)/shard_map/ppermute | solution.py:51
  4.3 5.4 %collective-permute-start.1 = (f32[64,128]{1,0:T(8,128)S(1)}, f32[64,128]{1,0:T(8,128)S(1)}, u32[]{:S(2)}, u32[]{:S(2)}) collective-permute-start(f32[64,128]{1,0:T(8,128)S(1)} %get-tuple-element.35), channel_id=1, source_target_pairs={{0,128},{8,136},{16,144},{24,152},{32,160},{40,168},{48,176},{56,1... | collective-permute-start | bytes 98312 | tf_op jit(solution)/shard_map/ppermute | solution.py:51
  7.2 5.1 %collective-permute-start.2 = (f32[64,128]{1,0:T(8,128)S(1)}, f32[64,128]{1,0:T(8,128)S(1)}, u32[]{:S(2)}, u32[]{:S(2)}) collective-permute-start(f32[64,128]{1,0:T(8,128)S(1)} %get-tuple-element.36), channel_id=1, source_target_pairs={{0,192},{8,200},{16,208},{24,216},{32,224},{40,232},{48,240},{56,2... | collective-permute-start | bytes 98312 | tf_op jit(solution)/shard_map/ppermute | solution.py:51
  12.3 4.0 %collective-permute-start.3 = (f32[64,128]{1,0:T(8,128)S(1)}, f32[64,128]{1,0:T(8,128)S(1)}, u32[]{:S(2)}, u32[]{:S(2)}) collective-permute-start(f32[64,128]{1,0:T(8,128)S(1)} %add_add_fusion.1), channel_id=1, source_target_pairs={{0,8},{8,0},{16,24},{24,16},{32,40},{40,32},{48,56},{56,48},{64,72... | collective-permute-start | bytes 98312 | tf_op jit(solution)/shard_map/ppermute | solution.py:51
  16.3 4.1 %collective-permute-start.4 = (f32[64,128]{1,0:T(8,128)S(1)}, f32[64,128]{1,0:T(8,128)S(1)}, u32[]{:S(2)}, u32[]{:S(2)}) collective-permute-start(f32[64,128]{1,0:T(8,128)S(1)} %add.45), channel_id=1, source_target_pairs={{0,24},{8,16},{16,8},{24,0},{32,56},{40,48},{48,40},{56,32},{64,88... | collective-permute-start | bytes 98312 | tf_op jit(solution)/shard_map/ppermute | solution.py:51
  20.4 7.6 %collective-permute-start.5 = (f32[64,128]{1,0:T(8,128)S(1)}, f32[64,128]{1,0:T(8,128)S(1)}, u32[]{:S(2)}, u32[]{:S(2)}) collective-permute-start(f32[64,128]{1,0:T(8,128)S(1)} %add.46), channel_id=1, source_target_pairs={{0,56},{8,48},{16,40},{24,32},{32,24},{40,16},{48,8},{56,0},{64,12... | collective-permute-start | bytes 98312 | tf_op jit(solution)/shard_map/ppermute | solution.py:51
  28.0 5.1 %collective-permute-start.8 = (f32[64,128]{1,0:T(8,128)S(1)}, f32[64,128]{1,0:T(8,128)S(1)}, u32[]{:S(2)}, u32[]{:S(2)}) collective-permute-start(f32[64,128]{1,0:T(8,128)S(1)} %add_multiply_fusion.refs_0_), channel_id=1, source_target_pairs={{0,192},{8,200},{16,208},{24,216},{32,224},{40,232},{48,240},{56,2... | collective-permute-start | bytes 98312 | tf_op jit(solution)/shard_map/ppermute | solution.py:51
  28.2 5.4 %collective-permute-start.7 = (f32[64,128]{1,0:T(8,128)S(1)}, f32[64,128]{1,0:T(8,128)S(1)}, u32[]{:S(2)}, u32[]{:S(2)}) collective-permute-start(f32[64,128]{1,0:T(8,128)S(1)} %add_multiply_fusion.refs_0_), channel_id=1, source_target_pairs={{0,128},{8,136},{16,144},{24,152},{32,160},{40,168},{48,176},{56,1... | collective-permute-start | bytes 98312 | tf_op jit(solution)/shard_map/ppermute | solution.py:51
  29.0 5.3 %collective-permute-start.6 = (f32[64,128]{1,0:T(8,128)S(1)}, f32[64,128]{1,0:T(8,128)S(1)}, u32[]{:S(2)}, u32[]{:S(2)}) collective-permute-start(f32[64,128]{1,0:T(8,128)S(1)} %add_multiply_fusion.refs_0_), channel_id=1, source_target_pairs={{0,64},{8,72},{16,80},{24,88},{32,96},{40,104},{48,112},{56,120},{... | collective-permute-start | bytes 98312 | tf_op jit(solution)/shard_map/ppermute | solution.py:51
  34.6 1.7 %collective-permute-start.9 = (f32[64,64]{1,0:T(8,128)S(1)}, f32[64,64]{1,0:T(8,128)S(1)}, u32[]{:S(2)}, u32[]{:S(2)}) collective-permute-start(f32[64,64]{1,0:T(8,128)S(1)} %get-tuple-element.37), channel_id=1, source_target_pairs={{0,1},{1,0},{2,3},{3,2},{4,5},{5,4},{6,7},{7,6},{8,9},{9,8},{10,11... | collective-permute-start | bytes 49160 | tf_op jit(solution)/shard_map/ppermute | solution.py:51
  36.3 22.6 %all-to-all-start = ((f32[32,16,128]{2,1,0:T(8,128)}), f32[32,16,128]{2,1,0:T(8,128)S(1)}, u32[]{:S(2)}, u32[]{:S(2)}) async-start(f32[32,16,128]{2,1,0:T(8,128)} %project.1), calls=%async_computation | async-start | bytes 524288 | tf_op jit(solution)/shard_map/all_to_all | solution.py:349
  46.0 5.2 %collective-permute-start.12 = (f32[64,64]{1,0:T(8,128)S(1)}, f32[64,64]{1,0:T(8,128)S(1)}, u32[]{:S(2)}, u32[]{:S(2)}) collective-permute-start(f32[64,64]{1,0:T(8,128)S(1)} %add.48), channel_id=1, source_target_pairs={{0,6},{1,7},{2,4},{3,5},{4,2},{5,3},{6,0},{7,1},{8,14},{9,15},{10,... | collective-permute-start | bytes 49160 | tf_op jit(solution)/shard_map/ppermute | solution.py:51
  48.8 5.4 %collective-permute-start.11 = (f32[64,64]{1,0:T(8,128)S(1)}, f32[64,64]{1,0:T(8,128)S(1)}, u32[]{:S(2)}, u32[]{:S(2)}) collective-permute-start(f32[64,64]{1,0:T(8,128)S(1)} %add.48), channel_id=1, source_target_pairs={{0,4},{1,5},{2,6},{3,7},{4,0},{5,1},{6,2},{7,3},{8,12},{9,13},{10,... | collective-permute-start | bytes 49160 | tf_op jit(solution)/shard_map/ppermute | solution.py:51
  49.6 4.6 %collective-permute-start.10 = (f32[64,64]{1,0:T(8,128)S(1)}, f32[64,64]{1,0:T(8,128)S(1)}, u32[]{:S(2)}, u32[]{:S(2)}) collective-permute-start(f32[64,64]{1,0:T(8,128)S(1)} %add.48), channel_id=1, source_target_pairs={{0,2},{1,3},{2,0},{3,1},{4,6},{5,7},{6,4},{7,5},{8,10},{9,11},{10,... | collective-permute-start | bytes 49160 | tf_op jit(solution)/shard_map/ppermute | solution.py:51
  60.2 4.9 %collective-permute-start.16 = (f32[16,128]{1,0:T(8,128)S(1)}, f32[16,128]{1,0:T(8,128)S(1)}, u32[]{:S(2)}, u32[]{:S(2)}) collective-permute-start(f32[16,128]{1,0:T(8,128)S(1)} %add.52), channel_id=1, source_target_pairs={{0,6},{1,7},{2,4},{3,5},{4,2},{5,3},{6,0},{7,1},{8,14},{9,15},{10,... | collective-permute-start | bytes 24584 | tf_op jit(solution)/shard_map/ppermute | solution.py:51
  63.0 5.2 %collective-permute-start.15 = (f32[16,128]{1,0:T(8,128)S(1)}, f32[16,128]{1,0:T(8,128)S(1)}, u32[]{:S(2)}, u32[]{:S(2)}) collective-permute-start(f32[16,128]{1,0:T(8,128)S(1)} %add.52), channel_id=1, source_target_pairs={{0,4},{1,5},{2,6},{3,7},{4,0},{5,1},{6,2},{7,3},{8,12},{9,13},{10,... | collective-permute-start | bytes 24584 | tf_op jit(solution)/shard_map/ppermute | solution.py:51
  63.8 4.4 %collective-permute-start.14 = (f32[16,128]{1,0:T(8,128)S(1)}, f32[16,128]{1,0:T(8,128)S(1)}, u32[]{:S(2)}, u32[]{:S(2)}) collective-permute-start(f32[16,128]{1,0:T(8,128)S(1)} %add.52), channel_id=1, source_target_pairs={{0,2},{1,3},{2,0},{3,1},{4,6},{5,7},{6,4},{7,5},{8,10},{9,11},{10,... | collective-permute-start | bytes 24584 | tf_op jit(solution)/shard_map/ppermute | solution.py:51
  68.7 4.1 %collective-permute-start.17 = (bf16[32,640]{1,0:T(8,128)(2,1)S(1)}, bf16[32,640]{1,0:T(8,128)(2,1)S(1)}, u32[]{:S(2)}, u32[]{:S(2)}) collective-permute-start(bf16[32,640]{1,0:T(8,128)(2,1)S(1)} %get-tuple-element.50), channel_id=1, source_target_pairs={{0,8},{8,0},{16,24},{24,16},{32,40},{40,32},{48,56},{56,48},{64,72... | collective-permute-start | bytes 122888 | tf_op jit(solution)/shard_map/ppermute | solution.py:51
  72.8 10.7 %collective-permute-start.20 = (bf16[2,32,640]{2,1,0:T(8,128)(2,1)S(1)}, bf16[2,32,640]{2,1,0:T(8,128)(2,1)S(1)}, u32[]{:S(2)}, u32[]{:S(2)}) collective-permute-start(bf16[2,32,640]{2,1,0:T(8,128)(2,1)S(1)} %pad_maximum_fusion), channel_id=1, source_target_pairs={{0,48},{8,56},{16,32},{24,40},{32,16},{40,24},{48,0},{56,8},{64,11... | collective-permute-start | bytes 245768 | tf_op jit(solution)/shard_map/ppermute | solution.py:51
  73.0 10.4 %collective-permute-start.19 = (bf16[2,32,640]{2,1,0:T(8,128)(2,1)S(1)}, bf16[2,32,640]{2,1,0:T(8,128)(2,1)S(1)}, u32[]{:S(2)}, u32[]{:S(2)}) collective-permute-start(bf16[2,32,640]{2,1,0:T(8,128)(2,1)S(1)} %pad_maximum_fusion), channel_id=1, source_target_pairs={{0,40},{8,32},{16,56},{24,48},{32,8},{40,0},{48,24},{56,16},{64,10... | collective-permute-start | bytes 245768 | tf_op jit(solution)/shard_map/ppermute | solution.py:51
  77.3 6.2 %collective-permute-start.18 = (bf16[2,32,640]{2,1,0:T(8,128)(2,1)S(1)}, bf16[2,32,640]{2,1,0:T(8,128)(2,1)S(1)}, u32[]{:S(2)}, u32[]{:S(2)}) collective-permute-start(bf16[2,32,640]{2,1,0:T(8,128)(2,1)S(1)} %pad_maximum_fusion), channel_id=1, source_target_pairs={{0,16},{8,24},{16,0},{24,8},{32,48},{40,56},{48,32},{56,40},{64,80... | collective-permute-start | bytes 245768 | tf_op jit(solution)/shard_map/ppermute | solution.py:51
  83.5 14.7 %collective-permute-start.23 = (bf16[8,32,640]{2,1,0:T(8,128)(2,1)S(1)}, bf16[8,32,640]{2,1,0:T(8,128)(2,1)S(1)}, u32[]{:S(2)}, u32[]{:S(2)}) collective-permute-start(bf16[8,32,640]{2,1,0:T(8,128)(2,1)S(1)} %constant_dynamic-update-slice_fusion.refs_0_), channel_id=1, source_target_pairs={{0,192},{8,200},{16,208},{24,216},{32,224},{40,232},{48,240},{56,2... | collective-permute-start | bytes 983048 | tf_op jit(solution)/shard_map/ppermute | solution.py:51
  83.9 14.3 %collective-permute-start.22 = (bf16[8,32,640]{2,1,0:T(8,128)(2,1)S(1)}, bf16[8,32,640]{2,1,0:T(8,128)(2,1)S(1)}, u32[]{:S(2)}, u32[]{:S(2)}) collective-permute-start(bf16[8,32,640]{2,1,0:T(8,128)(2,1)S(1)} %constant_dynamic-update-slice_fusion.refs_0_), channel_id=1, source_target_pairs={{0,128},{8,136},{16,144},{24,152},{32,160},{40,168},{48,176},{56,1... | collective-permute-start | bytes 983048 | tf_op jit(solution)/shard_map/ppermute | solution.py:51
  86.1 12.7 %collective-permute-start.21 = (bf16[8,32,640]{2,1,0:T(8,128)(2,1)S(1)}, bf16[8,32,640]{2,1,0:T(8,128)(2,1)S(1)}, u32[]{:S(2)}, u32[]{:S(2)}) collective-permute-start(bf16[8,32,640]{2,1,0:T(8,128)(2,1)S(1)} %constant_dynamic-update-slice_fusion.refs_0_), channel_id=1, source_target_pairs={{0,64},{8,72},{16,80},{24,88},{32,96},{40,104},{48,112},{56,120},{... | collective-permute-start | bytes 983048 | tf_op jit(solution)/shard_map/ppermute | solution.py:51
  (4 other events, 29.0 us)

commit v7 on v6

--- a/solution.py
+++ b/solution.py
@@ -53,11 +53,6 @@
 
 def sum_four(terms):
     return (terms[0] + terms[1]) + (terms[2] + terms[3])
-
-
-def shard_sum(value):
-    value = value + exchange(value, "shard", 1)
-    return sum_four([value] + [exchange(value, "shard", d) for d in X_STEPS])
 
 
 def call(kernel, outs, args, cost, name, aliases=None, out_specs=None, spare=(), scratch=()):
@@ -78,7 +73,8 @@
 
 
 def factor_kernel(warm_far, grad_far, feed_far, *refs):
-    outs, (grad_ref, feed_ref, warm_ref, parts_ref, total_ref, sems) = refs[:Y_SIZE], refs[Y_SIZE:]
+    states_far, outs = refs[:3], refs[3 : 3 + Y_SIZE]
+    grad_ref, feed_ref, state_ref, warm_ref, parts_ref, total_ref, sems = refs[3 + Y_SIZE :]
     rank, rows = warm_ref.shape
     quarter = outs[0].shape[1]
     size = rows // ROW_BLOCKS
@@ -90,6 +86,11 @@
         for k, (far, ref) in enumerate([(grad_far, grad_ref), (feed_far, feed_ref)]):
             copies.append(pltpu.make_async_copy(far.at[at], ref.at[at], sems.at[2 * i + k]))
             copies[-1].start()
+    states = []
+    for i, far in enumerate(states_far):
+        sem = sems.at[2 * ROW_BLOCKS + 1 + i]
+        states.append(pltpu.make_async_copy(far, state_ref.at[i], sem))
+        states[-1].start()
     warm_copy.wait()
     for i, part in enumerate(three_parts(warm_ref[...])):
         parts_ref[i * rank : (i + 1) * rank, :] = part
@@ -105,29 +106,33 @@
     own = lax.axis_index("rep") // Z_SIZE
     for d, out in enumerate(outs):
         out[...] = total_ref[:, pl.ds(pl.multiple_of((own ^ d) * quarter, quarter), quarter)]
-
-
-def local_factor(warm_t, gradient, feedback):
+    for copy in states:
+        copy.wait()
+
+
+def local_factor(warm_t, gradient, feedback, states):
     rank, rows = warm_t.shape
     columns = gradient.shape[1]
     near = pltpu.VMEM((rows, columns), BF16)
-    args = [pltpu.with_memory_space_constraint(v, pltpu.HBM) for v in (warm_t, gradient, feedback)]
+    far = (warm_t, gradient, feedback, *states)
+    args = [pltpu.with_memory_space_constraint(v, pltpu.HBM) for v in far]
     outs = pl.pallas_call(
         factor_kernel,
-        out_shape=[pltpu.VMEM((rank, columns // Y_SIZE), F32)] * Y_SIZE + [near] * 2,
-        in_specs=[pl.BlockSpec(memory_space=pl.ANY)] * 3,
-        out_specs=[pl.BlockSpec(memory_space=pltpu.VMEM)] * (Y_SIZE + 2),
+        out_shape=[pltpu.VMEM((rank, columns // Y_SIZE), F32)] * Y_SIZE
+        + [near, near, pltpu.VMEM((3, *states[0].shape), F32)],
+        in_specs=[pl.BlockSpec(memory_space=pl.ANY)] * 6,
+        out_specs=[pl.BlockSpec(memory_space=pltpu.VMEM)] * (Y_SIZE + 3),
         scratch_shapes=[
             pltpu.VMEM((rank, rows), F32),
             pltpu.VMEM((3 * rank, rows), BF16),
             pltpu.VMEM((rank, columns), F32),
-            pltpu.SemaphoreType.DMA((2 * ROW_BLOCKS + 1,)),
+            pltpu.SemaphoreType.DMA((2 * ROW_BLOCKS + 4,)),
         ],
         compiler_params=pltpu.CompilerParams(vmem_limit_bytes=16 * 2**20),
         cost_estimate=pl.CostEstimate(flops=10**9, bytes_accessed=2_500_000, transcendentals=0),
         name="local_factor",
     )(*args)
-    return outs[:Y_SIZE], outs[Y_SIZE], outs[Y_SIZE + 1]
+    return outs[:Y_SIZE], *outs[Y_SIZE:]
 
 
 def assemble_kernel(*refs):
@@ -154,29 +159,52 @@
     return call(assemble_kernel, outs, tuple(quarters), (10**8, 500_000), "assemble_factor")
 
 
-def project_kernel(grad_ref, feed_ref, parts_ref, out_ref):
-    replicas, half, _ = out_ref.shape
-    rows = grad_ref.shape[0]
+def project_kernel(which, grad_ref, feed_ref, parts_ref, out_ref):
+    replicas, quarter, _ = out_ref.shape
+    own_rows = grad_ref.shape[0] // replicas
     rank = parts_ref.shape[0] // 3
     parts = parts_ref[...]
-    groups = 8
-    size = rows // replicas * groups
-
-    for i in range(replicas // groups):
-        at = slice(i * size, (i + 1) * size)
-        total = native(grad_ref[at, :], parts, 1, 1) + native(feed_ref[at, :], parts, 1, 1)
+    groups = replicas // 2
+    first = (lax.axis_index("shard") % 2 ^ which) * (2 * quarter)
+
+    def rows_of(ref, i):
+        pieces = []
+        for r in range(i * groups, (i + 1) * groups):
+            at = pl.multiple_of(r * own_rows + first, 2 * quarter)
+            pieces.append(ref[pl.ds(at, 2 * quarter), :])
+        return jnp.concatenate(pieces, axis=0)
+
+    for i in range(2):
+        total = native(rows_of(grad_ref, i), parts, 1, 1)
+        total = total + native(rows_of(feed_ref, i), parts, 1, 1)
         value = (total[:, 2 * rank :] + total[:, rank : 2 * rank]) + total[:, :rank]
-        value = value.reshape(groups, 2, half, rank)
+        value = value.reshape(groups, 2, quarter, rank)
         out_ref[i * groups : (i + 1) * groups] = jnp.concatenate([value[:, 0], value[:, 1]], axis=-1)
 
 
-def project(gradient, feedback, parts, replicas):
+def project(which, gradient, feedback, parts, replicas):
     rank = parts.shape[0] // 3
-    half = gradient.shape[0] // replicas // 2
-    outs = [pltpu.VMEM((replicas, half, 2 * rank), F32)]
+    quarter = gradient.shape[0] // replicas // 4
     return call(
-        project_kernel, outs, (gradient, feedback, parts), (10**9, 2_500_000), "project"
+        lambda *refs: project_kernel(which, *refs),
+        [pltpu.VMEM((replicas, quarter, 2 * rank), F32)],
+        (gradient, feedback, parts),
+        (5 * 10**8, 1_300_000),
+        "project_send" if which else "project_keep",
     )[0]
+
+
+def pair_kernel(keep_ref, other_ref, out_ref):
+    for r in range(keep_ref.shape[0]):
+        total = keep_ref[r] + other_ref[r]
+        out_ref[r, 0] = total
+        out_ref[r ^ 1, 1] = total
+
+
+def pair_up(keep, other):
+    replicas, quarter, lanes = keep.shape
+    outs = [jax.ShapeDtypeStruct((replicas, 2, quarter, lanes), F32)]
+    return call(pair_kernel, outs, (keep, other), (10**6, 500_000), "pair_up")[0]
 
 
 def inverse_kernel(gram_ref, factor_ref, inverse_ref, unit_ref, parts_ref):
@@ -223,36 +251,47 @@
     return call(inverse_kernel, outs, (gram, factor_t), (2 * 10**9, 500_000), "invert")
 
 
-def update_kernel(replicas, sum_ref, inverse_ref, unit_ref, master_ref, moment_ref,
-                  second_ref, send_ref, master_out, moment_out, second_out):
+def update_kernel(replicas, half_ref, other_ref, inverse_ref, unit_ref, state_ref, neighbour_ref,
+                  send_ref, master_out, moment_out, second_out):
     rank = inverse_ref.shape[0]
-    columns = master_ref.shape[1]
-    packed = sum_ref[...]
-    own = jnp.concatenate([packed[:, :rank], packed[:, rank:]], axis=0)
-    right = exact(own, inverse_ref[...], 1, 1) / replicas
-    grad = exact(right, unit_ref[...], 1, 0)
-    moment = beta_one * moment_ref[...] + (1.0 - beta_one) * grad
-    second = beta_two * second_ref[...] + (1.0 - beta_two) * grad * grad
-    master = master_ref[...]
-    master = master - learn_rate * (
-        moment / (jnp.sqrt(second) + adam_eps) + decay_rate * master
-    )
-    moment_out[...] = moment
-    second_out[...] = second
-    master_out[...] = master
-    high = right.astype(BF16).astype(F32)
-    send_ref[:, :columns] = master.astype(BF16)
-    send_ref[:, columns:] = jnp.concatenate([high, right - high], axis=1).astype(BF16)
-
-
-def update(replicas, own_sum, inverse, unit_t, master, moment, second):
-    rows, columns = master.shape
+    columns = unit_ref.shape[1]
+    first_core = lax.axis_index("shard") % 2 == 0
+    low = jnp.where(first_core, half_ref[...], other_ref[...])
+    high = jnp.where(first_core, other_ref[...], half_ref[...])
+    pieces = []
+    for k in range(2):
+        for half in (low[k], high[k]):
+            pieces += [half[:, :rank], half[:, rank:]]
+    sums = jnp.concatenate(pieces, axis=0)
+    rights = exact(sums, inverse_ref[...], 1, 1) / replicas
+    grads = exact(rights, unit_ref[...], 1, 0)
+    own_rows = sums.shape[0] // 2
+    for k, ref in enumerate([state_ref, neighbour_ref]):
+        at = slice(k * own_rows, (k + 1) * own_rows)
+        right, grad = rights[at], grads[at]
+        master, moment, second = ref[0], ref[1], ref[2]
+        moment = beta_one * moment + (1.0 - beta_one) * grad
+        second = beta_two * second + (1.0 - beta_two) * grad * grad
+        master = master - learn_rate * (
+            moment / (jnp.sqrt(second) + adam_eps) + decay_rate * master
+        )
+        if k == 0:
+            master_out[...] = master
+            moment_out[...] = moment
+            second_out[...] = second
+        upper = right.astype(BF16).astype(F32)
+        send_ref[k, :, :columns] = master.astype(BF16)
+        send_ref[k, :, columns:] = jnp.concatenate([upper, right - upper], axis=1).astype(BF16)
+
+
+def update(replicas, half_sum, other_sum, inverse, unit_t, state, neighbour):
+    _, rows, columns = state.shape
     rank = inverse.shape[0]
-    block = pltpu.VMEM(master.shape, F32)
-    outs = [pltpu.VMEM((rows, columns + 2 * rank), BF16), block, block, block]
-    args = (own_sum, inverse, unit_t, master, moment, second)
+    block = pltpu.VMEM((rows, columns), F32)
+    outs = [pltpu.VMEM((2, rows, columns + 2 * rank), BF16), block, block, block]
+    args = (half_sum, other_sum, inverse, unit_t, state, neighbour)
     kernel = lambda *refs: update_kernel(replicas, *refs)
-    return call(kernel, outs, args, (5 * 10**7, 600_000), "update")
+    return call(kernel, outs, args, (10**8, 1_000_000), "update")
 
 
 def finish_kernel(begins, ds, *refs):
@@ -333,31 +372,35 @@
 
 def on_device(gradient, feedback, warm_start, master, moment, second):
     replicas = lax.axis_size("rep")
-    gradient, feedback = gradient[0], feedback[0]
-
-    pieces, gradient, feedback = local_factor(warm_start.T, gradient, feedback)
+
+    pieces, gradient, feedback, state = local_factor(
+        warm_start.T, gradient[0], feedback[0], (master, moment, second)
+    )
     quarter = sum_four([pieces[0]] + [exchange(p, "rep", d) for p, d in zip(pieces[1:], Y_STEPS)])
     for distance in Z_SUM_STEPS:
         quarter = quarter + exchange(quarter, "rep", distance)
     quarter = quarter / replicas
+    quarter, state = lax.optimization_barrier((quarter, state))
     quarters = [quarter] + [exchange(quarter, "rep", d) for d in Y_STEPS]
+    neighbour = exchange(state, "rep", 1)
     factor_t, parts, gram_term = assemble(quarters)
 
     gram_pair = gram_term + exchange(gram_term, "shard", 1)
-    packed = project(gradient, feedback, parts, replicas)
+    other_half = exchange(project(1, gradient, feedback, parts, replicas), "shard", 1)
+    packed = pair_up(project(0, gradient, feedback, parts, replicas), other_half)
     gram_pair, packed = lax.optimization_barrier((gram_pair, packed))
     received = lax.all_to_all(packed, "rep", 0, 0, tiled=True)
     gram = sum_four([gram_pair] + [exchange(gram_pair, "shard", d) for d in X_STEPS])
     inverse, unit_t, unit_parts = invert(gram, factor_t)
-    received, inverse, unit_t, unit_parts = lax.optimization_barrier(
-        (received, inverse, unit_t, unit_parts)
-    )
-    own_sum = shard_sum(received.sum(0))
-
-    send, master_out, moment_out, second_out = update(
-        replicas, own_sum, inverse, unit_t, master, moment, second
-    )
-    pair = jnp.stack([send, exchange(send, "rep", 1)])
+    received, inverse, unit_t, unit_parts, neighbour = lax.optimization_barrier(
+        (received, inverse, unit_t, unit_parts, neighbour)
+    )
+    half_sum = received.sum(0)
+    half_sum = sum_four([half_sum] + [exchange(half_sum, "shard", d) for d in X_STEPS])
+
+    pair, master_out, moment_out, second_out = update(
+        replicas, half_sum, exchange(half_sum, "shard", 1), inverse, unit_t, state, neighbour
+    )
     column = jnp.concatenate([pair] + [exchange(pair, "rep", d) for d in Z_PAIRS])
     others = [exchange(column, "rep", d) for d in Y_STEPS]
     begun = finish(True, (0,), [column], unit_parts, gradient, feedback)

time: 101 us -> 104 us (1.030); the launches traced: 101 us -> 103 us
    ppermute x24 -> x25, waiting for transfers between devices: 41.4 us -> 42.7 us  [exchange(): lax.ppermute(value, axis, [(i, i ^ distance) for i in range(lax.axis_size...]
    ppermute x24 -> x25, starting transfers between devices: 34.8 us -> 35.7 us  [exchange(): lax.ppermute(value, axis, [(i, i ^ distance) for i in range(lax.axis_size...]
    pallas_call x6 -> x8, Pallas kernels: 7.47 us -> 7.86 us  [call(): pl.pallas_call(kernel, out_shape=outs, in_specs=specs, out_specs=out_spec...]
  transfers between devices with their start and end apart: 25 -> 26, of which waited for: 18 -> 19; matrix products, arithmetic and copies ran while one was open for 2% -> 2% of each run, Pallas kernels for 5% -> 4%
where the time goes in v7:
time: 104 us; the launch traced here: 103 us
  starting transfers between devices  45.4 us (44%)
  waiting for transfers between devices  44.5 us (43%)
  Pallas kernels  9.84 us (9%)
  local copies, waits for them, and re-layouts  1.94 us (2%)
    ppermute x25, waiting for transfers between devices, exchange(): lax.ppermute(value, axis, [(i, i ^ distance) for i in range(lax.axis_size...  42.7 us
    ppermute x25, starting transfers between devices, exchange(): lax.ppermute(value, axis, [(i, i ^ distance) for i in range(lax.axis_size...  35.7 us
    all_to_all x1, starting transfers between devices, on_device(): received = lax.all_to_all(packed, 'rep', 0, 0, tiled=True)  9.68 us
    pallas_call x8, Pallas kernels, call(): pl.pallas_call(kernel, out_shape=outs, in_specs=specs, out_specs=out_spec...  7.86 us
  transfers between devices with their start and end apart: 26, of which 19 were waited for; matrix products, arithmetic and copies ran while one was open for 2% of the time, Pallas kernels for 4%

profile of v7, /device:TPU:32, one launch (start us, length us, event | category | flops | bytes accessed | tf_op | source)
XLA Modules:
  0.0 102.6 jit_solution(6060669994312125229)
XLA Ops:
  0.6 2.0 %local_factor.1 = (f32[64,128]{1,0:T(8,128)S(1)}, f32[64,128]{1,0:T(8,128)S(1)}, f32[64,128]{1,0:T(8,128)S(1)}, f32[64,128]{1,0:T(8,128)S(1)}, bf16[1024,512]{1,...) custom-call(f32[64,1024]{1,0:T(8,128)} %bitcast.8, bf16[1024,512]{1,0:T(8,128)(2,1)} %bitcast.6, ...), custom_call_target="tpu_custom_call" | custom-call | flops 1000000000 | bytes 2500000 | tf_op jit(solution)/shard_map/local_factor/pallas_call | solution.py:119
  2.6 1.7 %collective-permute-start = (f32[64,128]{1,0:T(8,128)S(1)}, f32[64,128]{1,0:T(8,128)S(1)}, u32[]{:S(2)}, u32[]{:S(2)}) collective-permute-start(f32[64,128]{1,0:T(8,128)S(1)} %get-tuple-element.38), channel_id=1, source_target_pairs={{0,64},{8,72},{16,80},{24,88},{32,96},{40,104},{48,112},{56,120},{... | collective-permute-start | bytes 98312 | tf_op jit(solution)/shard_map/ppermute | solution.py:51
  4.3 2.9 %collective-permute-start.1 = (f32[64,128]{1,0:T(8,128)S(1)}, f32[64,128]{1,0:T(8,128)S(1)}, u32[]{:S(2)}, u32[]{:S(2)}) collective-permute-start(f32[64,128]{1,0:T(8,128)S(1)} %get-tuple-element.39), channel_id=1, source_target_pairs={{0,128},{8,136},{16,144},{24,152},{32,160},{40,168},{48,176},{56,1... | collective-permute-start | bytes 98312 | tf_op jit(solution)/shard_map/ppermute | solution.py:51
  7.4 2.3 %collective-permute-done.1 = f32[64,128]{1,0:T(8,128)S(1)} collective-permute-done((f32[64,128]{1,0:T(8,128)S(1)}, f32[64,128]{1,0:T(8,128)S(1)}, u32[]{:S(2)}, u32[]{:S(2)}) %collective-permute-start.1) | collective-permute-done | bytes 32800 | tf_op jit(solution)/shard_map/ppermute | solution.py:51
  9.7 2.6 %collective-permute-done.2 = f32[64,128]{1,0:T(8,128)S(1)} collective-permute-done((f32[64,128]{1,0:T(8,128)S(1)}, f32[64,128]{1,0:T(8,128)S(1)}, u32[]{:S(2)}, u32[]{:S(2)}) %collective-permute-start.2) | collective-permute-done | bytes 32800 | tf_op jit(solution)/shard_map/ppermute | solution.py:51
  12.5 3.8 %collective-permute-done.3 = f32[64,128]{1,0:T(8,128)S(1)} collective-permute-done((f32[64,128]{1,0:T(8,128)S(1)}, f32[64,128]{1,0:T(8,128)S(1)}, u32[]{:S(2)}, u32[]{:S(2)}) %collective-permute-start.3) | collective-permute-done | bytes 32800 | tf_op jit(solution)/shard_map/ppermute | solution.py:51
  16.3 2.2 %collective-permute-start.4 = (f32[64,128]{1,0:T(8,128)S(1)}, f32[64,128]{1,0:T(8,128)S(1)}, u32[]{:S(2)}, u32[]{:S(2)}) collective-permute-start(f32[64,128]{1,0:T(8,128)S(1)} %add.42), channel_id=1, source_target_pairs={{0,24},{8,16},{16,8},{24,0},{32,56},{40,48},{48,40},{56,32},{64,88... | collective-permute-start | bytes 98312 | tf_op jit(solution)/shard_map/ppermute | solution.py:51
  18.5 1.9 %collective-permute-done.4 = f32[64,128]{1,0:T(8,128)S(1)} collective-permute-done((f32[64,128]{1,0:T(8,128)S(1)}, f32[64,128]{1,0:T(8,128)S(1)}, u32[]{:S(2)}, u32[]{:S(2)}) %collective-permute-start.4) | collective-permute-done | bytes 32800 | tf_op jit(solution)/shard_map/ppermute | solution.py:51
  20.4 5.7 %collective-permute-start.5 = (f32[64,128]{1,0:T(8,128)S(1)}, f32[64,128]{1,0:T(8,128)S(1)}, u32[]{:S(2)}, u32[]{:S(2)}) collective-permute-start(f32[64,128]{1,0:T(8,128)S(1)} %add.43), channel_id=1, source_target_pairs={{0,56},{8,48},{16,40},{24,32},{32,24},{40,16},{48,8},{56,0},{64,12... | collective-permute-start | bytes 98312 | tf_op jit(solution)/shard_map/ppermute | solution.py:51
  26.1 1.9 %collective-permute-done.5 = f32[64,128]{1,0:T(8,128)S(1)} collective-permute-done((f32[64,128]{1,0:T(8,128)S(1)}, f32[64,128]{1,0:T(8,128)S(1)}, u32[]{:S(2)}, u32[]{:S(2)}) %collective-permute-start.5) | collective-permute-done | bytes 32800 | tf_op jit(solution)/shard_map/ppermute | solution.py:51
  29.0 3.1 %collective-permute-start.6 = (f32[64,128]{1,0:T(8,128)S(1)}, f32[64,128]{1,0:T(8,128)S(1)}, u32[]{:S(2)}, u32[]{:S(2)}) collective-permute-start(f32[64,128]{1,0:T(8,128)S(1)} %add_multiply_fusion.refs_0_), channel_id=1, source_target_pairs={{0,64},{8,72},{16,80},{24,88},{32,96},{40,104},{48,112},{56,120},{... | collective-permute-start | bytes 98312 | tf_op jit(solution)/shard_map/ppermute | solution.py:51
  37.4 9.7 %all-to-all-start = ((f32[32,2,8,128]{3,2,1,0:T(8,128)}), f32[32,2,8,128]{3,2,1,0:T(8,128)S(1)}, u32[]{:S(2)}, u32[]{:S(2)}) async-start(f32[32,2,8,128]{3,2,1,0:T(8,128)} %pair_up.1), calls=%async_computation | async-start | bytes 524288 | tf_op jit(solution)/shard_map/all_to_all | solution.py:392
  47.1 2.8 %collective-permute-start.13 = (f32[64,64]{1,0:T(8,128)S(1)}, f32[64,64]{1,0:T(8,128)S(1)}, u32[]{:S(2)}, u32[]{:S(2)}) collective-permute-start(f32[64,64]{1,0:T(8,128)S(1)} %add.45), channel_id=1, source_target_pairs={{0,6},{1,7},{2,4},{3,5},{4,2},{5,3},{6,0},{7,1},{8,14},{9,15},{10,... | collective-permute-start | bytes 49160 | tf_op jit(solution)/shard_map/ppermute | solution.py:51
  52.3 3.1 %collective-permute-done.12 = f32[64,64]{1,0:T(8,128)S(1)} collective-permute-done((f32[64,64]{1,0:T(8,128)S(1)}, f32[64,64]{1,0:T(8,128)S(1)}, u32[]{:S(2)}, u32[]{:S(2)}) %collective-permute-start.12) | collective-permute-done | bytes 16416 | tf_op jit(solution)/shard_map/ppermute | solution.py:51
  55.4 2.2 %invert.1 = (f32[64,64]{1,0:T(8,128)S(1)}, f32[64,512]{1,0:T(8,128)S(1)}, bf16[384,512]{1,0:T(8,128)(2,1)S(1)}) custom-call(f32[64,64]{1,0:T(8,128)S(1)} %add_add_fusion.gram_ref, f32[64,512]{1,0:T(8,128)S(1)} %get-tuple-element.49.factor_ref), custom_call_target="tpu_custom_call" | custom-call | flops 2000000000 | bytes 500000 | tf_op jit(solution)/shard_map/invert/pallas_call | solution.py:62
  58.3 1.8 %all-to-all-done = f32[32,2,8,128]{3,2,1,0:T(8,128)S(1)} async-done(((f32[32,2,8,128]{3,2,1,0:T(8,128)}), f32[32,2,8,128]{3,2,1,0:T(8,128)S(1)}, u32[]{:S(2)}, u32[]{:S(2)}) %all-to-all-start) | async-done | bytes 262176 | tf_op jit(solution)/shard_map/all_to_all | solution.py:392
  60.1 3.0 %collective-permute-start.17 = (f32[2,8,128]{2,1,0:T(8,128)S(1)}, f32[2,8,128]{2,1,0:T(8,128)S(1)}, u32[]{:S(2)}, u32[]{:S(2)}) collective-permute-start(f32[2,8,128]{2,1,0:T(8,128)S(1)} %reduce_sum.9), channel_id=1, source_target_pairs={{0,6},{1,7},{2,4},{3,5},{4,2},{5,3},{6,0},{7,1},{8,14},{9,15},{10,... | collective-permute-start | bytes 24584 | tf_op jit(solution)/shard_map/ppermute | solution.py:51
  65.2 3.1 %collective-permute-done.16 = f32[2,8,128]{2,1,0:T(8,128)S(1)} collective-permute-done((f32[2,8,128]{2,1,0:T(8,128)S(1)}, f32[2,8,128]{2,1,0:T(8,128)S(1)}, u32[]{:S(2)}, u32[]{:S(2)}) %collective-permute-start.16) | collective-permute-done | bytes 8224 | tf_op jit(solution)/shard_map/ppermute | solution.py:51
  70.1 1.9 %collective-permute-start.21 = (bf16[2,32,640]{2,1,0:T(8,128)(2,1)S(1)}, bf16[2,32,640]{2,1,0:T(8,128)(2,1)S(1)}, u32[]{:S(2)}, u32[]{:S(2)}) collective-permute-start(bf16[2,32,640]{2,1,0:T(8,128)(2,1)S(1)} %get-tuple-element.58), channel_id=1, source_target_pairs={{0,48},{8,56},{16,32},{24,40},{32,16},{40,24},{48,0},{56,8},{64,11... | collective-permute-start | bytes 245768 | tf_op jit(solution)/shard_map/ppermute | solution.py:51
  72.0 2.9 %collective-permute-start.20 = (bf16[2,32,640]{2,1,0:T(8,128)(2,1)S(1)}, bf16[2,32,640]{2,1,0:T(8,128)(2,1)S(1)}, u32[]{:S(2)}, u32[]{:S(2)}) collective-permute-start(bf16[2,32,640]{2,1,0:T(8,128)(2,1)S(1)} %get-tuple-element.58), channel_id=1, source_target_pairs={{0,40},{8,32},{16,56},{24,48},{32,8},{40,0},{48,24},{56,16},{64,10... | collective-permute-start | bytes 245768 | tf_op jit(solution)/shard_map/ppermute | solution.py:51
  75.2 6.8 %collective-permute-done.19 = bf16[2,32,640]{2,1,0:T(8,128)(2,1)S(1)} collective-permute-done((bf16[2,32,640]{2,1,0:T(8,128)(2,1)S(1)}, bf16[2,32,640]{2,1,0:T(8,128)(2,1)S(1)}, u32[]{:S(2)}, u32[]{:S(2)}) %collective-permute-start.19) | collective-permute-done | bytes 81952 | tf_op jit(solution)/shard_map/ppermute | solution.py:51
  82.0 3.0 %collective-permute-start.24 = (bf16[8,32,640]{2,1,0:T(8,128)(2,1)S(1)}, bf16[8,32,640]{2,1,0:T(8,128)(2,1)S(1)}, u32[]{:S(2)}, u32[]{:S(2)}) collective-permute-start(bf16[8,32,640]{2,1,0:T(8,128)(2,1)S(1)} %constant_dynamic-update-slice_fusion.refs_0_), channel_id=1, source_target_pairs={{0,192},{8,200},{16,208},{24,216},{32,224},{40,232},{48,240},{56,2... | collective-permute-start | bytes 983048 | tf_op jit(solution)/shard_map/ppermute | solution.py:51
  89.2 10.7 %collective-permute-done.24.refs_3_ = bf16[8,32,640]{2,1,0:T(8,128)(2,1)S(1)} collective-permute-done((bf16[8,32,640]{2,1,0:T(8,128)(2,1)S(1)}, bf16[8,32,640]{2,1,0:T(8,128)(2,1)S(1)}, u32[]{:S(2)}, u32[]{:S(2)}) %collective-permute-start.24) | collective-permute-done | bytes 327712 | tf_op jit(solution)/shard_map/ppermute | solution.py:51
  100.6 1.9 %finish_rest.1 = (bf16[1024,512]{1,0:T(8,128)(2,1)}, bf16[1024,512]{1,0:T(8,128)(2,1)}, f32[64,1024]{1,0:T(8,128)}) custom-call(bf16[8,32,640]{2,1,0:T(8,128)(2,1)S(1)} %constant_dynamic-update-slice_fusion.refs_0_, bf16[8,32,640]{2,1,0:T(8,128)(2,1)S(1)} %collective-permute-done.22.refs_1_, ...), custom_call_target="tpu_custom_call", output_to_operand_aliasing={{0}: (7, {}), {1}: (8, {})} | custom-call | flops 900000000 | bytes 4500000 | tf_op jit(solution)/shard_map/finish_rest/pallas_call | solution.py:62
  (52 shorter events, 19.0 us)
Async XLA Ops:
  2.6 4.8 %collective-permute-start = (f32[64,128]{1,0:T(8,128)S(1)}, f32[64,128]{1,0:T(8,128)S(1)}, u32[]{:S(2)}, u32[]{:S(2)}) collective-permute-start(f32[64,128]{1,0:T(8,128)S(1)} %get-tuple-element.38), channel_id=1, source_target_pairs={{0,64},{8,72},{16,80},{24,88},{32,96},{40,104},{48,112},{56,120},{... | collective-permute-start | bytes 98312 | tf_op jit(solution)/shard_map/ppermute | solution.py:51
  4.3 5.4 %collective-permute-start.1 = (f32[64,128]{1,0:T(8,128)S(1)}, f32[64,128]{1,0:T(8,128)S(1)}, u32[]{:S(2)}, u32[]{:S(2)}) collective-permute-start(f32[64,128]{1,0:T(8,128)S(1)} %get-tuple-element.39), channel_id=1, source_target_pairs={{0,128},{8,136},{16,144},{24,152},{32,160},{40,168},{48,176},{56,1... | collective-permute-start | bytes 98312 | tf_op jit(solution)/shard_map/ppermute | solution.py:51
  7.2 5.1 %collective-permute-start.2 = (f32[64,128]{1,0:T(8,128)S(1)}, f32[64,128]{1,0:T(8,128)S(1)}, u32[]{:S(2)}, u32[]{:S(2)}) collective-permute-start(f32[64,128]{1,0:T(8,128)S(1)} %get-tuple-element.40), channel_id=1, source_target_pairs={{0,192},{8,200},{16,208},{24,216},{32,224},{40,232},{48,240},{56,2... | collective-permute-start | bytes 98312 | tf_op jit(solution)/shard_map/ppermute | solution.py:51
  12.3 4.0 %collective-permute-start.3 = (f32[64,128]{1,0:T(8,128)S(1)}, f32[64,128]{1,0:T(8,128)S(1)}, u32[]{:S(2)}, u32[]{:S(2)}) collective-permute-start(f32[64,128]{1,0:T(8,128)S(1)} %add_add_fusion.1), channel_id=1, source_target_pairs={{0,8},{8,0},{16,24},{24,16},{32,40},{40,32},{48,56},{56,48},{64,72... | collective-permute-start | bytes 98312 | tf_op jit(solution)/shard_map/ppermute | solution.py:51
  16.3 4.1 %collective-permute-start.4 = (f32[64,128]{1,0:T(8,128)S(1)}, f32[64,128]{1,0:T(8,128)S(1)}, u32[]{:S(2)}, u32[]{:S(2)}) collective-permute-start(f32[64,128]{1,0:T(8,128)S(1)} %add.42), channel_id=1, source_target_pairs={{0,24},{8,16},{16,8},{24,0},{32,56},{40,48},{48,40},{56,32},{64,88... | collective-permute-start | bytes 98312 | tf_op jit(solution)/shard_map/ppermute | solution.py:51
  20.4 7.6 %collective-permute-start.5 = (f32[64,128]{1,0:T(8,128)S(1)}, f32[64,128]{1,0:T(8,128)S(1)}, u32[]{:S(2)}, u32[]{:S(2)}) collective-permute-start(f32[64,128]{1,0:T(8,128)S(1)} %add.43), channel_id=1, source_target_pairs={{0,56},{8,48},{16,40},{24,32},{32,24},{40,16},{48,8},{56,0},{64,12... | collective-permute-start | bytes 98312 | tf_op jit(solution)/shard_map/ppermute | solution.py:51
  28.0 5.1 %collective-permute-start.8 = (f32[64,128]{1,0:T(8,128)S(1)}, f32[64,128]{1,0:T(8,128)S(1)}, u32[]{:S(2)}, u32[]{:S(2)}) collective-permute-start(f32[64,128]{1,0:T(8,128)S(1)} %add_multiply_fusion.refs_0_), channel_id=1, source_target_pairs={{0,192},{8,200},{16,208},{24,216},{32,224},{40,232},{48,240},{56,2... | collective-permute-start | bytes 98312 | tf_op jit(solution)/shard_map/ppermute | solution.py:51
  28.2 5.4 %collective-permute-start.7 = (f32[64,128]{1,0:T(8,128)S(1)}, f32[64,128]{1,0:T(8,128)S(1)}, u32[]{:S(2)}, u32[]{:S(2)}) collective-permute-start(f32[64,128]{1,0:T(8,128)S(1)} %add_multiply_fusion.refs_0_), channel_id=1, source_target_pairs={{0,128},{8,136},{16,144},{24,152},{32,160},{40,168},{48,176},{56,1... | collective-permute-start | bytes 98312 | tf_op jit(solution)/shard_map/ppermute | solution.py:51
  29.0 5.3 %collective-permute-start.6 = (f32[64,128]{1,0:T(8,128)S(1)}, f32[64,128]{1,0:T(8,128)S(1)}, u32[]{:S(2)}, u32[]{:S(2)}) collective-permute-start(f32[64,128]{1,0:T(8,128)S(1)} %add_multiply_fusion.refs_0_), channel_id=1, source_target_pairs={{0,64},{8,72},{16,80},{24,88},{32,96},{40,104},{48,112},{56,120},{... | collective-permute-start | bytes 98312 | tf_op jit(solution)/shard_map/ppermute | solution.py:51
  35.2 1.5 %collective-permute-start.10 = (f32[32,8,128]{2,1,0:T(8,128)S(1)}, f32[32,8,128]{2,1,0:T(8,128)S(1)}, u32[]{:S(2)}, u32[]{:S(2)}) collective-permute-start(f32[32,8,128]{2,1,0:T(8,128)S(1)} %project_send.1), channel_id=1, source_target_pairs={{0,1},{1,0},{2,3},{3,2},{4,5},{5,4},{6,7},{7,6},{8,9},{9,8},{10,11... | collective-permute-start | bytes 393224 | tf_op jit(solution)/shard_map/ppermute | solution.py:51
  37.4 22.6 %all-to-all-start = ((f32[32,2,8,128]{3,2,1,0:T(8,128)}), f32[32,2,8,128]{3,2,1,0:T(8,128)S(1)}, u32[]{:S(2)}, u32[]{:S(2)}) async-start(f32[32,2,8,128]{3,2,1,0:T(8,128)} %pair_up.1), calls=%async_computation | async-start | bytes 524288 | tf_op jit(solution)/shard_map/all_to_all | solution.py:392
  47.1 5.2 %collective-permute-start.13 = (f32[64,64]{1,0:T(8,128)S(1)}, f32[64,64]{1,0:T(8,128)S(1)}, u32[]{:S(2)}, u32[]{:S(2)}) collective-permute-start(f32[64,64]{1,0:T(8,128)S(1)} %add.45), channel_id=1, source_target_pairs={{0,6},{1,7},{2,4},{3,5},{4,2},{5,3},{6,0},{7,1},{8,14},{9,15},{10,... | collective-permute-start | bytes 49160 | tf_op jit(solution)/shard_map/ppermute | solution.py:51
  50.0 5.4 %collective-permute-start.12 = (f32[64,64]{1,0:T(8,128)S(1)}, f32[64,64]{1,0:T(8,128)S(1)}, u32[]{:S(2)}, u32[]{:S(2)}) collective-permute-start(f32[64,64]{1,0:T(8,128)S(1)} %add.45), channel_id=1, source_target_pairs={{0,4},{1,5},{2,6},{3,7},{4,0},{5,1},{6,2},{7,3},{8,12},{9,13},{10,... | collective-permute-start | bytes 49160 | tf_op jit(solution)/shard_map/ppermute | solution.py:51
  50.8 4.6 %collective-permute-start.11 = (f32[64,64]{1,0:T(8,128)S(1)}, f32[64,64]{1,0:T(8,128)S(1)}, u32[]{:S(2)}, u32[]{:S(2)}) collective-permute-start(f32[64,64]{1,0:T(8,128)S(1)} %add.45), channel_id=1, source_target_pairs={{0,2},{1,3},{2,0},{3,1},{4,6},{5,7},{6,4},{7,5},{8,10},{9,11},{10,... | collective-permute-start | bytes 49160 | tf_op jit(solution)/shard_map/ppermute | solution.py:51
  51.3 6.9 %collective-permute-start.14 = (f32[3,32,512]{2,1,0:T(8,128)S(1)}, f32[3,32,512]{2,1,0:T(8,128)S(1)}, u32[]{:S(2)}, u32[]{:S(2)}) collective-permute-start(f32[3,32,512]{2,1,0:T(8,128)S(1)} %get-tuple-element.53.refs_4_), channel_id=1, source_target_pairs={{0,8},{8,0},{16,24},{24,16},{32,40},{40,32},{48,56},{56,48},{64,72... | collective-permute-start | bytes 589832 | tf_op jit(solution)/shard_map/ppermute | solution.py:51
  60.1 5.1 %collective-permute-start.17 = (f32[2,8,128]{2,1,0:T(8,128)S(1)}, f32[2,8,128]{2,1,0:T(8,128)S(1)}, u32[]{:S(2)}, u32[]{:S(2)}) collective-permute-start(f32[2,8,128]{2,1,0:T(8,128)S(1)} %reduce_sum.9), channel_id=1, source_target_pairs={{0,6},{1,7},{2,4},{3,5},{4,2},{5,3},{6,0},{7,1},{8,14},{9,15},{10,... | collective-permute-start | bytes 24584 | tf_op jit(solution)/shard_map/ppermute | solution.py:51
  63.1 5.2 %collective-permute-start.16 = (f32[2,8,128]{2,1,0:T(8,128)S(1)}, f32[2,8,128]{2,1,0:T(8,128)S(1)}, u32[]{:S(2)}, u32[]{:S(2)}) collective-permute-start(f32[2,8,128]{2,1,0:T(8,128)S(1)} %reduce_sum.9), channel_id=1, source_target_pairs={{0,4},{1,5},{2,6},{3,7},{4,0},{5,1},{6,2},{7,3},{8,12},{9,13},{10,... | collective-permute-start | bytes 24584 | tf_op jit(solution)/shard_map/ppermute | solution.py:51
  63.9 4.3 %collective-permute-start.15 = (f32[2,8,128]{2,1,0:T(8,128)S(1)}, f32[2,8,128]{2,1,0:T(8,128)S(1)}, u32[]{:S(2)}, u32[]{:S(2)}) collective-permute-start(f32[2,8,128]{2,1,0:T(8,128)S(1)} %reduce_sum.9), channel_id=1, source_target_pairs={{0,2},{1,3},{2,0},{3,1},{4,6},{5,7},{6,4},{7,5},{8,10},{9,11},{10,... | collective-permute-start | bytes 24584 | tf_op jit(solution)/shard_map/ppermute | solution.py:51
  70.1 11.9 %collective-permute-start.21 = (bf16[2,32,640]{2,1,0:T(8,128)(2,1)S(1)}, bf16[2,32,640]{2,1,0:T(8,128)(2,1)S(1)}, u32[]{:S(2)}, u32[]{:S(2)}) collective-permute-start(bf16[2,32,640]{2,1,0:T(8,128)(2,1)S(1)} %get-tuple-element.58), channel_id=1, source_target_pairs={{0,48},{8,56},{16,32},{24,40},{32,16},{40,24},{48,0},{56,8},{64,11... | collective-permute-start | bytes 245768 | tf_op jit(solution)/shard_map/ppermute | solution.py:51
  72.0 10.0 %collective-permute-start.20 = (bf16[2,32,640]{2,1,0:T(8,128)(2,1)S(1)}, bf16[2,32,640]{2,1,0:T(8,128)(2,1)S(1)}, u32[]{:S(2)}, u32[]{:S(2)}) collective-permute-start(bf16[2,32,640]{2,1,0:T(8,128)(2,1)S(1)} %get-tuple-element.58), channel_id=1, source_target_pairs={{0,40},{8,32},{16,56},{24,48},{32,8},{40,0},{48,24},{56,16},{64,10... | collective-permute-start | bytes 245768 | tf_op jit(solution)/shard_map/ppermute | solution.py:51
  74.9 7.1 %collective-permute-start.19 = (bf16[2,32,640]{2,1,0:T(8,128)(2,1)S(1)}, bf16[2,32,640]{2,1,0:T(8,128)(2,1)S(1)}, u32[]{:S(2)}, u32[]{:S(2)}) collective-permute-start(bf16[2,32,640]{2,1,0:T(8,128)(2,1)S(1)} %get-tuple-element.58), channel_id=1, source_target_pairs={{0,16},{8,24},{16,0},{24,8},{32,48},{40,56},{48,32},{56,40},{64,80... | collective-permute-start | bytes 245768 | tf_op jit(solution)/shard_map/ppermute | solution.py:51
  82.0 17.9 %collective-permute-start.24 = (bf16[8,32,640]{2,1,0:T(8,128)(2,1)S(1)}, bf16[8,32,640]{2,1,0:T(8,128)(2,1)S(1)}, u32[]{:S(2)}, u32[]{:S(2)}) collective-permute-start(bf16[8,32,640]{2,1,0:T(8,128)(2,1)S(1)} %constant_dynamic-update-slice_fusion.refs_0_), channel_id=1, source_target_pairs={{0,192},{8,200},{16,208},{24,216},{32,224},{40,232},{48,240},{56,2... | collective-permute-start | bytes 983048 | tf_op jit(solution)/shard_map/ppermute | solution.py:51
  85.1 14.9 %collective-permute-start.23 = (bf16[8,32,640]{2,1,0:T(8,128)(2,1)S(1)}, bf16[8,32,640]{2,1,0:T(8,128)(2,1)S(1)}, u32[]{:S(2)}, u32[]{:S(2)}) collective-permute-start(bf16[8,32,640]{2,1,0:T(8,128)(2,1)S(1)} %constant_dynamic-update-slice_fusion.refs_0_), channel_id=1, source_target_pairs={{0,128},{8,136},{16,144},{24,152},{32,160},{40,168},{48,176},{56,1... | collective-permute-start | bytes 983048 | tf_op jit(solution)/shard_map/ppermute | solution.py:51
  85.9 14.8 %collective-permute-start.22 = (bf16[8,32,640]{2,1,0:T(8,128)(2,1)S(1)}, bf16[8,32,640]{2,1,0:T(8,128)(2,1)S(1)}, u32[]{:S(2)}, u32[]{:S(2)}) collective-permute-start(bf16[8,32,640]{2,1,0:T(8,128)(2,1)S(1)} %constant_dynamic-update-slice_fusion.refs_0_), channel_id=1, source_target_pairs={{0,64},{8,72},{16,80},{24,88},{32,96},{40,104},{48,112},{56,120},{... | collective-permute-start | bytes 983048 | tf_op jit(solution)/shard_map/ppermute | solution.py:51
  (2 other events, 2.6 us)

commit v8 on v6

--- a/solution.py
+++ b/solution.py
@@ -20,7 +20,7 @@
 X_STEPS = (2, 4, 6)
 Z_SUM_STEPS = (1, 3, 7)
 Z_PAIRS = (2, 5, 6)
-Z_ORDER = tuple(pair ^ bit for pair in (0,) + Z_PAIRS for bit in (0, 1))
+Y_ORDER, Z_ORDER = (0,) + Y_STEPS, (0,) + Z_PAIRS
 ROW_BLOCKS = 4
 
 
@@ -49,6 +49,16 @@
 
 def exchange(value, axis, distance):
     return lax.ppermute(value, axis, [(i, i ^ distance) for i in range(lax.axis_size(axis))])
+
+
+def exchange_by_core(value, first_distance, second_distance):
+    cores = lax.axis_size("shard")
+    pairs = []
+    for i in range(lax.axis_size("rep")):
+        for j in range(cores):
+            other = i ^ (second_distance if j % 2 else first_distance)
+            pairs.append((i * cores + j, other * cores + j))
+    return lax.ppermute(value, ("rep", "shard"), pairs)
 
 
 def sum_four(terms):
@@ -262,46 +272,52 @@
     if begins:
         new_far, weights_far, new_near, sems = rest
     else:
-        new_far, weights_far, right_far, new_near, right_near, sems = rest
+        new_far, weights_far, right_far, new_near, right_near, rights, sems = rest
     columns = grad_ref.shape[1]
     groups, own_rows, width = blocks[0].shape
-    size = groups * own_rows
     rank = (width - columns) // 2
-    own_y, own_z = lax.axis_index("rep") // Z_SIZE, lax.axis_index("rep") % Z_SIZE
+    own = lax.axis_index("rep")
+    core = lax.axis_index("shard") % 2
     copies = []
 
     def send(source, target):
         copies.append(pltpu.make_async_copy(source, target, sems.at[len(copies)]))
         copies[-1].start()
 
-    def piece_of(z):
-        step = own_z ^ z
-        return step ^ ((step >> 2) & (1 - ((step >> 1) & 1)))
-
-    def rights_of(block):
-        return jnp.concatenate([block[piece_of(z), :, columns:] for z in range(groups)], axis=0)
-
-    def rows_of(d):
-        return pl.ds(pl.multiple_of((own_y ^ d) * size, size), size)
+    def replica(d, k):
+        first, second = Y_ORDER[d] ^ Z_ORDER[k], Y_ORDER[k] ^ Z_ORDER[d]
+        return own ^ (first + core * (second - first))
+
+    def rows_of(d, j):
+        at = (replica(d, j // 2) ^ (j % 2)) * own_rows
+        return pl.ds(pl.multiple_of(at, own_rows), own_rows)
 
     for d in ds:
         for j in range(groups):
-            at = (own_y ^ d) * size + (own_z ^ Z_ORDER[j]) * own_rows
-            target = weights_far.at[pl.ds(pl.multiple_of(at, own_rows), own_rows)]
-            send(blocks[d].at[j, :, pl.ds(0, columns)], target)
+            send(blocks[d].at[j, :, pl.ds(0, columns)], weights_far.at[rows_of(d, j)])
     if not begins:
+        for d, block in enumerate(blocks):
+            for j in range(groups):
+                rights[rows_of(d, j), :] = block[j, :, columns:]
         row = lax.broadcasted_iota(jnp.int32, (rank, 2 * rank), 0)
         column = lax.broadcasted_iota(jnp.int32, (rank, 2 * rank), 1)
         both = jnp.where((row == column) | (row + rank == column), 1.0, 0.0).astype(BF16)
-        for d, block in enumerate(blocks):
-            right_near[:, rows_of(d)] = native(both, rights_of(block), 1, 1)
+        right_near[...] = native(both, rights[...], 1, 1)
         send(right_near, right_far)
     for i, d in enumerate(ds):
-        right = rights_of(blocks[d])
+        right = blocks[d][:, :, columns:].reshape(groups * own_rows, width - columns)
         approx = native(jnp.concatenate([right] * 3, axis=1), parts_ref[...], 1, 0)
-        merged = grad_ref[rows_of(d), :].astype(F32) + feed_ref[rows_of(d), :].astype(F32)
-        new_near[i] = (merged - approx).astype(BF16)
-        send(new_near.at[i], new_far.at[rows_of(d)])
+        for k in range(groups // 2):
+            for j in (2 * k, 2 * k + 1):
+                rows = rows_of(d, j)
+                merged = grad_ref[rows, :].astype(F32) + feed_ref[rows, :].astype(F32)
+                piece = (merged - approx[j * own_rows : (j + 1) * own_rows]).astype(BF16)
+                place = k * 2 * own_rows + ((replica(d, k) ^ j) % 2) * own_rows
+                new_near[i, pl.ds(pl.multiple_of(place, own_rows), own_rows), :] = piece
+            near = pl.ds(k * 2 * own_rows, 2 * own_rows)
+            at = (replica(d, k) // 2) * (2 * own_rows)
+            far = pl.ds(pl.multiple_of(at, 2 * own_rows), 2 * own_rows)
+            send(new_near.at[i, near], new_far.at[far])
     for copy in copies:
         copy.wait()
 
@@ -317,7 +333,7 @@
     if not begins:
         outs = outs + [jax.ShapeDtypeStruct((rank, rows), F32)]
         out_specs = out_specs + [far]
-        scratch = scratch + [pltpu.VMEM((rank, rows), F32)]
+        scratch = scratch + [pltpu.VMEM((rank, rows), F32), pltpu.VMEM((rows, 2 * rank), BF16)]
     return call(
         lambda *refs: finish_kernel(begins, ds, *refs),
         outs,
@@ -327,7 +343,7 @@
         aliases={} if begins else {Y_SIZE + 3: 0, Y_SIZE + 4: 1},
         out_specs=out_specs,
         spare=begun,
-        scratch=scratch + [pltpu.SemaphoreType.DMA((len(ds) * (groups + 1) + 1,))],
+        scratch=scratch + [pltpu.SemaphoreType.DMA((len(ds) * (groups + groups // 2) + 1,))],
     )
 
 
@@ -358,8 +374,10 @@
         replicas, own_sum, inverse, unit_t, master, moment, second
     )
     pair = jnp.stack([send, exchange(send, "rep", 1)])
-    column = jnp.concatenate([pair] + [exchange(pair, "rep", d) for d in Z_PAIRS])
-    others = [exchange(column, "rep", d) for d in Y_STEPS]
+    column = jnp.concatenate(
+        [pair] + [exchange_by_core(pair, z, y) for y, z in zip(Y_STEPS, Z_PAIRS)]
+    )
+    others = [exchange_by_core(column, y, z) for y, z in zip(Y_STEPS, Z_PAIRS)]
     begun = finish(True, (0,), [column], unit_parts, gradient, feedback)
     blocks = [column] + others
     new_feedback, weights, right_t = finish(

time: 101 us -> 103 us (1.020)
  waiting for transfers between devices: 43.9 us -> 46.1 us
    ppermute x0 -> x6, waiting for transfers between devices: none -> 15.8 us  [exchange_by_core(): return lax.ppermute(value, ('rep', 'shard'), pairs)]
    ppermute x24 -> x18, waiting for transfers between devices: 41.4 us -> 27.8 us  [exchange(): lax.ppermute(value, axis, [(i, i ^ distance) for i in range(lax.axis_size...]
    ppermute x24 -> x18, starting transfers between devices: 34.8 us -> 25.5 us  [exchange(): lax.ppermute(value, axis, [(i, i ^ distance) for i in range(lax.axis_size...]
    ppermute x0 -> x6, starting transfers between devices: none -> 9.29 us  [exchange_by_core(): return lax.ppermute(value, ('rep', 'shard'), pairs)]
  transfers between devices with their start and end apart: 25 -> 25, of which waited for: 18 -> 19; matrix products, arithmetic and copies ran while one was open for 2% -> 2% of each run, Pallas kernels for 5% -> 5%
where the time goes in v8:
time: 103 us
  waiting for transfers between devices  46.1 us (45%)
  starting transfers between devices  44.5 us (43%)
  Pallas kernels  9.26 us (9%)
  local copies, waits for them, and re-layouts  1.96 us (2%)
    ppermute x18, waiting for transfers between devices, exchange(): lax.ppermute(value, axis, [(i, i ^ distance) for i in range(lax.axis_size...  27.8 us
    ppermute x18, starting transfers between devices, exchange(): lax.ppermute(value, axis, [(i, i ^ distance) for i in range(lax.axis_size...  25.5 us
    ppermute x6, waiting for transfers between devices, exchange_by_core(): return lax.ppermute(value, ('rep', 'shard'), pairs)  15.8 us
    all_to_all x1, starting transfers between devices, on_device(): received = lax.all_to_all(packed, 'rep', 0, 0, tiled=True)  9.69 us
    ppermute x6, starting transfers between devices, exchange_by_core(): return lax.ppermute(value, ('rep', 'shard'), pairs)  9.29 us
    pallas_call x6, Pallas kernels, call(): pl.pallas_call(kernel, out_shape=outs, in_specs=specs, out_specs=out_spec...  7.31 us
    all_to_all x1, waiting for transfers between devices, on_device(): received = lax.all_to_all(packed, 'rep', 0, 0, tiled=True)  2.46 us
  transfers between devices with their start and end apart: 25, of which 19 were waited for; matrix products, arithmetic and copies ran while one was open for 2% of the time, Pallas kernels for 5%

profile of v8, /device:TPU:32, one launch (start us, length us, event | category | flops | bytes accessed | tf_op | source)
XLA Modules:
  0.0 102.8 jit_solution(2343309302968199505)
XLA Ops:
  0.6 1.9 %local_factor.1 = (f32[64,128]{1,0:T(8,128)S(1)}, f32[64,128]{1,0:T(8,128)S(1)}, f32[64,128]{1,0:T(8,128)S(1)}, f32[64,128]{1,0:T(8,128)S(1)}, bf16[1024,512]{1,...) custom-call(f32[64,1024]{1,0:T(8,128)} %bitcast.14, bf16[1024,512]{1,0:T(8,128)(2,1)} %bitcast.12, bf16[1024,512]{1,0:T(8,128)(2,1)} %bitcast.13), custom_call_target="tpu_custom_call" | custom-call | flops 1000000000 | bytes 2500000 | tf_op jit(solution)/shard_map/local_factor/pallas_call | solution.py:125
  4.3 2.9 %collective-permute-start.1 = (f32[64,128]{1,0:T(8,128)S(1)}, f32[64,128]{1,0:T(8,128)S(1)}, u32[]{:S(2)}, u32[]{:S(2)}) collective-permute-start(f32[64,128]{1,0:T(8,128)S(1)} %get-tuple-element.35), channel_id=1, source_target_pairs={{0,128},{8,136},{16,144},{24,152},{32,160},{40,168},{48,176},{56,1... | collective-permute-start | bytes 98312 | tf_op jit(solution)/shard_map/ppermute | solution.py:51
  7.4 2.3 %collective-permute-done.1 = f32[64,128]{1,0:T(8,128)S(1)} collective-permute-done((f32[64,128]{1,0:T(8,128)S(1)}, f32[64,128]{1,0:T(8,128)S(1)}, u32[]{:S(2)}, u32[]{:S(2)}) %collective-permute-start.1) | collective-permute-done | bytes 32800 | tf_op jit(solution)/shard_map/ppermute | solution.py:51
  9.7 2.6 %collective-permute-done.2 = f32[64,128]{1,0:T(8,128)S(1)} collective-permute-done((f32[64,128]{1,0:T(8,128)S(1)}, f32[64,128]{1,0:T(8,128)S(1)}, u32[]{:S(2)}, u32[]{:S(2)}) %collective-permute-start.2) | collective-permute-done | bytes 32800 | tf_op jit(solution)/shard_map/ppermute | solution.py:51
  12.5 3.8 %collective-permute-done.3 = f32[64,128]{1,0:T(8,128)S(1)} collective-permute-done((f32[64,128]{1,0:T(8,128)S(1)}, f32[64,128]{1,0:T(8,128)S(1)}, u32[]{:S(2)}, u32[]{:S(2)}) %collective-permute-start.3) | collective-permute-done | bytes 32800 | tf_op jit(solution)/shard_map/ppermute | solution.py:51
  16.3 2.2 %collective-permute-start.4 = (f32[64,128]{1,0:T(8,128)S(1)}, f32[64,128]{1,0:T(8,128)S(1)}, u32[]{:S(2)}, u32[]{:S(2)}) collective-permute-start(f32[64,128]{1,0:T(8,128)S(1)} %add.45), channel_id=1, source_target_pairs={{0,24},{8,16},{16,8},{24,0},{32,56},{40,48},{48,40},{56,32},{64,88... | collective-permute-start | bytes 98312 | tf_op jit(solution)/shard_map/ppermute | solution.py:51
  18.5 1.9 %collective-permute-done.4 = f32[64,128]{1,0:T(8,128)S(1)} collective-permute-done((f32[64,128]{1,0:T(8,128)S(1)}, f32[64,128]{1,0:T(8,128)S(1)}, u32[]{:S(2)}, u32[]{:S(2)}) %collective-permute-start.4) | collective-permute-done | bytes 32800 | tf_op jit(solution)/shard_map/ppermute | solution.py:51
  20.4 5.7 %collective-permute-start.5 = (f32[64,128]{1,0:T(8,128)S(1)}, f32[64,128]{1,0:T(8,128)S(1)}, u32[]{:S(2)}, u32[]{:S(2)}) collective-permute-start(f32[64,128]{1,0:T(8,128)S(1)} %add.46), channel_id=1, source_target_pairs={{0,56},{8,48},{16,40},{24,32},{32,24},{40,16},{48,8},{56,0},{64,12... | collective-permute-start | bytes 98312 | tf_op jit(solution)/shard_map/ppermute | solution.py:51
  26.1 1.9 %collective-permute-done.5 = f32[64,128]{1,0:T(8,128)S(1)} collective-permute-done((f32[64,128]{1,0:T(8,128)S(1)}, f32[64,128]{1,0:T(8,128)S(1)}, u32[]{:S(2)}, u32[]{:S(2)}) %collective-permute-start.5) | collective-permute-done | bytes 32800 | tf_op jit(solution)/shard_map/ppermute | solution.py:51
  29.0 3.1 %collective-permute-start.6 = (f32[64,128]{1,0:T(8,128)S(1)}, f32[64,128]{1,0:T(8,128)S(1)}, u32[]{:S(2)}, u32[]{:S(2)}) collective-permute-start(f32[64,128]{1,0:T(8,128)S(1)} %add_multiply_fusion.refs_0_), channel_id=1, source_target_pairs={{0,64},{8,72},{16,80},{24,88},{32,96},{40,104},{48,112},{56,120},{... | collective-permute-start | bytes 98312 | tf_op jit(solution)/shard_map/ppermute | solution.py:51
  36.3 9.7 %all-to-all-start = ((f32[32,16,128]{2,1,0:T(8,128)}), f32[32,16,128]{2,1,0:T(8,128)S(1)}, u32[]{:S(2)}, u32[]{:S(2)}) async-start(f32[32,16,128]{2,1,0:T(8,128)} %project.1), calls=%async_computation | async-start | bytes 524288 | tf_op jit(solution)/shard_map/all_to_all | solution.py:365
  46.0 2.8 %collective-permute-start.12 = (f32[64,64]{1,0:T(8,128)S(1)}, f32[64,64]{1,0:T(8,128)S(1)}, u32[]{:S(2)}, u32[]{:S(2)}) collective-permute-start(f32[64,64]{1,0:T(8,128)S(1)} %add.48), channel_id=1, source_target_pairs={{0,6},{1,7},{2,4},{3,5},{4,2},{5,3},{6,0},{7,1},{8,14},{9,15},{10,... | collective-permute-start | bytes 49160 | tf_op jit(solution)/shard_map/ppermute | solution.py:51
  51.2 3.1 %collective-permute-done.11 = f32[64,64]{1,0:T(8,128)S(1)} collective-permute-done((f32[64,64]{1,0:T(8,128)S(1)}, f32[64,64]{1,0:T(8,128)S(1)}, u32[]{:S(2)}, u32[]{:S(2)}) %collective-permute-start.11) | collective-permute-done | bytes 16416 | tf_op jit(solution)/shard_map/ppermute | solution.py:51
  54.3 2.2 %invert.1 = (f32[64,64]{1,0:T(8,128)S(1)}, f32[64,512]{1,0:T(8,128)S(1)}, bf16[384,512]{1,0:T(8,128)(2,1)S(1)}) custom-call(f32[64,64]{1,0:T(8,128)S(1)} %add_add_fusion.gram_ref, f32[64,512]{1,0:T(8,128)S(1)} %get-tuple-element.43.factor_ref), custom_call_target="tpu_custom_call" | custom-call | flops 2000000000 | bytes 500000 | tf_op jit(solution)/shard_map/invert/pallas_call | solution.py:77
  56.4 2.5 %all-to-all-done = f32[32,16,128]{2,1,0:T(8,128)S(1)} async-done(((f32[32,16,128]{2,1,0:T(8,128)}), f32[32,16,128]{2,1,0:T(8,128)S(1)}, u32[]{:S(2)}, u32[]{:S(2)}) %all-to-all-start) | async-done | bytes 262176 | tf_op jit(solution)/shard_map/all_to_all | solution.py:365
  60.2 2.8 %collective-permute-start.16 = (f32[16,128]{1,0:T(8,128)S(1)}, f32[16,128]{1,0:T(8,128)S(1)}, u32[]{:S(2)}, u32[]{:S(2)}) collective-permute-start(f32[16,128]{1,0:T(8,128)S(1)} %add.52), channel_id=1, source_target_pairs={{0,6},{1,7},{2,4},{3,5},{4,2},{5,3},{6,0},{7,1},{8,14},{9,15},{10,... | collective-permute-start | bytes 24584 | tf_op jit(solution)/shard_map/ppermute | solution.py:51
  65.1 3.1 %collective-permute-done.15 = f32[16,128]{1,0:T(8,128)S(1)} collective-permute-done((f32[16,128]{1,0:T(8,128)S(1)}, f32[16,128]{1,0:T(8,128)S(1)}, u32[]{:S(2)}, u32[]{:S(2)}) %collective-permute-start.15) | collective-permute-done | bytes 8224 | tf_op jit(solution)/shard_map/ppermute | solution.py:51
  68.8 4.0 %collective-permute-done.17 = bf16[32,640]{1,0:T(8,128)(2,1)S(1)} collective-permute-done((bf16[32,640]{1,0:T(8,128)(2,1)S(1)}, bf16[32,640]{1,0:T(8,128)(2,1)S(1)}, u32[]{:S(2)}, u32[]{:S(2)}) %collective-permute-start.17) | collective-permute-done | bytes 40992 | tf_op jit(solution)/shard_map/ppermute | solution.py:51
  73.0 4.3 %collective-permute-start.19 = (bf16[2,32,640]{2,1,0:T(8,128)(2,1)S(1)}, bf16[2,32,640]{2,1,0:T(8,128)(2,1)S(1)}, u32[]{:S(2)}, u32[]{:S(2)}) collective-permute-start(bf16[2,32,640]{2,1,0:T(8,128)(2,1)S(1)} %pad_maximum_fusion), channel_id=1, source_target_pairs={{0,40},{1,129},{2,42},{3,131},{4,44},{5,133},{6,46},{7,135},{8,32}... | collective-permute-start | bytes 245768 | tf_op jit(solution)/shard_map/ppermute | solution.py:61
  77.9 5.5 %collective-permute-done.18 = bf16[2,32,640]{2,1,0:T(8,128)(2,1)S(1)} collective-permute-done((bf16[2,32,640]{2,1,0:T(8,128)(2,1)S(1)}, bf16[2,32,640]{2,1,0:T(8,128)(2,1)S(1)}, u32[]{:S(2)}, u32[]{:S(2)}) %collective-permute-start.18) | collective-permute-done | bytes 81952 | tf_op jit(solution)/shard_map/ppermute | solution.py:61
  83.5 4.7 %collective-permute-done.19 = bf16[2,32,640]{2,1,0:T(8,128)(2,1)S(1)} collective-permute-done((bf16[2,32,640]{2,1,0:T(8,128)(2,1)S(1)}, bf16[2,32,640]{2,1,0:T(8,128)(2,1)S(1)}, u32[]{:S(2)}, u32[]{:S(2)}) %collective-permute-start.19) | collective-permute-done | bytes 81952 | tf_op jit(solution)/shard_map/ppermute | solution.py:61
  88.4 4.0 %collective-permute-start.21 = (bf16[8,32,640]{2,1,0:T(8,128)(2,1)S(1)}, bf16[8,32,640]{2,1,0:T(8,128)(2,1)S(1)}, u32[]{:S(2)}, u32[]{:S(2)}) collective-permute-start(bf16[8,32,640]{2,1,0:T(8,128)(2,1)S(1)} %constant_dynamic-update-slice_fusion.refs_0_), channel_id=1, source_target_pairs={{0,64},{1,17},{2,66},{3,19},{4,68},{5,21},{6,70},{7,23},{8,72},{9,... | collective-permute-start | bytes 983048 | tf_op jit(solution)/shard_map/ppermute | solution.py:61
  95.4 4.7 %collective-permute-done.23.refs_3_ = bf16[8,32,640]{2,1,0:T(8,128)(2,1)S(1)} collective-permute-done((bf16[8,32,640]{2,1,0:T(8,128)(2,1)S(1)}, bf16[8,32,640]{2,1,0:T(8,128)(2,1)S(1)}, u32[]{:S(2)}, u32[]{:S(2)}) %collective-permute-start.23) | collective-permute-done | bytes 327712 | tf_op jit(solution)/shard_map/ppermute | solution.py:61
  101.0 1.7 %finish_rest.1 = (bf16[1024,512]{1,0:T(8,128)(2,1)}, bf16[1024,512]{1,0:T(8,128)(2,1)}, f32[64,1024]{1,0:T(8,128)}) custom-call(bf16[8,32,640]{2,1,0:T(8,128)(2,1)S(1)} %constant_dynamic-update-slice_fusion.refs_0_, bf16[8,32,640]{2,1,0:T(8,128)(2,1)S(1)} %collective-permute-done.21.refs_1_, ...), custom_call_target="tpu_custom_call", output_to_operand_aliasing={{0}: (7, {}), {1}: (8, {})} | custom-call | flops 900000000 | bytes 4500000 | tf_op jit(solution)/shard_map/finish_rest/pallas_call | solution.py:77
  (57 shorter events, 18.6 us)
Async XLA Ops:
  2.6 4.8 %collective-permute-start = (f32[64,128]{1,0:T(8,128)S(1)}, f32[64,128]{1,0:T(8,128)S(1)}, u32[]{:S(2)}, u32[]{:S(2)}) collective-permute-start(f32[64,128]{1,0:T(8,128)S(1)} %get-tuple-element.34), channel_id=1, source_target_pairs={{0,64},{8,72},{16,80},{24,88},{32,96},{40,104},{48,112},{56,120},{... | collective-permute-start | bytes 98312 | tf_op jit(solution)/shard_map/ppermute | solution.py:51
  4.3 5.4 %collective-permute-start.1 = (f32[64,128]{1,0:T(8,128)S(1)}, f32[64,128]{1,0:T(8,128)S(1)}, u32[]{:S(2)}, u32[]{:S(2)}) collective-permute-start(f32[64,128]{1,0:T(8,128)S(1)} %get-tuple-element.35), channel_id=1, source_target_pairs={{0,128},{8,136},{16,144},{24,152},{32,160},{40,168},{48,176},{56,1... | collective-permute-start | bytes 98312 | tf_op jit(solution)/shard_map/ppermute | solution.py:51
  7.2 5.1 %collective-permute-start.2 = (f32[64,128]{1,0:T(8,128)S(1)}, f32[64,128]{1,0:T(8,128)S(1)}, u32[]{:S(2)}, u32[]{:S(2)}) collective-permute-start(f32[64,128]{1,0:T(8,128)S(1)} %get-tuple-element.36), channel_id=1, source_target_pairs={{0,192},{8,200},{16,208},{24,216},{32,224},{40,232},{48,240},{56,2... | collective-permute-start | bytes 98312 | tf_op jit(solution)/shard_map/ppermute | solution.py:51
  12.3 4.0 %collective-permute-start.3 = (f32[64,128]{1,0:T(8,128)S(1)}, f32[64,128]{1,0:T(8,128)S(1)}, u32[]{:S(2)}, u32[]{:S(2)}) collective-permute-start(f32[64,128]{1,0:T(8,128)S(1)} %add_add_fusion.1), channel_id=1, source_target_pairs={{0,8},{8,0},{16,24},{24,16},{32,40},{40,32},{48,56},{56,48},{64,72... | collective-permute-start | bytes 98312 | tf_op jit(solution)/shard_map/ppermute | solution.py:51
  16.3 4.1 %collective-permute-start.4 = (f32[64,128]{1,0:T(8,128)S(1)}, f32[64,128]{1,0:T(8,128)S(1)}, u32[]{:S(2)}, u32[]{:S(2)}) collective-permute-start(f32[64,128]{1,0:T(8,128)S(1)} %add.45), channel_id=1, source_target_pairs={{0,24},{8,16},{16,8},{24,0},{32,56},{40,48},{48,40},{56,32},{64,88... | collective-permute-start | bytes 98312 | tf_op jit(solution)/shard_map/ppermute | solution.py:51
  20.4 7.6 %collective-permute-start.5 = (f32[64,128]{1,0:T(8,128)S(1)}, f32[64,128]{1,0:T(8,128)S(1)}, u32[]{:S(2)}, u32[]{:S(2)}) collective-permute-start(f32[64,128]{1,0:T(8,128)S(1)} %add.46), channel_id=1, source_target_pairs={{0,56},{8,48},{16,40},{24,32},{32,24},{40,16},{48,8},{56,0},{64,12... | collective-permute-start | bytes 98312 | tf_op jit(solution)/shard_map/ppermute | solution.py:51
  28.0 5.1 %collective-permute-start.8 = (f32[64,128]{1,0:T(8,128)S(1)}, f32[64,128]{1,0:T(8,128)S(1)}, u32[]{:S(2)}, u32[]{:S(2)}) collective-permute-start(f32[64,128]{1,0:T(8,128)S(1)} %add_multiply_fusion.refs_0_), channel_id=1, source_target_pairs={{0,192},{8,200},{16,208},{24,216},{32,224},{40,232},{48,240},{56,2... | collective-permute-start | bytes 98312 | tf_op jit(solution)/shard_map/ppermute | solution.py:51
  28.2 5.4 %collective-permute-start.7 = (f32[64,128]{1,0:T(8,128)S(1)}, f32[64,128]{1,0:T(8,128)S(1)}, u32[]{:S(2)}, u32[]{:S(2)}) collective-permute-start(f32[64,128]{1,0:T(8,128)S(1)} %add_multiply_fusion.refs_0_), channel_id=1, source_target_pairs={{0,128},{8,136},{16,144},{24,152},{32,160},{40,168},{48,176},{56,1... | collective-permute-start | bytes 98312 | tf_op jit(solution)/shard_map/ppermute | solution.py:51
  29.0 5.3 %collective-permute-start.6 = (f32[64,128]{1,0:T(8,128)S(1)}, f32[64,128]{1,0:T(8,128)S(1)}, u32[]{:S(2)}, u32[]{:S(2)}) collective-permute-start(f32[64,128]{1,0:T(8,128)S(1)} %add_multiply_fusion.refs_0_), channel_id=1, source_target_pairs={{0,64},{8,72},{16,80},{24,88},{32,96},{40,104},{48,112},{56,120},{... | collective-permute-start | bytes 98312 | tf_op jit(solution)/shard_map/ppermute | solution.py:51
  34.6 1.7 %collective-permute-start.9 = (f32[64,64]{1,0:T(8,128)S(1)}, f32[64,64]{1,0:T(8,128)S(1)}, u32[]{:S(2)}, u32[]{:S(2)}) collective-permute-start(f32[64,64]{1,0:T(8,128)S(1)} %get-tuple-element.37), channel_id=1, source_target_pairs={{0,1},{1,0},{2,3},{3,2},{4,5},{5,4},{6,7},{7,6},{8,9},{9,8},{10,11... | collective-permute-start | bytes 49160 | tf_op jit(solution)/shard_map/ppermute | solution.py:51
  36.3 22.6 %all-to-all-start = ((f32[32,16,128]{2,1,0:T(8,128)}), f32[32,16,128]{2,1,0:T(8,128)S(1)}, u32[]{:S(2)}, u32[]{:S(2)}) async-start(f32[32,16,128]{2,1,0:T(8,128)} %project.1), calls=%async_computation | async-start | bytes 524288 | tf_op jit(solution)/shard_map/all_to_all | solution.py:365
  46.0 5.2 %collective-permute-start.12 = (f32[64,64]{1,0:T(8,128)S(1)}, f32[64,64]{1,0:T(8,128)S(1)}, u32[]{:S(2)}, u32[]{:S(2)}) collective-permute-start(f32[64,64]{1,0:T(8,128)S(1)} %add.48), channel_id=1, source_target_pairs={{0,6},{1,7},{2,4},{3,5},{4,2},{5,3},{6,0},{7,1},{8,14},{9,15},{10,... | collective-permute-start | bytes 49160 | tf_op jit(solution)/shard_map/ppermute | solution.py:51
  48.8 5.4 %collective-permute-start.11 = (f32[64,64]{1,0:T(8,128)S(1)}, f32[64,64]{1,0:T(8,128)S(1)}, u32[]{:S(2)}, u32[]{:S(2)}) collective-permute-start(f32[64,64]{1,0:T(8,128)S(1)} %add.48), channel_id=1, source_target_pairs={{0,4},{1,5},{2,6},{3,7},{4,0},{5,1},{6,2},{7,3},{8,12},{9,13},{10,... | collective-permute-start | bytes 49160 | tf_op jit(solution)/shard_map/ppermute | solution.py:51
  49.6 4.6 %collective-permute-start.10 = (f32[64,64]{1,0:T(8,128)S(1)}, f32[64,64]{1,0:T(8,128)S(1)}, u32[]{:S(2)}, u32[]{:S(2)}) collective-permute-start(f32[64,64]{1,0:T(8,128)S(1)} %add.48), channel_id=1, source_target_pairs={{0,2},{1,3},{2,0},{3,1},{4,6},{5,7},{6,4},{7,5},{8,10},{9,11},{10,... | collective-permute-start | bytes 49160 | tf_op jit(solution)/shard_map/ppermute | solution.py:51
  60.2 4.9 %collective-permute-start.16 = (f32[16,128]{1,0:T(8,128)S(1)}, f32[16,128]{1,0:T(8,128)S(1)}, u32[]{:S(2)}, u32[]{:S(2)}) collective-permute-start(f32[16,128]{1,0:T(8,128)S(1)} %add.52), channel_id=1, source_target_pairs={{0,6},{1,7},{2,4},{3,5},{4,2},{5,3},{6,0},{7,1},{8,14},{9,15},{10,... | collective-permute-start | bytes 24584 | tf_op jit(solution)/shard_map/ppermute | solution.py:51
  63.0 5.2 %collective-permute-start.15 = (f32[16,128]{1,0:T(8,128)S(1)}, f32[16,128]{1,0:T(8,128)S(1)}, u32[]{:S(2)}, u32[]{:S(2)}) collective-permute-start(f32[16,128]{1,0:T(8,128)S(1)} %add.52), channel_id=1, source_target_pairs={{0,4},{1,5},{2,6},{3,7},{4,0},{5,1},{6,2},{7,3},{8,12},{9,13},{10,... | collective-permute-start | bytes 24584 | tf_op jit(solution)/shard_map/ppermute | solution.py:51
  63.8 4.4 %collective-permute-start.14 = (f32[16,128]{1,0:T(8,128)S(1)}, f32[16,128]{1,0:T(8,128)S(1)}, u32[]{:S(2)}, u32[]{:S(2)}) collective-permute-start(f32[16,128]{1,0:T(8,128)S(1)} %add.52), channel_id=1, source_target_pairs={{0,2},{1,3},{2,0},{3,1},{4,6},{5,7},{6,4},{7,5},{8,10},{9,11},{10,... | collective-permute-start | bytes 24584 | tf_op jit(solution)/shard_map/ppermute | solution.py:51
  68.7 4.1 %collective-permute-start.17 = (bf16[32,640]{1,0:T(8,128)(2,1)S(1)}, bf16[32,640]{1,0:T(8,128)(2,1)S(1)}, u32[]{:S(2)}, u32[]{:S(2)}) collective-permute-start(bf16[32,640]{1,0:T(8,128)(2,1)S(1)} %get-tuple-element.50), channel_id=1, source_target_pairs={{0,8},{8,0},{16,24},{24,16},{32,40},{40,32},{48,56},{56,48},{64,72... | collective-permute-start | bytes 122888 | tf_op jit(solution)/shard_map/ppermute | solution.py:51
  72.8 15.4 %collective-permute-start.20 = (bf16[2,32,640]{2,1,0:T(8,128)(2,1)S(1)}, bf16[2,32,640]{2,1,0:T(8,128)(2,1)S(1)}, u32[]{:S(2)}, u32[]{:S(2)}) collective-permute-start(bf16[2,32,640]{2,1,0:T(8,128)(2,1)S(1)} %pad_maximum_fusion), channel_id=1, source_target_pairs={{0,48},{1,193},{2,50},{3,195},{4,52},{5,197},{6,54},{7,199},{8,56}... | collective-permute-start | bytes 245768 | tf_op jit(solution)/shard_map/ppermute | solution.py:61
  73.0 15.2 %collective-permute-start.19 = (bf16[2,32,640]{2,1,0:T(8,128)(2,1)S(1)}, bf16[2,32,640]{2,1,0:T(8,128)(2,1)S(1)}, u32[]{:S(2)}, u32[]{:S(2)}) collective-permute-start(bf16[2,32,640]{2,1,0:T(8,128)(2,1)S(1)} %pad_maximum_fusion), channel_id=1, source_target_pairs={{0,40},{1,129},{2,42},{3,131},{4,44},{5,133},{6,46},{7,135},{8,32}... | collective-permute-start | bytes 245768 | tf_op jit(solution)/shard_map/ppermute | solution.py:61
  77.3 6.2 %collective-permute-start.18 = (bf16[2,32,640]{2,1,0:T(8,128)(2,1)S(1)}, bf16[2,32,640]{2,1,0:T(8,128)(2,1)S(1)}, u32[]{:S(2)}, u32[]{:S(2)}) collective-permute-start(bf16[2,32,640]{2,1,0:T(8,128)(2,1)S(1)} %pad_maximum_fusion), channel_id=1, source_target_pairs={{0,16},{1,65},{2,18},{3,67},{4,20},{5,69},{6,22},{7,71},{8,24},{9,... | collective-permute-start | bytes 245768 | tf_op jit(solution)/shard_map/ppermute | solution.py:61
  88.2 11.9 %collective-permute-start.23 = (bf16[8,32,640]{2,1,0:T(8,128)(2,1)S(1)}, bf16[8,32,640]{2,1,0:T(8,128)(2,1)S(1)}, u32[]{:S(2)}, u32[]{:S(2)}) collective-permute-start(bf16[8,32,640]{2,1,0:T(8,128)(2,1)S(1)} %constant_dynamic-update-slice_fusion.refs_0_), channel_id=1, source_target_pairs={{0,192},{1,49},{2,194},{3,51},{4,196},{5,53},{6,198},{7,55},{8,200... | collective-permute-start | bytes 983048 | tf_op jit(solution)/shard_map/ppermute | solution.py:61
  88.3 11.8 %collective-permute-start.22 = (bf16[8,32,640]{2,1,0:T(8,128)(2,1)S(1)}, bf16[8,32,640]{2,1,0:T(8,128)(2,1)S(1)}, u32[]{:S(2)}, u32[]{:S(2)}) collective-permute-start(bf16[8,32,640]{2,1,0:T(8,128)(2,1)S(1)} %constant_dynamic-update-slice_fusion.refs_0_), channel_id=1, source_target_pairs={{0,128},{1,41},{2,130},{3,43},{4,132},{5,45},{6,134},{7,47},{8,136... | collective-permute-start | bytes 983048 | tf_op jit(solution)/shard_map/ppermute | solution.py:61
  88.4 12.5 %collective-permute-start.21 = (bf16[8,32,640]{2,1,0:T(8,128)(2,1)S(1)}, bf16[8,32,640]{2,1,0:T(8,128)(2,1)S(1)}, u32[]{:S(2)}, u32[]{:S(2)}) collective-permute-start(bf16[8,32,640]{2,1,0:T(8,128)(2,1)S(1)} %constant_dynamic-update-slice_fusion.refs_0_), channel_id=1, source_target_pairs={{0,64},{1,17},{2,66},{3,19},{4,68},{5,21},{6,70},{7,23},{8,72},{9,... | collective-permute-start | bytes 983048 | tf_op jit(solution)/shard_map/ppermute | solution.py:61
  (4 other events, 29.0 us)

commit v9 on v6

--- a/solution.py
+++ b/solution.py
@@ -21,6 +21,7 @@
 Z_SUM_STEPS = (1, 3, 7)
 Z_PAIRS = (2, 5, 6)
 Z_ORDER = tuple(pair ^ bit for pair in (0,) + Z_PAIRS for bit in (0, 1))
+LAST_STEPS = (0, 1, 3, 2)
 ROW_BLOCKS = 4
 
 
@@ -282,11 +283,11 @@
         return jnp.concatenate([block[piece_of(z), :, columns:] for z in range(groups)], axis=0)
 
     def rows_of(d):
-        return pl.ds(pl.multiple_of((own_y ^ d) * size, size), size)
+        return pl.ds(pl.multiple_of((own_y ^ LAST_STEPS[d]) * size, size), size)
 
     for d in ds:
         for j in range(groups):
-            at = (own_y ^ d) * size + (own_z ^ Z_ORDER[j]) * own_rows
+            at = (own_y ^ LAST_STEPS[d]) * size + (own_z ^ Z_ORDER[j]) * own_rows
             target = weights_far.at[pl.ds(pl.multiple_of(at, own_rows), own_rows)]
             send(blocks[d].at[j, :, pl.ds(0, columns)], target)
     if not begins:
@@ -359,7 +360,7 @@
     )
     pair = jnp.stack([send, exchange(send, "rep", 1)])
     column = jnp.concatenate([pair] + [exchange(pair, "rep", d) for d in Z_PAIRS])
-    others = [exchange(column, "rep", d) for d in Y_STEPS]
+    others = [exchange(column, "rep", Z_SIZE * d) for d in LAST_STEPS[1:]]
     begun = finish(True, (0,), [column], unit_parts, gradient, feedback)
     blocks = [column] + others
     new_feedback, weights, right_t = finish(

time: 101 us -> 101 us (level)
  no operation moved by 1% of the time
where the time goes in v9:
time: 101 us; the launch traced here: 100 us
  waiting for transfers between devices  44 us (44%)
  starting transfers between devices  43.9 us (43%)
  Pallas kernels  9.41 us (9%)
  local copies, waits for them, and re-layouts  1.96 us (2%)
    ppermute x24, waiting for transfers between devices, exchange(): lax.ppermute(value, axis, [(i, i ^ distance) for i in range(lax.axis_size...  41.5 us
    ppermute x24, starting transfers between devices, exchange(): lax.ppermute(value, axis, [(i, i ^ distance) for i in range(lax.axis_size...  34.2 us
    all_to_all x1, starting transfers between devices, on_device(): received = lax.all_to_all(packed, 'rep', 0, 0, tiled=True)  9.69 us
    pallas_call x6, Pallas kernels, call(): pl.pallas_call(kernel, out_shape=outs, in_specs=specs, out_specs=out_spec...  7.47 us
    all_to_all x1, waiting for transfers between devices, on_device(): received = lax.all_to_all(packed, 'rep', 0, 0, tiled=True)  2.46 us
  transfers between devices with their start and end apart: 25, of which 18 were waited for; matrix products, arithmetic and copies ran while one was open for 2% of the time, Pallas kernels for 5%

profile of v9, /device:TPU:32, one launch (start us, length us, event | category | flops | bytes accessed | tf_op | source)
XLA Modules:
  0.0 100.3 jit_solution(14748878424379866851)
XLA Ops:
  0.6 1.9 %local_factor.1 = (f32[64,128]{1,0:T(8,128)S(1)}, f32[64,128]{1,0:T(8,128)S(1)}, f32[64,128]{1,0:T(8,128)S(1)}, f32[64,128]{1,0:T(8,128)S(1)}, bf16[1024,512]{1,...) custom-call(f32[64,1024]{1,0:T(8,128)} %bitcast.14, bf16[1024,512]{1,0:T(8,128)(2,1)} %bitcast.12, bf16[1024,512]{1,0:T(8,128)(2,1)} %bitcast.13), custom_call_target="tpu_custom_call" | custom-call | flops 1000000000 | bytes 2500000 | tf_op jit(solution)/shard_map/local_factor/pallas_call | solution.py:116
  4.3 2.9 %collective-permute-start.1 = (f32[64,128]{1,0:T(8,128)S(1)}, f32[64,128]{1,0:T(8,128)S(1)}, u32[]{:S(2)}, u32[]{:S(2)}) collective-permute-start(f32[64,128]{1,0:T(8,128)S(1)} %get-tuple-element.35), channel_id=1, source_target_pairs={{0,128},{8,136},{16,144},{24,152},{32,160},{40,168},{48,176},{56,1... | collective-permute-start | bytes 98312 | tf_op jit(solution)/shard_map/ppermute | solution.py:52
  7.4 2.3 %collective-permute-done.1 = f32[64,128]{1,0:T(8,128)S(1)} collective-permute-done((f32[64,128]{1,0:T(8,128)S(1)}, f32[64,128]{1,0:T(8,128)S(1)}, u32[]{:S(2)}, u32[]{:S(2)}) %collective-permute-start.1) | collective-permute-done | bytes 32800 | tf_op jit(solution)/shard_map/ppermute | solution.py:52
  9.7 2.6 %collective-permute-done.2 = f32[64,128]{1,0:T(8,128)S(1)} collective-permute-done((f32[64,128]{1,0:T(8,128)S(1)}, f32[64,128]{1,0:T(8,128)S(1)}, u32[]{:S(2)}, u32[]{:S(2)}) %collective-permute-start.2) | collective-permute-done | bytes 32800 | tf_op jit(solution)/shard_map/ppermute | solution.py:52
  12.5 3.8 %collective-permute-done.3 = f32[64,128]{1,0:T(8,128)S(1)} collective-permute-done((f32[64,128]{1,0:T(8,128)S(1)}, f32[64,128]{1,0:T(8,128)S(1)}, u32[]{:S(2)}, u32[]{:S(2)}) %collective-permute-start.3) | collective-permute-done | bytes 32800 | tf_op jit(solution)/shard_map/ppermute | solution.py:52
  16.3 2.2 %collective-permute-start.4 = (f32[64,128]{1,0:T(8,128)S(1)}, f32[64,128]{1,0:T(8,128)S(1)}, u32[]{:S(2)}, u32[]{:S(2)}) collective-permute-start(f32[64,128]{1,0:T(8,128)S(1)} %add.45), channel_id=1, source_target_pairs={{0,24},{8,16},{16,8},{24,0},{32,56},{40,48},{48,40},{56,32},{64,88... | collective-permute-start | bytes 98312 | tf_op jit(solution)/shard_map/ppermute | solution.py:52
  18.5 1.9 %collective-permute-done.4 = f32[64,128]{1,0:T(8,128)S(1)} collective-permute-done((f32[64,128]{1,0:T(8,128)S(1)}, f32[64,128]{1,0:T(8,128)S(1)}, u32[]{:S(2)}, u32[]{:S(2)}) %collective-permute-start.4) | collective-permute-done | bytes 32800 | tf_op jit(solution)/shard_map/ppermute | solution.py:52
  20.4 5.7 %collective-permute-start.5 = (f32[64,128]{1,0:T(8,128)S(1)}, f32[64,128]{1,0:T(8,128)S(1)}, u32[]{:S(2)}, u32[]{:S(2)}) collective-permute-start(f32[64,128]{1,0:T(8,128)S(1)} %add.46), channel_id=1, source_target_pairs={{0,56},{8,48},{16,40},{24,32},{32,24},{40,16},{48,8},{56,0},{64,12... | collective-permute-start | bytes 98312 | tf_op jit(solution)/shard_map/ppermute | solution.py:52
  26.1 1.9 %collective-permute-done.5 = f32[64,128]{1,0:T(8,128)S(1)} collective-permute-done((f32[64,128]{1,0:T(8,128)S(1)}, f32[64,128]{1,0:T(8,128)S(1)}, u32[]{:S(2)}, u32[]{:S(2)}) %collective-permute-start.5) | collective-permute-done | bytes 32800 | tf_op jit(solution)/shard_map/ppermute | solution.py:52
  29.0 3.1 %collective-permute-start.6 = (f32[64,128]{1,0:T(8,128)S(1)}, f32[64,128]{1,0:T(8,128)S(1)}, u32[]{:S(2)}, u32[]{:S(2)}) collective-permute-start(f32[64,128]{1,0:T(8,128)S(1)} %add_multiply_fusion.refs_0_), channel_id=1, source_target_pairs={{0,64},{8,72},{16,80},{24,88},{32,96},{40,104},{48,112},{56,120},{... | collective-permute-start | bytes 98312 | tf_op jit(solution)/shard_map/ppermute | solution.py:52
  36.3 9.7 %all-to-all-start = ((f32[32,16,128]{2,1,0:T(8,128)}), f32[32,16,128]{2,1,0:T(8,128)S(1)}, u32[]{:S(2)}, u32[]{:S(2)}) async-start(f32[32,16,128]{2,1,0:T(8,128)} %project.1), calls=%async_computation | async-start | bytes 524288 | tf_op jit(solution)/shard_map/all_to_all | solution.py:350
  46.0 2.8 %collective-permute-start.12 = (f32[64,64]{1,0:T(8,128)S(1)}, f32[64,64]{1,0:T(8,128)S(1)}, u32[]{:S(2)}, u32[]{:S(2)}) collective-permute-start(f32[64,64]{1,0:T(8,128)S(1)} %add.48), channel_id=1, source_target_pairs={{0,6},{1,7},{2,4},{3,5},{4,2},{5,3},{6,0},{7,1},{8,14},{9,15},{10,... | collective-permute-start | bytes 49160 | tf_op jit(solution)/shard_map/ppermute | solution.py:52
  51.2 3.1 %collective-permute-done.11 = f32[64,64]{1,0:T(8,128)S(1)} collective-permute-done((f32[64,64]{1,0:T(8,128)S(1)}, f32[64,64]{1,0:T(8,128)S(1)}, u32[]{:S(2)}, u32[]{:S(2)}) %collective-permute-start.11) | collective-permute-done | bytes 16416 | tf_op jit(solution)/shard_map/ppermute | solution.py:52
  54.3 2.2 %invert.1 = (f32[64,64]{1,0:T(8,128)S(1)}, f32[64,512]{1,0:T(8,128)S(1)}, bf16[384,512]{1,0:T(8,128)(2,1)S(1)}) custom-call(f32[64,64]{1,0:T(8,128)S(1)} %add_add_fusion.gram_ref, f32[64,512]{1,0:T(8,128)S(1)} %get-tuple-element.43.factor_ref), custom_call_target="tpu_custom_call" | custom-call | flops 2000000000 | bytes 500000 | tf_op jit(solution)/shard_map/invert/pallas_call | solution.py:68
  56.4 2.5 %all-to-all-done = f32[32,16,128]{2,1,0:T(8,128)S(1)} async-done(((f32[32,16,128]{2,1,0:T(8,128)}), f32[32,16,128]{2,1,0:T(8,128)S(1)}, u32[]{:S(2)}, u32[]{:S(2)}) %all-to-all-start) | async-done | bytes 262176 | tf_op jit(solution)/shard_map/all_to_all | solution.py:350
  60.2 2.8 %collective-permute-start.16 = (f32[16,128]{1,0:T(8,128)S(1)}, f32[16,128]{1,0:T(8,128)S(1)}, u32[]{:S(2)}, u32[]{:S(2)}) collective-permute-start(f32[16,128]{1,0:T(8,128)S(1)} %add.52), channel_id=1, source_target_pairs={{0,6},{1,7},{2,4},{3,5},{4,2},{5,3},{6,0},{7,1},{8,14},{9,15},{10,... | collective-permute-start | bytes 24584 | tf_op jit(solution)/shard_map/ppermute | solution.py:52
  65.1 3.1 %collective-permute-done.15 = f32[16,128]{1,0:T(8,128)S(1)} collective-permute-done((f32[16,128]{1,0:T(8,128)S(1)}, f32[16,128]{1,0:T(8,128)S(1)}, u32[]{:S(2)}, u32[]{:S(2)}) %collective-permute-start.15) | collective-permute-done | bytes 8224 | tf_op jit(solution)/shard_map/ppermute | solution.py:52
  68.8 4.0 %collective-permute-done.17 = bf16[32,640]{1,0:T(8,128)(2,1)S(1)} collective-permute-done((bf16[32,640]{1,0:T(8,128)(2,1)S(1)}, bf16[32,640]{1,0:T(8,128)(2,1)S(1)}, u32[]{:S(2)}, u32[]{:S(2)}) %collective-permute-start.17) | collective-permute-done | bytes 40992 | tf_op jit(solution)/shard_map/ppermute | solution.py:52
  73.0 4.3 %collective-permute-start.19 = (bf16[2,32,640]{2,1,0:T(8,128)(2,1)S(1)}, bf16[2,32,640]{2,1,0:T(8,128)(2,1)S(1)}, u32[]{:S(2)}, u32[]{:S(2)}) collective-permute-start(bf16[2,32,640]{2,1,0:T(8,128)(2,1)S(1)} %pad_maximum_fusion), channel_id=1, source_target_pairs={{0,40},{8,32},{16,56},{24,48},{32,8},{40,0},{48,24},{56,16},{64,10... | collective-permute-start | bytes 245768 | tf_op jit(solution)/shard_map/ppermute | solution.py:52
  77.9 5.5 %collective-permute-done.18 = bf16[2,32,640]{2,1,0:T(8,128)(2,1)S(1)} collective-permute-done((bf16[2,32,640]{2,1,0:T(8,128)(2,1)S(1)}, bf16[2,32,640]{2,1,0:T(8,128)(2,1)S(1)}, u32[]{:S(2)}, u32[]{:S(2)}) %collective-permute-start.18) | collective-permute-done | bytes 81952 | tf_op jit(solution)/shard_map/ppermute | solution.py:52
  84.2 2.5 %collective-permute-start.22 = (bf16[8,32,640]{2,1,0:T(8,128)(2,1)S(1)}, bf16[8,32,640]{2,1,0:T(8,128)(2,1)S(1)}, u32[]{:S(2)}, u32[]{:S(2)}) collective-permute-start(bf16[8,32,640]{2,1,0:T(8,128)(2,1)S(1)} %constant_dynamic-update-slice_fusion.refs_0_), channel_id=1, source_target_pairs={{0,192},{8,200},{16,208},{24,216},{32,224},{40,232},{48,240},{56,2... | collective-permute-start | bytes 983048 | tf_op jit(solution)/shard_map/ppermute | solution.py:52
  90.0 5.0 %collective-permute-done.23.refs_3_ = bf16[8,32,640]{2,1,0:T(8,128)(2,1)S(1)} collective-permute-done((bf16[8,32,640]{2,1,0:T(8,128)(2,1)S(1)}, bf16[8,32,640]{2,1,0:T(8,128)(2,1)S(1)}, u32[]{:S(2)}, u32[]{:S(2)}) %collective-permute-start.23) | collective-permute-done | bytes 327712 | tf_op jit(solution)/shard_map/ppermute | solution.py:52
  95.1 3.2 %collective-permute-done.22.refs_2_ = bf16[8,32,640]{2,1,0:T(8,128)(2,1)S(1)} collective-permute-done((bf16[8,32,640]{2,1,0:T(8,128)(2,1)S(1)}, bf16[8,32,640]{2,1,0:T(8,128)(2,1)S(1)}, u32[]{:S(2)}, u32[]{:S(2)}) %collective-permute-start.22) | collective-permute-done | bytes 327712 | tf_op jit(solution)/shard_map/ppermute | solution.py:52
  98.3 1.9 %finish_rest.1 = (bf16[1024,512]{1,0:T(8,128)(2,1)}, bf16[1024,512]{1,0:T(8,128)(2,1)}, f32[64,1024]{1,0:T(8,128)}) custom-call(bf16[8,32,640]{2,1,0:T(8,128)(2,1)S(1)} %constant_dynamic-update-slice_fusion.refs_0_, bf16[8,32,640]{2,1,0:T(8,128)(2,1)S(1)} %collective-permute-done.21.refs_1_, ...), custom_call_target="tpu_custom_call", output_to_operand_aliasing={{0}: (7, {}), {1}: (8, {})} | custom-call | flops 900000000 | bytes 4500000 | tf_op jit(solution)/shard_map/finish_rest/pallas_call | solution.py:68
  (57 shorter events, 18.7 us)
Async XLA Ops:
  2.6 4.8 %collective-permute-start = (f32[64,128]{1,0:T(8,128)S(1)}, f32[64,128]{1,0:T(8,128)S(1)}, u32[]{:S(2)}, u32[]{:S(2)}) collective-permute-start(f32[64,128]{1,0:T(8,128)S(1)} %get-tuple-element.34), channel_id=1, source_target_pairs={{0,64},{8,72},{16,80},{24,88},{32,96},{40,104},{48,112},{56,120},{... | collective-permute-start | bytes 98312 | tf_op jit(solution)/shard_map/ppermute | solution.py:52
  4.3 5.4 %collective-permute-start.1 = (f32[64,128]{1,0:T(8,128)S(1)}, f32[64,128]{1,0:T(8,128)S(1)}, u32[]{:S(2)}, u32[]{:S(2)}) collective-permute-start(f32[64,128]{1,0:T(8,128)S(1)} %get-tuple-element.35), channel_id=1, source_target_pairs={{0,128},{8,136},{16,144},{24,152},{32,160},{40,168},{48,176},{56,1... | collective-permute-start | bytes 98312 | tf_op jit(solution)/shard_map/ppermute | solution.py:52
  7.2 5.1 %collective-permute-start.2 = (f32[64,128]{1,0:T(8,128)S(1)}, f32[64,128]{1,0:T(8,128)S(1)}, u32[]{:S(2)}, u32[]{:S(2)}) collective-permute-start(f32[64,128]{1,0:T(8,128)S(1)} %get-tuple-element.36), channel_id=1, source_target_pairs={{0,192},{8,200},{16,208},{24,216},{32,224},{40,232},{48,240},{56,2... | collective-permute-start | bytes 98312 | tf_op jit(solution)/shard_map/ppermute | solution.py:52
  12.3 4.0 %collective-permute-start.3 = (f32[64,128]{1,0:T(8,128)S(1)}, f32[64,128]{1,0:T(8,128)S(1)}, u32[]{:S(2)}, u32[]{:S(2)}) collective-permute-start(f32[64,128]{1,0:T(8,128)S(1)} %add_add_fusion.1), channel_id=1, source_target_pairs={{0,8},{8,0},{16,24},{24,16},{32,40},{40,32},{48,56},{56,48},{64,72... | collective-permute-start | bytes 98312 | tf_op jit(solution)/shard_map/ppermute | solution.py:52
  16.3 4.1 %collective-permute-start.4 = (f32[64,128]{1,0:T(8,128)S(1)}, f32[64,128]{1,0:T(8,128)S(1)}, u32[]{:S(2)}, u32[]{:S(2)}) collective-permute-start(f32[64,128]{1,0:T(8,128)S(1)} %add.45), channel_id=1, source_target_pairs={{0,24},{8,16},{16,8},{24,0},{32,56},{40,48},{48,40},{56,32},{64,88... | collective-permute-start | bytes 98312 | tf_op jit(solution)/shard_map/ppermute | solution.py:52
  20.4 7.6 %collective-permute-start.5 = (f32[64,128]{1,0:T(8,128)S(1)}, f32[64,128]{1,0:T(8,128)S(1)}, u32[]{:S(2)}, u32[]{:S(2)}) collective-permute-start(f32[64,128]{1,0:T(8,128)S(1)} %add.46), channel_id=1, source_target_pairs={{0,56},{8,48},{16,40},{24,32},{32,24},{40,16},{48,8},{56,0},{64,12... | collective-permute-start | bytes 98312 | tf_op jit(solution)/shard_map/ppermute | solution.py:52
  28.0 5.1 %collective-permute-start.8 = (f32[64,128]{1,0:T(8,128)S(1)}, f32[64,128]{1,0:T(8,128)S(1)}, u32[]{:S(2)}, u32[]{:S(2)}) collective-permute-start(f32[64,128]{1,0:T(8,128)S(1)} %add_multiply_fusion.refs_0_), channel_id=1, source_target_pairs={{0,192},{8,200},{16,208},{24,216},{32,224},{40,232},{48,240},{56,2... | collective-permute-start | bytes 98312 | tf_op jit(solution)/shard_map/ppermute | solution.py:52
  28.2 5.4 %collective-permute-start.7 = (f32[64,128]{1,0:T(8,128)S(1)}, f32[64,128]{1,0:T(8,128)S(1)}, u32[]{:S(2)}, u32[]{:S(2)}) collective-permute-start(f32[64,128]{1,0:T(8,128)S(1)} %add_multiply_fusion.refs_0_), channel_id=1, source_target_pairs={{0,128},{8,136},{16,144},{24,152},{32,160},{40,168},{48,176},{56,1... | collective-permute-start | bytes 98312 | tf_op jit(solution)/shard_map/ppermute | solution.py:52
  29.0 5.3 %collective-permute-start.6 = (f32[64,128]{1,0:T(8,128)S(1)}, f32[64,128]{1,0:T(8,128)S(1)}, u32[]{:S(2)}, u32[]{:S(2)}) collective-permute-start(f32[64,128]{1,0:T(8,128)S(1)} %add_multiply_fusion.refs_0_), channel_id=1, source_target_pairs={{0,64},{8,72},{16,80},{24,88},{32,96},{40,104},{48,112},{56,120},{... | collective-permute-start | bytes 98312 | tf_op jit(solution)/shard_map/ppermute | solution.py:52
  34.6 1.7 %collective-permute-start.9 = (f32[64,64]{1,0:T(8,128)S(1)}, f32[64,64]{1,0:T(8,128)S(1)}, u32[]{:S(2)}, u32[]{:S(2)}) collective-permute-start(f32[64,64]{1,0:T(8,128)S(1)} %get-tuple-element.37), channel_id=1, source_target_pairs={{0,1},{1,0},{2,3},{3,2},{4,5},{5,4},{6,7},{7,6},{8,9},{9,8},{10,11... | collective-permute-start | bytes 49160 | tf_op jit(solution)/shard_map/ppermute | solution.py:52
  36.3 22.6 %all-to-all-start = ((f32[32,16,128]{2,1,0:T(8,128)}), f32[32,16,128]{2,1,0:T(8,128)S(1)}, u32[]{:S(2)}, u32[]{:S(2)}) async-start(f32[32,16,128]{2,1,0:T(8,128)} %project.1), calls=%async_computation | async-start | bytes 524288 | tf_op jit(solution)/shard_map/all_to_all | solution.py:350
  46.0 5.2 %collective-permute-start.12 = (f32[64,64]{1,0:T(8,128)S(1)}, f32[64,64]{1,0:T(8,128)S(1)}, u32[]{:S(2)}, u32[]{:S(2)}) collective-permute-start(f32[64,64]{1,0:T(8,128)S(1)} %add.48), channel_id=1, source_target_pairs={{0,6},{1,7},{2,4},{3,5},{4,2},{5,3},{6,0},{7,1},{8,14},{9,15},{10,... | collective-permute-start | bytes 49160 | tf_op jit(solution)/shard_map/ppermute | solution.py:52
  48.8 5.4 %collective-permute-start.11 = (f32[64,64]{1,0:T(8,128)S(1)}, f32[64,64]{1,0:T(8,128)S(1)}, u32[]{:S(2)}, u32[]{:S(2)}) collective-permute-start(f32[64,64]{1,0:T(8,128)S(1)} %add.48), channel_id=1, source_target_pairs={{0,4},{1,5},{2,6},{3,7},{4,0},{5,1},{6,2},{7,3},{8,12},{9,13},{10,... | collective-permute-start | bytes 49160 | tf_op jit(solution)/shard_map/ppermute | solution.py:52
  49.6 4.6 %collective-permute-start.10 = (f32[64,64]{1,0:T(8,128)S(1)}, f32[64,64]{1,0:T(8,128)S(1)}, u32[]{:S(2)}, u32[]{:S(2)}) collective-permute-start(f32[64,64]{1,0:T(8,128)S(1)} %add.48), channel_id=1, source_target_pairs={{0,2},{1,3},{2,0},{3,1},{4,6},{5,7},{6,4},{7,5},{8,10},{9,11},{10,... | collective-permute-start | bytes 49160 | tf_op jit(solution)/shard_map/ppermute | solution.py:52
  60.2 4.9 %collective-permute-start.16 = (f32[16,128]{1,0:T(8,128)S(1)}, f32[16,128]{1,0:T(8,128)S(1)}, u32[]{:S(2)}, u32[]{:S(2)}) collective-permute-start(f32[16,128]{1,0:T(8,128)S(1)} %add.52), channel_id=1, source_target_pairs={{0,6},{1,7},{2,4},{3,5},{4,2},{5,3},{6,0},{7,1},{8,14},{9,15},{10,... | collective-permute-start | bytes 24584 | tf_op jit(solution)/shard_map/ppermute | solution.py:52
  63.0 5.2 %collective-permute-start.15 = (f32[16,128]{1,0:T(8,128)S(1)}, f32[16,128]{1,0:T(8,128)S(1)}, u32[]{:S(2)}, u32[]{:S(2)}) collective-permute-start(f32[16,128]{1,0:T(8,128)S(1)} %add.52), channel_id=1, source_target_pairs={{0,4},{1,5},{2,6},{3,7},{4,0},{5,1},{6,2},{7,3},{8,12},{9,13},{10,... | collective-permute-start | bytes 24584 | tf_op jit(solution)/shard_map/ppermute | solution.py:52
  63.8 4.4 %collective-permute-start.14 = (f32[16,128]{1,0:T(8,128)S(1)}, f32[16,128]{1,0:T(8,128)S(1)}, u32[]{:S(2)}, u32[]{:S(2)}) collective-permute-start(f32[16,128]{1,0:T(8,128)S(1)} %add.52), channel_id=1, source_target_pairs={{0,2},{1,3},{2,0},{3,1},{4,6},{5,7},{6,4},{7,5},{8,10},{9,11},{10,... | collective-permute-start | bytes 24584 | tf_op jit(solution)/shard_map/ppermute | solution.py:52
  68.7 4.1 %collective-permute-start.17 = (bf16[32,640]{1,0:T(8,128)(2,1)S(1)}, bf16[32,640]{1,0:T(8,128)(2,1)S(1)}, u32[]{:S(2)}, u32[]{:S(2)}) collective-permute-start(bf16[32,640]{1,0:T(8,128)(2,1)S(1)} %get-tuple-element.50), channel_id=1, source_target_pairs={{0,8},{8,0},{16,24},{24,16},{32,40},{40,32},{48,56},{56,48},{64,72... | collective-permute-start | bytes 122888 | tf_op jit(solution)/shard_map/ppermute | solution.py:52
  72.8 10.7 %collective-permute-start.20 = (bf16[2,32,640]{2,1,0:T(8,128)(2,1)S(1)}, bf16[2,32,640]{2,1,0:T(8,128)(2,1)S(1)}, u32[]{:S(2)}, u32[]{:S(2)}) collective-permute-start(bf16[2,32,640]{2,1,0:T(8,128)(2,1)S(1)} %pad_maximum_fusion), channel_id=1, source_target_pairs={{0,48},{8,56},{16,32},{24,40},{32,16},{40,24},{48,0},{56,8},{64,11... | collective-permute-start | bytes 245768 | tf_op jit(solution)/shard_map/ppermute | solution.py:52
  73.0 10.4 %collective-permute-start.19 = (bf16[2,32,640]{2,1,0:T(8,128)(2,1)S(1)}, bf16[2,32,640]{2,1,0:T(8,128)(2,1)S(1)}, u32[]{:S(2)}, u32[]{:S(2)}) collective-permute-start(bf16[2,32,640]{2,1,0:T(8,128)(2,1)S(1)} %pad_maximum_fusion), channel_id=1, source_target_pairs={{0,40},{8,32},{16,56},{24,48},{32,8},{40,0},{48,24},{56,16},{64,10... | collective-permute-start | bytes 245768 | tf_op jit(solution)/shard_map/ppermute | solution.py:52
  77.3 6.2 %collective-permute-start.18 = (bf16[2,32,640]{2,1,0:T(8,128)(2,1)S(1)}, bf16[2,32,640]{2,1,0:T(8,128)(2,1)S(1)}, u32[]{:S(2)}, u32[]{:S(2)}) collective-permute-start(bf16[2,32,640]{2,1,0:T(8,128)(2,1)S(1)} %pad_maximum_fusion), channel_id=1, source_target_pairs={{0,16},{8,24},{16,0},{24,8},{32,48},{40,56},{48,32},{56,40},{64,80... | collective-permute-start | bytes 245768 | tf_op jit(solution)/shard_map/ppermute | solution.py:52
  83.5 11.6 %collective-permute-start.23 = (bf16[8,32,640]{2,1,0:T(8,128)(2,1)S(1)}, bf16[8,32,640]{2,1,0:T(8,128)(2,1)S(1)}, u32[]{:S(2)}, u32[]{:S(2)}) collective-permute-start(bf16[8,32,640]{2,1,0:T(8,128)(2,1)S(1)} %constant_dynamic-update-slice_fusion.refs_0_), channel_id=1, source_target_pairs={{0,128},{8,136},{16,144},{24,152},{32,160},{40,168},{48,176},{56,1... | collective-permute-start | bytes 983048 | tf_op jit(solution)/shard_map/ppermute | solution.py:52
  84.2 14.1 %collective-permute-start.22 = (bf16[8,32,640]{2,1,0:T(8,128)(2,1)S(1)}, bf16[8,32,640]{2,1,0:T(8,128)(2,1)S(1)}, u32[]{:S(2)}, u32[]{:S(2)}) collective-permute-start(bf16[8,32,640]{2,1,0:T(8,128)(2,1)S(1)} %constant_dynamic-update-slice_fusion.refs_0_), channel_id=1, source_target_pairs={{0,192},{8,200},{16,208},{24,216},{32,224},{40,232},{48,240},{56,2... | collective-permute-start | bytes 983048 | tf_op jit(solution)/shard_map/ppermute | solution.py:52
  86.7 11.6 %collective-permute-start.21 = (bf16[8,32,640]{2,1,0:T(8,128)(2,1)S(1)}, bf16[8,32,640]{2,1,0:T(8,128)(2,1)S(1)}, u32[]{:S(2)}, u32[]{:S(2)}) collective-permute-start(bf16[8,32,640]{2,1,0:T(8,128)(2,1)S(1)} %constant_dynamic-update-slice_fusion.refs_0_), channel_id=1, source_target_pairs={{0,64},{8,72},{16,80},{24,88},{32,96},{40,104},{48,112},{56,120},{... | collective-permute-start | bytes 983048 | tf_op jit(solution)/shard_map/ppermute | solution.py:52
  (4 other events, 29.0 us)

commit v10 on v9

--- a/solution.py
+++ b/solution.py
@@ -256,14 +256,10 @@
     return call(kernel, outs, args, (5 * 10**7, 600_000), "update")
 
 
-def finish_kernel(begins, ds, *refs):
-    count = Y_SIZE if not begins else len(ds)
+def finish_kernel(ds, begun, *refs):
+    count = len(ds)
     blocks, (parts_ref, grad_ref, feed_ref) = refs[:count], refs[count : count + 3]
-    rest = refs[count + 3 :] if begins else refs[count + 5 :]
-    if begins:
-        new_far, weights_far, new_near, sems = rest
-    else:
-        new_far, weights_far, right_far, new_near, right_near, sems = rest
+    new_far, weights_far, right_far, new_near, right_near, sems = refs[count + 3 + begun :]
     columns = grad_ref.shape[1]
     groups, own_rows, width = blocks[0].shape
     size = groups * own_rows
@@ -279,26 +275,22 @@
         step = own_z ^ z
         return step ^ ((step >> 2) & (1 - ((step >> 1) & 1)))
 
-    def rights_of(block):
-        return jnp.concatenate([block[piece_of(z), :, columns:] for z in range(groups)], axis=0)
-
     def rows_of(d):
         return pl.ds(pl.multiple_of((own_y ^ LAST_STEPS[d]) * size, size), size)
 
-    for d in ds:
+    for i, d in enumerate(ds):
         for j in range(groups):
             at = (own_y ^ LAST_STEPS[d]) * size + (own_z ^ Z_ORDER[j]) * own_rows
             target = weights_far.at[pl.ds(pl.multiple_of(at, own_rows), own_rows)]
-            send(blocks[d].at[j, :, pl.ds(0, columns)], target)
-    if not begins:
-        row = lax.broadcasted_iota(jnp.int32, (rank, 2 * rank), 0)
-        column = lax.broadcasted_iota(jnp.int32, (rank, 2 * rank), 1)
-        both = jnp.where((row == column) | (row + rank == column), 1.0, 0.0).astype(BF16)
-        for d, block in enumerate(blocks):
-            right_near[:, rows_of(d)] = native(both, rights_of(block), 1, 1)
-        send(right_near, right_far)
+            send(blocks[i].at[j, :, pl.ds(0, columns)], target)
+    row = lax.broadcasted_iota(jnp.int32, (rank, 2 * rank), 0)
+    column = lax.broadcasted_iota(jnp.int32, (rank, 2 * rank), 1)
+    both = jnp.where((row == column) | (row + rank == column), 1.0, 0.0).astype(BF16)
     for i, d in enumerate(ds):
-        right = rights_of(blocks[d])
+        pieces = [blocks[i][piece_of(z), :, columns:] for z in range(groups)]
+        right = jnp.concatenate(pieces, axis=0)
+        right_near[i] = native(both, right, 1, 1)
+        send(right_near.at[i], right_far.at[:, rows_of(d)])
         approx = native(jnp.concatenate([right] * 3, axis=1), parts_ref[...], 1, 0)
         merged = grad_ref[rows_of(d), :].astype(F32) + feed_ref[rows_of(d), :].astype(F32)
         new_near[i] = (merged - approx).astype(BF16)
@@ -307,28 +299,27 @@
         copy.wait()
 
 
-def finish(begins, ds, blocks, parts, gradient, feedback, begun=()):
+def finish(name, ds, blocks, parts, gradient, feedback, begun=()):
     rows, columns = gradient.shape
     groups, own_rows, width = blocks[0].shape
     rank = (width - columns) // 2
-    far = pl.BlockSpec(memory_space=pl.ANY)
-    outs = [jax.ShapeDtypeStruct((rows, columns), BF16)] * 2
-    out_specs = [far, far]
-    scratch = [pltpu.VMEM((len(ds), groups * own_rows, columns), BF16)]
-    if not begins:
-        outs = outs + [jax.ShapeDtypeStruct((rank, rows), F32)]
-        out_specs = out_specs + [far]
-        scratch = scratch + [pltpu.VMEM((rank, rows), F32)]
+    size = groups * own_rows
+    count = len(ds)
     return call(
-        lambda *refs: finish_kernel(begins, ds, *refs),
-        outs,
+        lambda *refs: finish_kernel(ds, len(begun), *refs),
+        [jax.ShapeDtypeStruct((rows, columns), BF16)] * 2
+        + [jax.ShapeDtypeStruct((rank, rows), F32)],
         (*blocks, parts, gradient, feedback),
-        (len(ds) * 3 * 10**8, len(ds) * 1_500_000),
-        "finish_own" if begins else "finish_rest",
-        aliases={} if begins else {Y_SIZE + 3: 0, Y_SIZE + 4: 1},
-        out_specs=out_specs,
+        (count * 3 * 10**8, count * 1_500_000),
+        name,
+        aliases={count + 3 + i: i for i in range(len(begun))},
+        out_specs=[pl.BlockSpec(memory_space=pl.ANY)] * 3,
         spare=begun,
-        scratch=scratch + [pltpu.SemaphoreType.DMA((len(ds) * (groups + 1) + 1,))],
+        scratch=[
+            pltpu.VMEM((count, size, columns), BF16),
+            pltpu.VMEM((count, rank, size), F32),
+            pltpu.SemaphoreType.DMA((count * (groups + 2),)),
+        ],
     )
 
 
@@ -361,11 +352,10 @@
     pair = jnp.stack([send, exchange(send, "rep", 1)])
     column = jnp.concatenate([pair] + [exchange(pair, "rep", d) for d in Z_PAIRS])
     others = [exchange(column, "rep", Z_SIZE * d) for d in LAST_STEPS[1:]]
-    begun = finish(True, (0,), [column], unit_parts, gradient, feedback)
-    blocks = [column] + others
-    new_feedback, weights, right_t = finish(
-        False, (1, 2, 3), blocks, unit_parts, gradient, feedback, begun
-    )
+    rest = (unit_parts, gradient, feedback)
+    begun = finish("finish_own", (0,), [column], *rest)
+    begun = finish("finish_far", (3,), others[2:], *rest, begun)
+    new_feedback, weights, right_t = finish("finish_near", (1, 2), others[:2], *rest, begun)
     return (new_feedback[None], weights, master_out, moment_out, second_out, right_t.T)
 
 

time: 101 us -> 103 us (1.020)
  starting transfers between devices: 43.9 us -> 47 us
  waiting for transfers between devices: 44 us -> 41.2 us
    ppermute x24, starting transfers between devices: 34.2 us -> 36.6 us  [exchange(): lax.ppermute(value, axis, [(i, i ^ distance) for i in range(lax.axis_size...]
    ppermute x24, waiting for transfers between devices: 41.5 us -> 39.9 us  [exchange(): lax.ppermute(value, axis, [(i, i ^ distance) for i in range(lax.axis_size...]
    all_to_all x1, waiting for transfers between devices: 2.46 us -> 1.28 us  [on_device(): received = lax.all_to_all(packed, 'rep', 0, 0, tiled=True)]
    pallas_call x6 -> x7, Pallas kernels: 7.47 us -> 8.17 us  [call(): pl.pallas_call(kernel, out_shape=outs, in_specs=specs, out_specs=out_spec...]
  transfers between devices with their start and end apart: 25 -> 25, of which waited for: 18 -> 20; matrix products, arithmetic and copies ran while one was open for 2% -> 2% of each run, Pallas kernels for 5% -> 6%
where the time goes in v10:
time: 103 us; the launch traced here: 101 us
  starting transfers between devices  47 us (46%)
  waiting for transfers between devices  41.2 us (40%)
  Pallas kernels  10.1 us (10%)
  local copies, waits for them, and re-layouts  1.96 us (2%)
    ppermute x24, waiting for transfers between devices, exchange(): lax.ppermute(value, axis, [(i, i ^ distance) for i in range(lax.axis_size...  39.9 us
    ppermute x24, starting transfers between devices, exchange(): lax.ppermute(value, axis, [(i, i ^ distance) for i in range(lax.axis_size...  36.6 us
    all_to_all x1, starting transfers between devices, on_device(): received = lax.all_to_all(packed, 'rep', 0, 0, tiled=True)  10.4 us
    pallas_call x7, Pallas kernels, call(): pl.pallas_call(kernel, out_shape=outs, in_specs=specs, out_specs=out_spec...  8.17 us
  transfers between devices with their start and end apart: 25, of which 20 were waited for; matrix products, arithmetic and copies ran while one was open for 2% of the time, Pallas kernels for 6%

profile of v10, /device:TPU:32, one launch (start us, length us, event | category | flops | bytes accessed | tf_op | source)
XLA Modules:
  0.0 101.3 jit_solution(3731982119303273816)
XLA Ops:
  0.6 1.9 %local_factor.1 = (f32[64,128]{1,0:T(8,128)S(1)}, f32[64,128]{1,0:T(8,128)S(1)}, f32[64,128]{1,0:T(8,128)S(1)}, f32[64,128]{1,0:T(8,128)S(1)}, bf16[1024,512]{1,...) custom-call(f32[64,1024]{1,0:T(8,128)} %bitcast.15, bf16[1024,512]{1,0:T(8,128)(2,1)} %bitcast.13, bf16[1024,512]{1,0:T(8,128)(2,1)} %bitcast.14), custom_call_target="tpu_custom_call" | custom-call | flops 1000000000 | bytes 2500000 | tf_op jit(solution)/shard_map/local_factor/pallas_call | solution.py:116
  4.3 2.9 %collective-permute-start.1 = (f32[64,128]{1,0:T(8,128)S(1)}, f32[64,128]{1,0:T(8,128)S(1)}, u32[]{:S(2)}, u32[]{:S(2)}) collective-permute-start(f32[64,128]{1,0:T(8,128)S(1)} %get-tuple-element.39), channel_id=1, source_target_pairs={{0,128},{8,136},{16,144},{24,152},{32,160},{40,168},{48,176},{56,1... | collective-permute-start | bytes 98312 | tf_op jit(solution)/shard_map/ppermute | solution.py:52
  7.4 2.3 %collective-permute-done.1 = f32[64,128]{1,0:T(8,128)S(1)} collective-permute-done((f32[64,128]{1,0:T(8,128)S(1)}, f32[64,128]{1,0:T(8,128)S(1)}, u32[]{:S(2)}, u32[]{:S(2)}) %collective-permute-start.1) | collective-permute-done | bytes 32800 | tf_op jit(solution)/shard_map/ppermute | solution.py:52
  9.7 2.6 %collective-permute-done.2 = f32[64,128]{1,0:T(8,128)S(1)} collective-permute-done((f32[64,128]{1,0:T(8,128)S(1)}, f32[64,128]{1,0:T(8,128)S(1)}, u32[]{:S(2)}, u32[]{:S(2)}) %collective-permute-start.2) | collective-permute-done | bytes 32800 | tf_op jit(solution)/shard_map/ppermute | solution.py:52
  12.5 3.8 %collective-permute-done.3 = f32[64,128]{1,0:T(8,128)S(1)} collective-permute-done((f32[64,128]{1,0:T(8,128)S(1)}, f32[64,128]{1,0:T(8,128)S(1)}, u32[]{:S(2)}, u32[]{:S(2)}) %collective-permute-start.3) | collective-permute-done | bytes 32800 | tf_op jit(solution)/shard_map/ppermute | solution.py:52
  16.3 2.2 %collective-permute-start.4 = (f32[64,128]{1,0:T(8,128)S(1)}, f32[64,128]{1,0:T(8,128)S(1)}, u32[]{:S(2)}, u32[]{:S(2)}) collective-permute-start(f32[64,128]{1,0:T(8,128)S(1)} %add.45), channel_id=1, source_target_pairs={{0,24},{8,16},{16,8},{24,0},{32,56},{40,48},{48,40},{56,32},{64,88... | collective-permute-start | bytes 98312 | tf_op jit(solution)/shard_map/ppermute | solution.py:52
  18.5 1.9 %collective-permute-done.4 = f32[64,128]{1,0:T(8,128)S(1)} collective-permute-done((f32[64,128]{1,0:T(8,128)S(1)}, f32[64,128]{1,0:T(8,128)S(1)}, u32[]{:S(2)}, u32[]{:S(2)}) %collective-permute-start.4) | collective-permute-done | bytes 32800 | tf_op jit(solution)/shard_map/ppermute | solution.py:52
  20.4 5.7 %collective-permute-start.5 = (f32[64,128]{1,0:T(8,128)S(1)}, f32[64,128]{1,0:T(8,128)S(1)}, u32[]{:S(2)}, u32[]{:S(2)}) collective-permute-start(f32[64,128]{1,0:T(8,128)S(1)} %add.46), channel_id=1, source_target_pairs={{0,56},{8,48},{16,40},{24,32},{32,24},{40,16},{48,8},{56,0},{64,12... | collective-permute-start | bytes 98312 | tf_op jit(solution)/shard_map/ppermute | solution.py:52
  26.1 1.9 %collective-permute-done.5 = f32[64,128]{1,0:T(8,128)S(1)} collective-permute-done((f32[64,128]{1,0:T(8,128)S(1)}, f32[64,128]{1,0:T(8,128)S(1)}, u32[]{:S(2)}, u32[]{:S(2)}) %collective-permute-start.5) | collective-permute-done | bytes 32800 | tf_op jit(solution)/shard_map/ppermute | solution.py:52
  29.6 3.0 %collective-permute-start.8 = (f32[64,128]{1,0:T(8,128)S(1)}, f32[64,128]{1,0:T(8,128)S(1)}, u32[]{:S(2)}, u32[]{:S(2)}) collective-permute-start(f32[64,128]{1,0:T(8,128)S(1)} %add_multiply_fusion.refs_0_), channel_id=1, source_target_pairs={{0,192},{8,200},{16,208},{24,216},{32,224},{40,232},{48,240},{56,2... | collective-permute-start | bytes 98312 | tf_op jit(solution)/shard_map/ppermute | solution.py:52
  36.8 10.4 %all-to-all-start = ((f32[32,16,128]{2,1,0:T(8,128)}), f32[32,16,128]{2,1,0:T(8,128)S(1)}, u32[]{:S(2)}, u32[]{:S(2)}) async-start(f32[32,16,128]{2,1,0:T(8,128)} %project.1), calls=%async_computation | async-start | bytes 524288 | tf_op jit(solution)/shard_map/all_to_all | solution.py:341
  48.7 2.7 %collective-permute-start.11 = (f32[64,64]{1,0:T(8,128)S(1)}, f32[64,64]{1,0:T(8,128)S(1)}, u32[]{:S(2)}, u32[]{:S(2)}) collective-permute-start(f32[64,64]{1,0:T(8,128)S(1)} %add.48), channel_id=1, source_target_pairs={{0,4},{1,5},{2,6},{3,7},{4,0},{5,1},{6,2},{7,3},{8,12},{9,13},{10,... | collective-permute-start | bytes 49160 | tf_op jit(solution)/shard_map/ppermute | solution.py:52
  51.9 2.2 %collective-permute-done.11 = f32[64,64]{1,0:T(8,128)S(1)} collective-permute-done((f32[64,64]{1,0:T(8,128)S(1)}, f32[64,64]{1,0:T(8,128)S(1)}, u32[]{:S(2)}, u32[]{:S(2)}) %collective-permute-start.11) | collective-permute-done | bytes 16416 | tf_op jit(solution)/shard_map/ppermute | solution.py:52
  54.1 2.4 %collective-permute-done.12 = f32[64,64]{1,0:T(8,128)S(1)} collective-permute-done((f32[64,64]{1,0:T(8,128)S(1)}, f32[64,64]{1,0:T(8,128)S(1)}, u32[]{:S(2)}, u32[]{:S(2)}) %collective-permute-start.12) | collective-permute-done | bytes 16416 | tf_op jit(solution)/shard_map/ppermute | solution.py:52
  56.6 2.2 %invert.1 = (f32[64,64]{1,0:T(8,128)S(1)}, f32[64,512]{1,0:T(8,128)S(1)}, bf16[384,512]{1,0:T(8,128)(2,1)S(1)}) custom-call(f32[64,64]{1,0:T(8,128)S(1)} %add_add_fusion.gram_ref, f32[64,512]{1,0:T(8,128)S(1)} %get-tuple-element.47.factor_ref), custom_call_target="tpu_custom_call" | custom-call | flops 2000000000 | bytes 500000 | tf_op jit(solution)/shard_map/invert/pallas_call | solution.py:68
  62.9 2.7 %collective-permute-start.15 = (f32[16,128]{1,0:T(8,128)S(1)}, f32[16,128]{1,0:T(8,128)S(1)}, u32[]{:S(2)}, u32[]{:S(2)}) collective-permute-start(f32[16,128]{1,0:T(8,128)S(1)} %add.52), channel_id=1, source_target_pairs={{0,4},{1,5},{2,6},{3,7},{4,0},{5,1},{6,2},{7,3},{8,12},{9,13},{10,... | collective-permute-start | bytes 24584 | tf_op jit(solution)/shard_map/ppermute | solution.py:52
  66.1 1.9 %collective-permute-done.15 = f32[16,128]{1,0:T(8,128)S(1)} collective-permute-done((f32[16,128]{1,0:T(8,128)S(1)}, f32[16,128]{1,0:T(8,128)S(1)}, u32[]{:S(2)}, u32[]{:S(2)}) %collective-permute-start.15) | collective-permute-done | bytes 8224 | tf_op jit(solution)/shard_map/ppermute | solution.py:52
  68.0 2.4 %collective-permute-done.16 = f32[16,128]{1,0:T(8,128)S(1)} collective-permute-done((f32[16,128]{1,0:T(8,128)S(1)}, f32[16,128]{1,0:T(8,128)S(1)}, u32[]{:S(2)}, u32[]{:S(2)}) %collective-permute-start.16) | collective-permute-done | bytes 8224 | tf_op jit(solution)/shard_map/ppermute | solution.py:52
  71.1 4.0 %collective-permute-done.17 = bf16[32,640]{1,0:T(8,128)(2,1)S(1)} collective-permute-done((bf16[32,640]{1,0:T(8,128)(2,1)S(1)}, bf16[32,640]{1,0:T(8,128)(2,1)S(1)}, u32[]{:S(2)}, u32[]{:S(2)}) %collective-permute-start.17) | collective-permute-done | bytes 40992 | tf_op jit(solution)/shard_map/ppermute | solution.py:52
  76.1 2.6 %collective-permute-start.19 = (bf16[2,32,640]{2,1,0:T(8,128)(2,1)S(1)}, bf16[2,32,640]{2,1,0:T(8,128)(2,1)S(1)}, u32[]{:S(2)}, u32[]{:S(2)}) collective-permute-start(bf16[2,32,640]{2,1,0:T(8,128)(2,1)S(1)} %pad_maximum_fusion), channel_id=1, source_target_pairs={{0,40},{8,32},{16,56},{24,48},{32,8},{40,0},{48,24},{56,16},{64,10... | collective-permute-start | bytes 245768 | tf_op jit(solution)/shard_map/ppermute | solution.py:52
  81.0 3.0 %collective-permute-done.19 = bf16[2,32,640]{2,1,0:T(8,128)(2,1)S(1)} collective-permute-done((bf16[2,32,640]{2,1,0:T(8,128)(2,1)S(1)}, bf16[2,32,640]{2,1,0:T(8,128)(2,1)S(1)}, u32[]{:S(2)}, u32[]{:S(2)}) %collective-permute-start.19) | collective-permute-done | bytes 81952 | tf_op jit(solution)/shard_map/ppermute | solution.py:52
  84.0 2.0 %collective-permute-done.20 = bf16[2,32,640]{2,1,0:T(8,128)(2,1)S(1)} collective-permute-done((bf16[2,32,640]{2,1,0:T(8,128)(2,1)S(1)}, bf16[2,32,640]{2,1,0:T(8,128)(2,1)S(1)}, u32[]{:S(2)}, u32[]{:S(2)}) %collective-permute-start.20) | collective-permute-done | bytes 81952 | tf_op jit(solution)/shard_map/ppermute | solution.py:52
  88.2 2.0 %collective-permute-start.22 = (bf16[8,32,640]{2,1,0:T(8,128)(2,1)S(1)}, bf16[8,32,640]{2,1,0:T(8,128)(2,1)S(1)}, u32[]{:S(2)}, u32[]{:S(2)}) collective-permute-start(bf16[8,32,640]{2,1,0:T(8,128)(2,1)S(1)} %constant_dynamic-update-slice_fusion.refs_0_), channel_id=1, source_target_pairs={{0,192},{8,200},{16,208},{24,216},{32,224},{40,232},{48,240},{56,2... | collective-permute-start | bytes 983048 | tf_op jit(solution)/shard_map/ppermute | solution.py:52
  93.2 3.2 %collective-permute-done.23.refs_0_ = bf16[8,32,640]{2,1,0:T(8,128)(2,1)S(1)} collective-permute-done((bf16[8,32,640]{2,1,0:T(8,128)(2,1)S(1)}, bf16[8,32,640]{2,1,0:T(8,128)(2,1)S(1)}, u32[]{:S(2)}, u32[]{:S(2)}) %collective-permute-start.23) | collective-permute-done | bytes 327712 | tf_op jit(solution)/shard_map/ppermute | solution.py:52
  (58 shorter events, 28.4 us)
Async XLA Ops:
  2.6 4.8 %collective-permute-start = (f32[64,128]{1,0:T(8,128)S(1)}, f32[64,128]{1,0:T(8,128)S(1)}, u32[]{:S(2)}, u32[]{:S(2)}) collective-permute-start(f32[64,128]{1,0:T(8,128)S(1)} %get-tuple-element.38), channel_id=1, source_target_pairs={{0,64},{8,72},{16,80},{24,88},{32,96},{40,104},{48,112},{56,120},{... | collective-permute-start | bytes 98312 | tf_op jit(solution)/shard_map/ppermute | solution.py:52
  4.3 5.4 %collective-permute-start.1 = (f32[64,128]{1,0:T(8,128)S(1)}, f32[64,128]{1,0:T(8,128)S(1)}, u32[]{:S(2)}, u32[]{:S(2)}) collective-permute-start(f32[64,128]{1,0:T(8,128)S(1)} %get-tuple-element.39), channel_id=1, source_target_pairs={{0,128},{8,136},{16,144},{24,152},{32,160},{40,168},{48,176},{56,1... | collective-permute-start | bytes 98312 | tf_op jit(solution)/shard_map/ppermute | solution.py:52
  7.2 5.1 %collective-permute-start.2 = (f32[64,128]{1,0:T(8,128)S(1)}, f32[64,128]{1,0:T(8,128)S(1)}, u32[]{:S(2)}, u32[]{:S(2)}) collective-permute-start(f32[64,128]{1,0:T(8,128)S(1)} %get-tuple-element.40), channel_id=1, source_target_pairs={{0,192},{8,200},{16,208},{24,216},{32,224},{40,232},{48,240},{56,2... | collective-permute-start | bytes 98312 | tf_op jit(solution)/shard_map/ppermute | solution.py:52
  12.3 4.0 %collective-permute-start.3 = (f32[64,128]{1,0:T(8,128)S(1)}, f32[64,128]{1,0:T(8,128)S(1)}, u32[]{:S(2)}, u32[]{:S(2)}) collective-permute-start(f32[64,128]{1,0:T(8,128)S(1)} %add_add_fusion.1), channel_id=1, source_target_pairs={{0,8},{8,0},{16,24},{24,16},{32,40},{40,32},{48,56},{56,48},{64,72... | collective-permute-start | bytes 98312 | tf_op jit(solution)/shard_map/ppermute | solution.py:52
  16.3 4.1 %collective-permute-start.4 = (f32[64,128]{1,0:T(8,128)S(1)}, f32[64,128]{1,0:T(8,128)S(1)}, u32[]{:S(2)}, u32[]{:S(2)}) collective-permute-start(f32[64,128]{1,0:T(8,128)S(1)} %add.45), channel_id=1, source_target_pairs={{0,24},{8,16},{16,8},{24,0},{32,56},{40,48},{48,40},{56,32},{64,88... | collective-permute-start | bytes 98312 | tf_op jit(solution)/shard_map/ppermute | solution.py:52
  20.4 7.6 %collective-permute-start.5 = (f32[64,128]{1,0:T(8,128)S(1)}, f32[64,128]{1,0:T(8,128)S(1)}, u32[]{:S(2)}, u32[]{:S(2)}) collective-permute-start(f32[64,128]{1,0:T(8,128)S(1)} %add.46), channel_id=1, source_target_pairs={{0,56},{8,48},{16,40},{24,32},{32,24},{40,16},{48,8},{56,0},{64,12... | collective-permute-start | bytes 98312 | tf_op jit(solution)/shard_map/ppermute | solution.py:52
  28.0 4.7 %collective-permute-start.6 = (f32[64,128]{1,0:T(8,128)S(1)}, f32[64,128]{1,0:T(8,128)S(1)}, u32[]{:S(2)}, u32[]{:S(2)}) collective-permute-start(f32[64,128]{1,0:T(8,128)S(1)} %add_multiply_fusion.refs_0_), channel_id=1, source_target_pairs={{0,64},{8,72},{16,80},{24,88},{32,96},{40,104},{48,112},{56,120},{... | collective-permute-start | bytes 98312 | tf_op jit(solution)/shard_map/ppermute | solution.py:52
  28.0 5.5 %collective-permute-start.7 = (f32[64,128]{1,0:T(8,128)S(1)}, f32[64,128]{1,0:T(8,128)S(1)}, u32[]{:S(2)}, u32[]{:S(2)}) collective-permute-start(f32[64,128]{1,0:T(8,128)S(1)} %add_multiply_fusion.refs_0_), channel_id=1, source_target_pairs={{0,128},{8,136},{16,144},{24,152},{32,160},{40,168},{48,176},{56,1... | collective-permute-start | bytes 98312 | tf_op jit(solution)/shard_map/ppermute | solution.py:52
  29.6 5.1 %collective-permute-start.8 = (f32[64,128]{1,0:T(8,128)S(1)}, f32[64,128]{1,0:T(8,128)S(1)}, u32[]{:S(2)}, u32[]{:S(2)}) collective-permute-start(f32[64,128]{1,0:T(8,128)S(1)} %add_multiply_fusion.refs_0_), channel_id=1, source_target_pairs={{0,192},{8,200},{16,208},{24,216},{32,224},{40,232},{48,240},{56,2... | collective-permute-start | bytes 98312 | tf_op jit(solution)/shard_map/ppermute | solution.py:52
  35.1 1.7 %collective-permute-start.9 = (f32[64,64]{1,0:T(8,128)S(1)}, f32[64,64]{1,0:T(8,128)S(1)}, u32[]{:S(2)}, u32[]{:S(2)}) collective-permute-start(f32[64,64]{1,0:T(8,128)S(1)} %get-tuple-element.41), channel_id=1, source_target_pairs={{0,1},{1,0},{2,3},{3,2},{4,5},{5,4},{6,7},{7,6},{8,9},{9,8},{10,11... | collective-permute-start | bytes 49160 | tf_op jit(solution)/shard_map/ppermute | solution.py:52
  36.8 23.3 %all-to-all-start = ((f32[32,16,128]{2,1,0:T(8,128)}), f32[32,16,128]{2,1,0:T(8,128)S(1)}, u32[]{:S(2)}, u32[]{:S(2)}) async-start(f32[32,16,128]{2,1,0:T(8,128)} %project.1), calls=%async_computation | async-start | bytes 524288 | tf_op jit(solution)/shard_map/all_to_all | solution.py:341
  47.1 4.8 %collective-permute-start.10 = (f32[64,64]{1,0:T(8,128)S(1)}, f32[64,64]{1,0:T(8,128)S(1)}, u32[]{:S(2)}, u32[]{:S(2)}) collective-permute-start(f32[64,64]{1,0:T(8,128)S(1)} %add.48), channel_id=1, source_target_pairs={{0,2},{1,3},{2,0},{3,1},{4,6},{5,7},{6,4},{7,5},{8,10},{9,11},{10,... | collective-permute-start | bytes 49160 | tf_op jit(solution)/shard_map/ppermute | solution.py:52
  48.7 5.4 %collective-permute-start.11 = (f32[64,64]{1,0:T(8,128)S(1)}, f32[64,64]{1,0:T(8,128)S(1)}, u32[]{:S(2)}, u32[]{:S(2)}) collective-permute-start(f32[64,64]{1,0:T(8,128)S(1)} %add.48), channel_id=1, source_target_pairs={{0,4},{1,5},{2,6},{3,7},{4,0},{5,1},{6,2},{7,3},{8,12},{9,13},{10,... | collective-permute-start | bytes 49160 | tf_op jit(solution)/shard_map/ppermute | solution.py:52
  51.4 5.1 %collective-permute-start.12 = (f32[64,64]{1,0:T(8,128)S(1)}, f32[64,64]{1,0:T(8,128)S(1)}, u32[]{:S(2)}, u32[]{:S(2)}) collective-permute-start(f32[64,64]{1,0:T(8,128)S(1)} %add.48), channel_id=1, source_target_pairs={{0,6},{1,7},{2,4},{3,5},{4,2},{5,3},{6,0},{7,1},{8,14},{9,15},{10,... | collective-permute-start | bytes 49160 | tf_op jit(solution)/shard_map/ppermute | solution.py:52
  61.4 4.7 %collective-permute-start.14 = (f32[16,128]{1,0:T(8,128)S(1)}, f32[16,128]{1,0:T(8,128)S(1)}, u32[]{:S(2)}, u32[]{:S(2)}) collective-permute-start(f32[16,128]{1,0:T(8,128)S(1)} %add.52), channel_id=1, source_target_pairs={{0,2},{1,3},{2,0},{3,1},{4,6},{5,7},{6,4},{7,5},{8,10},{9,11},{10,... | collective-permute-start | bytes 24584 | tf_op jit(solution)/shard_map/ppermute | solution.py:52
  62.9 5.2 %collective-permute-start.15 = (f32[16,128]{1,0:T(8,128)S(1)}, f32[16,128]{1,0:T(8,128)S(1)}, u32[]{:S(2)}, u32[]{:S(2)}) collective-permute-start(f32[16,128]{1,0:T(8,128)S(1)} %add.52), channel_id=1, source_target_pairs={{0,4},{1,5},{2,6},{3,7},{4,0},{5,1},{6,2},{7,3},{8,12},{9,13},{10,... | collective-permute-start | bytes 24584 | tf_op jit(solution)/shard_map/ppermute | solution.py:52
  65.6 4.9 %collective-permute-start.16 = (f32[16,128]{1,0:T(8,128)S(1)}, f32[16,128]{1,0:T(8,128)S(1)}, u32[]{:S(2)}, u32[]{:S(2)}) collective-permute-start(f32[16,128]{1,0:T(8,128)S(1)} %add.52), channel_id=1, source_target_pairs={{0,6},{1,7},{2,4},{3,5},{4,2},{5,3},{6,0},{7,1},{8,14},{9,15},{10,... | collective-permute-start | bytes 24584 | tf_op jit(solution)/shard_map/ppermute | solution.py:52
  71.0 4.1 %collective-permute-start.17 = (bf16[32,640]{1,0:T(8,128)(2,1)S(1)}, bf16[32,640]{1,0:T(8,128)(2,1)S(1)}, u32[]{:S(2)}, u32[]{:S(2)}) collective-permute-start(bf16[32,640]{1,0:T(8,128)(2,1)S(1)} %get-tuple-element.54), channel_id=1, source_target_pairs={{0,8},{8,0},{16,24},{24,16},{32,40},{40,32},{48,56},{56,48},{64,72... | collective-permute-start | bytes 122888 | tf_op jit(solution)/shard_map/ppermute | solution.py:52
  75.1 5.9 %collective-permute-start.18 = (bf16[2,32,640]{2,1,0:T(8,128)(2,1)S(1)}, bf16[2,32,640]{2,1,0:T(8,128)(2,1)S(1)}, u32[]{:S(2)}, u32[]{:S(2)}) collective-permute-start(bf16[2,32,640]{2,1,0:T(8,128)(2,1)S(1)} %pad_maximum_fusion), channel_id=1, source_target_pairs={{0,16},{8,24},{16,0},{24,8},{32,48},{40,56},{48,32},{56,40},{64,80... | collective-permute-start | bytes 245768 | tf_op jit(solution)/shard_map/ppermute | solution.py:52
  76.1 7.9 %collective-permute-start.19 = (bf16[2,32,640]{2,1,0:T(8,128)(2,1)S(1)}, bf16[2,32,640]{2,1,0:T(8,128)(2,1)S(1)}, u32[]{:S(2)}, u32[]{:S(2)}) collective-permute-start(bf16[2,32,640]{2,1,0:T(8,128)(2,1)S(1)} %pad_maximum_fusion), channel_id=1, source_target_pairs={{0,40},{8,32},{16,56},{24,48},{32,8},{40,0},{48,24},{56,16},{64,10... | collective-permute-start | bytes 245768 | tf_op jit(solution)/shard_map/ppermute | solution.py:52
  78.7 7.3 %collective-permute-start.20 = (bf16[2,32,640]{2,1,0:T(8,128)(2,1)S(1)}, bf16[2,32,640]{2,1,0:T(8,128)(2,1)S(1)}, u32[]{:S(2)}, u32[]{:S(2)}) collective-permute-start(bf16[2,32,640]{2,1,0:T(8,128)(2,1)S(1)} %pad_maximum_fusion), channel_id=1, source_target_pairs={{0,48},{8,56},{16,32},{24,40},{32,16},{40,24},{48,0},{56,8},{64,11... | collective-permute-start | bytes 245768 | tf_op jit(solution)/shard_map/ppermute | solution.py:52
  86.0 10.4 %collective-permute-start.23 = (bf16[8,32,640]{2,1,0:T(8,128)(2,1)S(1)}, bf16[8,32,640]{2,1,0:T(8,128)(2,1)S(1)}, u32[]{:S(2)}, u32[]{:S(2)}) collective-permute-start(bf16[8,32,640]{2,1,0:T(8,128)(2,1)S(1)} %constant_dynamic-update-slice_fusion.refs_0_), channel_id=1, source_target_pairs={{0,128},{8,136},{16,144},{24,152},{32,160},{40,168},{48,176},{56,1... | collective-permute-start | bytes 983048 | tf_op jit(solution)/shard_map/ppermute | solution.py:52
  87.7 11.1 %collective-permute-start.21 = (bf16[8,32,640]{2,1,0:T(8,128)(2,1)S(1)}, bf16[8,32,640]{2,1,0:T(8,128)(2,1)S(1)}, u32[]{:S(2)}, u32[]{:S(2)}) collective-permute-start(bf16[8,32,640]{2,1,0:T(8,128)(2,1)S(1)} %constant_dynamic-update-slice_fusion.refs_0_), channel_id=1, source_target_pairs={{0,64},{8,72},{16,80},{24,88},{32,96},{40,104},{48,112},{56,120},{... | collective-permute-start | bytes 983048 | tf_op jit(solution)/shard_map/ppermute | solution.py:52
  88.2 11.6 %collective-permute-start.22 = (bf16[8,32,640]{2,1,0:T(8,128)(2,1)S(1)}, bf16[8,32,640]{2,1,0:T(8,128)(2,1)S(1)}, u32[]{:S(2)}, u32[]{:S(2)}) collective-permute-start(bf16[8,32,640]{2,1,0:T(8,128)(2,1)S(1)} %constant_dynamic-update-slice_fusion.refs_0_), channel_id=1, source_target_pairs={{0,192},{8,200},{16,208},{24,216},{32,224},{40,232},{48,240},{56,2... | collective-permute-start | bytes 983048 | tf_op jit(solution)/shard_map/ppermute | solution.py:52
  (4 other events, 32.5 us)

commit v11 on v10

--- a/solution.py
+++ b/solution.py
@@ -22,6 +22,7 @@
 Z_PAIRS = (2, 5, 6)
 Z_ORDER = tuple(pair ^ bit for pair in (0,) + Z_PAIRS for bit in (0, 1))
 LAST_STEPS = (0, 1, 3, 2)
+GATHER_STEPS = (0, 3, 2, 1)
 ROW_BLOCKS = 4
 
 
@@ -58,7 +59,7 @@
 
 def shard_sum(value):
     value = value + exchange(value, "shard", 1)
-    return sum_four([value] + [exchange(value, "shard", d) for d in X_STEPS])
+    return sum_four([value] + [exchange(value, "shard", d) for d in X_STEPS[::-1]])
 
 
 def call(kernel, outs, args, cost, name, aliases=None, out_specs=None, spare=(), scratch=()):
@@ -135,7 +136,7 @@
     quarters, (factor_ref, parts_ref, gram_ref) = refs[:Y_SIZE], refs[Y_SIZE:]
     rank, quarter = quarters[0].shape
     own = lax.axis_index("rep") // Z_SIZE
-    for d, block in enumerate(quarters):
+    for d, block in zip(GATHER_STEPS, quarters):
         at = pl.ds(pl.multiple_of((own ^ d) * quarter, quarter), quarter)
         factor_ref[:, at] = block[...]
     factor = factor_ref[...]
@@ -332,14 +333,14 @@
     for distance in Z_SUM_STEPS:
         quarter = quarter + exchange(quarter, "rep", distance)
     quarter = quarter / replicas
-    quarters = [quarter] + [exchange(quarter, "rep", d) for d in Y_STEPS]
+    quarters = [quarter] + [exchange(quarter, "rep", Z_SIZE * d) for d in GATHER_STEPS[1:]]
     factor_t, parts, gram_term = assemble(quarters)
 
     gram_pair = gram_term + exchange(gram_term, "shard", 1)
     packed = project(gradient, feedback, parts, replicas)
     gram_pair, packed = lax.optimization_barrier((gram_pair, packed))
     received = lax.all_to_all(packed, "rep", 0, 0, tiled=True)
-    gram = sum_four([gram_pair] + [exchange(gram_pair, "shard", d) for d in X_STEPS])
+    gram = sum_four([gram_pair] + [exchange(gram_pair, "shard", d) for d in X_STEPS[::-1]])
     inverse, unit_t, unit_parts = invert(gram, factor_t)
     received, inverse, unit_t, unit_parts = lax.optimization_barrier(
         (received, inverse, unit_t, unit_parts)

time: 103 us -> 101 us (0.981)
  starting transfers between devices: 47 us -> 44.5 us
    ppermute x24, starting transfers between devices: 36.6 us -> 34.8 us  [exchange(): lax.ppermute(value, axis, [(i, i ^ distance) for i in range(lax.axis_size...]
    all_to_all x1, waiting for transfers between devices: 1.28 us -> 2.46 us  [on_device(): received = lax.all_to_all(packed, 'rep', 0, 0, tiled=True)]
    ppermute x24, waiting for transfers between devices: 39.9 us -> 38.9 us  [exchange(): lax.ppermute(value, axis, [(i, i ^ distance) for i in range(lax.axis_size...]
  transfers between devices with their start and end apart: 25 -> 25, of which waited for: 20 -> 21; matrix products, arithmetic and copies ran while one was open for 2% -> 2% of each run, Pallas kernels for 6% -> 6%
where the time goes in v11:
time: 101 us; the launch traced here: 99 us
  starting transfers between devices  44.5 us (44%)
  waiting for transfers between devices  41.3 us (41%)
  Pallas kernels  10.1 us (10%)
  local copies, waits for them, and re-layouts  1.96 us (2%)
    ppermute x24, waiting for transfers between devices, exchange(): lax.ppermute(value, axis, [(i, i ^ distance) for i in range(lax.axis_size...  38.9 us
    ppermute x24, starting transfers between devices, exchange(): lax.ppermute(value, axis, [(i, i ^ distance) for i in range(lax.axis_size...  34.8 us
    all_to_all x1, starting transfers between devices, on_device(): received = lax.all_to_all(packed, 'rep', 0, 0, tiled=True)  9.69 us
    pallas_call x7, Pallas kernels, call(): pl.pallas_call(kernel, out_shape=outs, in_specs=specs, out_specs=out_spec...  8.17 us
    all_to_all x1, waiting for transfers between devices, on_device(): received = lax.all_to_all(packed, 'rep', 0, 0, tiled=True)  2.46 us
  transfers between devices with their start and end apart: 25, of which 21 were waited for; matrix products, arithmetic and copies ran while one was open for 2% of the time, Pallas kernels for 6%

profile of v11, /device:TPU:32, one launch (start us, length us, event | category | flops | bytes accessed | tf_op | source)
XLA Modules:
  0.0 99.0 jit_solution(2155242834630667944)
XLA Ops:
  0.6 1.9 %local_factor.1 = (f32[64,128]{1,0:T(8,128)S(1)}, f32[64,128]{1,0:T(8,128)S(1)}, f32[64,128]{1,0:T(8,128)S(1)}, f32[64,128]{1,0:T(8,128)S(1)}, bf16[1024,512]{1,...) custom-call(f32[64,1024]{1,0:T(8,128)} %bitcast.15, bf16[1024,512]{1,0:T(8,128)(2,1)} %bitcast.13, bf16[1024,512]{1,0:T(8,128)(2,1)} %bitcast.14), custom_call_target="tpu_custom_call" | custom-call | flops 1000000000 | bytes 2500000 | tf_op jit(solution)/shard_map/local_factor/pallas_call | solution.py:117
  2.6 1.7 %collective-permute-start = (f32[64,128]{1,0:T(8,128)S(1)}, f32[64,128]{1,0:T(8,128)S(1)}, u32[]{:S(2)}, u32[]{:S(2)}) collective-permute-start(f32[64,128]{1,0:T(8,128)S(1)} %get-tuple-element.38), channel_id=1, source_target_pairs={{0,64},{8,72},{16,80},{24,88},{32,96},{40,104},{48,112},{56,120},{... | collective-permute-start | bytes 98312 | tf_op jit(solution)/shard_map/ppermute | solution.py:53
  4.3 2.9 %collective-permute-start.1 = (f32[64,128]{1,0:T(8,128)S(1)}, f32[64,128]{1,0:T(8,128)S(1)}, u32[]{:S(2)}, u32[]{:S(2)}) collective-permute-start(f32[64,128]{1,0:T(8,128)S(1)} %get-tuple-element.39), channel_id=1, source_target_pairs={{0,128},{8,136},{16,144},{24,152},{32,160},{40,168},{48,176},{56,1... | collective-permute-start | bytes 98312 | tf_op jit(solution)/shard_map/ppermute | solution.py:53
  7.4 2.3 %collective-permute-done.1 = f32[64,128]{1,0:T(8,128)S(1)} collective-permute-done((f32[64,128]{1,0:T(8,128)S(1)}, f32[64,128]{1,0:T(8,128)S(1)}, u32[]{:S(2)}, u32[]{:S(2)}) %collective-permute-start.1) | collective-permute-done | bytes 32800 | tf_op jit(solution)/shard_map/ppermute | solution.py:53
  9.7 2.6 %collective-permute-done.2 = f32[64,128]{1,0:T(8,128)S(1)} collective-permute-done((f32[64,128]{1,0:T(8,128)S(1)}, f32[64,128]{1,0:T(8,128)S(1)}, u32[]{:S(2)}, u32[]{:S(2)}) %collective-permute-start.2) | collective-permute-done | bytes 32800 | tf_op jit(solution)/shard_map/ppermute | solution.py:53
  12.5 3.8 %collective-permute-done.3 = f32[64,128]{1,0:T(8,128)S(1)} collective-permute-done((f32[64,128]{1,0:T(8,128)S(1)}, f32[64,128]{1,0:T(8,128)S(1)}, u32[]{:S(2)}, u32[]{:S(2)}) %collective-permute-start.3) | collective-permute-done | bytes 32800 | tf_op jit(solution)/shard_map/ppermute | solution.py:53
  16.3 2.2 %collective-permute-start.4 = (f32[64,128]{1,0:T(8,128)S(1)}, f32[64,128]{1,0:T(8,128)S(1)}, u32[]{:S(2)}, u32[]{:S(2)}) collective-permute-start(f32[64,128]{1,0:T(8,128)S(1)} %add.45), channel_id=1, source_target_pairs={{0,24},{8,16},{16,8},{24,0},{32,56},{40,48},{48,40},{56,32},{64,88... | collective-permute-start | bytes 98312 | tf_op jit(solution)/shard_map/ppermute | solution.py:53
  18.5 1.9 %collective-permute-done.4 = f32[64,128]{1,0:T(8,128)S(1)} collective-permute-done((f32[64,128]{1,0:T(8,128)S(1)}, f32[64,128]{1,0:T(8,128)S(1)}, u32[]{:S(2)}, u32[]{:S(2)}) %collective-permute-start.4) | collective-permute-done | bytes 32800 | tf_op jit(solution)/shard_map/ppermute | solution.py:53
  20.4 5.7 %collective-permute-start.5 = (f32[64,128]{1,0:T(8,128)S(1)}, f32[64,128]{1,0:T(8,128)S(1)}, u32[]{:S(2)}, u32[]{:S(2)}) collective-permute-start(f32[64,128]{1,0:T(8,128)S(1)} %add.46), channel_id=1, source_target_pairs={{0,56},{8,48},{16,40},{24,32},{32,24},{40,16},{48,8},{56,0},{64,12... | collective-permute-start | bytes 98312 | tf_op jit(solution)/shard_map/ppermute | solution.py:53
  26.1 1.9 %collective-permute-done.5 = f32[64,128]{1,0:T(8,128)S(1)} collective-permute-done((f32[64,128]{1,0:T(8,128)S(1)}, f32[64,128]{1,0:T(8,128)S(1)}, u32[]{:S(2)}, u32[]{:S(2)}) %collective-permute-start.5) | collective-permute-done | bytes 32800 | tf_op jit(solution)/shard_map/ppermute | solution.py:53
  29.0 3.1 %collective-permute-start.8 = (f32[64,128]{1,0:T(8,128)S(1)}, f32[64,128]{1,0:T(8,128)S(1)}, u32[]{:S(2)}, u32[]{:S(2)}) collective-permute-start(f32[64,128]{1,0:T(8,128)S(1)} %add_multiply_fusion.refs_0_), channel_id=1, source_target_pairs={{0,64},{8,72},{16,80},{24,88},{32,96},{40,104},{48,112},{56,120},{... | collective-permute-start | bytes 98312 | tf_op jit(solution)/shard_map/ppermute | solution.py:53
  36.3 9.7 %all-to-all-start = ((f32[32,16,128]{2,1,0:T(8,128)}), f32[32,16,128]{2,1,0:T(8,128)S(1)}, u32[]{:S(2)}, u32[]{:S(2)}) async-start(f32[32,16,128]{2,1,0:T(8,128)} %project.1), calls=%async_computation | async-start | bytes 524288 | tf_op jit(solution)/shard_map/all_to_all | solution.py:342
  46.0 2.8 %collective-permute-start.10 = (f32[64,64]{1,0:T(8,128)S(1)}, f32[64,64]{1,0:T(8,128)S(1)}, u32[]{:S(2)}, u32[]{:S(2)}) collective-permute-start(f32[64,64]{1,0:T(8,128)S(1)} %add.48), channel_id=1, source_target_pairs={{0,6},{1,7},{2,4},{3,5},{4,2},{5,3},{6,0},{7,1},{8,14},{9,15},{10,... | collective-permute-start | bytes 49160 | tf_op jit(solution)/shard_map/ppermute | solution.py:53
  51.2 3.1 %collective-permute-done.11 = f32[64,64]{1,0:T(8,128)S(1)} collective-permute-done((f32[64,64]{1,0:T(8,128)S(1)}, f32[64,64]{1,0:T(8,128)S(1)}, u32[]{:S(2)}, u32[]{:S(2)}) %collective-permute-start.11) | collective-permute-done | bytes 16416 | tf_op jit(solution)/shard_map/ppermute | solution.py:53
  54.3 2.2 %invert.1 = (f32[64,64]{1,0:T(8,128)S(1)}, f32[64,512]{1,0:T(8,128)S(1)}, bf16[384,512]{1,0:T(8,128)(2,1)S(1)}) custom-call(f32[64,64]{1,0:T(8,128)S(1)} %add_add_fusion.gram_ref, f32[64,512]{1,0:T(8,128)S(1)} %get-tuple-element.47.factor_ref), custom_call_target="tpu_custom_call" | custom-call | flops 2000000000 | bytes 500000 | tf_op jit(solution)/shard_map/invert/pallas_call | solution.py:69
  56.4 2.5 %all-to-all-done = f32[32,16,128]{2,1,0:T(8,128)S(1)} async-done(((f32[32,16,128]{2,1,0:T(8,128)}), f32[32,16,128]{2,1,0:T(8,128)S(1)}, u32[]{:S(2)}, u32[]{:S(2)}) %all-to-all-start) | async-done | bytes 262176 | tf_op jit(solution)/shard_map/all_to_all | solution.py:342
  60.2 2.8 %collective-permute-start.14 = (f32[16,128]{1,0:T(8,128)S(1)}, f32[16,128]{1,0:T(8,128)S(1)}, u32[]{:S(2)}, u32[]{:S(2)}) collective-permute-start(f32[16,128]{1,0:T(8,128)S(1)} %add.52), channel_id=1, source_target_pairs={{0,6},{1,7},{2,4},{3,5},{4,2},{5,3},{6,0},{7,1},{8,14},{9,15},{10,... | collective-permute-start | bytes 24584 | tf_op jit(solution)/shard_map/ppermute | solution.py:53
  65.1 3.1 %collective-permute-done.15 = f32[16,128]{1,0:T(8,128)S(1)} collective-permute-done((f32[16,128]{1,0:T(8,128)S(1)}, f32[16,128]{1,0:T(8,128)S(1)}, u32[]{:S(2)}, u32[]{:S(2)}) %collective-permute-start.15) | collective-permute-done | bytes 8224 | tf_op jit(solution)/shard_map/ppermute | solution.py:53
  68.8 4.0 %collective-permute-done.17 = bf16[32,640]{1,0:T(8,128)(2,1)S(1)} collective-permute-done((bf16[32,640]{1,0:T(8,128)(2,1)S(1)}, bf16[32,640]{1,0:T(8,128)(2,1)S(1)}, u32[]{:S(2)}, u32[]{:S(2)}) %collective-permute-start.17) | collective-permute-done | bytes 40992 | tf_op jit(solution)/shard_map/ppermute | solution.py:53
  73.7 2.3 %collective-permute-start.19 = (bf16[2,32,640]{2,1,0:T(8,128)(2,1)S(1)}, bf16[2,32,640]{2,1,0:T(8,128)(2,1)S(1)}, u32[]{:S(2)}, u32[]{:S(2)}) collective-permute-start(bf16[2,32,640]{2,1,0:T(8,128)(2,1)S(1)} %pad_maximum_fusion), channel_id=1, source_target_pairs={{0,40},{8,32},{16,56},{24,48},{32,8},{40,0},{48,24},{56,16},{64,10... | collective-permute-start | bytes 245768 | tf_op jit(solution)/shard_map/ppermute | solution.py:53
  76.0 1.9 %collective-permute-start.20 = (bf16[2,32,640]{2,1,0:T(8,128)(2,1)S(1)}, bf16[2,32,640]{2,1,0:T(8,128)(2,1)S(1)}, u32[]{:S(2)}, u32[]{:S(2)}) collective-permute-start(bf16[2,32,640]{2,1,0:T(8,128)(2,1)S(1)} %pad_maximum_fusion), channel_id=1, source_target_pairs={{0,48},{8,56},{16,32},{24,40},{32,16},{40,24},{48,0},{56,8},{64,11... | collective-permute-start | bytes 245768 | tf_op jit(solution)/shard_map/ppermute | solution.py:53
  79.0 4.5 %collective-permute-done.19 = bf16[2,32,640]{2,1,0:T(8,128)(2,1)S(1)} collective-permute-done((bf16[2,32,640]{2,1,0:T(8,128)(2,1)S(1)}, bf16[2,32,640]{2,1,0:T(8,128)(2,1)S(1)}, u32[]{:S(2)}, u32[]{:S(2)}) %collective-permute-start.19) | collective-permute-done | bytes 81952 | tf_op jit(solution)/shard_map/ppermute | solution.py:53
  85.9 2.0 %collective-permute-start.22 = (bf16[8,32,640]{2,1,0:T(8,128)(2,1)S(1)}, bf16[8,32,640]{2,1,0:T(8,128)(2,1)S(1)}, u32[]{:S(2)}, u32[]{:S(2)}) collective-permute-start(bf16[8,32,640]{2,1,0:T(8,128)(2,1)S(1)} %constant_dynamic-update-slice_fusion.refs_0_), channel_id=1, source_target_pairs={{0,192},{8,200},{16,208},{24,216},{32,224},{40,232},{48,240},{56,2... | collective-permute-start | bytes 983048 | tf_op jit(solution)/shard_map/ppermute | solution.py:53
  90.9 3.1 %collective-permute-done.23.refs_0_ = bf16[8,32,640]{2,1,0:T(8,128)(2,1)S(1)} collective-permute-done((bf16[8,32,640]{2,1,0:T(8,128)(2,1)S(1)}, bf16[8,32,640]{2,1,0:T(8,128)(2,1)S(1)}, u32[]{:S(2)}, u32[]{:S(2)}) %collective-permute-start.23) | collective-permute-done | bytes 327712 | tf_op jit(solution)/shard_map/ppermute | solution.py:53
  (58 shorter events, 24.3 us)
Async XLA Ops:
  2.6 4.8 %collective-permute-start = (f32[64,128]{1,0:T(8,128)S(1)}, f32[64,128]{1,0:T(8,128)S(1)}, u32[]{:S(2)}, u32[]{:S(2)}) collective-permute-start(f32[64,128]{1,0:T(8,128)S(1)} %get-tuple-element.38), channel_id=1, source_target_pairs={{0,64},{8,72},{16,80},{24,88},{32,96},{40,104},{48,112},{56,120},{... | collective-permute-start | bytes 98312 | tf_op jit(solution)/shard_map/ppermute | solution.py:53
  4.3 5.4 %collective-permute-start.1 = (f32[64,128]{1,0:T(8,128)S(1)}, f32[64,128]{1,0:T(8,128)S(1)}, u32[]{:S(2)}, u32[]{:S(2)}) collective-permute-start(f32[64,128]{1,0:T(8,128)S(1)} %get-tuple-element.39), channel_id=1, source_target_pairs={{0,128},{8,136},{16,144},{24,152},{32,160},{40,168},{48,176},{56,1... | collective-permute-start | bytes 98312 | tf_op jit(solution)/shard_map/ppermute | solution.py:53
  7.2 5.1 %collective-permute-start.2 = (f32[64,128]{1,0:T(8,128)S(1)}, f32[64,128]{1,0:T(8,128)S(1)}, u32[]{:S(2)}, u32[]{:S(2)}) collective-permute-start(f32[64,128]{1,0:T(8,128)S(1)} %get-tuple-element.40), channel_id=1, source_target_pairs={{0,192},{8,200},{16,208},{24,216},{32,224},{40,232},{48,240},{56,2... | collective-permute-start | bytes 98312 | tf_op jit(solution)/shard_map/ppermute | solution.py:53
  12.3 4.0 %collective-permute-start.3 = (f32[64,128]{1,0:T(8,128)S(1)}, f32[64,128]{1,0:T(8,128)S(1)}, u32[]{:S(2)}, u32[]{:S(2)}) collective-permute-start(f32[64,128]{1,0:T(8,128)S(1)} %add_add_fusion.1), channel_id=1, source_target_pairs={{0,8},{8,0},{16,24},{24,16},{32,40},{40,32},{48,56},{56,48},{64,72... | collective-permute-start | bytes 98312 | tf_op jit(solution)/shard_map/ppermute | solution.py:53
  16.3 4.1 %collective-permute-start.4 = (f32[64,128]{1,0:T(8,128)S(1)}, f32[64,128]{1,0:T(8,128)S(1)}, u32[]{:S(2)}, u32[]{:S(2)}) collective-permute-start(f32[64,128]{1,0:T(8,128)S(1)} %add.45), channel_id=1, source_target_pairs={{0,24},{8,16},{16,8},{24,0},{32,56},{40,48},{48,40},{56,32},{64,88... | collective-permute-start | bytes 98312 | tf_op jit(solution)/shard_map/ppermute | solution.py:53
  20.4 7.6 %collective-permute-start.5 = (f32[64,128]{1,0:T(8,128)S(1)}, f32[64,128]{1,0:T(8,128)S(1)}, u32[]{:S(2)}, u32[]{:S(2)}) collective-permute-start(f32[64,128]{1,0:T(8,128)S(1)} %add.46), channel_id=1, source_target_pairs={{0,56},{8,48},{16,40},{24,32},{32,24},{40,16},{48,8},{56,0},{64,12... | collective-permute-start | bytes 98312 | tf_op jit(solution)/shard_map/ppermute | solution.py:53
  28.0 5.1 %collective-permute-start.6 = (f32[64,128]{1,0:T(8,128)S(1)}, f32[64,128]{1,0:T(8,128)S(1)}, u32[]{:S(2)}, u32[]{:S(2)}) collective-permute-start(f32[64,128]{1,0:T(8,128)S(1)} %add_multiply_fusion.refs_0_), channel_id=1, source_target_pairs={{0,192},{8,200},{16,208},{24,216},{32,224},{40,232},{48,240},{56,2... | collective-permute-start | bytes 98312 | tf_op jit(solution)/shard_map/ppermute | solution.py:53
  28.2 5.4 %collective-permute-start.7 = (f32[64,128]{1,0:T(8,128)S(1)}, f32[64,128]{1,0:T(8,128)S(1)}, u32[]{:S(2)}, u32[]{:S(2)}) collective-permute-start(f32[64,128]{1,0:T(8,128)S(1)} %add_multiply_fusion.refs_0_), channel_id=1, source_target_pairs={{0,128},{8,136},{16,144},{24,152},{32,160},{40,168},{48,176},{56,1... | collective-permute-start | bytes 98312 | tf_op jit(solution)/shard_map/ppermute | solution.py:53
  29.0 5.3 %collective-permute-start.8 = (f32[64,128]{1,0:T(8,128)S(1)}, f32[64,128]{1,0:T(8,128)S(1)}, u32[]{:S(2)}, u32[]{:S(2)}) collective-permute-start(f32[64,128]{1,0:T(8,128)S(1)} %add_multiply_fusion.refs_0_), channel_id=1, source_target_pairs={{0,64},{8,72},{16,80},{24,88},{32,96},{40,104},{48,112},{56,120},{... | collective-permute-start | bytes 98312 | tf_op jit(solution)/shard_map/ppermute | solution.py:53
  34.6 1.7 %collective-permute-start.9 = (f32[64,64]{1,0:T(8,128)S(1)}, f32[64,64]{1,0:T(8,128)S(1)}, u32[]{:S(2)}, u32[]{:S(2)}) collective-permute-start(f32[64,64]{1,0:T(8,128)S(1)} %get-tuple-element.41), channel_id=1, source_target_pairs={{0,1},{1,0},{2,3},{3,2},{4,5},{5,4},{6,7},{7,6},{8,9},{9,8},{10,11... | collective-permute-start | bytes 49160 | tf_op jit(solution)/shard_map/ppermute | solution.py:53
  36.3 22.6 %all-to-all-start = ((f32[32,16,128]{2,1,0:T(8,128)}), f32[32,16,128]{2,1,0:T(8,128)S(1)}, u32[]{:S(2)}, u32[]{:S(2)}) async-start(f32[32,16,128]{2,1,0:T(8,128)} %project.1), calls=%async_computation | async-start | bytes 524288 | tf_op jit(solution)/shard_map/all_to_all | solution.py:342
  46.0 5.2 %collective-permute-start.10 = (f32[64,64]{1,0:T(8,128)S(1)}, f32[64,64]{1,0:T(8,128)S(1)}, u32[]{:S(2)}, u32[]{:S(2)}) collective-permute-start(f32[64,64]{1,0:T(8,128)S(1)} %add.48), channel_id=1, source_target_pairs={{0,6},{1,7},{2,4},{3,5},{4,2},{5,3},{6,0},{7,1},{8,14},{9,15},{10,... | collective-permute-start | bytes 49160 | tf_op jit(solution)/shard_map/ppermute | solution.py:53
  48.8 5.4 %collective-permute-start.11 = (f32[64,64]{1,0:T(8,128)S(1)}, f32[64,64]{1,0:T(8,128)S(1)}, u32[]{:S(2)}, u32[]{:S(2)}) collective-permute-start(f32[64,64]{1,0:T(8,128)S(1)} %add.48), channel_id=1, source_target_pairs={{0,4},{1,5},{2,6},{3,7},{4,0},{5,1},{6,2},{7,3},{8,12},{9,13},{10,... | collective-permute-start | bytes 49160 | tf_op jit(solution)/shard_map/ppermute | solution.py:53
  49.6 4.6 %collective-permute-start.12 = (f32[64,64]{1,0:T(8,128)S(1)}, f32[64,64]{1,0:T(8,128)S(1)}, u32[]{:S(2)}, u32[]{:S(2)}) collective-permute-start(f32[64,64]{1,0:T(8,128)S(1)} %add.48), channel_id=1, source_target_pairs={{0,2},{1,3},{2,0},{3,1},{4,6},{5,7},{6,4},{7,5},{8,10},{9,11},{10,... | collective-permute-start | bytes 49160 | tf_op jit(solution)/shard_map/ppermute | solution.py:53
  60.2 4.9 %collective-permute-start.14 = (f32[16,128]{1,0:T(8,128)S(1)}, f32[16,128]{1,0:T(8,128)S(1)}, u32[]{:S(2)}, u32[]{:S(2)}) collective-permute-start(f32[16,128]{1,0:T(8,128)S(1)} %add.52), channel_id=1, source_target_pairs={{0,6},{1,7},{2,4},{3,5},{4,2},{5,3},{6,0},{7,1},{8,14},{9,15},{10,... | collective-permute-start | bytes 24584 | tf_op jit(solution)/shard_map/ppermute | solution.py:53
  63.0 5.2 %collective-permute-start.15 = (f32[16,128]{1,0:T(8,128)S(1)}, f32[16,128]{1,0:T(8,128)S(1)}, u32[]{:S(2)}, u32[]{:S(2)}) collective-permute-start(f32[16,128]{1,0:T(8,128)S(1)} %add.52), channel_id=1, source_target_pairs={{0,4},{1,5},{2,6},{3,7},{4,0},{5,1},{6,2},{7,3},{8,12},{9,13},{10,... | collective-permute-start | bytes 24584 | tf_op jit(solution)/shard_map/ppermute | solution.py:53
  63.8 4.4 %collective-permute-start.16 = (f32[16,128]{1,0:T(8,128)S(1)}, f32[16,128]{1,0:T(8,128)S(1)}, u32[]{:S(2)}, u32[]{:S(2)}) collective-permute-start(f32[16,128]{1,0:T(8,128)S(1)} %add.52), channel_id=1, source_target_pairs={{0,2},{1,3},{2,0},{3,1},{4,6},{5,7},{6,4},{7,5},{8,10},{9,11},{10,... | collective-permute-start | bytes 24584 | tf_op jit(solution)/shard_map/ppermute | solution.py:53
  68.7 4.1 %collective-permute-start.17 = (bf16[32,640]{1,0:T(8,128)(2,1)S(1)}, bf16[32,640]{1,0:T(8,128)(2,1)S(1)}, u32[]{:S(2)}, u32[]{:S(2)}) collective-permute-start(bf16[32,640]{1,0:T(8,128)(2,1)S(1)} %get-tuple-element.54), channel_id=1, source_target_pairs={{0,8},{8,0},{16,24},{24,16},{32,40},{40,32},{48,56},{56,48},{64,72... | collective-permute-start | bytes 122888 | tf_op jit(solution)/shard_map/ppermute | solution.py:53
  72.8 6.2 %collective-permute-start.18 = (bf16[2,32,640]{2,1,0:T(8,128)(2,1)S(1)}, bf16[2,32,640]{2,1,0:T(8,128)(2,1)S(1)}, u32[]{:S(2)}, u32[]{:S(2)}) collective-permute-start(bf16[2,32,640]{2,1,0:T(8,128)(2,1)S(1)} %pad_maximum_fusion), channel_id=1, source_target_pairs={{0,16},{8,24},{16,0},{24,8},{32,48},{40,56},{48,32},{56,40},{64,80... | collective-permute-start | bytes 245768 | tf_op jit(solution)/shard_map/ppermute | solution.py:53
  73.7 9.8 %collective-permute-start.19 = (bf16[2,32,640]{2,1,0:T(8,128)(2,1)S(1)}, bf16[2,32,640]{2,1,0:T(8,128)(2,1)S(1)}, u32[]{:S(2)}, u32[]{:S(2)}) collective-permute-start(bf16[2,32,640]{2,1,0:T(8,128)(2,1)S(1)} %pad_maximum_fusion), channel_id=1, source_target_pairs={{0,40},{8,32},{16,56},{24,48},{32,8},{40,0},{48,24},{56,16},{64,10... | collective-permute-start | bytes 245768 | tf_op jit(solution)/shard_map/ppermute | solution.py:53
  76.0 7.7 %collective-permute-start.20 = (bf16[2,32,640]{2,1,0:T(8,128)(2,1)S(1)}, bf16[2,32,640]{2,1,0:T(8,128)(2,1)S(1)}, u32[]{:S(2)}, u32[]{:S(2)}) collective-permute-start(bf16[2,32,640]{2,1,0:T(8,128)(2,1)S(1)} %pad_maximum_fusion), channel_id=1, source_target_pairs={{0,48},{8,56},{16,32},{24,40},{32,16},{40,24},{48,0},{56,8},{64,11... | collective-permute-start | bytes 245768 | tf_op jit(solution)/shard_map/ppermute | solution.py:53
  83.7 10.3 %collective-permute-start.23 = (bf16[8,32,640]{2,1,0:T(8,128)(2,1)S(1)}, bf16[8,32,640]{2,1,0:T(8,128)(2,1)S(1)}, u32[]{:S(2)}, u32[]{:S(2)}) collective-permute-start(bf16[8,32,640]{2,1,0:T(8,128)(2,1)S(1)} %constant_dynamic-update-slice_fusion.refs_0_), channel_id=1, source_target_pairs={{0,128},{8,136},{16,144},{24,152},{32,160},{40,168},{48,176},{56,1... | collective-permute-start | bytes 983048 | tf_op jit(solution)/shard_map/ppermute | solution.py:53
  85.3 11.4 %collective-permute-start.21 = (bf16[8,32,640]{2,1,0:T(8,128)(2,1)S(1)}, bf16[8,32,640]{2,1,0:T(8,128)(2,1)S(1)}, u32[]{:S(2)}, u32[]{:S(2)}) collective-permute-start(bf16[8,32,640]{2,1,0:T(8,128)(2,1)S(1)} %constant_dynamic-update-slice_fusion.refs_0_), channel_id=1, source_target_pairs={{0,64},{8,72},{16,80},{24,88},{32,96},{40,104},{48,112},{56,120},{... | collective-permute-start | bytes 983048 | tf_op jit(solution)/shard_map/ppermute | solution.py:53
  85.9 11.5 %collective-permute-start.22 = (bf16[8,32,640]{2,1,0:T(8,128)(2,1)S(1)}, bf16[8,32,640]{2,1,0:T(8,128)(2,1)S(1)}, u32[]{:S(2)}, u32[]{:S(2)}) collective-permute-start(bf16[8,32,640]{2,1,0:T(8,128)(2,1)S(1)} %constant_dynamic-update-slice_fusion.refs_0_), channel_id=1, source_target_pairs={{0,192},{8,200},{16,208},{24,216},{32,224},{40,232},{48,240},{56,2... | collective-permute-start | bytes 983048 | tf_op jit(solution)/shard_map/ppermute | solution.py:53
  (4 other events, 29.0 us)

commit v12 on v11

--- a/solution.py
+++ b/solution.py
@@ -19,9 +19,9 @@
 Y_STEPS = (8, 16, 24)
 X_STEPS = (2, 4, 6)
 Z_SUM_STEPS = (1, 3, 7)
-Z_PAIRS = (2, 5, 6)
+Z_PAIRS = (6, 5, 2)
 Z_ORDER = tuple(pair ^ bit for pair in (0,) + Z_PAIRS for bit in (0, 1))
-LAST_STEPS = (0, 1, 3, 2)
+LAST_STEPS = (0, 3, 1, 2)
 GATHER_STEPS = (0, 3, 2, 1)
 ROW_BLOCKS = 4
 
@@ -274,7 +274,8 @@
 
     def piece_of(z):
         step = own_z ^ z
-        return step ^ ((step >> 2) & (1 - ((step >> 1) & 1)))
+        swapped = (step >> 2) & (1 - ((step >> 1) & 1))
+        return ((4 - (step >> 1)) & 3) * 2 + ((step & 1) ^ swapped)
 
     def rows_of(d):
         return pl.ds(pl.multiple_of((own_y ^ LAST_STEPS[d]) * size, size), size)

time: 101 us -> 100 us (0.990); the launches traced: 99 us -> 99.8 us
  waiting for transfers between devices: 41.3 us -> 42.8 us
    ppermute x24, waiting for transfers between devices: 38.9 us -> 40.3 us  [exchange(): lax.ppermute(value, axis, [(i, i ^ distance) for i in range(lax.axis_size...]
  transfers between devices with their start and end apart: 25 -> 25, of which waited for: 21 -> 20; matrix products, arithmetic and copies ran while one was open for 2% -> 2% of each run, Pallas kernels for 6% -> 6%
where the time goes in v12:
time: 100 us; the launch traced here: 99.8 us
  starting transfers between devices  43.9 us (44%)
  waiting for transfers between devices  42.8 us (43%)
  Pallas kernels  10.2 us (10%)
  local copies, waits for them, and re-layouts  1.96 us (2%)
    ppermute x24, waiting for transfers between devices, exchange(): lax.ppermute(value, axis, [(i, i ^ distance) for i in range(lax.axis_size...  40.3 us
    ppermute x24, starting transfers between devices, exchange(): lax.ppermute(value, axis, [(i, i ^ distance) for i in range(lax.axis_size...  34.2 us
    all_to_all x1, starting transfers between devices, on_device(): received = lax.all_to_all(packed, 'rep', 0, 0, tiled=True)  9.69 us
    pallas_call x7, Pallas kernels, call(): pl.pallas_call(kernel, out_shape=outs, in_specs=specs, out_specs=out_spec...  8.2 us
    all_to_all x1, waiting for transfers between devices, on_device(): received = lax.all_to_all(packed, 'rep', 0, 0, tiled=True)  2.46 us
  transfers between devices with their start and end apart: 25, of which 20 were waited for; matrix products, arithmetic and copies ran while one was open for 2% of the time, Pallas kernels for 6%

profile of v12, /device:TPU:32, one launch (start us, length us, event | category | flops | bytes accessed | tf_op | source)
XLA Modules:
  0.0 99.8 jit_solution(119503006373770189)
XLA Ops:
  0.6 1.9 %local_factor.1 = (f32[64,128]{1,0:T(8,128)S(1)}, f32[64,128]{1,0:T(8,128)S(1)}, f32[64,128]{1,0:T(8,128)S(1)}, f32[64,128]{1,0:T(8,128)S(1)}, bf16[1024,512]{1,...) custom-call(f32[64,1024]{1,0:T(8,128)} %bitcast.15, bf16[1024,512]{1,0:T(8,128)(2,1)} %bitcast.13, bf16[1024,512]{1,0:T(8,128)(2,1)} %bitcast.14), custom_call_target="tpu_custom_call" | custom-call | flops 1000000000 | bytes 2500000 | tf_op jit(solution)/shard_map/local_factor/pallas_call | solution.py:117
  4.3 2.9 %collective-permute-start.1 = (f32[64,128]{1,0:T(8,128)S(1)}, f32[64,128]{1,0:T(8,128)S(1)}, u32[]{:S(2)}, u32[]{:S(2)}) collective-permute-start(f32[64,128]{1,0:T(8,128)S(1)} %get-tuple-element.39), channel_id=1, source_target_pairs={{0,128},{8,136},{16,144},{24,152},{32,160},{40,168},{48,176},{56,1... | collective-permute-start | bytes 98312 | tf_op jit(solution)/shard_map/ppermute | solution.py:53
  7.4 2.3 %collective-permute-done.1 = f32[64,128]{1,0:T(8,128)S(1)} collective-permute-done((f32[64,128]{1,0:T(8,128)S(1)}, f32[64,128]{1,0:T(8,128)S(1)}, u32[]{:S(2)}, u32[]{:S(2)}) %collective-permute-start.1) | collective-permute-done | bytes 32800 | tf_op jit(solution)/shard_map/ppermute | solution.py:53
  9.7 2.6 %collective-permute-done.2 = f32[64,128]{1,0:T(8,128)S(1)} collective-permute-done((f32[64,128]{1,0:T(8,128)S(1)}, f32[64,128]{1,0:T(8,128)S(1)}, u32[]{:S(2)}, u32[]{:S(2)}) %collective-permute-start.2) | collective-permute-done | bytes 32800 | tf_op jit(solution)/shard_map/ppermute | solution.py:53
  12.5 3.8 %collective-permute-done.3 = f32[64,128]{1,0:T(8,128)S(1)} collective-permute-done((f32[64,128]{1,0:T(8,128)S(1)}, f32[64,128]{1,0:T(8,128)S(1)}, u32[]{:S(2)}, u32[]{:S(2)}) %collective-permute-start.3) | collective-permute-done | bytes 32800 | tf_op jit(solution)/shard_map/ppermute | solution.py:53
  16.3 2.2 %collective-permute-start.4 = (f32[64,128]{1,0:T(8,128)S(1)}, f32[64,128]{1,0:T(8,128)S(1)}, u32[]{:S(2)}, u32[]{:S(2)}) collective-permute-start(f32[64,128]{1,0:T(8,128)S(1)} %add.45), channel_id=1, source_target_pairs={{0,24},{8,16},{16,8},{24,0},{32,56},{40,48},{48,40},{56,32},{64,88... | collective-permute-start | bytes 98312 | tf_op jit(solution)/shard_map/ppermute | solution.py:53
  18.5 1.9 %collective-permute-done.4 = f32[64,128]{1,0:T(8,128)S(1)} collective-permute-done((f32[64,128]{1,0:T(8,128)S(1)}, f32[64,128]{1,0:T(8,128)S(1)}, u32[]{:S(2)}, u32[]{:S(2)}) %collective-permute-start.4) | collective-permute-done | bytes 32800 | tf_op jit(solution)/shard_map/ppermute | solution.py:53
  20.4 5.7 %collective-permute-start.5 = (f32[64,128]{1,0:T(8,128)S(1)}, f32[64,128]{1,0:T(8,128)S(1)}, u32[]{:S(2)}, u32[]{:S(2)}) collective-permute-start(f32[64,128]{1,0:T(8,128)S(1)} %add.46), channel_id=1, source_target_pairs={{0,56},{8,48},{16,40},{24,32},{32,24},{40,16},{48,8},{56,0},{64,12... | collective-permute-start | bytes 98312 | tf_op jit(solution)/shard_map/ppermute | solution.py:53
  26.1 1.9 %collective-permute-done.5 = f32[64,128]{1,0:T(8,128)S(1)} collective-permute-done((f32[64,128]{1,0:T(8,128)S(1)}, f32[64,128]{1,0:T(8,128)S(1)}, u32[]{:S(2)}, u32[]{:S(2)}) %collective-permute-start.5) | collective-permute-done | bytes 32800 | tf_op jit(solution)/shard_map/ppermute | solution.py:53
  29.0 3.1 %collective-permute-start.8 = (f32[64,128]{1,0:T(8,128)S(1)}, f32[64,128]{1,0:T(8,128)S(1)}, u32[]{:S(2)}, u32[]{:S(2)}) collective-permute-start(f32[64,128]{1,0:T(8,128)S(1)} %add_multiply_fusion.refs_0_), channel_id=1, source_target_pairs={{0,64},{8,72},{16,80},{24,88},{32,96},{40,104},{48,112},{56,120},{... | collective-permute-start | bytes 98312 | tf_op jit(solution)/shard_map/ppermute | solution.py:53
  36.3 9.7 %all-to-all-start = ((f32[32,16,128]{2,1,0:T(8,128)}), f32[32,16,128]{2,1,0:T(8,128)S(1)}, u32[]{:S(2)}, u32[]{:S(2)}) async-start(f32[32,16,128]{2,1,0:T(8,128)} %project.1), calls=%async_computation | async-start | bytes 524288 | tf_op jit(solution)/shard_map/all_to_all | solution.py:343
  46.0 2.8 %collective-permute-start.10 = (f32[64,64]{1,0:T(8,128)S(1)}, f32[64,64]{1,0:T(8,128)S(1)}, u32[]{:S(2)}, u32[]{:S(2)}) collective-permute-start(f32[64,64]{1,0:T(8,128)S(1)} %add.48), channel_id=1, source_target_pairs={{0,6},{1,7},{2,4},{3,5},{4,2},{5,3},{6,0},{7,1},{8,14},{9,15},{10,... | collective-permute-start | bytes 49160 | tf_op jit(solution)/shard_map/ppermute | solution.py:53
  51.2 3.1 %collective-permute-done.11 = f32[64,64]{1,0:T(8,128)S(1)} collective-permute-done((f32[64,64]{1,0:T(8,128)S(1)}, f32[64,64]{1,0:T(8,128)S(1)}, u32[]{:S(2)}, u32[]{:S(2)}) %collective-permute-start.11) | collective-permute-done | bytes 16416 | tf_op jit(solution)/shard_map/ppermute | solution.py:53
  54.3 2.2 %invert.1 = (f32[64,64]{1,0:T(8,128)S(1)}, f32[64,512]{1,0:T(8,128)S(1)}, bf16[384,512]{1,0:T(8,128)(2,1)S(1)}) custom-call(f32[64,64]{1,0:T(8,128)S(1)} %add_add_fusion.gram_ref, f32[64,512]{1,0:T(8,128)S(1)} %get-tuple-element.47.factor_ref), custom_call_target="tpu_custom_call" | custom-call | flops 2000000000 | bytes 500000 | tf_op jit(solution)/shard_map/invert/pallas_call | solution.py:69
  56.4 2.5 %all-to-all-done = f32[32,16,128]{2,1,0:T(8,128)S(1)} async-done(((f32[32,16,128]{2,1,0:T(8,128)}), f32[32,16,128]{2,1,0:T(8,128)S(1)}, u32[]{:S(2)}, u32[]{:S(2)}) %all-to-all-start) | async-done | bytes 262176 | tf_op jit(solution)/shard_map/all_to_all | solution.py:343
  60.2 2.8 %collective-permute-start.14 = (f32[16,128]{1,0:T(8,128)S(1)}, f32[16,128]{1,0:T(8,128)S(1)}, u32[]{:S(2)}, u32[]{:S(2)}) collective-permute-start(f32[16,128]{1,0:T(8,128)S(1)} %add.52), channel_id=1, source_target_pairs={{0,6},{1,7},{2,4},{3,5},{4,2},{5,3},{6,0},{7,1},{8,14},{9,15},{10,... | collective-permute-start | bytes 24584 | tf_op jit(solution)/shard_map/ppermute | solution.py:53
  65.1 3.1 %collective-permute-done.15 = f32[16,128]{1,0:T(8,128)S(1)} collective-permute-done((f32[16,128]{1,0:T(8,128)S(1)}, f32[16,128]{1,0:T(8,128)S(1)}, u32[]{:S(2)}, u32[]{:S(2)}) %collective-permute-start.15) | collective-permute-done | bytes 8224 | tf_op jit(solution)/shard_map/ppermute | solution.py:53
  68.8 4.0 %collective-permute-done.17 = bf16[32,640]{1,0:T(8,128)(2,1)S(1)} collective-permute-done((bf16[32,640]{1,0:T(8,128)(2,1)S(1)}, bf16[32,640]{1,0:T(8,128)(2,1)S(1)}, u32[]{:S(2)}, u32[]{:S(2)}) %collective-permute-start.17) | collective-permute-done | bytes 40992 | tf_op jit(solution)/shard_map/ppermute | solution.py:53
  73.0 4.3 %collective-permute-start.19 = (bf16[2,32,640]{2,1,0:T(8,128)(2,1)S(1)}, bf16[2,32,640]{2,1,0:T(8,128)(2,1)S(1)}, u32[]{:S(2)}, u32[]{:S(2)}) collective-permute-start(bf16[2,32,640]{2,1,0:T(8,128)(2,1)S(1)} %pad_maximum_fusion), channel_id=1, source_target_pairs={{0,40},{8,32},{16,56},{24,48},{32,8},{40,0},{48,24},{56,16},{64,10... | collective-permute-start | bytes 245768 | tf_op jit(solution)/shard_map/ppermute | solution.py:53
  77.9 2.2 %collective-permute-done.18 = bf16[2,32,640]{2,1,0:T(8,128)(2,1)S(1)} collective-permute-done((bf16[2,32,640]{2,1,0:T(8,128)(2,1)S(1)}, bf16[2,32,640]{2,1,0:T(8,128)(2,1)S(1)}, u32[]{:S(2)}, u32[]{:S(2)}) %collective-permute-start.18) | collective-permute-done | bytes 81952 | tf_op jit(solution)/shard_map/ppermute | solution.py:53
  80.2 2.4 %collective-permute-done.19 = bf16[2,32,640]{2,1,0:T(8,128)(2,1)S(1)} collective-permute-done((bf16[2,32,640]{2,1,0:T(8,128)(2,1)S(1)}, bf16[2,32,640]{2,1,0:T(8,128)(2,1)S(1)}, u32[]{:S(2)}, u32[]{:S(2)}) %collective-permute-start.19) | collective-permute-done | bytes 81952 | tf_op jit(solution)/shard_map/ppermute | solution.py:53
  84.2 2.5 %collective-permute-start.21 = (bf16[8,32,640]{2,1,0:T(8,128)(2,1)S(1)}, bf16[8,32,640]{2,1,0:T(8,128)(2,1)S(1)}, u32[]{:S(2)}, u32[]{:S(2)}) collective-permute-start(bf16[8,32,640]{2,1,0:T(8,128)(2,1)S(1)} %constant_dynamic-update-slice_fusion.refs_0_), channel_id=1, source_target_pairs={{0,192},{8,200},{16,208},{24,216},{32,224},{40,232},{48,240},{56,2... | collective-permute-start | bytes 983048 | tf_op jit(solution)/shard_map/ppermute | solution.py:53
  90.0 5.0 %collective-permute-done.23.refs_0_ = bf16[8,32,640]{2,1,0:T(8,128)(2,1)S(1)} collective-permute-done((bf16[8,32,640]{2,1,0:T(8,128)(2,1)S(1)}, bf16[8,32,640]{2,1,0:T(8,128)(2,1)S(1)}, u32[]{:S(2)}, u32[]{:S(2)}) %collective-permute-start.23) | collective-permute-done | bytes 327712 | tf_op jit(solution)/shard_map/ppermute | solution.py:53
  96.2 2.1 %collective-permute-done.21.refs_0_ = bf16[8,32,640]{2,1,0:T(8,128)(2,1)S(1)} collective-permute-done((bf16[8,32,640]{2,1,0:T(8,128)(2,1)S(1)}, bf16[8,32,640]{2,1,0:T(8,128)(2,1)S(1)}, u32[]{:S(2)}, u32[]{:S(2)}) %collective-permute-start.21) | collective-permute-done | bytes 327712 | tf_op jit(solution)/shard_map/ppermute | solution.py:53
  (58 shorter events, 22.1 us)
Async XLA Ops:
  2.6 4.8 %collective-permute-start = (f32[64,128]{1,0:T(8,128)S(1)}, f32[64,128]{1,0:T(8,128)S(1)}, u32[]{:S(2)}, u32[]{:S(2)}) collective-permute-start(f32[64,128]{1,0:T(8,128)S(1)} %get-tuple-element.38), channel_id=1, source_target_pairs={{0,64},{8,72},{16,80},{24,88},{32,96},{40,104},{48,112},{56,120},{... | collective-permute-start | bytes 98312 | tf_op jit(solution)/shard_map/ppermute | solution.py:53
  4.3 5.4 %collective-permute-start.1 = (f32[64,128]{1,0:T(8,128)S(1)}, f32[64,128]{1,0:T(8,128)S(1)}, u32[]{:S(2)}, u32[]{:S(2)}) collective-permute-start(f32[64,128]{1,0:T(8,128)S(1)} %get-tuple-element.39), channel_id=1, source_target_pairs={{0,128},{8,136},{16,144},{24,152},{32,160},{40,168},{48,176},{56,1... | collective-permute-start | bytes 98312 | tf_op jit(solution)/shard_map/ppermute | solution.py:53
  7.2 5.1 %collective-permute-start.2 = (f32[64,128]{1,0:T(8,128)S(1)}, f32[64,128]{1,0:T(8,128)S(1)}, u32[]{:S(2)}, u32[]{:S(2)}) collective-permute-start(f32[64,128]{1,0:T(8,128)S(1)} %get-tuple-element.40), channel_id=1, source_target_pairs={{0,192},{8,200},{16,208},{24,216},{32,224},{40,232},{48,240},{56,2... | collective-permute-start | bytes 98312 | tf_op jit(solution)/shard_map/ppermute | solution.py:53
  12.3 4.0 %collective-permute-start.3 = (f32[64,128]{1,0:T(8,128)S(1)}, f32[64,128]{1,0:T(8,128)S(1)}, u32[]{:S(2)}, u32[]{:S(2)}) collective-permute-start(f32[64,128]{1,0:T(8,128)S(1)} %add_add_fusion.1), channel_id=1, source_target_pairs={{0,8},{8,0},{16,24},{24,16},{32,40},{40,32},{48,56},{56,48},{64,72... | collective-permute-start | bytes 98312 | tf_op jit(solution)/shard_map/ppermute | solution.py:53
  16.3 4.1 %collective-permute-start.4 = (f32[64,128]{1,0:T(8,128)S(1)}, f32[64,128]{1,0:T(8,128)S(1)}, u32[]{:S(2)}, u32[]{:S(2)}) collective-permute-start(f32[64,128]{1,0:T(8,128)S(1)} %add.45), channel_id=1, source_target_pairs={{0,24},{8,16},{16,8},{24,0},{32,56},{40,48},{48,40},{56,32},{64,88... | collective-permute-start | bytes 98312 | tf_op jit(solution)/shard_map/ppermute | solution.py:53
  20.4 7.6 %collective-permute-start.5 = (f32[64,128]{1,0:T(8,128)S(1)}, f32[64,128]{1,0:T(8,128)S(1)}, u32[]{:S(2)}, u32[]{:S(2)}) collective-permute-start(f32[64,128]{1,0:T(8,128)S(1)} %add.46), channel_id=1, source_target_pairs={{0,56},{8,48},{16,40},{24,32},{32,24},{40,16},{48,8},{56,0},{64,12... | collective-permute-start | bytes 98312 | tf_op jit(solution)/shard_map/ppermute | solution.py:53
  28.0 5.1 %collective-permute-start.6 = (f32[64,128]{1,0:T(8,128)S(1)}, f32[64,128]{1,0:T(8,128)S(1)}, u32[]{:S(2)}, u32[]{:S(2)}) collective-permute-start(f32[64,128]{1,0:T(8,128)S(1)} %add_multiply_fusion.refs_0_), channel_id=1, source_target_pairs={{0,192},{8,200},{16,208},{24,216},{32,224},{40,232},{48,240},{56,2... | collective-permute-start | bytes 98312 | tf_op jit(solution)/shard_map/ppermute | solution.py:53
  28.2 5.4 %collective-permute-start.7 = (f32[64,128]{1,0:T(8,128)S(1)}, f32[64,128]{1,0:T(8,128)S(1)}, u32[]{:S(2)}, u32[]{:S(2)}) collective-permute-start(f32[64,128]{1,0:T(8,128)S(1)} %add_multiply_fusion.refs_0_), channel_id=1, source_target_pairs={{0,128},{8,136},{16,144},{24,152},{32,160},{40,168},{48,176},{56,1... | collective-permute-start | bytes 98312 | tf_op jit(solution)/shard_map/ppermute | solution.py:53
  29.0 5.3 %collective-permute-start.8 = (f32[64,128]{1,0:T(8,128)S(1)}, f32[64,128]{1,0:T(8,128)S(1)}, u32[]{:S(2)}, u32[]{:S(2)}) collective-permute-start(f32[64,128]{1,0:T(8,128)S(1)} %add_multiply_fusion.refs_0_), channel_id=1, source_target_pairs={{0,64},{8,72},{16,80},{24,88},{32,96},{40,104},{48,112},{56,120},{... | collective-permute-start | bytes 98312 | tf_op jit(solution)/shard_map/ppermute | solution.py:53
  34.6 1.7 %collective-permute-start.9 = (f32[64,64]{1,0:T(8,128)S(1)}, f32[64,64]{1,0:T(8,128)S(1)}, u32[]{:S(2)}, u32[]{:S(2)}) collective-permute-start(f32[64,64]{1,0:T(8,128)S(1)} %get-tuple-element.41), channel_id=1, source_target_pairs={{0,1},{1,0},{2,3},{3,2},{4,5},{5,4},{6,7},{7,6},{8,9},{9,8},{10,11... | collective-permute-start | bytes 49160 | tf_op jit(solution)/shard_map/ppermute | solution.py:53
  36.3 22.6 %all-to-all-start = ((f32[32,16,128]{2,1,0:T(8,128)}), f32[32,16,128]{2,1,0:T(8,128)S(1)}, u32[]{:S(2)}, u32[]{:S(2)}) async-start(f32[32,16,128]{2,1,0:T(8,128)} %project.1), calls=%async_computation | async-start | bytes 524288 | tf_op jit(solution)/shard_map/all_to_all | solution.py:343
  46.0 5.2 %collective-permute-start.10 = (f32[64,64]{1,0:T(8,128)S(1)}, f32[64,64]{1,0:T(8,128)S(1)}, u32[]{:S(2)}, u32[]{:S(2)}) collective-permute-start(f32[64,64]{1,0:T(8,128)S(1)} %add.48), channel_id=1, source_target_pairs={{0,6},{1,7},{2,4},{3,5},{4,2},{5,3},{6,0},{7,1},{8,14},{9,15},{10,... | collective-permute-start | bytes 49160 | tf_op jit(solution)/shard_map/ppermute | solution.py:53
  48.8 5.4 %collective-permute-start.11 = (f32[64,64]{1,0:T(8,128)S(1)}, f32[64,64]{1,0:T(8,128)S(1)}, u32[]{:S(2)}, u32[]{:S(2)}) collective-permute-start(f32[64,64]{1,0:T(8,128)S(1)} %add.48), channel_id=1, source_target_pairs={{0,4},{1,5},{2,6},{3,7},{4,0},{5,1},{6,2},{7,3},{8,12},{9,13},{10,... | collective-permute-start | bytes 49160 | tf_op jit(solution)/shard_map/ppermute | solution.py:53
  49.6 4.6 %collective-permute-start.12 = (f32[64,64]{1,0:T(8,128)S(1)}, f32[64,64]{1,0:T(8,128)S(1)}, u32[]{:S(2)}, u32[]{:S(2)}) collective-permute-start(f32[64,64]{1,0:T(8,128)S(1)} %add.48), channel_id=1, source_target_pairs={{0,2},{1,3},{2,0},{3,1},{4,6},{5,7},{6,4},{7,5},{8,10},{9,11},{10,... | collective-permute-start | bytes 49160 | tf_op jit(solution)/shard_map/ppermute | solution.py:53
  60.2 4.9 %collective-permute-start.14 = (f32[16,128]{1,0:T(8,128)S(1)}, f32[16,128]{1,0:T(8,128)S(1)}, u32[]{:S(2)}, u32[]{:S(2)}) collective-permute-start(f32[16,128]{1,0:T(8,128)S(1)} %add.52), channel_id=1, source_target_pairs={{0,6},{1,7},{2,4},{3,5},{4,2},{5,3},{6,0},{7,1},{8,14},{9,15},{10,... | collective-permute-start | bytes 24584 | tf_op jit(solution)/shard_map/ppermute | solution.py:53
  63.0 5.2 %collective-permute-start.15 = (f32[16,128]{1,0:T(8,128)S(1)}, f32[16,128]{1,0:T(8,128)S(1)}, u32[]{:S(2)}, u32[]{:S(2)}) collective-permute-start(f32[16,128]{1,0:T(8,128)S(1)} %add.52), channel_id=1, source_target_pairs={{0,4},{1,5},{2,6},{3,7},{4,0},{5,1},{6,2},{7,3},{8,12},{9,13},{10,... | collective-permute-start | bytes 24584 | tf_op jit(solution)/shard_map/ppermute | solution.py:53
  63.8 4.4 %collective-permute-start.16 = (f32[16,128]{1,0:T(8,128)S(1)}, f32[16,128]{1,0:T(8,128)S(1)}, u32[]{:S(2)}, u32[]{:S(2)}) collective-permute-start(f32[16,128]{1,0:T(8,128)S(1)} %add.52), channel_id=1, source_target_pairs={{0,2},{1,3},{2,0},{3,1},{4,6},{5,7},{6,4},{7,5},{8,10},{9,11},{10,... | collective-permute-start | bytes 24584 | tf_op jit(solution)/shard_map/ppermute | solution.py:53
  68.7 4.1 %collective-permute-start.17 = (bf16[32,640]{1,0:T(8,128)(2,1)S(1)}, bf16[32,640]{1,0:T(8,128)(2,1)S(1)}, u32[]{:S(2)}, u32[]{:S(2)}) collective-permute-start(bf16[32,640]{1,0:T(8,128)(2,1)S(1)} %get-tuple-element.54), channel_id=1, source_target_pairs={{0,8},{8,0},{16,24},{24,16},{32,40},{40,32},{48,56},{56,48},{64,72... | collective-permute-start | bytes 122888 | tf_op jit(solution)/shard_map/ppermute | solution.py:53
  72.8 7.4 %collective-permute-start.18 = (bf16[2,32,640]{2,1,0:T(8,128)(2,1)S(1)}, bf16[2,32,640]{2,1,0:T(8,128)(2,1)S(1)}, u32[]{:S(2)}, u32[]{:S(2)}) collective-permute-start(bf16[2,32,640]{2,1,0:T(8,128)(2,1)S(1)} %pad_maximum_fusion), channel_id=1, source_target_pairs={{0,48},{8,56},{16,32},{24,40},{32,16},{40,24},{48,0},{56,8},{64,11... | collective-permute-start | bytes 245768 | tf_op jit(solution)/shard_map/ppermute | solution.py:53
  73.0 9.6 %collective-permute-start.19 = (bf16[2,32,640]{2,1,0:T(8,128)(2,1)S(1)}, bf16[2,32,640]{2,1,0:T(8,128)(2,1)S(1)}, u32[]{:S(2)}, u32[]{:S(2)}) collective-permute-start(bf16[2,32,640]{2,1,0:T(8,128)(2,1)S(1)} %pad_maximum_fusion), channel_id=1, source_target_pairs={{0,40},{8,32},{16,56},{24,48},{32,8},{40,0},{48,24},{56,16},{64,10... | collective-permute-start | bytes 245768 | tf_op jit(solution)/shard_map/ppermute | solution.py:53
  77.3 6.2 %collective-permute-start.20 = (bf16[2,32,640]{2,1,0:T(8,128)(2,1)S(1)}, bf16[2,32,640]{2,1,0:T(8,128)(2,1)S(1)}, u32[]{:S(2)}, u32[]{:S(2)}) collective-permute-start(bf16[2,32,640]{2,1,0:T(8,128)(2,1)S(1)} %pad_maximum_fusion), channel_id=1, source_target_pairs={{0,16},{8,24},{16,0},{24,8},{32,48},{40,56},{48,32},{56,40},{64,80... | collective-permute-start | bytes 245768 | tf_op jit(solution)/shard_map/ppermute | solution.py:53
  83.4 11.6 %collective-permute-start.23 = (bf16[8,32,640]{2,1,0:T(8,128)(2,1)S(1)}, bf16[8,32,640]{2,1,0:T(8,128)(2,1)S(1)}, u32[]{:S(2)}, u32[]{:S(2)}) collective-permute-start(bf16[8,32,640]{2,1,0:T(8,128)(2,1)S(1)} %constant_dynamic-update-slice_fusion.refs_0_), channel_id=1, source_target_pairs={{0,128},{8,136},{16,144},{24,152},{32,160},{40,168},{48,176},{56,1... | collective-permute-start | bytes 983048 | tf_op jit(solution)/shard_map/ppermute | solution.py:53
  84.2 14.1 %collective-permute-start.21 = (bf16[8,32,640]{2,1,0:T(8,128)(2,1)S(1)}, bf16[8,32,640]{2,1,0:T(8,128)(2,1)S(1)}, u32[]{:S(2)}, u32[]{:S(2)}) collective-permute-start(bf16[8,32,640]{2,1,0:T(8,128)(2,1)S(1)} %constant_dynamic-update-slice_fusion.refs_0_), channel_id=1, source_target_pairs={{0,192},{8,200},{16,208},{24,216},{32,224},{40,232},{48,240},{56,2... | collective-permute-start | bytes 983048 | tf_op jit(solution)/shard_map/ppermute | solution.py:53
  86.6 11.6 %collective-permute-start.22 = (bf16[8,32,640]{2,1,0:T(8,128)(2,1)S(1)}, bf16[8,32,640]{2,1,0:T(8,128)(2,1)S(1)}, u32[]{:S(2)}, u32[]{:S(2)}) collective-permute-start(bf16[8,32,640]{2,1,0:T(8,128)(2,1)S(1)} %constant_dynamic-update-slice_fusion.refs_0_), channel_id=1, source_target_pairs={{0,64},{8,72},{16,80},{24,88},{32,96},{40,104},{48,112},{56,120},{... | collective-permute-start | bytes 983048 | tf_op jit(solution)/shard_map/ppermute | solution.py:53
  (4 other events, 29.0 us)

commit v13 on v12

--- a/solution.py
+++ b/solution.py
@@ -330,7 +330,9 @@
     gradient, feedback = gradient[0], feedback[0]
 
     pieces, gradient, feedback = local_factor(warm_start.T, gradient, feedback)
-    quarter = sum_four([pieces[0]] + [exchange(p, "rep", d) for p, d in zip(pieces[1:], Y_STEPS)])
+    quarter = sum_four(
+        [pieces[0]] + [exchange(pieces[d], "rep", Z_SIZE * d) for d in GATHER_STEPS[1:]]
+    )
     for distance in Z_SUM_STEPS:
         quarter = quarter + exchange(quarter, "rep", distance)
     quarter = quarter / replicas

time: 100 us -> 98.9 us (0.989)
  starting transfers between devices: 43.9 us -> 42.9 us
  transfers between devices with their start and end apart: 25 -> 25, of which waited for: 20 -> 19; matrix products, arithmetic and copies ran while one was open for 2% -> 2% of each run, Pallas kernels for 6% -> 6%
where the time goes in v13:
time: 98.9 us; the launch traced here: 98.7 us
  starting transfers between devices  42.9 us (43%)
  waiting for transfers between devices  42.7 us (43%)
  Pallas kernels  10.2 us (10%)
  local copies, waits for them, and re-layouts  1.96 us (2%)
    ppermute x24, waiting for transfers between devices, exchange(): lax.ppermute(value, axis, [(i, i ^ distance) for i in range(lax.axis_size...  40.2 us
    ppermute x24, starting transfers between devices, exchange(): lax.ppermute(value, axis, [(i, i ^ distance) for i in range(lax.axis_size...  33.5 us
    all_to_all x1, starting transfers between devices, on_device(): received = lax.all_to_all(packed, 'rep', 0, 0, tiled=True)  9.38 us
    pallas_call x7, Pallas kernels, call(): pl.pallas_call(kernel, out_shape=outs, in_specs=specs, out_specs=out_spec...  8.21 us
    all_to_all x1, waiting for transfers between devices, on_device(): received = lax.all_to_all(packed, 'rep', 0, 0, tiled=True)  2.46 us
  transfers between devices with their start and end apart: 25, of which 19 were waited for; matrix products, arithmetic and copies ran while one was open for 2% of the time, Pallas kernels for 6%

profile of v13, /device:TPU:32, one launch (start us, length us, event | category | flops | bytes accessed | tf_op | source)
XLA Modules:
  0.0 98.7 jit_solution(2699835236862940636)
XLA Ops:
  0.6 1.9 %local_factor.1 = (f32[64,128]{1,0:T(8,128)S(1)}, f32[64,128]{1,0:T(8,128)S(1)}, f32[64,128]{1,0:T(8,128)S(1)}, f32[64,128]{1,0:T(8,128)S(1)}, bf16[1024,512]{1,...) custom-call(f32[64,1024]{1,0:T(8,128)} %bitcast.15, bf16[1024,512]{1,0:T(8,128)(2,1)} %bitcast.13, bf16[1024,512]{1,0:T(8,128)(2,1)} %bitcast.14), custom_call_target="tpu_custom_call" | custom-call | flops 1000000000 | bytes 2500000 | tf_op jit(solution)/shard_map/local_factor/pallas_call | solution.py:117
  2.6 3.1 %collective-permute-start = (f32[64,128]{1,0:T(8,128)S(1)}, f32[64,128]{1,0:T(8,128)S(1)}, u32[]{:S(2)}, u32[]{:S(2)}) collective-permute-start(f32[64,128]{1,0:T(8,128)S(1)} %get-tuple-element.38), channel_id=1, source_target_pairs={{0,192},{8,200},{16,208},{24,216},{32,224},{40,232},{48,240},{56,2... | collective-permute-start | bytes 98312 | tf_op jit(solution)/shard_map/ppermute | solution.py:53
  7.8 3.3 %collective-permute-done.1 = f32[64,128]{1,0:T(8,128)S(1)} collective-permute-done((f32[64,128]{1,0:T(8,128)S(1)}, f32[64,128]{1,0:T(8,128)S(1)}, u32[]{:S(2)}, u32[]{:S(2)}) %collective-permute-start.1) | collective-permute-done | bytes 32800 | tf_op jit(solution)/shard_map/ppermute | solution.py:53
  11.3 3.8 %collective-permute-done.3 = f32[64,128]{1,0:T(8,128)S(1)} collective-permute-done((f32[64,128]{1,0:T(8,128)S(1)}, f32[64,128]{1,0:T(8,128)S(1)}, u32[]{:S(2)}, u32[]{:S(2)}) %collective-permute-start.3) | collective-permute-done | bytes 32800 | tf_op jit(solution)/shard_map/ppermute | solution.py:53
  15.1 1.9 %collective-permute-start.4 = (f32[64,128]{1,0:T(8,128)S(1)}, f32[64,128]{1,0:T(8,128)S(1)}, u32[]{:S(2)}, u32[]{:S(2)}) collective-permute-start(f32[64,128]{1,0:T(8,128)S(1)} %add.45), channel_id=1, source_target_pairs={{0,24},{8,16},{16,8},{24,0},{32,56},{40,48},{48,40},{56,32},{64,88... | collective-permute-start | bytes 98312 | tf_op jit(solution)/shard_map/ppermute | solution.py:53
  17.1 2.0 %collective-permute-done.4 = f32[64,128]{1,0:T(8,128)S(1)} collective-permute-done((f32[64,128]{1,0:T(8,128)S(1)}, f32[64,128]{1,0:T(8,128)S(1)}, u32[]{:S(2)}, u32[]{:S(2)}) %collective-permute-start.4) | collective-permute-done | bytes 32800 | tf_op jit(solution)/shard_map/ppermute | solution.py:53
  19.1 5.8 %collective-permute-start.5 = (f32[64,128]{1,0:T(8,128)S(1)}, f32[64,128]{1,0:T(8,128)S(1)}, u32[]{:S(2)}, u32[]{:S(2)}) collective-permute-start(f32[64,128]{1,0:T(8,128)S(1)} %add.46), channel_id=1, source_target_pairs={{0,56},{8,48},{16,40},{24,32},{32,24},{40,16},{48,8},{56,0},{64,12... | collective-permute-start | bytes 98312 | tf_op jit(solution)/shard_map/ppermute | solution.py:53
  24.9 1.9 %collective-permute-done.5 = f32[64,128]{1,0:T(8,128)S(1)} collective-permute-done((f32[64,128]{1,0:T(8,128)S(1)}, f32[64,128]{1,0:T(8,128)S(1)}, u32[]{:S(2)}, u32[]{:S(2)}) %collective-permute-start.5) | collective-permute-done | bytes 32800 | tf_op jit(solution)/shard_map/ppermute | solution.py:53
  29.0 1.9 %collective-permute-start.8 = (f32[64,128]{1,0:T(8,128)S(1)}, f32[64,128]{1,0:T(8,128)S(1)}, u32[]{:S(2)}, u32[]{:S(2)}) collective-permute-start(f32[64,128]{1,0:T(8,128)S(1)} %add_multiply_fusion.refs_0_), channel_id=1, source_target_pairs={{0,64},{8,72},{16,80},{24,88},{32,96},{40,104},{48,112},{56,120},{... | collective-permute-start | bytes 98312 | tf_op jit(solution)/shard_map/ppermute | solution.py:53
  31.9 1.6 %collective-permute-done.7.refs_2_ = f32[64,128]{1,0:T(8,128)S(1)} collective-permute-done((f32[64,128]{1,0:T(8,128)S(1)}, f32[64,128]{1,0:T(8,128)S(1)}, u32[]{:S(2)}, u32[]{:S(2)}) %collective-permute-start.7) | collective-permute-done | bytes 32800 | tf_op jit(solution)/shard_map/ppermute | solution.py:53
  35.5 9.4 %all-to-all-start = ((f32[32,16,128]{2,1,0:T(8,128)}), f32[32,16,128]{2,1,0:T(8,128)S(1)}, u32[]{:S(2)}, u32[]{:S(2)}) async-start(f32[32,16,128]{2,1,0:T(8,128)} %project.1), calls=%async_computation | async-start | bytes 524288 | tf_op jit(solution)/shard_map/all_to_all | solution.py:345
  44.9 2.8 %collective-permute-start.10 = (f32[64,64]{1,0:T(8,128)S(1)}, f32[64,64]{1,0:T(8,128)S(1)}, u32[]{:S(2)}, u32[]{:S(2)}) collective-permute-start(f32[64,64]{1,0:T(8,128)S(1)} %add.48), channel_id=1, source_target_pairs={{0,6},{1,7},{2,4},{3,5},{4,2},{5,3},{6,0},{7,1},{8,14},{9,15},{10,... | collective-permute-start | bytes 49160 | tf_op jit(solution)/shard_map/ppermute | solution.py:53
  50.1 3.0 %collective-permute-done.11 = f32[64,64]{1,0:T(8,128)S(1)} collective-permute-done((f32[64,64]{1,0:T(8,128)S(1)}, f32[64,64]{1,0:T(8,128)S(1)}, u32[]{:S(2)}, u32[]{:S(2)}) %collective-permute-start.11) | collective-permute-done | bytes 16416 | tf_op jit(solution)/shard_map/ppermute | solution.py:53
  53.2 2.2 %invert.1 = (f32[64,64]{1,0:T(8,128)S(1)}, f32[64,512]{1,0:T(8,128)S(1)}, bf16[384,512]{1,0:T(8,128)(2,1)S(1)}) custom-call(f32[64,64]{1,0:T(8,128)S(1)} %add_add_fusion.gram_ref, f32[64,512]{1,0:T(8,128)S(1)} %get-tuple-element.47.factor_ref), custom_call_target="tpu_custom_call" | custom-call | flops 2000000000 | bytes 500000 | tf_op jit(solution)/shard_map/invert/pallas_call | solution.py:69
  55.4 2.5 %all-to-all-done = f32[32,16,128]{2,1,0:T(8,128)S(1)} async-done(((f32[32,16,128]{2,1,0:T(8,128)}), f32[32,16,128]{2,1,0:T(8,128)S(1)}, u32[]{:S(2)}, u32[]{:S(2)}) %all-to-all-start) | async-done | bytes 262176 | tf_op jit(solution)/shard_map/all_to_all | solution.py:345
  59.1 2.8 %collective-permute-start.14 = (f32[16,128]{1,0:T(8,128)S(1)}, f32[16,128]{1,0:T(8,128)S(1)}, u32[]{:S(2)}, u32[]{:S(2)}) collective-permute-start(f32[16,128]{1,0:T(8,128)S(1)} %add.52), channel_id=1, source_target_pairs={{0,6},{1,7},{2,4},{3,5},{4,2},{5,3},{6,0},{7,1},{8,14},{9,15},{10,... | collective-permute-start | bytes 24584 | tf_op jit(solution)/shard_map/ppermute | solution.py:53
  64.0 3.0 %collective-permute-done.15 = f32[16,128]{1,0:T(8,128)S(1)} collective-permute-done((f32[16,128]{1,0:T(8,128)S(1)}, f32[16,128]{1,0:T(8,128)S(1)}, u32[]{:S(2)}, u32[]{:S(2)}) %collective-permute-start.15) | collective-permute-done | bytes 8224 | tf_op jit(solution)/shard_map/ppermute | solution.py:53
  67.7 4.0 %collective-permute-done.17 = bf16[32,640]{1,0:T(8,128)(2,1)S(1)} collective-permute-done((bf16[32,640]{1,0:T(8,128)(2,1)S(1)}, bf16[32,640]{1,0:T(8,128)(2,1)S(1)}, u32[]{:S(2)}, u32[]{:S(2)}) %collective-permute-start.17) | collective-permute-done | bytes 40992 | tf_op jit(solution)/shard_map/ppermute | solution.py:53
  71.9 4.3 %collective-permute-start.19 = (bf16[2,32,640]{2,1,0:T(8,128)(2,1)S(1)}, bf16[2,32,640]{2,1,0:T(8,128)(2,1)S(1)}, u32[]{:S(2)}, u32[]{:S(2)}) collective-permute-start(bf16[2,32,640]{2,1,0:T(8,128)(2,1)S(1)} %pad_maximum_fusion), channel_id=1, source_target_pairs={{0,40},{8,32},{16,56},{24,48},{32,8},{40,0},{48,24},{56,16},{64,10... | collective-permute-start | bytes 245768 | tf_op jit(solution)/shard_map/ppermute | solution.py:53
  76.8 2.2 %collective-permute-done.18 = bf16[2,32,640]{2,1,0:T(8,128)(2,1)S(1)} collective-permute-done((bf16[2,32,640]{2,1,0:T(8,128)(2,1)S(1)}, bf16[2,32,640]{2,1,0:T(8,128)(2,1)S(1)}, u32[]{:S(2)}, u32[]{:S(2)}) %collective-permute-start.18) | collective-permute-done | bytes 81952 | tf_op jit(solution)/shard_map/ppermute | solution.py:53
  79.1 2.4 %collective-permute-done.19 = bf16[2,32,640]{2,1,0:T(8,128)(2,1)S(1)} collective-permute-done((bf16[2,32,640]{2,1,0:T(8,128)(2,1)S(1)}, bf16[2,32,640]{2,1,0:T(8,128)(2,1)S(1)}, u32[]{:S(2)}, u32[]{:S(2)}) %collective-permute-start.19) | collective-permute-done | bytes 81952 | tf_op jit(solution)/shard_map/ppermute | solution.py:53
  83.1 2.5 %collective-permute-start.21 = (bf16[8,32,640]{2,1,0:T(8,128)(2,1)S(1)}, bf16[8,32,640]{2,1,0:T(8,128)(2,1)S(1)}, u32[]{:S(2)}, u32[]{:S(2)}) collective-permute-start(bf16[8,32,640]{2,1,0:T(8,128)(2,1)S(1)} %constant_dynamic-update-slice_fusion.refs_0_), channel_id=1, source_target_pairs={{0,192},{8,200},{16,208},{24,216},{32,224},{40,232},{48,240},{56,2... | collective-permute-start | bytes 983048 | tf_op jit(solution)/shard_map/ppermute | solution.py:53
  88.9 5.0 %collective-permute-done.23.refs_0_ = bf16[8,32,640]{2,1,0:T(8,128)(2,1)S(1)} collective-permute-done((bf16[8,32,640]{2,1,0:T(8,128)(2,1)S(1)}, bf16[8,32,640]{2,1,0:T(8,128)(2,1)S(1)}, u32[]{:S(2)}, u32[]{:S(2)}) %collective-permute-start.23) | collective-permute-done | bytes 327712 | tf_op jit(solution)/shard_map/ppermute | solution.py:53
  95.1 2.1 %collective-permute-done.21.refs_0_ = bf16[8,32,640]{2,1,0:T(8,128)(2,1)S(1)} collective-permute-done((bf16[8,32,640]{2,1,0:T(8,128)(2,1)S(1)}, bf16[8,32,640]{2,1,0:T(8,128)(2,1)S(1)}, u32[]{:S(2)}, u32[]{:S(2)}) %collective-permute-start.21) | collective-permute-done | bytes 327712 | tf_op jit(solution)/shard_map/ppermute | solution.py:53
  (58 shorter events, 22.3 us)
Async XLA Ops:
  2.6 5.2 %collective-permute-start = (f32[64,128]{1,0:T(8,128)S(1)}, f32[64,128]{1,0:T(8,128)S(1)}, u32[]{:S(2)}, u32[]{:S(2)}) collective-permute-start(f32[64,128]{1,0:T(8,128)S(1)} %get-tuple-element.38), channel_id=1, source_target_pairs={{0,192},{8,200},{16,208},{24,216},{32,224},{40,232},{48,240},{56,2... | collective-permute-start | bytes 98312 | tf_op jit(solution)/shard_map/ppermute | solution.py:53
  5.7 5.4 %collective-permute-start.1 = (f32[64,128]{1,0:T(8,128)S(1)}, f32[64,128]{1,0:T(8,128)S(1)}, u32[]{:S(2)}, u32[]{:S(2)}) collective-permute-start(f32[64,128]{1,0:T(8,128)S(1)} %get-tuple-element.39), channel_id=1, source_target_pairs={{0,128},{8,136},{16,144},{24,152},{32,160},{40,168},{48,176},{56,1... | collective-permute-start | bytes 98312 | tf_op jit(solution)/shard_map/ppermute | solution.py:53
  6.3 4.8 %collective-permute-start.2 = (f32[64,128]{1,0:T(8,128)S(1)}, f32[64,128]{1,0:T(8,128)S(1)}, u32[]{:S(2)}, u32[]{:S(2)}) collective-permute-start(f32[64,128]{1,0:T(8,128)S(1)} %get-tuple-element.40), channel_id=1, source_target_pairs={{0,64},{8,72},{16,80},{24,88},{32,96},{40,104},{48,112},{56,120},{... | collective-permute-start | bytes 98312 | tf_op jit(solution)/shard_map/ppermute | solution.py:53
  11.1 4.0 %collective-permute-start.3 = (f32[64,128]{1,0:T(8,128)S(1)}, f32[64,128]{1,0:T(8,128)S(1)}, u32[]{:S(2)}, u32[]{:S(2)}) collective-permute-start(f32[64,128]{1,0:T(8,128)S(1)} %add_add_fusion.1), channel_id=1, source_target_pairs={{0,8},{8,0},{16,24},{24,16},{32,40},{40,32},{48,56},{56,48},{64,72... | collective-permute-start | bytes 98312 | tf_op jit(solution)/shard_map/ppermute | solution.py:53
  15.1 3.9 %collective-permute-start.4 = (f32[64,128]{1,0:T(8,128)S(1)}, f32[64,128]{1,0:T(8,128)S(1)}, u32[]{:S(2)}, u32[]{:S(2)}) collective-permute-start(f32[64,128]{1,0:T(8,128)S(1)} %add.45), channel_id=1, source_target_pairs={{0,24},{8,16},{16,8},{24,0},{32,56},{40,48},{48,40},{56,32},{64,88... | collective-permute-start | bytes 98312 | tf_op jit(solution)/shard_map/ppermute | solution.py:53
  19.1 7.7 %collective-permute-start.5 = (f32[64,128]{1,0:T(8,128)S(1)}, f32[64,128]{1,0:T(8,128)S(1)}, u32[]{:S(2)}, u32[]{:S(2)}) collective-permute-start(f32[64,128]{1,0:T(8,128)S(1)} %add.46), channel_id=1, source_target_pairs={{0,56},{8,48},{16,40},{24,32},{32,24},{40,16},{48,8},{56,0},{64,12... | collective-permute-start | bytes 98312 | tf_op jit(solution)/shard_map/ppermute | solution.py:53
  26.8 5.1 %collective-permute-start.6 = (f32[64,128]{1,0:T(8,128)S(1)}, f32[64,128]{1,0:T(8,128)S(1)}, u32[]{:S(2)}, u32[]{:S(2)}) collective-permute-start(f32[64,128]{1,0:T(8,128)S(1)} %add_multiply_fusion.refs_0_), channel_id=1, source_target_pairs={{0,192},{8,200},{16,208},{24,216},{32,224},{40,232},{48,240},{56,2... | collective-permute-start | bytes 98312 | tf_op jit(solution)/shard_map/ppermute | solution.py:53
  28.1 5.4 %collective-permute-start.7 = (f32[64,128]{1,0:T(8,128)S(1)}, f32[64,128]{1,0:T(8,128)S(1)}, u32[]{:S(2)}, u32[]{:S(2)}) collective-permute-start(f32[64,128]{1,0:T(8,128)S(1)} %add_multiply_fusion.refs_0_), channel_id=1, source_target_pairs={{0,128},{8,136},{16,144},{24,152},{32,160},{40,168},{48,176},{56,1... | collective-permute-start | bytes 98312 | tf_op jit(solution)/shard_map/ppermute | solution.py:53
  29.0 4.5 %collective-permute-start.8 = (f32[64,128]{1,0:T(8,128)S(1)}, f32[64,128]{1,0:T(8,128)S(1)}, u32[]{:S(2)}, u32[]{:S(2)}) collective-permute-start(f32[64,128]{1,0:T(8,128)S(1)} %add_multiply_fusion.refs_0_), channel_id=1, source_target_pairs={{0,64},{8,72},{16,80},{24,88},{32,96},{40,104},{48,112},{56,120},{... | collective-permute-start | bytes 98312 | tf_op jit(solution)/shard_map/ppermute | solution.py:53
  33.8 1.7 %collective-permute-start.9 = (f32[64,64]{1,0:T(8,128)S(1)}, f32[64,64]{1,0:T(8,128)S(1)}, u32[]{:S(2)}, u32[]{:S(2)}) collective-permute-start(f32[64,64]{1,0:T(8,128)S(1)} %get-tuple-element.41), channel_id=1, source_target_pairs={{0,1},{1,0},{2,3},{3,2},{4,5},{5,4},{6,7},{7,6},{8,9},{9,8},{10,11... | collective-permute-start | bytes 49160 | tf_op jit(solution)/shard_map/ppermute | solution.py:53
  35.5 22.3 %all-to-all-start = ((f32[32,16,128]{2,1,0:T(8,128)}), f32[32,16,128]{2,1,0:T(8,128)S(1)}, u32[]{:S(2)}, u32[]{:S(2)}) async-start(f32[32,16,128]{2,1,0:T(8,128)} %project.1), calls=%async_computation | async-start | bytes 524288 | tf_op jit(solution)/shard_map/all_to_all | solution.py:345
  44.9 5.2 %collective-permute-start.10 = (f32[64,64]{1,0:T(8,128)S(1)}, f32[64,64]{1,0:T(8,128)S(1)}, u32[]{:S(2)}, u32[]{:S(2)}) collective-permute-start(f32[64,64]{1,0:T(8,128)S(1)} %add.48), channel_id=1, source_target_pairs={{0,6},{1,7},{2,4},{3,5},{4,2},{5,3},{6,0},{7,1},{8,14},{9,15},{10,... | collective-permute-start | bytes 49160 | tf_op jit(solution)/shard_map/ppermute | solution.py:53
  47.7 5.4 %collective-permute-start.11 = (f32[64,64]{1,0:T(8,128)S(1)}, f32[64,64]{1,0:T(8,128)S(1)}, u32[]{:S(2)}, u32[]{:S(2)}) collective-permute-start(f32[64,64]{1,0:T(8,128)S(1)} %add.48), channel_id=1, source_target_pairs={{0,4},{1,5},{2,6},{3,7},{4,0},{5,1},{6,2},{7,3},{8,12},{9,13},{10,... | collective-permute-start | bytes 49160 | tf_op jit(solution)/shard_map/ppermute | solution.py:53
  48.5 4.6 %collective-permute-start.12 = (f32[64,64]{1,0:T(8,128)S(1)}, f32[64,64]{1,0:T(8,128)S(1)}, u32[]{:S(2)}, u32[]{:S(2)}) collective-permute-start(f32[64,64]{1,0:T(8,128)S(1)} %add.48), channel_id=1, source_target_pairs={{0,2},{1,3},{2,0},{3,1},{4,6},{5,7},{6,4},{7,5},{8,10},{9,11},{10,... | collective-permute-start | bytes 49160 | tf_op jit(solution)/shard_map/ppermute | solution.py:53
  59.1 4.9 %collective-permute-start.14 = (f32[16,128]{1,0:T(8,128)S(1)}, f32[16,128]{1,0:T(8,128)S(1)}, u32[]{:S(2)}, u32[]{:S(2)}) collective-permute-start(f32[16,128]{1,0:T(8,128)S(1)} %add.52), channel_id=1, source_target_pairs={{0,6},{1,7},{2,4},{3,5},{4,2},{5,3},{6,0},{7,1},{8,14},{9,15},{10,... | collective-permute-start | bytes 24584 | tf_op jit(solution)/shard_map/ppermute | solution.py:53
  61.9 5.2 %collective-permute-start.15 = (f32[16,128]{1,0:T(8,128)S(1)}, f32[16,128]{1,0:T(8,128)S(1)}, u32[]{:S(2)}, u32[]{:S(2)}) collective-permute-start(f32[16,128]{1,0:T(8,128)S(1)} %add.52), channel_id=1, source_target_pairs={{0,4},{1,5},{2,6},{3,7},{4,0},{5,1},{6,2},{7,3},{8,12},{9,13},{10,... | collective-permute-start | bytes 24584 | tf_op jit(solution)/shard_map/ppermute | solution.py:53
  62.7 4.4 %collective-permute-start.16 = (f32[16,128]{1,0:T(8,128)S(1)}, f32[16,128]{1,0:T(8,128)S(1)}, u32[]{:S(2)}, u32[]{:S(2)}) collective-permute-start(f32[16,128]{1,0:T(8,128)S(1)} %add.52), channel_id=1, source_target_pairs={{0,2},{1,3},{2,0},{3,1},{4,6},{5,7},{6,4},{7,5},{8,10},{9,11},{10,... | collective-permute-start | bytes 24584 | tf_op jit(solution)/shard_map/ppermute | solution.py:53
  67.6 4.1 %collective-permute-start.17 = (bf16[32,640]{1,0:T(8,128)(2,1)S(1)}, bf16[32,640]{1,0:T(8,128)(2,1)S(1)}, u32[]{:S(2)}, u32[]{:S(2)}) collective-permute-start(bf16[32,640]{1,0:T(8,128)(2,1)S(1)} %get-tuple-element.54), channel_id=1, source_target_pairs={{0,8},{8,0},{16,24},{24,16},{32,40},{40,32},{48,56},{56,48},{64,72... | collective-permute-start | bytes 122888 | tf_op jit(solution)/shard_map/ppermute | solution.py:53
  71.7 7.4 %collective-permute-start.18 = (bf16[2,32,640]{2,1,0:T(8,128)(2,1)S(1)}, bf16[2,32,640]{2,1,0:T(8,128)(2,1)S(1)}, u32[]{:S(2)}, u32[]{:S(2)}) collective-permute-start(bf16[2,32,640]{2,1,0:T(8,128)(2,1)S(1)} %pad_maximum_fusion), channel_id=1, source_target_pairs={{0,48},{8,56},{16,32},{24,40},{32,16},{40,24},{48,0},{56,8},{64,11... | collective-permute-start | bytes 245768 | tf_op jit(solution)/shard_map/ppermute | solution.py:53
  71.9 9.6 %collective-permute-start.19 = (bf16[2,32,640]{2,1,0:T(8,128)(2,1)S(1)}, bf16[2,32,640]{2,1,0:T(8,128)(2,1)S(1)}, u32[]{:S(2)}, u32[]{:S(2)}) collective-permute-start(bf16[2,32,640]{2,1,0:T(8,128)(2,1)S(1)} %pad_maximum_fusion), channel_id=1, source_target_pairs={{0,40},{8,32},{16,56},{24,48},{32,8},{40,0},{48,24},{56,16},{64,10... | collective-permute-start | bytes 245768 | tf_op jit(solution)/shard_map/ppermute | solution.py:53
  76.2 6.2 %collective-permute-start.20 = (bf16[2,32,640]{2,1,0:T(8,128)(2,1)S(1)}, bf16[2,32,640]{2,1,0:T(8,128)(2,1)S(1)}, u32[]{:S(2)}, u32[]{:S(2)}) collective-permute-start(bf16[2,32,640]{2,1,0:T(8,128)(2,1)S(1)} %pad_maximum_fusion), channel_id=1, source_target_pairs={{0,16},{8,24},{16,0},{24,8},{32,48},{40,56},{48,32},{56,40},{64,80... | collective-permute-start | bytes 245768 | tf_op jit(solution)/shard_map/ppermute | solution.py:53
  82.3 11.6 %collective-permute-start.23 = (bf16[8,32,640]{2,1,0:T(8,128)(2,1)S(1)}, bf16[8,32,640]{2,1,0:T(8,128)(2,1)S(1)}, u32[]{:S(2)}, u32[]{:S(2)}) collective-permute-start(bf16[8,32,640]{2,1,0:T(8,128)(2,1)S(1)} %constant_dynamic-update-slice_fusion.refs_0_), channel_id=1, source_target_pairs={{0,128},{8,136},{16,144},{24,152},{32,160},{40,168},{48,176},{56,1... | collective-permute-start | bytes 983048 | tf_op jit(solution)/shard_map/ppermute | solution.py:53
  83.1 14.1 %collective-permute-start.21 = (bf16[8,32,640]{2,1,0:T(8,128)(2,1)S(1)}, bf16[8,32,640]{2,1,0:T(8,128)(2,1)S(1)}, u32[]{:S(2)}, u32[]{:S(2)}) collective-permute-start(bf16[8,32,640]{2,1,0:T(8,128)(2,1)S(1)} %constant_dynamic-update-slice_fusion.refs_0_), channel_id=1, source_target_pairs={{0,192},{8,200},{16,208},{24,216},{32,224},{40,232},{48,240},{56,2... | collective-permute-start | bytes 983048 | tf_op jit(solution)/shard_map/ppermute | solution.py:53
  85.6 11.6 %collective-permute-start.22 = (bf16[8,32,640]{2,1,0:T(8,128)(2,1)S(1)}, bf16[8,32,640]{2,1,0:T(8,128)(2,1)S(1)}, u32[]{:S(2)}, u32[]{:S(2)}) collective-permute-start(bf16[8,32,640]{2,1,0:T(8,128)(2,1)S(1)} %constant_dynamic-update-slice_fusion.refs_0_), channel_id=1, source_target_pairs={{0,64},{8,72},{16,80},{24,88},{32,96},{40,104},{48,112},{56,120},{... | collective-permute-start | bytes 983048 | tf_op jit(solution)/shard_map/ppermute | solution.py:53
  (4 other events, 29.0 us)
